TPU v7x, 32 devices: a whole 2x2x4 slice. The times are simulated.
32 devices in a mesh: dp: 8 (over z, x), expert: 4 (over y, core).
Axes of the slice: x: 2, y: 2, z: 4, core: 2. Of those that a mesh axis runs over, the one named last changes fastest.
Arguments:
- tokens: bfloat16 [6144, 768], P(('dp', 'expert')), may hold values from -6 to 6
- seq_lengths: int32 [8, 4, 4], P('dp'), may hold values from 1 to 96, 192 in all within a row
- block_perm: int32 [8, 4], P('dp'), may hold values from 0 to 3, each once within a row
- routes: int32 [2, 6144, 2], P(None, ('dp', 'expert')), may hold values from 0 to 11, all different within a row; in each aligned block of 192 rows (0 to 191, 192 to 383, ..., all dimensions but the last counted through in order) at most 48 rows name the same one
- norm_gains: float32 [2, 2, 768], P(None, None, 'dp'), may hold values from 0.5 to 1.5
- w_qkv: float32 [2, 768, 2304], P(None, None, 'dp'), may hold values from -0.21875 to 0.21875
- w_out: float32 [2, 768, 768], P(None, 'dp'), may hold values from -1.25 to 1.25
- w_router: float32 [2, 768, 12], P(None, 'dp'), may hold values from -0.15625 to 0.15625
- w_residual: float32 [12, 12], replicated, may hold values from -1.25 to 1.25
- w_const: float32 [2, 2, 768, 2], P(None, None, 'dp'), may hold values from -0.21875 to 0.21875
- v_const: float32 [2, 2, 768], P(None, None, 'dp'), may hold values from -6 to 6
- w_gate: float32 [2, 8, 768, 2048], P(None, 'expert', None, 'dp'), may hold values from -0.21875 to 0.21875
- w_up: float32 [2, 8, 768, 2048], P(None, 'expert', None, 'dp'), may hold values from -0.21875 to 0.21875
- w_down: float32 [2, 8, 2048, 768], P(None, 'expert', 'dp'), may hold values from -0.125 to 0.125
- cotangent: bfloat16 [6144, 768], P(('dp', 'expert')), may hold values from -6 to 6
Outputs:
- output: bfloat16 [6144, 768], P(('dp', 'expert'))
- tokens_grad: float32 [6144, 768], P(('dp', 'expert'))
- gains_grad: float32 [2, 2, 768], P(None, None, 'dp')
- qkv_grad: float32 [2, 768, 2304], P(None, None, 'dp')
- out_grad: float32 [2, 768, 768], P(None, 'dp')
- router_grad: float32 [2, 768, 12], P(None, 'dp')
- residual_grad: float32 [12, 12], replicated
- const_grad: float32 [2, 2, 768, 2], P(None, None, 'dp')
- vector_grad: float32 [2, 2, 768], P(None, None, 'dp')
- gate_grad: float32 [2, 8, 768, 2048], P(None, 'expert', None, 'dp')
- up_grad: float32 [2, 8, 768, 2048], P(None, 'expert', None, 'dp')
- down_grad: float32 [2, 8, 2048, 768], P(None, 'expert', 'dp')
Inputs may be any that keep to these rules, and one draw needn't show every extreme that they name: `seq_lengths`: entry [g, i] holds the lengths of the 4 sequences of initial device block g * 4 + i, in order; they sum to 192, and the longest is exactly 96. `block_perm`: each row is a permutation of 0 to 3. `routes`: each token names two different targets in each layer: under 8 a feed-forward expert, 8 the zero expert, 9 the copy expert, 10 and 11 the constant experts. In one layer the rows of one device name no target more than 48 times, a bound that some block reaches.
All inputs are finite; a program needn't handle non-finite values.
Results may differ from a plain program's by a relative error of at most 0.017.
The roundings to bfloat16 on the way count: a program that leaves them out, or rounds other values in their place, can miss the bound.
Values may be sent and summed in bfloat16 or wider, within the bound.
A program may use at most 320 MiB of HBM per device.

v0:
```python
import math

import jax
import jax.numpy as jnp
from jax import lax
from jax.sharding import PartitionSpec as P

HEADS = 12
CAP = 48


EPSILON = 1e-05
MASKED = -1e30
HIGH = lax.Precision.HIGHEST


def rms_scale(values):
    return lax.rsqrt(jnp.mean(values * values, axis=-1, keepdims=True) + EPSILON)


def norm_backward(grad_out, values, row_scale, gain_row):
    weighted = grad_out * gain_row
    row_inner = jnp.mean(weighted * values, axis=-1, keepdims=True)
    grad_in = row_scale * weighted - values * row_scale * row_scale * row_scale * row_inner
    grad_gain = jnp.sum(grad_out * values * row_scale, axis=0)
    return (grad_in, grad_gain)


def attention_mask(lengths, row_count):
    doc_ends = jnp.cumsum(lengths)
    places = jnp.arange(row_count, dtype=jnp.int32)
    doc_owner = jnp.sum((places[:, None] >= doc_ends[None, :]).astype(jnp.int32), axis=1)
    same_doc = doc_owner[:, None] == doc_owner[None, :]
    return jnp.logical_and(same_doc, places[:, None] >= places[None, :])


def slot_plan(route_rows, experts, capacity):
    flat_routes = route_rows.reshape(-1)
    labels = jnp.arange(experts, dtype=jnp.int32)
    onehot = (flat_routes[:, None] == labels[None, :]).astype(jnp.int32)
    before = jnp.cumsum(onehot, axis=0) - 1
    slot_place = jnp.sum(before * onehot, axis=1)
    is_valid = flat_routes < experts
    slot_ids = jnp.where(is_valid, flat_routes * capacity + slot_place, experts * capacity)
    pair_ids = jnp.arange(flat_routes.shape[0], dtype=jnp.int32)
    owner_pair = jnp.zeros((experts * capacity,), jnp.int32).at[slot_ids].set(pair_ids, mode="drop")
    filled = jnp.zeros((experts * capacity,), jnp.float32).at[slot_ids].set(1.0, mode="drop")
    return (slot_ids, is_valid, owner_pair, filled)


def attention_forward(attn_in, qkv_weight, attend_mask, head_count):
    row_count = attn_in.shape[0]
    qkv_rows = jnp.dot(attn_in, qkv_weight, preferred_element_type=jnp.float32).astype(jnp.bfloat16)
    pieces = qkv_rows.reshape(row_count, 3, head_count, -1)
    query_rows, key_rows, value_rows = (pieces[:, 0], pieces[:, 1], pieces[:, 2])
    factor = 1.0 / math.sqrt(query_rows.shape[-1])
    scores = (
        jnp.einsum("qhd,khd->hqk", query_rows, key_rows, preferred_element_type=jnp.float32)
        * factor
    )
    scores = jnp.where(attend_mask[None], scores, MASKED)
    row_peak = jnp.max(scores, axis=-1, keepdims=True)
    exponent = jnp.exp(scores - row_peak)
    row_total = jnp.sum(exponent, axis=-1, keepdims=True)
    softmaxed = exponent / row_total
    logsum = row_peak + jnp.log(row_total)
    mixed_heads = jnp.einsum(
        "hqk,khd->qhd",
        softmaxed.astype(jnp.bfloat16),
        value_rows,
        preferred_element_type=jnp.float32,
    )
    attn_out = mixed_heads.reshape(row_count, -1).astype(jnp.bfloat16)
    return (qkv_rows, logsum, attn_out)


def attention_backward(grad_attn, qkv_rows, logsum, attn_in, qkv_weight, attend_mask, head_count):
    row_count = qkv_rows.shape[0]
    pieces = qkv_rows.reshape(row_count, 3, head_count, -1)
    query_rows, key_rows, value_rows = (pieces[:, 0], pieces[:, 1], pieces[:, 2])
    factor = 1.0 / math.sqrt(query_rows.shape[-1])
    scores = (
        jnp.einsum("qhd,khd->hqk", query_rows, key_rows, preferred_element_type=jnp.float32)
        * factor
    )
    scores = jnp.where(attend_mask[None], scores, MASKED)
    softmaxed = jnp.exp(scores - logsum)
    grad_heads = grad_attn.reshape(row_count, head_count, -1)
    grad_probs = jnp.einsum(
        "qhd,khd->hqk", grad_heads, value_rows, preferred_element_type=jnp.float32
    )
    row_inner = jnp.sum(softmaxed * grad_probs, axis=-1, keepdims=True)
    grad_scores = (softmaxed * (grad_probs - row_inner)).astype(jnp.bfloat16)
    grad_query = (
        jnp.einsum("hqk,khd->qhd", grad_scores, key_rows, preferred_element_type=jnp.float32)
        * factor
    )
    grad_key = (
        jnp.einsum("hqk,qhd->khd", grad_scores, query_rows, preferred_element_type=jnp.float32)
        * factor
    )
    grad_value = jnp.einsum(
        "hqk,qhd->khd",
        softmaxed.astype(jnp.bfloat16),
        grad_heads,
        preferred_element_type=jnp.float32,
    )
    grad_qkv = (
        jnp.stack([grad_query, grad_key, grad_value], axis=1)
        .reshape(row_count, -1)
        .astype(jnp.bfloat16)
    )
    grad_weight = jnp.einsum("td,te->de", attn_in, grad_qkv, preferred_element_type=jnp.float32)
    grad_in = jnp.einsum("te,de->td", grad_qkv, qkv_weight, preferred_element_type=jnp.float32)
    return (grad_weight, grad_in)


def per_device(
    tokens,
    seq_lengths,
    block_perm,
    routes,
    norm_gains,
    w_qkv,
    w_out,
    w_router,
    w_residual,
    w_const,
    v_const,
    w_gate,
    w_up,
    w_down,
    cotangent,
):
    row_count, model_width = tokens.shape
    owners = lax.axis_size("expert")
    local_experts = w_gate.shape[1]
    experts = local_experts * owners
    layers = routes.shape[0]
    head_count = HEADS
    my_place = lax.axis_index("expert")
    owner_ids = jnp.arange(owners, dtype=jnp.int32)
    perm_row = block_perm[0]
    target = jnp.sum(perm_row * (owner_ids == my_place).astype(jnp.int32))
    source = jnp.sum(owner_ids * (perm_row == my_place).astype(jnp.int32))
    send_pick = (owner_ids == target)[:, None, None]
    tokens_out = jnp.where(send_pick, tokens[None], jnp.zeros((), jnp.bfloat16))
    cot_out = jnp.where(send_pick, cotangent[None], jnp.zeros((), jnp.bfloat16))
    tokens_in, cot_in = (
        lax.all_to_all(tokens_out, "expert", split_axis=0, concat_axis=0, tiled=True),
        lax.all_to_all(cot_out, "expert", split_axis=0, concat_axis=0, tiled=True),
    )
    dealt_tokens = lax.dynamic_index_in_dim(tokens_in, source, 0, keepdims=False)
    dealt_cot = lax.dynamic_index_in_dim(cot_in, source, 0, keepdims=False)
    dealt_lengths = lax.dynamic_index_in_dim(seq_lengths[0], source, 0, keepdims=False)
    gains_all, qkv_all, out_all, router_all, const_all, vector_all = (
        lax.all_gather(norm_gains.astype(jnp.bfloat16), "dp", axis=2, tiled=True),
        lax.all_gather(w_qkv.astype(jnp.bfloat16), "dp", axis=2, tiled=True),
        lax.all_gather(w_out.astype(jnp.bfloat16), "dp", axis=1, tiled=True),
        lax.all_gather(w_router.astype(jnp.bfloat16), "dp", axis=1, tiled=True),
        lax.all_gather(w_const.astype(jnp.bfloat16), "dp", axis=2, tiled=True),
        lax.all_gather(v_const.astype(jnp.bfloat16), "dp", axis=2, tiled=True),
    )
    gate_all, up_all, down_all = (
        lax.all_gather(w_gate.astype(jnp.bfloat16), "dp", axis=3, tiled=True),
        lax.all_gather(w_up.astype(jnp.bfloat16), "dp", axis=3, tiled=True),
        lax.all_gather(w_down.astype(jnp.bfloat16), "dp", axis=2, tiled=True),
    )
    attend_mask = attention_mask(dealt_lengths, row_count)
    labels = jnp.arange(w_residual.shape[0], dtype=jnp.int32)
    const_ids = experts + 2 + jnp.arange(2, dtype=jnp.int32)
    stream = dealt_tokens.astype(jnp.float32)
    prev_logits = None
    kept_state = []
    for layer_index in range(layers):
        gains_layer = gains_all[layer_index].astype(jnp.float32)
        scale_attn = rms_scale(stream)
        attn_in = (stream * scale_attn * gains_layer[0]).astype(jnp.bfloat16)
        qkv_rows, logsum, attn_out = attention_forward(
            attn_in, qkv_all[layer_index], attend_mask, head_count
        )
        stream_mid = stream + jnp.dot(
            attn_out, out_all[layer_index], preferred_element_type=jnp.float32
        )
        scale_ffn = rms_scale(stream_mid)
        hidden_full = stream_mid * scale_ffn * gains_layer[1]
        hidden = hidden_full.astype(jnp.bfloat16)
        logits = jnp.dot(hidden, router_all[layer_index], preferred_element_type=jnp.float32)
        if prev_logits is not None:
            logits = logits + jnp.dot(prev_logits, w_residual, precision=HIGH)
        route_rows = routes[layer_index]
        route_picks = (route_rows[:, :, None] == labels[None, None, :]).astype(jnp.float32)
        gate_share = jax.nn.softmax(jnp.sum(route_picks * logits[:, None, :], axis=-1), axis=-1)
        slot_ids, is_valid, owner_pair, filled = slot_plan(route_rows, experts, CAP)
        token_of_slot = owner_pair // 2
        outgoing = jnp.where(
            filled[:, None] > 0, hidden[token_of_slot], jnp.zeros((), jnp.bfloat16)
        )
        outgoing = outgoing.reshape(owners, local_experts, CAP, model_width)
        gate_weight = gate_all[layer_index]
        up_weight = up_all[layer_index]
        down_weight = down_all[layer_index]
        received = lax.all_to_all(outgoing, "expert", split_axis=0, concat_axis=0, tiled=True)
        gate_proj = jnp.einsum(
            "sjcd,jdf->sjcf", received, gate_weight, preferred_element_type=jnp.float32
        )
        up_proj = jnp.einsum(
            "sjcd,jdf->sjcf", received, up_weight, preferred_element_type=jnp.float32
        )
        run_activated = (jax.nn.silu(gate_proj) * up_proj).astype(jnp.bfloat16)
        result = jnp.einsum(
            "sjcf,jfd->sjcd", run_activated, down_weight, preferred_element_type=jnp.float32
        ).astype(jnp.bfloat16)
        received, gate_proj, up_proj, result = (received, gate_proj, up_proj, result)
        returned = lax.all_to_all(
            result, "expert", split_axis=0, concat_axis=0, tiled=True
        ).reshape(experts * CAP, model_width)
        valid_f = is_valid.astype(jnp.float32)
        pair_out = (
            returned[jnp.minimum(slot_ids, experts * CAP - 1)].astype(jnp.float32)
            * valid_f[:, None]
        ).reshape(row_count, 2, model_width)
        valid_pairs = valid_f.reshape(row_count, 2)
        ffn_weight = gate_share * valid_pairs
        copy_pick = (route_rows == experts + 1).astype(jnp.float32)
        copy_weight = jnp.sum(gate_share * copy_pick, axis=1)
        const_pick = (route_rows[:, :, None] == const_ids[None, None, :]).astype(jnp.float32)
        const_weight = jnp.sum(gate_share[:, :, None] * const_pick, axis=1)
        const_probs = jax.nn.softmax(
            jnp.einsum(
                "td,jdc->tjc", hidden, const_all[layer_index], preferred_element_type=jnp.float32
            ),
            axis=-1,
        )
        vector_f = vector_all[layer_index].astype(jnp.float32)
        local_weight = copy_weight + jnp.sum(const_weight * const_probs[:, :, 0], axis=1)
        moe_out = (
            jnp.sum(ffn_weight[:, :, None] * pair_out, axis=1) + local_weight[:, None] * hidden_full
        )
        moe_out = moe_out + jnp.dot(const_weight * const_probs[:, :, 1], vector_f, precision=HIGH)
        kept_state.append(
            (
                stream,
                scale_attn,
                attn_in,
                qkv_rows,
                logsum,
                attn_out,
                stream_mid,
                scale_ffn,
                hidden_full,
                hidden,
                prev_logits,
                route_picks,
                gate_share,
                ffn_weight,
                valid_pairs,
                copy_pick,
                const_pick,
                const_weight,
                const_probs,
                local_weight,
                pair_out,
                owner_pair,
                filled,
                received,
                gate_proj,
                up_proj,
            )
        )
        stream = stream_mid + moe_out
        prev_logits = logits
    output_dealt = stream.astype(jnp.bfloat16)
    grad_stream = dealt_cot.astype(jnp.float32)
    extra_logits = None
    dense_parts = []
    expert_parts = []
    residual_part = None
    for layer_index in reversed(range(layers)):
        (
            stream_in,
            scale_attn,
            attn_in,
            qkv_rows,
            logsum,
            attn_out,
            stream_mid,
            scale_ffn,
            hidden_full,
            hidden,
            prev_logits,
            route_picks,
            gate_share,
            ffn_weight,
            valid_pairs,
            copy_pick,
            const_pick,
            const_weight,
            const_probs,
            local_weight,
            pair_out,
            owner_pair,
            filled,
            received,
            gate_proj,
            up_proj,
        ) = kept_state[layer_index]
        gains_layer = gains_all[layer_index].astype(jnp.float32)
        vector_f = vector_all[layer_index].astype(jnp.float32)
        grad_moe = grad_stream
        dot_ffn = jnp.sum(grad_moe[:, None, :] * pair_out, axis=-1)
        dot_hidden = jnp.sum(grad_moe * hidden_full, axis=-1)
        dot_vector = jnp.dot(grad_moe, vector_f.T, precision=HIGH)
        const_value = const_probs[:, :, 0] * dot_hidden[:, None] + const_probs[:, :, 1] * dot_vector
        grad_share = (
            valid_pairs * dot_ffn
            + copy_pick * dot_hidden[:, None]
            + jnp.sum(const_pick * const_value[:, None, :], axis=-1)
        )
        grad_chosen = gate_share * (
            grad_share - jnp.sum(gate_share * grad_share, axis=1, keepdims=True)
        )
        grad_logits = jnp.sum(grad_chosen[:, :, None] * route_picks, axis=1)
        if extra_logits is not None:
            grad_logits = grad_logits + extra_logits
        grad_cprob = jnp.stack(
            [const_weight * dot_hidden[:, None], const_weight * dot_vector], axis=-1
        )
        grad_clog = const_probs * (
            grad_cprob - jnp.sum(const_probs * grad_cprob, axis=-1, keepdims=True)
        )
        router_f = router_all[layer_index].astype(jnp.float32)
        const_f = const_all[layer_index].astype(jnp.float32)
        grad_hidden = jnp.dot(grad_logits, router_f.T, precision=HIGH)
        grad_hidden = grad_hidden + jnp.einsum("tjc,jdc->td", grad_clog, const_f, precision=HIGH)
        hidden_wide = hidden.astype(jnp.float32)
        router_part = jnp.dot(hidden_wide.T, grad_logits, precision=HIGH)
        const_part = jnp.einsum("td,tjc->jdc", hidden_wide, grad_clog, precision=HIGH)
        vector_part = jnp.dot((const_weight * const_probs[:, :, 1]).T, grad_moe, precision=HIGH)
        if prev_logits is not None:
            residual_part = jnp.dot(prev_logits.T, grad_logits, precision=HIGH)
            extra_logits = jnp.dot(grad_logits, w_residual.T, precision=HIGH)
        else:
            extra_logits = None
        token_of_slot = owner_pair // 2
        slot_share = ffn_weight.reshape(-1)[owner_pair] * filled
        grad_send = (grad_moe[token_of_slot] * slot_share[:, None]).astype(jnp.bfloat16)
        grad_send = grad_send.reshape(owners, local_experts, CAP, model_width)
        at_owner = lax.all_to_all(grad_send, "expert", split_axis=0, concat_axis=0, tiled=True)
        gate_weight = gate_all[layer_index]
        up_weight = up_all[layer_index]
        down_weight = down_all[layer_index]
        grad_act = jnp.einsum(
            "sjcd,jfd->sjcf", at_owner, down_weight, preferred_element_type=jnp.float32
        )
        sigma = jax.nn.sigmoid(gate_proj)
        swish = gate_proj * sigma
        grad_gate_proj = (grad_act * up_proj * sigma * (1.0 + gate_proj * (1.0 - sigma))).astype(
            jnp.bfloat16
        )
        grad_up_proj = (grad_act * swish).astype(jnp.bfloat16)
        activated = (swish * up_proj).astype(jnp.bfloat16)
        down_part = jnp.einsum(
            "sjcf,sjcd->jfd", activated, at_owner, preferred_element_type=jnp.float32
        )
        gate_part = jnp.einsum(
            "sjcd,sjcf->jdf", received, grad_gate_proj, preferred_element_type=jnp.float32
        )
        up_part = jnp.einsum(
            "sjcd,sjcf->jdf", received, grad_up_proj, preferred_element_type=jnp.float32
        )
        grad_expert_in = jnp.einsum(
            "sjcf,jdf->sjcd", grad_gate_proj, gate_weight, preferred_element_type=jnp.float32
        )
        grad_expert_in = (
            grad_expert_in
            + jnp.einsum(
                "sjcf,jdf->sjcd", grad_up_proj, up_weight, preferred_element_type=jnp.float32
            )
        ).astype(jnp.bfloat16)
        grad_back = lax.all_to_all(
            grad_expert_in, "expert", split_axis=0, concat_axis=0, tiled=True
        ).reshape(experts * CAP, model_width)
        grad_hidden = grad_hidden + jnp.zeros((row_count, model_width), jnp.float32).at[
            token_of_slot
        ].add(grad_back.astype(jnp.float32) * filled[:, None])
        grad_full = grad_hidden + grad_moe * local_weight[:, None]
        grad_mid, gain_ffn_part = norm_backward(grad_full, stream_mid, scale_ffn, gains_layer[1])
        grad_mid = grad_mid + grad_moe
        grad_branch = grad_mid.astype(jnp.bfloat16)
        out_part = jnp.einsum(
            "td,te->de", attn_out, grad_branch, preferred_element_type=jnp.float32
        )
        grad_attn = jnp.einsum(
            "te,de->td", grad_branch, out_all[layer_index], preferred_element_type=jnp.float32
        ).astype(jnp.bfloat16)
        qkv_part, grad_attn_in = attention_backward(
            grad_attn, qkv_rows, logsum, attn_in, qkv_all[layer_index], attend_mask, head_count
        )
        grad_in, gain_attn_part = norm_backward(grad_attn_in, stream_in, scale_attn, gains_layer[0])
        grad_stream = grad_in + grad_mid
        dense_parts.append(
            (
                jnp.stack([gain_attn_part, gain_ffn_part]),
                qkv_part,
                out_part,
                router_part,
                const_part,
                vector_part,
            )
        )
        expert_parts.append((gate_part, up_part, down_part))
    dense_parts = dense_parts[::-1]
    expert_parts = expert_parts[::-1]
    gains_local = jnp.stack([layer_part[0] for layer_part in dense_parts])
    qkv_local = jnp.stack([layer_part[1] for layer_part in dense_parts])
    out_local = jnp.stack([layer_part[2] for layer_part in dense_parts])
    router_local = jnp.stack([layer_part[3] for layer_part in dense_parts])
    const_local = jnp.stack([layer_part[4] for layer_part in dense_parts])
    vector_local = jnp.stack([layer_part[5] for layer_part in dense_parts])
    gate_stack = jnp.stack([layer_part[0] for layer_part in expert_parts])
    up_stack = jnp.stack([layer_part[1] for layer_part in expert_parts])
    down_stack = jnp.stack([layer_part[2] for layer_part in expert_parts])
    gate_grad, up_grad, down_grad = (
        lax.psum_scatter(gate_stack, "dp", scatter_dimension=3, tiled=True),
        lax.psum_scatter(up_stack, "dp", scatter_dimension=3, tiled=True),
        lax.psum_scatter(down_stack, "dp", scatter_dimension=2, tiled=True),
    )
    gains_share, qkv_share, out_share, router_share, const_share, vector_share = (
        lax.psum_scatter(gains_local, "dp", scatter_dimension=2, tiled=True),
        lax.psum_scatter(qkv_local, "dp", scatter_dimension=2, tiled=True),
        lax.psum_scatter(out_local, "dp", scatter_dimension=1, tiled=True),
        lax.psum_scatter(router_local, "dp", scatter_dimension=1, tiled=True),
        lax.psum_scatter(const_local, "dp", scatter_dimension=2, tiled=True),
        lax.psum_scatter(vector_local, "dp", scatter_dimension=2, tiled=True),
    )
    gains_grad, qkv_grad, out_grad, router_grad, const_grad, vector_grad = lax.psum(
        (gains_share, qkv_share, out_share, router_share, const_share, vector_share), "expert"
    )
    residual_grad = lax.psum(residual_part, ("dp", "expert"))
    back_pick = (owner_ids == source)[:, None, None]
    output_home = jnp.where(back_pick, output_dealt.astype(jnp.float32)[None], 0.0)
    grad_home = jnp.where(back_pick, grad_stream[None], 0.0)
    output_from, grad_from = (
        lax.all_to_all(output_home, "expert", split_axis=0, concat_axis=0, tiled=True),
        lax.all_to_all(grad_home, "expert", split_axis=0, concat_axis=0, tiled=True),
    )
    output = lax.dynamic_index_in_dim(output_from, target, 0, keepdims=False).astype(jnp.bfloat16)
    tokens_grad = lax.dynamic_index_in_dim(grad_from, target, 0, keepdims=False)
    return (
        output,
        tokens_grad,
        gains_grad,
        qkv_grad,
        out_grad,
        router_grad,
        residual_grad,
        const_grad,
        vector_grad,
        gate_grad,
        up_grad,
        down_grad,
    )


def solution(mesh):
    in_specs = (
        P(("dp", "expert"), None),
        P("dp", None, None),
        P("dp", None),
        P(None, ("dp", "expert"), None),
        P(None, None, "dp"),
        P(None, None, "dp"),
        P(None, "dp", None),
        P(None, "dp", None),
        P(),
        P(None, None, "dp", None),
        P(None, None, "dp"),
        P(None, "expert", None, "dp"),
        P(None, "expert", None, "dp"),
        P(None, "expert", "dp", None),
        P(("dp", "expert"), None),
    )
    out_specs = (
        P(("dp", "expert"), None),
        P(("dp", "expert"), None),
        P(None, None, "dp"),
        P(None, None, "dp"),
        P(None, "dp", None),
        P(None, "dp", None),
        P(),
        P(None, None, "dp", None),
        P(None, None, "dp"),
        P(None, "expert", None, "dp"),
        P(None, "expert", None, "dp"),
        P(None, "expert", "dp", None),
    )
    return jax.shard_map(
        per_device, mesh=mesh, in_specs=in_specs, out_specs=out_specs, check_vma=False
    )
```

profile of v0, /device:TPU:0, one launch (start us, length us, event | category | flops | bytes accessed | tf_op | source)
XLA Modules:
  0.0 3095.1 jit_solution(17798994385846774548)
XLA Ops:
  13.2 3.3 convert_element_type.331
  22.0 4.4 all-to-all-start.6
  30.7 33.3 %all_gather.35 = bf16[2,2,768]{1,0,2:T(2,128)(2,1)S(1)} all-gather(bf16[2,2,96]{1,0,2:T(2,128)(2,1)S(1)} %copy.370), channel_id=1, replica_groups=mesh['dp'=8,'expert'=4] {'dp'}, dimensions={2}, use_global_device_ids=true | all-gather | bytes 6912 | tf_op jit(solution)/shard_map/all_gather | solution.py:162
  65.6 35.0 %all_gather.34 = bf16[2,2,768,2]{3,1,0,2:T(2,128)(2,1)S(1)} all-gather(bf16[2,2,96,2]{3,1,0,2:T(2,128)(2,1)S(1)} %copy.367), channel_id=1, replica_groups=mesh['dp'=8,'expert'=4] {'dp'}, dimensions={2}, use_global_device_ids=true | all-gather | bytes 13824 | tf_op jit(solution)/shard_map/all_gather | solution.py:161
  101.8 32.3 %all_gather.30 = bf16[2,768,12]{2,0,1:T(2,128)(2,1)S(1)} all-gather(bf16[2,96,12]{2,0,1:T(2,128)(2,1)S(1)} %copy.356), channel_id=1, replica_groups=mesh['dp'=8,'expert'=4] {'dp'}, dimensions={1}, use_global_device_ids=true | all-gather | bytes 41472 | tf_op jit(solution)/shard_map/all_gather | solution.py:160
  147.7 3.1 scatter_custom_fusion.3
  156.6 32.1 %all_gather.27 = bf16[2,2,768]{1,0,2:T(2,128)(2,1)S(1)} all-gather(bf16[2,2,96]{1,0,2:T(2,128)(2,1)S(1)} %copy.353), channel_id=1, replica_groups=mesh['dp'=8,'expert'=4] {'dp'}, dimensions={2}, use_global_device_ids=true | all-gather | bytes 6912 | tf_op jit(solution)/shard_map/all_gather | solution.py:157
  191.3 3.5 all-to-all-start
  195.5 9.5 slice_reduce_fusion
  210.8 4.0 convolution_convert_fusion.1
  226.3 3.5 all-to-all-start.1
  231.9 7.3 all-to-all-done.1
  239.3 140.3 %all-gather.10.cloned.1.call-done = bf16[2,2,768,2048]{3,2,1,0:T(8,128)(2,1)} async-done(((bf16[2,2,768,256]{3,2,1,0:T(8,128)(2,1)}), bf16[2,2,768,2048]{3,2,1,0:T(8,128)(2,1)}) %all-gather.10.cloned.1.call-update) | async-done | bytes 12582928 | tf_op jit(solution)/shard_map/all_gather | solution.py:165
  379.6 5.9 fusion.2
  385.5 171.3 %all-gather.12.cloned.1.call-done = bf16[2,2,768,2048]{3,2,1,0:T(8,128)(2,1)} async-done(((bf16[2,2,768,256]{3,2,1,0:T(8,128)(2,1)}), bf16[2,2,768,2048]{3,2,1,0:T(8,128)(2,1)}) %all-gather.12.cloned.1.call-update) | async-done | bytes 12582928 | tf_op jit(solution)/shard_map/all_gather | solution.py:166
  556.8 7.8 fusion.26
  564.6 169.5 %all-gather.14.cloned.1.call-done = bf16[2,2,2048,768]{3,2,1,0:T(8,128)(2,1)} async-done(((bf16[2,2,256,768]{3,2,1,0:T(8,128)(2,1)}), bf16[2,2,2048,768]{3,2,1,0:T(8,128)(2,1)}) %all-gather.14.cloned.1.call-update) | async-done | bytes 12582928 | tf_op jit(solution)/shard_map/all_gather | solution.py:167
  734.1 4.7 fusion.57
  739.7 3.9 all-to-all-start.2
  747.9 5.2 all-to-all-done.2
  763.0 3.3 convolution_convert_fusion
  779.2 3.5 all-to-all-start.3
  791.0 4.1 gather_fusion.5
  806.8 4.3 all-to-all-start.7
  811.1 5.9 fusion.8
  817.0 5.9 fusion.10
  822.9 9.1 fusion.20
  832.0 4.8 fusion.58
  837.7 3.5 all-to-all-start.4
  841.1 5.6 fusion.7
  846.8 5.0 fusion.49
  852.6 4.3 all-to-all-start.8
  871.1 5.6 scatter_custom_fusion.4
  900.3 3.0 mul.922
  914.4 4.6 all-to-all-start.9
  920.2 5.6 convolution_bitcast_fusion
  928.6 7.2 fusion.16
  935.8 6.1 fusion.1
  941.9 5.0 fusion.50
  947.8 4.2 all-to-all-start.10
  956.6 5.0 all-to-all-done.10
  961.6 5.7 scatter_custom_fusion.5
  979.0 5.3 convolution_bitcast_fusion.1
  984.3 11.1 pad_maximum_fusion.3
  995.4 21.7 copy.406
  1025.1 7.8 convolution_bitcast_fusion.6
  1041.2 4.5 fusion.84
  1047.4 404.2 %all-reduce.6.cloned.1.call-done = f32[2,768,2304]{1,0,2:T(2,128)} async-done(((f32[2,768,2304]{1,0,2:T(2,128)}), f32[2,768,2304]{1,0,2:T(2,128)}) %all-reduce.6.cloned.1.call-update) | async-done | bytes 14155792
  1451.6 3.3 constant_dynamic-slice_fusion.1
  1454.9 94.7 %reduce-scatter.17.cloned.1.call-done = f32[2,96,768]{2,1,0:T(8,128)} async-done(((f32[2,768,768]{2,1,0:T(8,128)}), f32[2,96,768]{2,1,0:T(8,128)}) %reduce-scatter.17.cloned.1.call-update) | async-done | bytes 589840 | tf_op jit(solution)/shard_map/reduce_scatter | solution.py:432
  1551.6 15.1 pad_maximum_fusion
  1572.0 8.9 pad_maximum_fusion.1
  1588.3 8.7 pad_maximum_fusion.2
  1602.3 3.7 all-to-all-start.5
  1608.9 12.9 all-to-all-done.5
  1621.8 3.6 all-to-all-start.11
  1628.1 58.8 %psum.53 = f32[12,12]{1,0:T(8,128)} all-reduce(f32[12,12]{1,0:T(8,128)S(1)} %fusion.195), channel_id=1, replica_groups=mesh['dp'=8,'expert'=4] {'dp','expert'}, use_global_device_ids=true, to_apply=%region_72.73 | all-reduce | flops 144 | bytes 1152 | tf_op jit(solution)/shard_map/psum | solution.py:440
  1692.2 49.3 %reduce-scatter.27.cloned.1.call-done = f32[96,24]{1,0:T(8,128)} async-done(((f32[768,24]{1,0:T(8,128)}), f32[96,24]{1,0:T(8,128)}) %reduce-scatter.27.cloned.1.call-update) | async-done | bytes 9232
  1745.4 59.8 %reduce-scatter.25.cloned.1.call-done = f32[96,4]{1,0:T(8,128)} async-done(((f32[768,4]{1,0:T(8,128)}), f32[96,4]{1,0:T(8,128)}) %reduce-scatter.25.cloned.1.call-update) | async-done | bytes 1552
  1806.2 11.3 all-reduce.1
  1819.0 44.1 %all-reduce.8.cloned.1.call-done = (f32[2,768,288]{1,0,2:T(2,128)}, f32[2,96,768]{2,1,0:T(8,128)}) async-done(((f32[2,768,288]{1,0,2:T(2,128)}, f32[2,96,768]{2,1,0:T(8,128)}), (f32[2,768,288]{1,0,2:T(2,128)}, f32[2,96,768]{2,1,0:T(8,128)})) %all-reduce.8.cloned.1.call-update) | async-done | bytes 2359312 | tf_op jit(solution)/shard_map/psum | solution.py:437
  1866.0 406.2 %reduce-scatter.19.cloned.1.call-done = f32[2,2,768,256]{3,2,1,0:T(8,128)} async-done(((f32[2,2,768,2048]{3,2,1,0:T(8,128)}), f32[2,2,768,256]{3,2,1,0:T(8,128)}) %reduce-scatter.19.cloned.1.call-update) | async-done | bytes 3145744 | tf_op jit(solution)/shard_map/reduce_scatter | solution.py:425
  2272.1 408.0 %reduce-scatter.21.cloned.1.call-done = f32[2,2,768,256]{3,2,1,0:T(8,128)} async-done(((f32[2,2,768,2048]{3,2,1,0:T(8,128)}), f32[2,2,768,256]{3,2,1,0:T(8,128)}) %reduce-scatter.21.cloned.1.call-update) | async-done | bytes 3145744 | tf_op jit(solution)/shard_map/reduce_scatter | solution.py:426
  2680.1 407.2 %reduce-scatter.23.cloned.1.call-done = f32[2,2,256,768]{3,2,1,0:T(8,128)} async-done(((f32[2,2,2048,768]{3,2,1,0:T(8,128)}), f32[2,2,256,768]{3,2,1,0:T(8,128)}) %reduce-scatter.23.cloned.1.call-update) | async-done | bytes 3145744 | tf_op jit(solution)/shard_map/reduce_scatter | solution.py:427
  (599 shorter events, 232.9 us)
Async XLA Ops:
  7.2 776.4 %copy-start = (f32[12,12]{1,0:T(8,128)S(1)}, f32[12,12]{1,0:T(8,128)}, u32[]{:S(2)}) copy-start(f32[12,12]{1,0:T(8,128)} %param.23) | copy-start | bytes 1732
  7.2 203.6 %all-gather.6.cloned.1.call-start = ((), (), s32[]{:S(2)}) async-start(), calls=%async_computation.20 | async-start | bytes 7962624 | tf_op jit(solution)/shard_map/all_gather | solution.py:158
  9.9 210.3 %all-gather.8.cloned.1.call-start = ((), (), s32[]{:S(2)}) async-start(), calls=%async_computation.21 | async-start | bytes 2654208 | tf_op jit(solution)/shard_map/all_gather | solution.py:159
  11.8 367.8 %all-gather.10.cloned.1.call-start = ((), (), s32[]{:S(2)}) async-start(), calls=%async_computation.22 | async-start | bytes 14155776 | tf_op jit(solution)/shard_map/all_gather | solution.py:165
  13.2 543.7 %all-gather.12.cloned.1.call-start = ((), (), s32[]{:S(2)}) async-start(), calls=%async_computation.23 | async-start | bytes 14155776 | tf_op jit(solution)/shard_map/all_gather | solution.py:166
  16.6 717.5 %all-gather.14.cloned.1.call-start = ((), (), s32[]{:S(2)}) async-start(), calls=%async_computation.24 | async-start | bytes 14155776 | tf_op jit(solution)/shard_map/all_gather | solution.py:167
  19.3 8.6 copy-start.130
  19.3 11.3 copy-start.131
  22.0 43.4 %copy-start.127 = (f32[2,2,96,2]{2,3,1,0:T(2,128)S(1)}, f32[2,2,96,2]{2,3,1,0:T(2,128)}, u32[]{:S(2)}) copy-start(f32[2,2,96,2]{2,3,1,0:T(2,128)} %param.24) | copy-start | bytes 9220
  22.0 169.2 %all-to-all-start.6 = ((bf16[4,192,768]{2,1,0:T(8,128)(2,1)}), bf16[4,192,768]{2,1,0:T(8,128)(2,1)S(1)}, u32[]{:S(2)}, u32[]{:S(2)}) async-start(bf16[4,192,768]{2,1,0:T(8,128)(2,1)} %get-tuple-element.158), calls=%async_computation.6 | async-start | bytes 2359296 | tf_op jit(solution)/shard_map/all_to_all | solution.py:151
  27.0 203.9 %copy-start.76 = (s32[192,2]{0,1:T(2,128)}, s32[192,2]{0,1:T(2,128)S(1)}, u32[]{:S(2)}) copy-start(s32[192,2]{0,1:T(2,128)S(1)} %get-tuple-element.143) | copy-start | bytes 4612
  27.9 110.6 %copy-start.101 = (s32[384]{0:T(512)}, s32[384]{0:T(512)S(1)}, u32[]{:S(2)}) copy-start(s32[384]{0:T(512)S(1)} %eq.191) | copy-start | bytes 4612
  64.0 37.6 %copy-start.114 = (f32[2,96,12]{1,0,2:T(2,128)S(1)}, f32[2,96,12]{1,0,2:T(2,128)}, u32[]{:S(2)}) copy-start(f32[2,96,12]{1,0,2:T(2,128)} %param.22) | copy-start | bytes 27652
  101.6 129.5 %copy-start.96 = (bf16[1,2,768,2]{2,3,1,0:T(2,128)(2,1)}, bf16[1,2,768,2]{2,3,1,0:T(2,128)(2,1)S(1)}, u32[]{:S(2)}) copy-start(bf16[1,2,768,2]{2,3,1,0:T(2,128)(2,1)S(1)} %copy.443) | copy-start | bytes 18436
  134.9 94.8 %copy-start.49 = (bf16[1,768,12]{1,2,0:T(8,128)(2,1)}, bf16[1,768,12]{1,2,0:T(8,128)(2,1)S(1)}, u32[]{:S(2)}) copy-start(bf16[1,768,12]{1,2,0:T(8,128)(2,1)S(1)} %copy.442) | copy-start | bytes 55300
  144.5 46.7 %copy-start.88 = (f32[384]{0:T(512)}, f32[384]{0:T(512)S(1)}, u32[]{:S(2)}) copy-start(f32[384]{0:T(512)S(1)} %scatter_custom_fusion) | copy-start | bytes 4612
  147.7 43.6 %copy-start.90 = (f32[384]{0:T(512)}, f32[384]{0:T(512)S(1)}, u32[]{:S(2)}) copy-start(f32[384]{0:T(512)S(1)} %scatter_custom_fusion.2) | copy-start | bytes 4612
  152.5 43.0 %copy-start.33 = (f32[192,2]{1,0:T(8,128)}, f32[192,2]{1,0:T(8,128)S(1)}, u32[]{:S(2)}) copy-start(f32[192,2]{1,0:T(8,128)S(1)} %copy.383) | copy-start | bytes 4612
  188.7 34.5 %copy-start.102 = (s32[1024]{0:T(1024)}, s32[1024]{0:T(1024)S(1)}, u32[]{:S(2)}) copy-start(s32[1024]{0:T(1024)S(1)} %pad_clamp_fusion.5) | copy-start | bytes 12292
  189.3 41.7 %copy-start.124 = (s32[2]{0:T(128)}, s32[2]{0:T(128)S(1)}, u32[]{:S(2)}) copy-start(s32[2]{0:T(128)S(1)} %iota_add_fusion) | copy-start | bytes 28
  189.3 15.7 copy-start.122
  189.3 15.8 copy-start.103
  191.2 13.8 copy-start.18
  191.3 19.4 all-to-all-start
  194.9 21.6 copy-start.77
  205.0 556.4 %copy-start.50 = (f32[768]{0:T(1024)}, f32[768]{0:T(1024)S(1)}, u32[]{:S(2)}) copy-start(f32[768]{0:T(1024)S(1)} %get-tuple-element.186) | copy-start | bytes 9220
  226.3 13.0 all-to-all-start.1
  229.9 155.6 %copy-start.56 = (f32[192,12]{0,1:T(8,128)}, f32[192,12]{0,1:T(8,128)S(1)}, u32[]{:S(2)}) copy-start(f32[192,12]{0,1:T(8,128)S(1)} %fusion.125) | copy-start | bytes 27652
  230.7 154.8 %copy-start.64 = (f32[192,2]{0,1:T(2,128)}, f32[192,2]{0,1:T(2,128)S(1)}, u32[]{:S(2)}) copy-start(f32[192,2]{0,1:T(2,128)S(1)} %get-tuple-element.120) | copy-start | bytes 4612
  231.1 516.2 %copy-start.62 = (f32[192,2]{0,1:T(2,128)}, f32[192,2]{0,1:T(2,128)S(1)}, u32[]{:S(2)}) copy-start(f32[192,2]{0,1:T(2,128)S(1)} %fusion.134) | copy-start | bytes 4612
  231.3 154.2 %copy-start.113 = (f32[192,2,2]{0,2,1:T(2,128)}, f32[192,2,2]{0,2,1:T(2,128)S(1)}, u32[]{:S(2)}) copy-start(f32[192,2,2]{0,2,1:T(2,128)S(1)} %get-tuple-element.167) | copy-start | bytes 9220
  231.3 154.2 %copy-start.123 = (f32[192,2]{0,1:T(2,128)}, f32[192,2]{0,1:T(2,128)S(1)}, u32[]{:S(2)}) copy-start(f32[192,2]{0,1:T(2,128)S(1)} %get-tuple-element.166) | copy-start | bytes 4612
  231.3 154.2 %copy-start.71 = (f32[192,2,2]{0,2,1:T(2,128)}, f32[192,2,2]{0,2,1:T(2,128)S(1)}, u32[]{:S(2)}) copy-start(f32[192,2,2]{0,2,1:T(2,128)S(1)} %broadcast_divide_fusion.1) | copy-start | bytes 9220
  231.9 515.3 %copy-start.100 = (f32[192,2,1]{0,2,1:T(1,128)}, f32[192,2,1]{0,2,1:T(1,128)S(1)}, u32[]{:S(2)}) copy-start(f32[192,2,1]{0,2,1:T(1,128)S(1)} %get-tuple-element.139) | copy-start | bytes 4612
  239.3 317.6 %copy-start.35 = (bf16[4,2,48,768]{3,2,1,0:T(8,128)(2,1)}, bf16[4,2,48,768]{3,2,1,0:T(8,128)(2,1)S(1)}, u32[]{:S(2)}) copy-start(bf16[4,2,48,768]{3,2,1,0:T(8,128)(2,1)S(1)} %all-to-all-done.1) | copy-start | bytes 1769476
  738.8 8.5 copy-start.66
  738.8 14.3 copy-start.116
  739.7 13.4 all-to-all-start.2
  747.3 14.2 copy-start.115
  779.2 27.6 all-to-all-start.3
  806.8 10.2 copy-start.37
  806.8 16.1 all-to-all-start.7
  837.7 15.0 all-to-all-start.4
  852.6 18.5 all-to-all-start.8
  859.8 16.9 copy-start.5
  865.9 10.8 copy-start.60
  914.4 14.2 all-to-all-start.9
  947.8 13.8 all-to-all-start.10
  951.9 499.7 %all-reduce.6.cloned.1.call-start = ((), (), s32[]{:S(2)}) async-start(), calls=%async_computation.33 | async-start | bytes 28311552
  1017.1 532.6 %reduce-scatter.17.cloned.1.call-start = ((), (), s32[]{:S(2)}) async-start(), calls=%async_computation.25 | async-start | bytes 5308416 | tf_op jit(solution)/shard_map/reduce_scatter | solution.py:432
  1021.8 665.1 %reduce-scatter.31.cloned.1.call-start = ((), (), s32[]{:S(2)}) async-start(), calls=%async_computation.32 | async-start | bytes 442368
  1035.9 653.6 %reduce-scatter.29.cloned.1.call-start = ((), (), s32[]{:S(2)}) async-start(), calls=%async_computation.31 | async-start | bytes 442368
  1039.1 702.4 %reduce-scatter.27.cloned.1.call-start = ((), (), s32[]{:S(2)}) async-start(), calls=%async_computation.30 | async-start | bytes 442368
  1041.1 764.1 %reduce-scatter.25.cloned.1.call-start = ((), (), s32[]{:S(2)}) async-start(), calls=%async_computation.29 | async-start | bytes 442368
  1047.4 502.3 %copy-start.36 = (bf16[4,2,48,768]{3,2,1,0:T(8,128)(2,1)S(1)}, bf16[4,2,48,768]{3,2,1,0:T(8,128)(2,1)}, u32[]{:S(2)}) copy-start(bf16[4,2,48,768]{3,2,1,0:T(8,128)(2,1)} %copy-done.35) | copy-start | bytes 1769476
  1047.4 502.3 %copy-start.140 = (bf16[4,2,48,2048]{3,2,0,1:T(8,128)(2,1)S(1)}, bf16[4,2,48,2048]{3,2,0,1:T(8,128)(2,1)}, u32[]{:S(2)}) copy-start(bf16[4,2,48,2048]{3,2,0,1:T(8,128)(2,1)} %copy-done.139) | copy-start | bytes 4718596
  1047.4 815.7 %all-reduce.8.cloned.1.call-start = ((), (), s32[]{:S(2)}) async-start(), calls=%async_computation.34 | async-start | bytes 4718592 | tf_op jit(solution)/shard_map/psum | solution.py:437
  1549.6 722.5 %reduce-scatter.19.cloned.1.call-start = ((), (), s32[]{:S(2)}) async-start(), calls=%async_computation.26 | async-start | bytes 28311552 | tf_op jit(solution)/shard_map/reduce_scatter | solution.py:425
  1566.7 1113.5 %reduce-scatter.21.cloned.1.call-start = ((), (), s32[]{:S(2)}) async-start(), calls=%async_computation.27 | async-start | bytes 28311552 | tf_op jit(solution)/shard_map/reduce_scatter | solution.py:426
  1580.9 1506.4 %reduce-scatter.23.cloned.1.call-start = ((), (), s32[]{:S(2)}) async-start(), calls=%async_computation.28 | async-start | bytes 28311552 | tf_op jit(solution)/shard_map/reduce_scatter | solution.py:427
  1602.3 19.5 all-to-all-start.5
  1621.8 196.4 %all-to-all-start.11 = ((f32[4,192,768]{2,1,0:T(8,128)}), f32[4,192,768]{2,1,0:T(8,128)S(1)}, u32[]{:S(2)}, u32[]{:S(2)}) async-start(f32[4,192,768]{2,1,0:T(8,128)} %broadcast_select_fusion), calls=%async_computation.11 | async-start | bytes 4718592 | tf_op jit(solution)/shard_map/all_to_all | solution.py:446
  1863.1 1224.3 %copy-start.40 = (f32[2,96,768]{2,1,0:T(8,128)S(1)}, f32[2,96,768]{2,1,0:T(8,128)}, u32[]{:S(2)}) copy-start(f32[2,96,768]{2,1,0:T(8,128)} %get-tuple-element.193) | copy-start | bytes 1769476
  1863.1 1225.1 %copy-start.1 = (f32[12,12]{1,0:T(8,128)S(1)}, f32[12,12]{1,0:T(8,128)}, u32[]{:S(2)}) copy-start(f32[12,12]{1,0:T(8,128)} %param.23) | copy-start | bytes 1732
  (109 other events, 343.8 us)
Sparse Core Ops, SparseCore 0:
  10.2 135.0 all-gather.5
  148.0 53.1 all-gather.7
  203.9 175.6 all-gather.9
  382.0 174.7 all-gather.11
  559.4 174.6 all-gather.13
  1017.2 434.4 all-reduce.5
  1455.3 94.2 reduce-scatter.16
  1552.9 61.1 reduce-scatter.30
  1617.4 60.4 reduce-scatter.28
  1681.0 60.4 reduce-scatter.26
  1744.8 60.3 reduce-scatter.24
  1808.1 54.9 all-reduce.7
  1867.5 404.5 reduce-scatter.18
  2276.5 403.6 reduce-scatter.20
  2684.4 402.8 reduce-scatter.22
where the time goes:
time: 3110 us; the launch traced here: 3100 us
  waiting for transfers between devices  2390 us (77%)
  blocking collectives  203 us (7%)
  matrix products  158 us (5%)
  local copies, waits for them, and re-layouts  146 us (5%)
  other arithmetic  130 us (4%)
  starting transfers between devices  48 us (2%)
    unnamed x20, waiting for transfers between devices  514 us
    reduce_scatter x1, waiting for transfers between devices, per_device(): lax.psum_scatter(up_stack, 'dp', scatter_dimension=3, tiled=True)  408 us
    reduce_scatter x1, waiting for transfers between devices, per_device(): lax.psum_scatter(down_stack, 'dp', scatter_dimension=2, tiled=True)  407 us
    reduce_scatter x1, waiting for transfers between devices, per_device(): lax.psum_scatter(gate_stack, 'dp', scatter_dimension=3, tiled=True)  406 us
    all_gather x1, waiting for transfers between devices, per_device(): lax.all_gather(w_up.astype(jnp.bfloat16), 'dp', axis=3, tiled=True)  171 us
    all_gather x1, waiting for transfers between devices, per_device(): lax.all_gather(w_down.astype(jnp.bfloat16), 'dp', axis=2, tiled=True)  169 us
    all_gather x1, waiting for transfers between devices, per_device(): lax.all_gather(w_gate.astype(jnp.bfloat16), 'dp', axis=3, tiled=True)  140 us
    reduce_scatter x1, waiting for transfers between devices, per_device(): lax.psum_scatter(out_local, 'dp', scatter_dimension=1, tiled=True)  94.7 us
  transfers between devices with their start and end apart: 27, of which 17 were waited for; matrix products, arithmetic and copies ran while one was open for 8% of the time, Pallas kernels for 0%

commit v1 on v0

v1 whole, which is shorter than its diff:
```python
import functools

import jax
import jax.numpy as jnp
from jax import lax
from jax.experimental import pallas as pl
from jax.experimental.pallas import tpu as pltpu
from jax.sharding import PartitionSpec as P

HEADS = 12
CAP = 48
LINE = 4
EPSILON = 1e-05
MASKED = -1e30
HIGH = lax.Precision.HIGHEST
F32 = jnp.float32
BF16 = jnp.bfloat16
MESH = pl.DeviceIdType.MESH
VMEM = pl.BlockSpec(memory_space=pltpu.VMEM)
ANY = pl.BlockSpec(memory_space=pl.ANY)

CONST0, GAIN0, VECTOR0 = 12, 16, 18
STAT = {
    name: i
    for i, name in enumerate(
        ("r0", "r1", "share0", "share1", "slot0", "slot1", "p00", "p01", "p10", "p11")
    )
}


def dot_nn(a, b, **kw):
    return lax.dot_general(a, b, (((1,), (0,)), ((), ())), preferred_element_type=F32, **kw)


def dot_nt(a, b, **kw):
    return lax.dot_general(a, b, (((1,), (1,)), ((), ())), preferred_element_type=F32, **kw)


def dot_tn(a, b, **kw):
    return lax.dot_general(a, b, (((0,), (0,)), ((), ())), preferred_element_type=F32, **kw)


def lanes(rows, width=128):
    return lax.broadcasted_iota(jnp.int32, (rows, width), 1)


def rms_scale(values):
    return lax.rsqrt(jnp.mean(values * values, axis=-1, keepdims=True) + EPSILON)


def row_vectors(small):
    pick = lax.broadcasted_iota(jnp.int32, (8, 128), 0) + GAIN0 == lanes(8)
    rows = dot_nt(pick.astype(BF16), small)
    return rows[0:1], rows[1:2], rows[2:3], rows[3:4]


def stat_columns(stat):
    return {name: stat[:, i : i + 1] for name, i in STAT.items()}


def slot_picks(stat, slots):
    place = lanes(stat["slot0"].shape[0], slots).astype(F32)
    first = (place == stat["slot0"]).astype(BF16)
    second = (place == stat["slot1"]).astype(BF16)
    return first, second


def const_weights(stat, experts):
    out = []
    for kind in (experts + 1, experts + 2, experts + 3):
        out.append(
            stat["share0"] * (stat["r0"] == kind).astype(F32)
            + stat["share1"] * (stat["r1"] == kind).astype(F32)
        )
    return out


def attend_part(stream, small, w_qkv_t, w_out, doc_col, doc_row, attn_in_ref, qkv_ref, probs_ref, attn_ref):
    rows, width = stream.shape
    gain, _, _, _ = row_vectors(small)
    attn_in_ref[...] = (stream * rms_scale(stream) * gain).astype(BF16)

    def project(i, carry):
        at = pl.multiple_of(i * width, width)
        qkv_ref[:, pl.ds(at, width)] = dot_nt(
            attn_in_ref[...], w_qkv_t[pl.ds(at, width), :]
        ).astype(BF16)
        return carry

    lax.fori_loop(0, 3, project, 0)
    head_dim = width // HEADS
    factor = 1.0 / head_dim**0.5
    allowed = jnp.logical_and(
        doc_col[...] == doc_row[...],
        lax.broadcasted_iota(jnp.int32, (rows, rows), 0)
        >= lax.broadcasted_iota(jnp.int32, (rows, rows), 1),
    )

    def heads(i, carry):
        at = pl.multiple_of(i * 2 * head_dim, 2 * head_dim)
        query = qkv_ref[:, pl.ds(at, 2 * head_dim)]
        key = qkv_ref[:, pl.ds(pl.multiple_of(at + width, 128), 2 * head_dim)]
        value = qkv_ref[:, pl.ds(pl.multiple_of(at + 2 * width, 128), 2 * head_dim)]
        second = lanes(rows, 2 * head_dim) >= head_dim
        mixed = []
        for sub in (0, 1):
            mine = second if sub else jnp.logical_not(second)
            scores = dot_nt(jnp.where(mine, query, jnp.zeros_like(query)), key) * factor
            scores = jnp.where(allowed, scores, MASKED)
            exponent = jnp.exp(scores - jnp.max(scores, axis=-1, keepdims=True))
            probs = exponent / jnp.sum(exponent, axis=-1, keepdims=True)
            probs_ref[2 * i + sub] = probs
            mixed.append(dot_nn(probs.astype(BF16), value))
        attn_ref[:, pl.ds(at, 2 * head_dim)] = jnp.where(second, mixed[1], mixed[0]).astype(BF16)
        return carry

    lax.fori_loop(0, HEADS // 2, heads, 0, unroll=2)
    return stream + dot_nn(attn_ref[...], w_out[...])


def route_part(mid, small, routes, prev_logits, w_res, experts):
    rows = mid.shape[0]
    _, gain, _, _ = row_vectors(small)
    hidden = (mid * rms_scale(mid) * gain).astype(BF16)
    lane = lanes(rows)
    raw = dot_nn(hidden, small)
    logits = jnp.where(lane < CONST0, raw, 0.0)
    if prev_logits is not None:
        logits = logits + dot_nn(prev_logits, w_res, precision=HIGH)
    r0, r1 = routes[:, 0:1], routes[:, 1:2]
    hot0, hot1 = (lane == r0).astype(F32), (lane == r1).astype(F32)
    c0 = jnp.sum(hot0 * logits, axis=-1, keepdims=True)
    c1 = jnp.sum(hot1 * logits, axis=-1, keepdims=True)
    peak = jnp.maximum(c0, c1)
    e0, e1 = jnp.exp(c0 - peak), jnp.exp(c1 - peak)
    total = e0 + e1
    share0, share1 = e0 / total, e1 / total
    probs = []
    for j in (0, 1):
        a = raw[:, CONST0 + 2 * j : CONST0 + 2 * j + 1]
        b = raw[:, CONST0 + 2 * j + 1 : CONST0 + 2 * j + 2]
        top = jnp.maximum(a, b)
        ea, eb = jnp.exp(a - top), jnp.exp(b - top)
        probs += [ea / (ea + eb), eb / (ea + eb)]
    earlier = lax.broadcasted_iota(jnp.int32, (rows, rows), 0) > lax.broadcasted_iota(
        jnp.int32, (rows, rows), 1
    )
    before = dot_nn(earlier.astype(BF16), (hot0 + hot1).astype(BF16))
    f0, f1 = r0.astype(F32), r1.astype(F32)
    slot0 = jnp.where(
        r0 < experts, f0 * CAP + jnp.sum(before * hot0, axis=-1, keepdims=True), -1.0
    )
    slot1 = jnp.where(
        r1 < experts, f1 * CAP + jnp.sum(before * hot1, axis=-1, keepdims=True), -1.0
    )
    stat = jnp.zeros((rows, 128), F32)
    for i, column in enumerate([f0, f1, share0, share1, slot0, slot1] + probs):
        stat = jnp.where(lane == i, column, stat)
    first, second = slot_picks({"slot0": slot0, "slot1": slot1}, experts * CAP)
    outgoing = dot_tn(first + second, hidden).astype(BF16)
    return logits, stat, outgoing


def combine_part(mid, small, stat, returned, experts):
    _, gain, vec0, vec1 = row_vectors(small)
    hidden_full = mid * rms_scale(mid) * gain
    first, second = slot_picks(stat, experts * CAP)
    pair0, pair1 = dot_nn(first, returned), dot_nn(second, returned)
    copy, const0, const1 = const_weights(stat, experts)
    local = copy + const0 * stat["p00"] + const1 * stat["p10"]
    moe = stat["share0"] * pair0 + stat["share1"] * pair1 + local * hidden_full
    moe = moe + (const0 * stat["p01"]) * vec0 + (const1 * stat["p11"]) * vec1
    return mid + moe, hidden_full, pair0, pair1


def share_backward(grad, small, stat, hidden_full, pair0, pair1, extra, experts):
    rows = grad.shape[0]
    _, _, vec0, vec1 = row_vectors(small)
    first, second = slot_picks(stat, experts * CAP)
    lane = lanes(rows).astype(F32)
    rowsum = functools.partial(jnp.sum, axis=-1, keepdims=True)
    dot_hidden = rowsum(grad * hidden_full)
    dot_vec = (rowsum(grad * vec0), rowsum(grad * vec1))
    _, const0, const1 = const_weights(stat, experts)
    probs = ((stat["p00"], stat["p01"]), (stat["p10"], stat["p11"]))
    value = [probs[j][0] * dot_hidden + probs[j][1] * dot_vec[j] for j in (0, 1)]
    shares = []
    for r, pair in ((stat["r0"], pair0), (stat["r1"], pair1)):
        shares.append(
            rowsum(grad * pair)
            + (r == experts + 1).astype(F32) * dot_hidden
            + (r == experts + 2).astype(F32) * value[0]
            + (r == experts + 3).astype(F32) * value[1]
        )
    inner = stat["share0"] * shares[0] + stat["share1"] * shares[1]
    g_small = (lane == stat["r0"]).astype(F32) * (stat["share0"] * (shares[0] - inner))
    g_small = g_small + (lane == stat["r1"]).astype(F32) * (stat["share1"] * (shares[1] - inner))
    if extra is not None:
        g_small = g_small + extra
    g_logits = g_small
    for j, weight in ((0, const0), (1, const1)):
        q = (weight * dot_hidden, weight * dot_vec[j])
        mean = probs[j][0] * q[0] + probs[j][1] * q[1]
        for c in (0, 1):
            g_small = jnp.where(lane == CONST0 + 2 * j + c, probs[j][c] * (q[c] - mean), g_small)
    sent0 = (jnp.where(stat["r0"] < experts, stat["share0"], 0.0) * grad).astype(BF16)
    sent1 = (jnp.where(stat["r1"] < experts, stat["share1"], 0.0) * grad).astype(BF16)
    outgoing = (dot_tn(first, sent0) + dot_tn(second, sent1)).astype(BF16)
    hidden = hidden_full.astype(BF16).astype(F32)
    projections = dot_tn(g_small, hidden, precision=HIGH)
    vector0 = jnp.sum((const0 * stat["p01"]) * grad, axis=0, keepdims=True)
    vector1 = jnp.sum((const1 * stat["p11"]) * grad, axis=0, keepdims=True)
    return g_small, g_logits, outgoing, projections, vector0, vector1


def store_small(ref, projections, vector0, vector1):
    ref[0:16, :] = projections[0:16]
    ref[16:24, :] = jnp.zeros((8, ref.shape[1]), F32)
    ref[VECTOR0 : VECTOR0 + 1, :] = vector0
    ref[VECTOR0 + 1 : VECTOR0 + 2, :] = vector1


def first_kernel(experts, tokens, small, w_qkv_t, w_out, doc_col, doc_row, routes,
                 attn_in, qkv, probs, attn, mid_ref, logits_ref, stat_ref, out_ref):
    mid = attend_part(tokens[...].astype(F32), small[...], w_qkv_t, w_out, doc_col, doc_row, attn_in, qkv, probs, attn)
    mid_ref[...] = mid
    logits, stat, out = route_part(mid, small[...], routes[...], None, None, experts)
    logits_ref[...], stat_ref[...], out_ref[...] = logits, stat, out


def middle_kernel(experts, mid_in, small_in, stat_in, returned, small, w_qkv_t, w_out, doc_col, doc_row, routes, logits_in, w_res,
                  stream_ref, attn_in, qkv, probs, attn, mid_ref, stat_ref, out_ref):
    stream, _, _, _ = combine_part(mid_in[...], small_in[...], stat_columns(stat_in[...]), returned[...], experts)
    stream_ref[...] = stream
    mid = attend_part(stream, small[...], w_qkv_t, w_out, doc_col, doc_row, attn_in, qkv, probs, attn)
    mid_ref[...] = mid
    _, stat, out = route_part(mid, small[...], routes[...], logits_in[...], w_res[...], experts)
    stat_ref[...], out_ref[...] = stat, out


def turn_kernel(experts, mid, small, stat_in, returned, cotangent, logits_in, w_res,
                output, g_small_ref, extra_ref, out_ref, small_grad, res_grad):
    stat = stat_columns(stat_in[...])
    stream, hidden_full, pair0, pair1 = combine_part(mid[...], small[...], stat, returned[...], experts)
    output[...] = stream.astype(BF16)
    grad = cotangent[...].astype(F32)
    g_small, g_logits, out, projections, v0, v1 = share_backward(grad, small[...], stat, hidden_full, pair0, pair1, None, experts)
    g_small_ref[...] = g_small
    out_ref[...] = out
    store_small(small_grad, projections, v0, v1)
    res_grad[...] = dot_tn(logits_in[...], g_logits, precision=HIGH)
    extra_ref[...] = dot_nt(g_logits, w_res[...], precision=HIGH)


def layer_backward(experts, grad, back, g_small, stat, mid, small, stream, w_qkv_t, w_out, attn_in, qkv, probs, attn,
                   qkv_grad, out_grad, small_grad, g_qkv, g_attn):
    rows, width = mid.shape
    gain1, gain2, _, _ = row_vectors(small)
    first, second = slot_picks(stat, experts * CAP)
    copy, const0, const1 = const_weights(stat, experts)
    local = copy + const0 * stat["p00"] + const1 * stat["p10"]
    g_full = dot_nt(g_small, small.astype(F32), precision=HIGH) + dot_nn(first + second, back)
    g_full = g_full + grad * local
    s2 = rms_scale(mid)
    small_grad[GAIN0 + 1 : GAIN0 + 2, :] = jnp.sum(g_full * mid * s2, axis=0, keepdims=True)
    m = g_full * gain2
    g_mid = grad + s2 * m - mid * (s2 * s2 * s2 * jnp.mean(m * mid, axis=-1, keepdims=True))
    branch = g_mid.astype(BF16)
    out_grad[...] = dot_tn(attn[...], branch).astype(out_grad.dtype)
    g_attn[...] = dot_nt(branch, w_out[...]).astype(BF16)
    head_dim = width // HEADS
    factor = 1.0 / head_dim**0.5

    def heads(i, carry):
        at = pl.multiple_of(i * 2 * head_dim, 2 * head_dim)
        at_k = pl.multiple_of(at + width, 128)
        at_v = pl.multiple_of(at + 2 * width, 128)
        query = qkv[:, pl.ds(at, 2 * head_dim)]
        key = qkv[:, pl.ds(at_k, 2 * head_dim)]
        value = qkv[:, pl.ds(at_v, 2 * head_dim)]
        ga = g_attn[:, pl.ds(at, 2 * head_dim)]
        second_half = lanes(rows, 2 * head_dim) >= head_dim
        gq, gk, gv = [], [], []
        for sub in (0, 1):
            mine = second_half if sub else jnp.logical_not(second_half)
            p = probs[2 * i + sub]
            gp = dot_nt(jnp.where(mine, ga, jnp.zeros_like(ga)), value)
            gs = (p * (gp - jnp.sum(p * gp, axis=-1, keepdims=True))).astype(BF16)
            gq.append(dot_nn(gs, key))
            gk.append(dot_tn(gs, query))
            gv.append(dot_tn(p.astype(BF16), ga))
        g_qkv[:, pl.ds(at, 2 * head_dim)] = (jnp.where(second_half, gq[1], gq[0]) * factor).astype(BF16)
        g_qkv[:, pl.ds(at_k, 2 * head_dim)] = (jnp.where(second_half, gk[1], gk[0]) * factor).astype(BF16)
        g_qkv[:, pl.ds(at_v, 2 * head_dim)] = jnp.where(second_half, gv[1], gv[0]).astype(BF16)
        return carry

    lax.fori_loop(0, HEADS // 2, heads, 0, unroll=2)

    def weights(i, carry):
        at = pl.multiple_of(i * width, width)
        qkv_grad[pl.ds(at, width), :] = dot_tn(g_qkv[:, pl.ds(at, width)], attn_in[...]).astype(qkv_grad.dtype)
        return carry + dot_nn(g_qkv[:, pl.ds(at, width)], w_qkv_t[pl.ds(at, width), :])

    g_in = lax.fori_loop(0, 3, weights, jnp.zeros((rows, width), F32))
    s1 = rms_scale(stream)
    small_grad[GAIN0 : GAIN0 + 1, :] = jnp.sum(g_in * stream * s1, axis=0, keepdims=True)
    n = g_in * gain1
    return g_mid + s1 * n - stream * (s1 * s1 * s1 * jnp.mean(n * stream, axis=-1, keepdims=True))


def between_kernel(experts, cotangent, back, g_small, stat_in, mid, small, stream, w_qkv_t, w_out, attn_in, qkv, probs, attn, small_grad_in,
                   mid0, small0, stat0_in, returned0, extra,
                   qkv_grad, out_grad, small_grad, grad_ref, g_small0_ref, out_ref, small_grad0, g_qkv, g_attn):
    small_grad[...] = small_grad_in[...]
    grad = layer_backward(experts, cotangent[...].astype(F32), back[...], g_small[...], stat_columns(stat_in[...]), mid[...],
                          small[...], stream[...], w_qkv_t, w_out, attn_in, qkv, probs, attn, qkv_grad, out_grad, small_grad, g_qkv, g_attn)
    grad_ref[...] = grad
    stat0 = stat_columns(stat0_in[...])
    _, hidden_full, pair0, pair1 = combine_part(mid0[...], small0[...], stat0, returned0[...], experts)
    g_small0, _, out, projections, v0, v1 = share_backward(grad, small0[...], stat0, hidden_full, pair0, pair1, extra[...], experts)
    g_small0_ref[...] = g_small0
    out_ref[...] = out
    store_small(small_grad0, projections, v0, v1)


def last_kernel(experts, grad_in, back, g_small, stat_in, mid, small, tokens, w_qkv_t, w_out, attn_in, qkv, probs, attn, small_grad_in,
                qkv_grad, out_grad, small_grad, grad_ref, g_qkv, g_attn):
    small_grad[...] = small_grad_in[...]
    grad_ref[...] = layer_backward(experts, grad_in[...], back[...], g_small[...], stat_columns(stat_in[...]), mid[...], small[...],
                                   tokens[...].astype(F32), w_qkv_t, w_out, attn_in, qkv, probs, attn, qkv_grad, out_grad, small_grad,
                                   g_qkv, g_attn)


def local_call(kernel, experts, args, outs, scratch=()):
    return pl.pallas_call(
        functools.partial(kernel, experts),
        out_shape=[jax.ShapeDtypeStruct(shape, dtype) for shape, dtype in outs],
        in_specs=[VMEM] * len(args),
        out_specs=[VMEM] * len(outs),
        scratch_shapes=[pltpu.VMEM(shape, dtype) for shape, dtype in scratch],
        compiler_params=pltpu.CompilerParams(vmem_limit_bytes=60 * 2**20),
    )(*args)


def mate(place, step, owners):
    if owners != 4 or step == 0:
        return lax.rem(place + step, owners)
    if step == 1:
        return place + 1 - 2 * lax.rem(place, 2)
    return lax.rem(place + 2, 4) if step == 2 else 3 - place


class Line:
    def __init__(self, spread, owners, x, part, stage, arrived, final, returned, sems):
        self.owners, self.spread = owners, spread
        self.d, self.e = lax.axis_index("dp"), lax.axis_index("expert")
        self.t = self.d // spread
        self.x, self.part, self.stage, self.arrived = x, part, stage, arrived
        self.final, self.returned = final, returned
        (self.out_send, self.x_recv, self.x_send, self.sum_send, self.sum_recv, self.ret_send, self.ret_recv) = sems
        self.above, self.below = self.t < LINE - 1, self.t > 0

    def greet(self):
        barrier = pltpu.get_barrier_semaphore()
        for i in range(1, self.owners):
            pl.semaphore_signal(barrier, inc=1, device_id=(self.d, mate(self.e, i, self.owners)), device_id_type=MESH)

        @pl.when(self.above)
        def _():
            pl.semaphore_signal(barrier, inc=1, device_id=(self.d + self.spread, self.e), device_id_type=MESH)

        @pl.when(self.below)
        def _():
            pl.semaphore_signal(barrier, inc=1, device_id=(self.d - self.spread, self.e), device_id_type=MESH)

        ends = self.above.astype(jnp.int32) + self.below.astype(jnp.int32)
        pl.semaphore_wait(barrier, self.owners - 1 + ends)

    def slot_copy(self, out, i):
        to = mate(self.e, i, self.owners)
        return pltpu.make_async_remote_copy(
            src_ref=out.at[to], dst_ref=self.x.at[:, self.t, self.e], send_sem=self.out_send.at[i],
            recv_sem=self.x_recv.at[self.t, self.e], device_id=(self.d, to), device_id_type=MESH)

    def x_copy(self, up, s, b):
        to = self.d + self.spread if up else self.d - self.spread
        return pltpu.make_async_remote_copy(
            src_ref=self.x.at[:, s, b], dst_ref=self.x.at[:, s, b], send_sem=self.x_send.at[up, s, b],
            recv_sem=self.x_recv.at[s, b], device_id=(to, self.e), device_id_type=MESH)

    def sum_copy(self, up, s, b):
        to = self.d + self.spread if up else self.d - self.spread
        return pltpu.make_async_remote_copy(
            src_ref=self.stage.at[s, :, b], dst_ref=self.arrived.at[up, s, :, b], send_sem=self.sum_send.at[s, b],
            recv_sem=self.sum_recv.at[up, s, b], device_id=(to, self.e), device_id_type=MESH)

    def ret_copy(self, i):
        to = mate(self.e, i, self.owners)
        return pltpu.make_async_remote_copy(
            src_ref=self.final.at[to], dst_ref=self.returned.at[self.e], send_sem=self.ret_send.at[i],
            recv_sem=self.ret_recv.at[self.e], device_id=(self.d, to), device_id_type=MESH)

    def run(self, out, compute, meanwhile, keep):
        t, e, owners = self.t, self.e, self.owners
        self.greet()
        for i in list(range(2, owners)) + [1]:
            self.slot_copy(out, i).start()
        self.x[:, t, e] = out[e]
        for i in range(owners):
            b = mate(e, i, owners)
            if i:
                self.x_copy(0, t, b).wait_recv()
            for up, there in ((0, self.below), (1, self.above)):

                @pl.when(there)
                def _(up=up, b=b):
                    self.x_copy(up, t, b).start()

        keep(t)
        compute(t)

        def step(k, carry):
            for i in range(owners):
                b = mate(e, i, owners)

                @pl.when(t + k < LINE)
                def _(b=b):
                    self.x_copy(0, t + k, b).wait_recv()

                    @pl.when(self.below)
                    def _():
                        self.x_copy(0, t + k, b).start()

                @pl.when(t - k >= 0)
                def _(b=b):
                    self.x_copy(1, t - k, b).wait_recv()

                    @pl.when(self.above)
                    def _():
                        self.x_copy(1, t - k, b).start()

            def side(up, carry):
                s = t + k - 2 * k * up

                @pl.when(jnp.logical_and(s >= 0, s < LINE))
                def _():
                    keep(s)
                    compute(s)

                return carry

            lax.fori_loop(0, 2, side, 0)
            for up, first, s in ((1, t == 0, k), (0, t == LINE - 1, LINE - 1 - k)):

                @pl.when(first)
                def _(up=up, s=s):
                    for i in (list(range(2, owners)) + [0, 1])[:owners]:
                        b = mate(e, i, owners)
                        self.stage[s, :, b] = self.part[s, :, b].astype(BF16)
                        self.sum_copy(up, s, b).start()

            return carry

        lax.fori_loop(1, LINE, step, 0)
        meanwhile()

        def relay(k, carry):
            for i in (list(range(2, owners)) + [0, 1])[:owners]:
                b = mate(e, i, owners)
                for up, s, inside in (
                    (1, k, jnp.logical_and(t > 0, t < k)),
                    (0, LINE - 1 - k, jnp.logical_and(t > LINE - 1 - k, t < LINE - 1)),
                ):

                    @pl.when(inside)
                    def _(up=up, s=s, b=b):
                        self.sum_copy(up, s, b).wait_recv()
                        total = self.part[s, :, b] + self.arrived[up, s, :, b].astype(F32)
                        self.stage[s, :, b] = total.astype(BF16)
                        self.sum_copy(up, s, b).start()

            return carry

        lax.fori_loop(2, LINE, relay, 0)
        for i in (list(range(2, owners)) + [0, 1])[:owners]:
            b = mate(e, i, owners)
            for up, there in ((1, self.below), (0, self.above)):

                @pl.when(there)
                def _(up=up, b=b):
                    self.sum_copy(up, t, b).wait_recv()
                    self.part[t, :, b] = self.part[t, :, b] + self.arrived[up, t, :, b].astype(F32)

            if i:
                self.final[b] = self.part[t, :, b].astype(BF16)
                self.ret_copy(i).start()
            else:
                self.returned[e] = self.part[t, :, e].astype(BF16)

        def sent(s, carry):
            for i in range(owners):
                for up, mine in ((0, jnp.logical_and(self.below, s >= t)), (1, jnp.logical_and(self.above, s <= t))):

                    @pl.when(mine)
                    def _(up=up, i=i):
                        self.x_copy(up, s, i).wait_send()

                @pl.when(s != t)
                def _(i=i):
                    self.sum_copy(0, s, i).wait_send()

            return carry

        for i in range(1, owners):
            self.slot_copy(out, i).wait_send()
        lax.fori_loop(0, LINE, sent, 0)
        for i in range(1, owners):
            self.ret_copy(i).wait_send()
            pltpu.make_async_remote_copy(
                src_ref=self.final.at[e], dst_ref=self.returned.at[mate(e, i, owners)], send_sem=self.ret_send.at[i],
                recv_sem=self.ret_recv.at[mate(e, i, owners)], device_id=(self.d, mate(e, i, owners)), device_id_type=MESH).wait_recv()


def line_scratch(local, owners, width):
    shape = (local, owners, CAP, width)
    dma = pltpu.SemaphoreType.DMA
    return [
        pltpu.VMEM((local, LINE, owners, CAP, width), BF16),
        pltpu.VMEM((LINE,) + shape, F32),
        pltpu.VMEM((LINE,) + shape, BF16),
        pltpu.VMEM((2, LINE) + shape, BF16),
        pltpu.VMEM((owners, local, CAP, width), BF16),
        dma((owners,)), dma((LINE, owners)), dma((2, LINE, owners)), dma((LINE, owners)), dma((2, LINE, owners)),
        dma((owners,)), dma((owners,)),
    ]


def expert_forward_kernel(spread, parts, out, *refs):
    gate, up, down = refs[:parts], refs[parts : 2 * parts], refs[2 * parts : 3 * parts]
    returned, x_keep, g_keep, u_keep, x, part, stage, arrived, final = refs[3 * parts : 3 * parts + 9]
    sems, (g_all, u_all, keep_sem) = refs[3 * parts + 9 : 3 * parts + 16], refs[3 * parts + 16 :]
    local, _, owners, _, width = x.shape
    rows = owners * CAP
    line = Line(spread, owners, x, part, stage, arrived, final, returned, sems)

    def kept(s):
        yield pltpu.make_async_copy(x.at[:, s], x_keep.at[:, s], keep_sem.at[0, s])
        yield pltpu.make_async_copy(g_all.at[s], g_keep.at[s], keep_sem.at[1, s])
        yield pltpu.make_async_copy(u_all.at[s], u_keep.at[s], keep_sem.at[2, s])

    def compute(s):
        def one(l, carry):
            rows_in = x[l, s].reshape(rows, width)
            total = jnp.zeros((rows, width), F32)
            for p in range(parts):
                cols = gate[p].shape[2]
                g = dot_nn(rows_in, gate[p][l])
                u = dot_nn(rows_in, up[p][l])
                g_all[s, l, :, p * cols : (p + 1) * cols] = g
                u_all[s, l, :, p * cols : (p + 1) * cols] = u
                act = (g * jax.nn.sigmoid(g) * u).astype(BF16)
                total = total + dot_nn(act, down[p][l])
            part[s, l] = total.reshape(owners, CAP, width)
            return carry

        lax.fori_loop(0, local, one, 0)
        for copy in list(kept(s))[1:]:
            copy.start()

    line.run(out, compute, lambda: None, lambda s: next(kept(s)).start())
    for s in range(LINE):
        for copy in kept(s):
            copy.wait()


def expert_backward_kernel(spread, parts, out, x_in, g_all, u_all, *refs):
    gate, up, down = refs[:parts], refs[parts : 2 * parts], refs[2 * parts : 3 * parts]
    returned = refs[3 * parts]
    grads = refs[3 * parts + 1 : 6 * parts + 1]
    x, part, stage, arrived, final = refs[6 * parts + 1 : 6 * parts + 6]
    sems, (act_all, gg_all, gu_all) = refs[6 * parts + 6 : 6 * parts + 13], refs[6 * parts + 13 :]
    local, _, owners, _, width = x.shape
    rows = owners * CAP
    line = Line(spread, owners, x, part, stage, arrived, final, returned, sems)

    def compute(s):
        at = pl.multiple_of(s * rows, rows)

        def one(l, carry):
            rows_in = x[l, s].reshape(rows, width)
            total = jnp.zeros((rows, width), F32)
            for p in range(parts):
                cols = gate[p].shape[2]
                here = slice(p * cols, (p + 1) * cols)
                g, u = g_all[s, l, :, here], u_all[s, l, :, here]
                g_act = dot_nt(rows_in, down[p][l])
                sigma = jax.nn.sigmoid(g)
                swish = g * sigma
                gg = (g_act * u * sigma * (1.0 + g * (1.0 - sigma))).astype(BF16)
                gu = (g_act * swish).astype(BF16)
                act_all[l, pl.ds(at, rows), here] = (swish * u).astype(BF16)
                gg_all[l, pl.ds(at, rows), here] = gg
                gu_all[l, pl.ds(at, rows), here] = gu
                total = total + dot_nt(gg, gate[p][l]) + dot_nt(gu, up[p][l])
            part[s, l] = total.reshape(owners, CAP, width)
            return carry

        lax.fori_loop(0, local, one, 0)

    def weights():
        def one(l, carry):
            x_rows = x_in[l].reshape(LINE * rows, width)
            g_rows = x[l].reshape(LINE * rows, width)
            for p in range(parts):
                cols = gate[p].shape[2]
                here = slice(p * cols, (p + 1) * cols)
                for grad, value in (
                    (grads[p], dot_tn(x_rows, gg_all[l, :, here])),
                    (grads[parts + p], dot_tn(x_rows, gu_all[l, :, here])),
                    (grads[2 * parts + p], dot_tn(act_all[l, :, here], g_rows)),
                ):
                    grad[l] = value.astype(grad.dtype)
            return carry

        lax.fori_loop(0, local, one, 0)

    line.run(out, compute, weights, lambda s: None)


def expert_forward(spread, call_id, out, weights):
    parts = len(weights) // 3
    owners, local, cap, width = out.shape
    columns = sum(w.shape[2] for w in weights[:parts])
    kept = (LINE, local, owners * cap, columns)
    return pl.pallas_call(
        functools.partial(expert_forward_kernel, spread, parts),
        out_shape=[
            jax.ShapeDtypeStruct(out.shape, BF16),
            jax.ShapeDtypeStruct((local, LINE, owners, cap, width), BF16),
            jax.ShapeDtypeStruct(kept, F32),
            jax.ShapeDtypeStruct(kept, F32),
        ],
        in_specs=[VMEM] * (1 + len(weights)),
        out_specs=[VMEM, ANY, ANY, ANY],
        scratch_shapes=line_scratch(local, owners, width)
        + [pltpu.VMEM(kept, F32), pltpu.VMEM(kept, F32), pltpu.SemaphoreType.DMA((3, LINE))],
        compiler_params=pltpu.CompilerParams(
            collective_id=call_id, has_side_effects=True, vmem_limit_bytes=60 * 2**20
        ),
    )(out, *weights)


def expert_backward(spread, call_id, out, kept, weights):
    parts = len(weights) // 3
    owners, local, cap, width = out.shape
    columns = sum(w.shape[2] for w in weights[:parts])
    shapes = [
        jax.ShapeDtypeStruct(w.shape, F32 if i % parts == 0 else BF16) for i, w in enumerate(weights)
    ]
    wide = pltpu.VMEM((local, LINE * owners * cap, columns), BF16)
    return pl.pallas_call(
        functools.partial(expert_backward_kernel, spread, parts),
        out_shape=[jax.ShapeDtypeStruct(out.shape, BF16)] + shapes,
        in_specs=[VMEM] * (4 + len(weights)),
        out_specs=[VMEM] * (1 + len(weights)),
        scratch_shapes=line_scratch(local, owners, width) + [wide] * 3,
        compiler_params=pltpu.CompilerParams(
            collective_id=call_id, has_side_effects=True, vmem_limit_bytes=60 * 2**20
        ),
    )(out, *kept, *weights)


def from_partner(array, shift, spread, groups):
    pairs = [
        (t * spread + (f + shift) % spread, t * spread + f) for t in range(groups) for f in range(spread)
    ]
    return lax.ppermute(array, "dp", pairs)


def to_partner(array, shift, spread, groups):
    pairs = [
        (t * spread + f, t * spread + (f + shift) % spread) for t in range(groups) for f in range(spread)
    ]
    return lax.ppermute(array, "dp", pairs)


def pair_weights(shard, axis, spread):
    shard = shard.astype(BF16)
    parts = [shard] + [from_partner(shard, i, spread, LINE) for i in range(1, spread)]
    if shard.shape[axis] % 128:
        return [jnp.concatenate(parts, axis=axis)]
    return parts


def pair_sum(parts, axis, spread):
    if len(parts) == 1 and spread > 1:
        parts = jnp.split(parts[0], spread, axis=axis)
    total = parts[0]
    for i in range(1, spread):
        total = total + to_partner(parts[i].astype(BF16), i, spread, LINE).astype(F32)
    return total


def per_device(
    tokens, seq_lengths, block_perm, routes, norm_gains, w_qkv, w_out, w_router, w_residual, w_const, v_const,
    w_gate, w_up, w_down, cotangent,
):
    rows, width = tokens.shape
    owners = lax.axis_size("expert")
    shards = lax.axis_size("dp")
    spread = shards // LINE
    local = w_gate.shape[1]
    experts = local * owners
    layers = routes.shape[0]
    slots = experts * CAP
    place = lax.axis_index("expert")

    my_place = jnp.sum(jnp.where(jnp.arange(owners) == place, block_perm[0], 0))
    all_routes = lax.all_gather(routes, "expert", axis=0)
    my_routes = lax.dynamic_index_in_dim(all_routes, my_place, 0, keepdims=False)
    lengths = lax.dynamic_index_in_dim(seq_lengths[0], place, 0, keepdims=False)
    order = jnp.arange(lengths.shape[0])
    ends = jnp.sum(jnp.where(order[:, None] <= order[None, :], lengths[:, None], 0), axis=0)
    doc = jnp.sum((jnp.arange(rows)[:, None] >= ends[None, :]).astype(jnp.int32), axis=1)
    doc_col, doc_row = doc[:, None], doc[None, :]

    weights = []
    for l in range(layers):
        weights.append(
            pair_weights(w_gate[l], 2, spread) + pair_weights(w_up[l], 2, spread) + pair_weights(w_down[l], 1, spread)
        )

    depth = w_out.shape[1]
    small = jnp.concatenate(
        [
            w_router, w_const[:, 0], w_const[:, 1], jnp.swapaxes(norm_gains, 1, 2), jnp.swapaxes(v_const, 1, 2),
            jnp.zeros((layers, depth, 108), F32),
        ],
        axis=2,
    ).astype(BF16)
    qkv_t = jnp.swapaxes(w_qkv, 1, 2).astype(BF16)
    qkv_all = lax.all_gather(qkv_t, "dp", axis=1, tiled=True)
    out_all = lax.all_gather(w_out.astype(BF16), "dp", axis=1, tiled=True)
    small_all = lax.all_gather(small, "dp", axis=1, tiled=True)
    dense = [(small_all[l], qkv_all[l], out_all[l]) for l in range(layers)]
    w_res = jnp.zeros((128, 128), F32).at[: w_residual.shape[0], : w_residual.shape[1]].set(w_residual)

    cols = ((rows, width), F32)
    attention = [((rows, width), BF16), ((rows, 3 * width), BF16), ((HEADS, rows, rows), F32), ((rows, width), BF16)]
    per_token, sent = ((rows, 128), F32), ((slots, width), BF16)

    def group(array):
        return array.reshape(owners, local, CAP, width)

    attn_in0, qkv0, probs0, attn0, mid0, logits0, stat0, out = local_call(
        first_kernel, experts, (tokens, *dense[0], doc_col, doc_row, my_routes[0]),
        attention + [cols, per_token, per_token, sent])
    ret0, *kept0 = expert_forward(spread, 0, group(out), weights[0])
    ret0 = ret0.reshape(slots, width)
    stream1, attn_in1, qkv1, probs1, attn1, mid1, stat1, out = local_call(
        middle_kernel, experts,
        (mid0, dense[0][0], stat0, ret0, *dense[1], doc_col, doc_row, my_routes[1], logits0, w_res),
        [cols] + attention + [cols, per_token, sent])
    ret1, *kept1 = expert_forward(spread, 1, group(out), weights[1])
    ret1 = ret1.reshape(slots, width)

    small_grads = ((24, width), F32)
    output, g_small1, extra, out, small_grad1, res_grad = local_call(
        turn_kernel, experts, (mid1, dense[1][0], stat1, ret1, cotangent, logits0, w_res),
        [((rows, width), BF16), per_token, per_token, sent, small_grads, ((128, 128), F32)])
    back, *expert_grads1 = expert_backward(spread, 2, group(out), kept1, weights[1])
    dense_grads = [((3 * width, width), F32), ((width, width), F32), small_grads]
    attention_scratch = [((rows, 3 * width), BF16), ((rows, width), BF16)]
    qkv_grad1, out_grad1, small_grad1, grad, g_small0, out, small_grad0 = local_call(
        between_kernel, experts,
        (cotangent, back.reshape(slots, width), g_small1, stat1, mid1, dense[1][0], stream1, dense[1][1], dense[1][2],
         attn_in1, qkv1, probs1, attn1, small_grad1, mid0, dense[0][0], stat0, ret0, extra),
        dense_grads + [cols, per_token, sent, small_grads], attention_scratch)
    back, *expert_grads0 = expert_backward(spread, 3, group(out), kept0, weights[0])
    qkv_grad0, out_grad0, small_grad0, tokens_grad = local_call(
        last_kernel, experts,
        (grad, back.reshape(slots, width), g_small0, stat0, mid0, dense[0][0], tokens, dense[0][1], dense[0][2],
         attn_in0, qkv0, probs0, attn0, small_grad0),
        dense_grads + [cols], attention_scratch)

    expert_out = []
    for axis, at in ((2, 0), (2, 1), (1, 2)):
        per_layer = []
        for grads in (expert_grads0, expert_grads1):
            n = len(grads) // 3
            per_layer.append(pair_sum(grads[at * n : (at + 1) * n], axis, spread))
        expert_out.append(jnp.stack(per_layer))
    gate_grad, up_grad, down_grad = expert_out
    qkv_grad = lax.psum(
        lax.psum_scatter(jnp.stack([qkv_grad0, qkv_grad1]), "dp", scatter_dimension=1, tiled=True), "expert")
    out_grad = lax.psum(
        lax.psum_scatter(jnp.stack([out_grad0, out_grad1]), "dp", scatter_dimension=1, tiled=True), "expert")
    packed = jnp.concatenate([small_grad0, small_grad1, jnp.pad(res_grad[:16], ((0, 0), (0, width - 128)))])
    packed = lax.psum(packed, ("dp", "expert"))
    mine = lax.dynamic_slice_in_dim(packed, lax.axis_index("dp") * depth, depth, axis=1)
    mine = jnp.stack([mine[:24], mine[24:48]])
    router_grad = jnp.swapaxes(mine[:, :CONST0], 1, 2)
    const_grad = jnp.swapaxes(mine[:, CONST0:GAIN0].reshape(layers, 2, 2, depth), 2, 3)
    residual_grad = packed[48 : 48 + CONST0, :CONST0]
    return (
        output, tokens_grad, mine[:, GAIN0 : GAIN0 + 2], jnp.swapaxes(qkv_grad, 1, 2), out_grad, router_grad,
        residual_grad, const_grad, mine[:, VECTOR0 : VECTOR0 + 2], gate_grad, up_grad, down_grad,
    )


def solution(mesh):
    in_specs = (
        P(("dp", "expert"), None), P("dp", None, None), P("dp", None), P(None, ("dp", "expert"), None),
        P(None, None, "dp"), P(None, None, "dp"), P(None, "dp", None), P(None, "dp", None), P(),
        P(None, None, "dp", None), P(None, None, "dp"), P(None, "expert", None, "dp"), P(None, "expert", None, "dp"),
        P(None, "expert", "dp", None), P(("dp", "expert"), None),
    )
    out_specs = (
        P(("dp", "expert"), None), P(("dp", "expert"), None), P(None, None, "dp"), P(None, None, "dp"),
        P(None, "dp", None), P(None, "dp", None), P(), P(None, None, "dp", None), P(None, None, "dp"),
        P(None, "expert", None, "dp"), P(None, "expert", None, "dp"), P(None, "expert", "dp", None),
    )
    return jax.shard_map(per_device, mesh=mesh, in_specs=in_specs, out_specs=out_specs, check_vma=False)
```

time: 3110 us -> 1200 us (0.39)
  waiting for transfers between devices: 2390 us -> 528 us
  Pallas kernels: 0 us -> 443 us
  matrix products: 158 us -> 0 us
  local copies, waits for them, and re-layouts: 146 us -> 27.5 us
  other arithmetic: 130 us -> 41.9 us
  blocking collectives: 203 us -> 121 us
  starting transfers between devices: 48 us -> 16.2 us
    reduce_scatter x4 -> x2, waiting for transfers between devices: 1320 us -> 322 us  [the longest x1 232 us: per_device(): lax.psum_scatter(jnp.stack([qkv_grad0, qkv_grad1]), 'dp', scatter_dimensi...]
    unnamed x20 -> x6, waiting for transfers between devices: 514 us -> 0.1 us
    pallas_call x0 -> x9, Pallas kernels: none -> 443 us  [the longest x2 196 us: expert_backward(): pl.pallas_call(functools.partial(expert_backward_kernel, spread, parts),...]
    all_gather x5 -> x2, waiting for transfers between devices: 481 us -> 57.6 us  [the longest x1 57.6 us: per_device(): qkv_all = lax.all_gather(qkv_t, 'dp', axis=1, tiled=True)]
    dot_general x62 -> x0, matrix products: 158 us -> none  [the longest x2 16.3 us: per_device(): jnp.einsum('sjcd,jfd->sjcf', at_owner, down_weight, preferred_element_typ...]
    psum x1 -> x2, waiting for transfers between devices: 44.1 us -> 148 us  [the longest x1 101 us: per_device(): packed = lax.psum(packed, ('dp', 'expert'))]
    psum x2 -> x0, blocking collectives: 70.1 us -> none  [the longest x1 58.8 us: per_device(): residual_grad = lax.psum(residual_part, ('dp', 'expert'))]
    all_to_all x12 -> x0, starting transfers between devices: 46.9 us -> none  [the longest x2 8.88 us: per_device(): lax.all_to_all(grad_send, 'expert', split_axis=0, concat_axis=0, tiled=True)]
  transfers between devices with their start and end apart: 27 -> 18, of which waited for: 17 -> 5; matrix products, arithmetic and copies ran while one was open for 8% -> 5% of each run, Pallas kernels for 0% -> 10%
where the time goes in v1:
time: 1200 us; the launch traced here: 1190 us
  waiting for transfers between devices  528 us (44%)
  Pallas kernels  443 us (37%)
  blocking collectives  121 us (10%)
  other arithmetic  41.9 us (3%)
  local copies, waits for them, and re-layouts  27.5 us (2%)
  between operations  17 us (1%)
  starting transfers between devices  16.2 us (1%)
    reduce_scatter x1, waiting for transfers between devices, per_device(): lax.psum_scatter(jnp.stack([qkv_grad0, qkv_grad1]), 'dp', scatter_dimensi...  232 us
    pallas_call x2, Pallas kernels, expert_backward(): pl.pallas_call(functools.partial(expert_backward_kernel, spread, parts),...  196 us
    pallas_call x2, Pallas kernels, expert_forward(): pl.pallas_call(functools.partial(expert_forward_kernel, spread, parts), o...  184 us
    all_gather x1, blocking collectives, per_device(): small_all = lax.all_gather(small, 'dp', axis=1, tiled=True)  116 us
    psum x1, waiting for transfers between devices, per_device(): packed = lax.psum(packed, ('dp', 'expert'))  101 us
    reduce_scatter x1, waiting for transfers between devices, per_device(): lax.psum_scatter(jnp.stack([out_grad0, out_grad1]), 'dp', scatter_dimensi...  89.4 us
    pallas_call x5, Pallas kernels, local_call(): pl.pallas_call(functools.partial(kernel, experts), out_shape=[jax.ShapeDt...  62.5 us
    all_gather x1, waiting for transfers between devices, per_device(): qkv_all = lax.all_gather(qkv_t, 'dp', axis=1, tiled=True)  57.6 us
  transfers between devices with their start and end apart: 18, of which 5 were waited for; matrix products, arithmetic and copies ran while one was open for 5% of the time, Pallas kernels for 10%

profile of v1, /device:TPU:0, one launch (start us, length us, event | category | flops | bytes accessed | tf_op | source)
XLA Modules:
  0.0 1194.4 jit_solution(14566854665617762347)
XLA Ops:
  7.2 1.8 convert_element_type.53
  9.1 2.5 convert_bitcast_fusion
  11.7 2.0 convert.37
  13.9 3.0 collective-permute-start
  17.1 1.0 slice_bitcast_fusion.5
  18.0 2.2 collective-permute-start.1
  20.5 1.0 slice_bitcast_fusion.4
  21.5 1.5 collective-permute-start.2
  23.0 0.6 collective-permute-start.3
  23.6 1.5 collective-permute-start.4
  25.0 0.6 fusion.4
  27.0 5.2 all-gather
  32.2 1.2 copy.53
  33.5 0.8 copy.54.doc_col
  35.6 0.6 scatter.4.w_res
  36.4 1.6 dynamic-slice_bitcast_fusion
  38.0 116.2 %all_gather.15 = bf16[2,768,128]{2,1,0:T(8,128)(2,1)S(1)} all-gather(bf16[2,96,128]{2,1,0:T(8,128)(2,1)S(1)} %concatenate.9), channel_id=1, replica_groups=mesh['dp'=8,'expert'=4] {'dp'}, dimensions={1}, use_global_device_ids=true | all-gather | bytes 442368 | tf_op jit(solution)/shard_map/all_gather | solution.py:744
  154.2 0.8 slice_bitcast_fusion.10
  155.0 3.3 slice_bitcast_fusion.2
  158.2 1.2 collective-permute-start.5
  159.5 57.6 %all-gather.4.cloned.1.call-done = bf16[2,2304,768]{2,1,0:T(8,128)(2,1)} async-done(((bf16[2,288,768]{2,1,0:T(8,128)(2,1)}), bf16[2,2304,768]{2,1,0:T(8,128)(2,1)}) %all-gather.4.cloned.1.call-update) | async-done | bytes 7077904 | tf_op jit(solution)/shard_map/all_gather | solution.py:742
  217.0 6.5 slice_bitcast_fusion
  223.5 10.8 shard_map.238
  234.3 92.2 %shard_map.239 = (bf16[4,2,48,768]{3,2,1,0:T(8,128)(2,1)}, bf16[2,4,4,48,768]{4,3,2,1,0:T(8,128)(2,1)}, f32[4,2,192,512]{3,2,1,0:T(8,128)}, f32[4,2,192,512]{3,2,1,0:T(8,128)}) custom-call(bf16[4,2,48,768]{3,2,1,0:T(8,128)(2,1)} %bitcast.87, bf16[2,768,256]{2,1,0:T(8,128)(2,1)} %copy-done.2, bf16[2,768,256]{2,1,0:T(8,128)(2,1)} %collective-permute-done.refs_1_, ...), custom_call_target="tpu_custom_call" | custom-call | tf_op jit(solution)/shard_map/pallas_call | solution.py:635
  326.5 11.6 shard_map.240
  338.2 0.9 copy-done.10
  339.0 92.1 %shard_map.241 = (bf16[4,2,48,768]{3,2,1,0:T(8,128)(2,1)}, bf16[2,4,4,48,768]{4,3,2,1,0:T(8,128)(2,1)}, f32[4,2,192,512]{3,2,1,0:T(8,128)}, f32[4,2,192,512]{3,2,1,0:T(8,128)}) custom-call(bf16[4,2,48,768]{3,2,1,0:T(8,128)(2,1)} %bitcast.86, bf16[2,768,256]{2,1,0:T(8,128)(2,1)} %copy-done.5, bf16[2,768,256]{2,1,0:T(8,128)(2,1)} %collective-permute-done.3.refs_1_, ...), custom_call_target="tpu_custom_call" | custom-call | tf_op jit(solution)/shard_map/pallas_call | solution.py:635
  431.1 5.6 shard_map.242
  436.7 0.7 slice.118
  437.4 98.2 %shard_map.243 = (bf16[4,2,48,768]{3,2,1,0:T(8,128)(2,1)}, f32[2,768,256]{2,1,0:T(8,128)}, bf16[2,768,256]{2,1,0:T(8,128)(2,1)}, f32[2,768,256]{2,1,0:T(8,128)},...) custom-call(bf16[4,2,48,768]{3,2,1,0:T(8,128)(2,1)} %bitcast.91, ...), custom_call_target="tpu_custom_call" | custom-call | tf_op jit(solution)/shard_map/pallas_call | solution.py:661
  535.6 17.9 %shard_map.244 = (f32[2304,768]{1,0:T(8,128)}, f32[768,768]{1,0:T(8,128)}, f32[24,768]{1,0:T(8,128)}, f32[192,768]{1,0:T(8,128)}, f32[192,128]{1,0:T(8,128)}, /*...) custom-call(bf16[192,768]{1,0:T(8,128)(2,1)} %cotangent.3, bf16[384,768]{1,0:T(8,128)(2,1)} %bitcast.89, ...), custom_call_target="tpu_custom_call" | custom-call | tf_op jit(solution)/shard_map/pallas_call | solution.py:335
  553.5 97.6 %shard_map.245 = (bf16[4,2,48,768]{3,2,1,0:T(8,128)(2,1)}, f32[2,768,256]{2,1,0:T(8,128)}, bf16[2,768,256]{2,1,0:T(8,128)(2,1)}, f32[2,768,256]{2,1,0:T(8,128)},...) custom-call(bf16[4,2,48,768]{3,2,1,0:T(8,128)(2,1)} %bitcast.90, ...), custom_call_target="tpu_custom_call" | custom-call | tf_op jit(solution)/shard_map/pallas_call | solution.py:661
  651.1 16.6 %shard_map.246 = (f32[2304,768]{1,0:T(8,128)}, f32[768,768]{1,0:T(8,128)}, f32[24,768]{1,0:T(8,128)}, f32[192,768]{1,0:T(8,128)}) custom-call(f32[192,768]{1,0:T(8,128)} %get-tuple-element.102.grad_in, bf16[384,768]{1,0:T(8,128)(2,1)} %bitcast.85, f32[192,128]{1,0:T(8,128)} %get-tuple-element.108.g_small, f32[192,128]{1,0:T(8,128)} %get-tuple-element.80.stat_in.stat0_in, ...), custom_call_target="tpu_custom_call" | custom-call | tf_op jit(solution)/shard_map/pallas_call | solution.py:335
  667.7 1.6 select_maximum_fusion
  669.4 4.4 pad_maximum_fusion.1
  673.9 11.0 pad_maximum_fusion
  684.9 0.3 all-reduce.8.cloned.1.call-start
  685.3 2.0 collective-permute-start.11
  687.4 1.9 collective-permute-start.9
  689.5 101.0 %all-reduce.6.cloned.1.call-done = f32[64,768]{1,0:T(8,128)} async-done(((f32[64,768]{1,0:T(8,128)}), f32[64,768]{1,0:T(8,128)}) %all-reduce.6.cloned.1.call-update) | async-done | bytes 196624 | tf_op jit(solution)/shard_map/psum | solution.py:799
  790.4 0.8 dynamic-slice_bitcast_fusion.3
  791.3 0.6 fusion.2
  791.9 0.6 copy.56
  792.5 1.3 slice.142
  793.8 0.6 pad_maximum_fusion.5
  794.3 1.5 collective-permute-start.7
  795.9 1.4 add_bitcast_fusion.1
  797.3 0.2 copy-done.14
  797.5 1.4 add_bitcast_fusion
  798.9 0.2 copy-done.16
  799.1 2.5 add_bitcast_fusion.3
  801.7 2.5 add_bitcast_fusion.2
  804.2 89.4 %reduce-scatter.5.cloned.1.call-done = f32[2,96,768]{2,1,0:T(8,128)} async-done(((f32[2,768,768]{2,1,0:T(8,128)}), f32[2,96,768]{2,1,0:T(8,128)}) %reduce-scatter.5.cloned.1.call-update) | async-done | bytes 589840 | tf_op jit(solution)/shard_map/reduce_scatter | solution.py:797
  893.6 232.5 %reduce-scatter.3.cloned.1.call-done = f32[2,288,768]{2,1,0:T(8,128)} async-done(((f32[2,2304,768]{2,1,0:T(8,128)}), f32[2,288,768]{2,1,0:T(8,128)}) %reduce-scatter.3.cloned.1.call-update) | async-done | bytes 1769488 | tf_op jit(solution)/shard_map/reduce_scatter | solution.py:795
  1126.1 1.9 pad_maximum_fusion.4
  1128.1 1.1 copy-done.7
  1129.1 1.9 pad_maximum_fusion.3
  1131.2 1.5 add_bitcast_fusion.5
  1132.6 0.2 copy-done.12
  1132.8 1.3 add_bitcast_fusion.4
  1134.1 1.9 pad_maximum_fusion.2
  1136.0 47.4 %all-reduce.8.cloned.1.call-done = (f32[2,768,288]{1,2,0:T(8,128)}, f32[2,96,768]{2,1,0:T(8,128)}) async-done(((f32[2,768,288]{1,2,0:T(8,128)}, f32[2,96,768]{2,1,0:T(8,128)}), (f32[2,768,288]{1,2,0:T(8,128)}, f32[2,96,768]{2,1,0:T(8,128)})) %all-reduce.8.cloned.1.call-update) | async-done | bytes 2359312 | tf_op jit(solution)/shard_map/psum | solution.py:794
  1183.4 2.9 copy.60
  1186.3 0.8 copy.61
  (97 shorter events, 2.2 us)
Async XLA Ops:
  7.2 26.2 %copy-start = (s32[1,4,4]{2,1,0:T(4,128)S(1)}, s32[1,4,4]{2,1,0:T(4,128)}, u32[]{:S(2)}) copy-start(s32[1,4,4]{2,1,0:T(4,128)} %param.18) | copy-start | bytes 196
  7.2 147.8 %all-gather.6.cloned.1.call-start = ((), (), s32[]{:S(2)}) async-start(), calls=%async_computation.3 | async-start | bytes 2654208 | tf_op jit(solution)/shard_map/all_gather | solution.py:743
  9.1 208.0 %all-gather.4.cloned.1.call-start = ((), (), s32[]{:S(2)}) async-start(), calls=%async_computation.2 | async-start | bytes 7962624 | tf_op jit(solution)/shard_map/all_gather | solution.py:742
  11.6 778.8 %all-reduce.6.cloned.1.call-start = ((), (), s32[]{:S(2)}) async-start(), calls=%async_computation.4 | async-start | bytes 393216 | tf_op jit(solution)/shard_map/psum | solution.py:799
  13.7 3.1 copy-start.8
  13.8 3.2 copy-start.2
  13.9 9.1 copy-start.5
  13.9 144.4 %collective-permute-start = (bf16[2,768,256]{2,1,0:T(8,128)(2,1)S(1)}, bf16[2,768,256]{2,1,0:T(8,128)(2,1)}, u32[]{:S(2)}, u32[]{:S(2)}) collective-permute-start(bf16[2,768,256]{2,1,0:T(8,128)(2,1)S(1)} %get-tuple-element.193.refs_0_), channel_id=1, source_target_pairs={{4,0},{0,4},{12,8},{8,12},{20,16},{16,20},{28,24},{24,28},{5,1},{1... | collective-permute-start | bytes 2359304 | tf_op jit(solution)/shard_map/ppermute | solution.py:677
  17.0 3.2 copy-start.9
  18.0 2.4 copy-start.3
  18.0 216.3 %collective-permute-start.1 = (bf16[2,768,256]{2,1,0:T(8,128)(2,1)S(1)}, bf16[2,768,256]{2,1,0:T(8,128)(2,1)}, u32[]{:S(2)}, u32[]{:S(2)}) collective-permute-start(bf16[2,768,256]{2,1,0:T(8,128)(2,1)S(1)} %get-tuple-element.191.refs_2_), channel_id=1, source_target_pairs={{4,0},{0,4},{12,8},{8,12},{20,16},{16,20},{28,24},{24,28},{5,1},{1... | collective-permute-start | bytes 2359304 | tf_op jit(solution)/shard_map/ppermute | solution.py:677
  20.5 4.6 copy-start.28
  20.5 6.5 copy-start.24
  20.5 13.8 %copy-start.25 = (f32[2,2,96,2]{2,3,1,0:T(2,128)S(1)}, f32[2,2,96,2]{2,3,1,0:T(2,128)}, u32[]{:S(2)}) copy-start(f32[2,2,96,2]{2,3,1,0:T(2,128)} %param.26) | copy-start | bytes 9220
  20.5 14.0 %copy-start.21 = (f32[2,96,12]{1,0,2:T(2,128)S(1)}, f32[2,96,12]{1,0,2:T(2,128)}, u32[]{:S(2)}) copy-start(f32[2,96,12]{1,0,2:T(2,128)} %param.24) | copy-start | bytes 27652
  20.5 14.1 %copy-start.26 = (f32[2,2,96]{2,1,0:T(2,128)S(1)}, f32[2,2,96]{2,1,0:T(2,128)}, u32[]{:S(2)}) copy-start(f32[2,2,96]{2,1,0:T(2,128)} %param.21) | copy-start | bytes 4612
  20.5 14.2 %copy-start.27 = (f32[2,2,96]{2,1,0:T(2,128)S(1)}, f32[2,2,96]{2,1,0:T(2,128)}, u32[]{:S(2)}) copy-start(f32[2,2,96]{2,1,0:T(2,128)} %param.27) | copy-start | bytes 4612
  20.5 15.0 %copy-start.23 = (f32[12,12]{1,0:T(8,128)S(1)}, f32[12,12]{1,0:T(8,128)}, u32[]{:S(2)}) copy-start(f32[12,12]{1,0:T(8,128)} %param.25) | copy-start | bytes 1732
  21.5 133.4 %copy-start.4 = (bf16[2,256,768]{2,1,0:T(8,128)(2,1)}, bf16[2,256,768]{2,1,0:T(8,128)(2,1)S(1)}, u32[]{:S(2)}) copy-start(bf16[2,256,768]{2,1,0:T(8,128)(2,1)S(1)} %get-tuple-element.189.refs_4_) | copy-start | bytes 2359300
  21.5 212.8 %collective-permute-start.2 = (bf16[2,256,768]{2,1,0:T(8,128)(2,1)S(1)}, bf16[2,256,768]{2,1,0:T(8,128)(2,1)}, u32[]{:S(2)}, u32[]{:S(2)}) collective-permute-start(bf16[2,256,768]{2,1,0:T(8,128)(2,1)S(1)} %get-tuple-element.189.refs_4_), channel_id=1, source_target_pairs={{4,0},{0,4},{12,8},{8,12},{20,16},{16,20},{28,24},{24,28},{5,1},{1... | collective-permute-start | bytes 2359304 | tf_op jit(solution)/shard_map/ppermute | solution.py:677
  23.0 315.1 %collective-permute-start.3 = (bf16[2,768,256]{2,1,0:T(8,128)(2,1)S(1)}, bf16[2,768,256]{2,1,0:T(8,128)(2,1)}, u32[]{:S(2)}, u32[]{:S(2)}) collective-permute-start(bf16[2,768,256]{2,1,0:T(8,128)(2,1)S(1)} %get-tuple-element.192.refs_0_), channel_id=1, source_target_pairs={{4,0},{0,4},{12,8},{8,12},{20,16},{16,20},{28,24},{24,28},{5,1},{1... | collective-permute-start | bytes 2359304 | tf_op jit(solution)/shard_map/ppermute | solution.py:677
  23.6 314.6 %collective-permute-start.4 = (bf16[2,768,256]{2,1,0:T(8,128)(2,1)}, bf16[2,768,256]{2,1,0:T(8,128)(2,1)}, u32[]{:S(2)}, u32[]{:S(2)}) collective-permute-start(bf16[2,768,256]{2,1,0:T(8,128)(2,1)} %get-tuple-element.190.refs_2_), channel_id=1, source_target_pairs={{4,0},{0,4},{12,8},{8,12},{20,16},{16,20},{28,24},{24,28},{5,1},{1... | collective-permute-start | bytes 2359304 | tf_op jit(solution)/shard_map/ppermute | solution.py:677
  33.5 124.7 %copy-start.22 = (s32[192]{0:T(256)}, s32[192]{0:T(256)S(1)}, u32[]{:S(2)}) copy-start(s32[192]{0:T(256)S(1)} %convert_reduce_fusion) | copy-start | bytes 2308
  158.2 179.9 %collective-permute-start.5 = (bf16[2,256,768]{2,1,0:T(8,128)(2,1)}, bf16[2,256,768]{2,1,0:T(8,128)(2,1)S(1)}, u32[]{:S(2)}, u32[]{:S(2)}) collective-permute-start(bf16[2,256,768]{2,1,0:T(8,128)(2,1)} %get-tuple-element.188.refs_4_), channel_id=1, source_target_pairs={{4,0},{0,4},{12,8},{8,12},{20,16},{16,20},{28,24},{24,28},{5,1},{1... | collective-permute-start | bytes 2359304 | tf_op jit(solution)/shard_map/ppermute | solution.py:677
  338.1 0.9 copy-start.10
  651.1 16.7 %copy-start.20 = (f32[24,768]{1,0:T(8,128)S(1)}, f32[24,768]{1,0:T(8,128)}, u32[]{:S(2)}) copy-start(f32[24,768]{1,0:T(8,128)} %get-tuple-element.116) | copy-start | bytes 221188
  651.1 18.3 %copy-start.11 = (f32[768,768]{1,0:T(8,128)S(1)}, f32[768,768]{1,0:T(8,128)}, u32[]{:S(2)}) copy-start(f32[768,768]{1,0:T(8,128)} %get-tuple-element.121) | copy-start | bytes 7077892
  669.3 224.3 %reduce-scatter.5.cloned.1.call-start = ((), (), s32[]{:S(2)}) async-start(), calls=%async_computation.6 | async-start | bytes 5308416 | tf_op jit(solution)/shard_map/reduce_scatter | solution.py:797
  673.8 452.3 %reduce-scatter.3.cloned.1.call-start = ((), (), s32[]{:S(2)}) async-start(), calls=%async_computation.5 | async-start | bytes 15925248 | tf_op jit(solution)/shard_map/reduce_scatter | solution.py:795
  684.9 111.0 %copy-start.17 = (f32[2,256,768]{2,1,0:T(8,128)S(1)}, f32[2,256,768]{2,1,0:T(8,128)}, u32[]{:S(2)}) copy-start(f32[2,256,768]{2,1,0:T(8,128)} %get-tuple-element.130) | copy-start | bytes 4718596
  684.9 498.5 %all-reduce.8.cloned.1.call-start = ((), (), s32[]{:S(2)}) async-start(), calls=%async_computation.7 | async-start | bytes 4718592 | tf_op jit(solution)/shard_map/psum | solution.py:794
  685.2 109.1 %collective-permute-start.10 = (bf16[2,256,768]{2,1,0:T(8,128)(2,1)}, bf16[2,256,768]{2,1,0:T(8,128)(2,1)S(1)}, u32[]{:S(2)}, u32[]{:S(2)}) collective-permute-start(bf16[2,256,768]{2,1,0:T(8,128)(2,1)} %get-tuple-element.131), channel_id=1, source_target_pairs={{0,4},{4,0},{8,12},{12,8},{16,20},{20,16},{24,28},{28,24},{1,5},{5... | collective-permute-start | bytes 2359304 | tf_op jit(solution)/shard_map/ppermute | solution.py:684
  685.3 112.0 %collective-permute-start.11 = (bf16[2,256,768]{2,1,0:T(8,128)(2,1)}, bf16[2,256,768]{2,1,0:T(8,128)(2,1)}, u32[]{:S(2)}, u32[]{:S(2)}) collective-permute-start(bf16[2,256,768]{2,1,0:T(8,128)(2,1)} %get-tuple-element.133), channel_id=1, source_target_pairs={{0,4},{4,0},{8,12},{12,8},{16,20},{20,16},{24,28},{28,24},{1,5},{5... | collective-permute-start | bytes 2359304 | tf_op jit(solution)/shard_map/ppermute | solution.py:684
  687.3 111.6 %collective-permute-start.8 = (bf16[2,768,256]{2,1,0:T(8,128)(2,1)}, bf16[2,768,256]{2,1,0:T(8,128)(2,1)}, u32[]{:S(2)}, u32[]{:S(2)}) collective-permute-start(bf16[2,768,256]{2,1,0:T(8,128)(2,1)} %get-tuple-element.127), channel_id=1, source_target_pairs={{0,4},{4,0},{8,12},{12,8},{16,20},{20,16},{24,28},{28,24},{1,5},{5... | collective-permute-start | bytes 2359304 | tf_op jit(solution)/shard_map/ppermute | solution.py:684
  687.4 114.3 %collective-permute-start.9 = (bf16[2,768,256]{2,1,0:T(8,128)(2,1)}, bf16[2,768,256]{2,1,0:T(8,128)(2,1)}, u32[]{:S(2)}, u32[]{:S(2)}) collective-permute-start(bf16[2,768,256]{2,1,0:T(8,128)(2,1)} %get-tuple-element.129), channel_id=1, source_target_pairs={{0,4},{4,0},{8,12},{12,8},{16,20},{20,16},{24,28},{28,24},{1,5},{5... | collective-permute-start | bytes 2359304 | tf_op jit(solution)/shard_map/ppermute | solution.py:684
  689.4 441.6 %collective-permute-start.6 = (bf16[2,768,256]{2,1,0:T(8,128)(2,1)}, bf16[2,768,256]{2,1,0:T(8,128)(2,1)}, u32[]{:S(2)}, u32[]{:S(2)}) collective-permute-start(bf16[2,768,256]{2,1,0:T(8,128)(2,1)} %get-tuple-element.123), channel_id=1, source_target_pairs={{0,4},{4,0},{8,12},{12,8},{16,20},{20,16},{24,28},{28,24},{1,5},{5... | collective-permute-start | bytes 2359304 | tf_op jit(solution)/shard_map/ppermute | solution.py:684
  794.3 1.5 copy-start.18
  794.3 338.3 %collective-permute-start.7 = (bf16[2,768,256]{2,1,0:T(8,128)(2,1)}, bf16[2,768,256]{2,1,0:T(8,128)(2,1)}, u32[]{:S(2)}, u32[]{:S(2)}) collective-permute-start(bf16[2,768,256]{2,1,0:T(8,128)(2,1)} %get-tuple-element.125), channel_id=1, source_target_pairs={{0,4},{4,0},{8,12},{12,8},{16,20},{20,16},{24,28},{28,24},{1,5},{5... | collective-permute-start | bytes 2359304 | tf_op jit(solution)/shard_map/ppermute | solution.py:684
  795.9 1.6 copy-start.14
  797.5 1.6 copy-start.16
  799.1 2.6 copy-start.13
  1126.1 1.9 copy-start.6
  1126.1 3.0 copy-start.7
  1129.1 2.0 copy-start.15
  1131.2 1.6 copy-start.12
  1183.4 3.7 copy-start.1
  1183.4 2.9 copy-start.19
Sparse Core Ops, SparseCore 0:
  10.8 70.2 all-gather.5
  83.8 133.1 all-gather.3
  669.4 120.9 all-reduce.5
  793.9 99.6 reduce-scatter.4
  897.1 228.9 reduce-scatter.2
  1128.4 54.9 all-reduce.7

commit v2 on v1

--- a/solution.py
+++ b/solution.py
@@ -543,10 +543,14 @@
     rows = owners * CAP
     line = Line(spread, owners, x, part, stage, arrived, final, returned, sems)
 
-    def kept(s):
-        yield pltpu.make_async_copy(x.at[:, s], x_keep.at[:, s], keep_sem.at[0, s])
-        yield pltpu.make_async_copy(g_all.at[s], g_keep.at[s], keep_sem.at[1, s])
-        yield pltpu.make_async_copy(u_all.at[s], u_keep.at[s], keep_sem.at[2, s])
+    def keep_x(s):
+        return pltpu.make_async_copy(x.at[:, s], x_keep.at[:, s], keep_sem.at[0, s])
+
+    def keep_g(s):
+        return pltpu.make_async_copy(g_all.at[s], g_keep.at[s], keep_sem.at[1, s])
+
+    def keep_u(s):
+        return pltpu.make_async_copy(u_all.at[s], u_keep.at[s], keep_sem.at[2, s])
 
     def compute(s):
         def one(l, carry):
@@ -564,13 +568,14 @@
             return carry
 
         lax.fori_loop(0, local, one, 0)
-        for copy in list(kept(s))[1:]:
-            copy.start()
-
-    line.run(out, compute, lambda: None, lambda s: next(kept(s)).start())
+        keep_g(s).start()
+        keep_u(s).start()
+
+    line.run(out, compute, lambda: None, lambda s: keep_x(s).start())
     for s in range(LINE):
-        for copy in kept(s):
-            copy.wait()
+        keep_x(s).wait()
+        keep_g(s).wait()
+        keep_u(s).wait()
 
 
 def expert_backward_kernel(spread, parts, out, x_in, g_all, u_all, *refs):
@@ -701,6 +706,477 @@
     return total
 
 
+class Place:
+    def __init__(self, spread):
+        self.spread = spread
+        self.d, self.e = lax.axis_index("dp"), lax.axis_index("expert")
+        self.t, self.f = self.d // spread, lax.rem(self.d, spread)
+        self.y, self.c = self.e // 2, lax.rem(self.e, 2)
+        self.above, self.below = self.t < LINE - 1, self.t > 0
+        self.sibling = (self.d, self.e + 1 - 2 * self.c)
+        self.across = (self.d, lax.rem(self.e + 2, 4))
+        self.corner = (self.d, 3 - self.e)
+        self.beside = (self.t * spread + 1 - self.f, self.e)
+
+    def on_line(self, up):
+        return (self.d + self.spread if up else self.d - self.spread, self.e)
+
+
+def greet(always, place):
+    barrier = pltpu.get_barrier_semaphore()
+    for device in always:
+        pl.semaphore_signal(barrier, inc=1, device_id=device, device_id_type=MESH)
+    for up, there in ((1, place.above), (0, place.below)):
+
+        @pl.when(there)
+        def _(up=up):
+            pl.semaphore_signal(barrier, inc=1, device_id=place.on_line(up), device_id_type=MESH)
+
+    ends = place.above.astype(jnp.int32) + place.below.astype(jnp.int32)
+    pl.semaphore_wait(barrier, len(always) + ends)
+
+
+def remote(src, dst, send, recv, device):
+    return pltpu.make_async_remote_copy(
+        src_ref=src, dst_ref=dst, send_sem=send, recv_sem=recv, device_id=device, device_id_type=MESH)
+
+
+class DenseGather:
+    def __init__(self, place, shards, whole, sems):
+        self.p, self.shards, self.whole = place, shards, whole
+        self.z_send, self.z_recv, self.x_send, self.x_recv, self.y_send, self.y_recv, self.c_send, self.c_recv = sems
+
+    @staticmethod
+    def scratch(count):
+        dma = pltpu.SemaphoreType.DMA
+        return [dma((2, LINE, 3)), dma((LINE, 3)), dma((LINE, 3)), dma((LINE, 3)),
+                dma((count, 2)), dma((count, 2)), dma((count, 2, 2)), dma((count, 2, 2))]
+
+    def region(self, kind, s, y, c):
+        depth = self.shards[kind].shape[0]
+        if kind == 2:
+            return self.whole[2].at[pl.ds(pl.multiple_of(s * depth, 16), depth)]
+        half, wide = depth // 2, self.shards[kind].shape[1] // 2
+        return self.whole[kind].at[
+            pl.ds(pl.multiple_of(s * depth + y * half, 16), half), pl.ds(pl.multiple_of(c * wide, 128), wide)]
+
+    def z_copy(self, kind, up, t):
+        at = self.region(kind, t * self.p.spread + self.p.f, self.p.y, self.p.c)
+        return remote(at, at, self.z_send.at[up, t, kind], self.z_recv.at[t, kind], self.p.on_line(up))
+
+    def x_copy(self, kind, t, f):
+        at = self.region(kind, t * self.p.spread + f, self.p.y, self.p.c)
+        return remote(at, at, self.x_send.at[t, kind], self.x_recv.at[t, kind], self.p.beside)
+
+    def y_copy(self, kind, s, y):
+        at = self.region(kind, s, y, self.p.c)
+        return remote(at, at, self.y_send.at[s, kind], self.y_recv.at[s, kind], self.p.across)
+
+    def c_copy(self, kind, s, y, c):
+        at = self.region(kind, s, y, c)
+        return remote(at, at, self.c_send.at[s, y, kind], self.c_recv.at[s, y, kind], self.p.sibling)
+
+    def spread_out(self, t, f):
+        for kind in (0, 1):
+            self.y_copy(kind, t * self.p.spread + f, self.p.y).start()
+            self.c_copy(kind, t * self.p.spread + f, self.p.y, self.p.c).start()
+
+    def begin(self):
+        p = self.p
+        for kind in range(3):
+            depth = self.shards[kind].shape[0]
+            self.whole[kind][pl.ds(pl.multiple_of(p.d * depth, 16), depth), :] = self.shards[kind][...]
+        for up, there in ((0, p.below), (1, p.above)):
+
+            @pl.when(there)
+            def _(up=up):
+                for kind in range(3):
+                    self.z_copy(kind, up, p.t).start()
+
+        for kind in range(3):
+            self.x_copy(kind, p.t, p.f).start()
+
+    def step(self, k):
+        p = self.p
+        for up, there, onward in ((0, p.t + k < LINE, p.below), (1, p.t - k >= 0, p.above)):
+            t = p.t - k if up else p.t + k
+
+            @pl.when(there)
+            def _(up=up, onward=onward, t=t):
+                for kind in range(3):
+                    self.z_copy(kind, up, t).wait_recv()
+
+                @pl.when(onward)
+                def _():
+                    for kind in range(3):
+                        self.z_copy(kind, up, t).start()
+
+                for kind in range(3):
+                    self.x_copy(kind, t, p.f).start()
+                self.spread_out(t, p.f)
+
+    def in_order(self, body):
+        body(self.p.t)
+
+        def step(k, carry):
+            for t in (self.p.t + k, self.p.t - k):
+
+                @pl.when(jnp.logical_and(t >= 0, t < LINE))
+                def _(t=t):
+                    body(t)
+
+            return carry
+
+        lax.fori_loop(1, LINE, step, 0)
+
+    def after_x(self):
+        def body(t):
+            for kind in range(3):
+                self.x_copy(kind, t, 1 - self.p.f).wait_recv()
+            self.spread_out(t, 1 - self.p.f)
+
+        self.in_order(body)
+
+    def after_y(self):
+        p = self.p
+
+        def body(t, f):
+            for kind in (0, 1):
+                self.y_copy(kind, t * p.spread + f, 1 - p.y).wait_recv()
+                self.c_copy(kind, t * p.spread + f, 1 - p.y, p.c).start()
+
+        def came_on_line(t):
+            @pl.when(t != p.t)
+            def _():
+                body(t, p.f)
+
+        self.in_order(came_on_line)
+        self.in_order(lambda t: body(t, 1 - p.f))
+
+    def finish(self):
+        p = self.p
+
+        def line(t, carry):
+            for up, mine in ((0, jnp.logical_and(p.below, t >= p.t)), (1, jnp.logical_and(p.above, t <= p.t))):
+
+                @pl.when(mine)
+                def _(up=up):
+                    for kind in range(3):
+                        self.z_copy(kind, up, t).wait_send()
+
+            for kind in range(3):
+                self.x_copy(kind, t, p.f).wait_send()
+            for f in range(p.spread):
+                s = t * p.spread + f
+
+                @pl.when(s != p.d)
+                def _(s=s):
+                    for kind in (0, 1):
+                        self.y_copy(kind, s, p.y).wait_send()
+                        for y in (0, 1):
+                            self.c_copy(kind, s, y, p.c).wait_send()
+                            self.c_copy(kind, s, y, 1 - p.c).wait_recv()
+
+            return carry
+
+        lax.fori_loop(0, LINE, line, 0)
+
+
+def dense_gather_kernel(spread, qkv, out, small, routes, qkv_all, out_all, small_all, routes_all, *sems):
+    p = Place(spread)
+    r_send, r_recv = sems[-2:]
+    gather = DenseGather(p, (qkv, out, small), (qkv_all, out_all, small_all), sems[:-2])
+    mates = [p.sibling, p.across, p.corner]
+    greet(mates + [p.beside], p)
+    routes_all[p.e] = routes[...]
+    for i, mate_id in enumerate(mates):
+        remote(routes, routes_all.at[p.e], r_send.at[i], r_recv.at[p.e], mate_id).start()
+    gather.begin()
+    lax.fori_loop(1, LINE, lambda k, carry: (gather.step(k), carry)[1], 0)
+    gather.after_x()
+    gather.after_y()
+    gather.finish()
+    for i, mate_id in enumerate(mates):
+        remote(routes, routes_all.at[p.e], r_send.at[i], r_recv.at[p.e], mate_id).wait_send()
+        remote(routes, routes_all.at[mate_id[1]], r_send.at[i], r_recv.at[mate_id[1]], mate_id).wait_recv()
+
+
+def dense_gather(spread, call_id, shards, routes):
+    count = spread * LINE
+    shapes = [jax.ShapeDtypeStruct((count * s.shape[0], s.shape[1]), s.dtype) for s in shards]
+    dma = pltpu.SemaphoreType.DMA
+    return pl.pallas_call(
+        functools.partial(dense_gather_kernel, spread),
+        out_shape=shapes + [jax.ShapeDtypeStruct((4,) + routes.shape, routes.dtype)],
+        in_specs=[VMEM] * 4,
+        out_specs=[VMEM] * 4,
+        scratch_shapes=DenseGather.scratch(count) + [dma((3,)), dma((4,))],
+        compiler_params=pltpu.CompilerParams(
+            collective_id=call_id, has_side_effects=True, vmem_limit_bytes=60 * 2**20),
+    )(*shards, routes)
+
+
+class DenseReduce:
+    def __init__(self, place, grads, sums, scratch):
+        self.p, self.grads, self.sums = place, grads, sums
+        (self.core, self.stage_y, self.came_y, self.quarter, self.stage_z, self.came_z, self.stage_x, self.came_x,
+         self.a_send, self.a_recv, self.y_send, self.y_recv, self.z_send, self.z_recv, self.x_send, self.x_recv,
+         self.e_send, self.e_recv) = scratch
+        self.depths = [g.shape[0] // (LINE * place.spread) for g in grads]
+        self.wide = grads[0].shape[1] // 2
+        self.rows = sum(self.depths) // 2
+
+    @staticmethod
+    def scratch(spread, depths, width):
+        count, rows, wide = LINE * spread, sum(depths) // 2, width // 2
+        dma = pltpu.SemaphoreType.DMA
+        return [
+            pltpu.VMEM((count * sum(depths), wide), BF16),
+            pltpu.VMEM((LINE, spread, rows, wide), BF16),
+            pltpu.VMEM((LINE, spread, rows, wide), BF16),
+            pltpu.VMEM((LINE, spread, rows, wide), F32),
+            pltpu.VMEM((LINE, spread, rows, wide), BF16),
+            pltpu.VMEM((2, LINE, spread, rows, wide), BF16),
+            pltpu.VMEM((rows, wide), BF16),
+            pltpu.VMEM((rows, wide), BF16),
+            dma((2,)), dma((2,)), dma((LINE,)), dma((LINE,)), dma((LINE,)), dma((2, LINE)), dma(()), dma(()),
+            dma((3, 2)), dma((3, 2)),
+        ]
+
+    def lanes(self, c):
+        return pl.ds(pl.multiple_of(c * self.wide, 128), self.wide)
+
+    def a_copy(self, kind):
+        first = 0 if kind == 0 else self.grads[0].shape[0]
+        count = self.grads[kind].shape[0]
+        return remote(self.grads[kind].at[:, self.lanes(1 - self.p.c)], self.core.at[first : first + count],
+                      self.a_send.at[kind], self.a_recv.at[kind], self.p.sibling)
+
+    def y_copy(self, t):
+        return remote(self.stage_y.at[t], self.came_y.at[t], self.y_send.at[t], self.y_recv.at[t], self.p.across)
+
+    def z_copy(self, up, t):
+        return remote(self.stage_z.at[t], self.came_z.at[up, t], self.z_send.at[t], self.z_recv.at[up, t], self.p.on_line(up))
+
+    def x_copy(self):
+        return remote(self.stage_x, self.came_x, self.x_send, self.x_recv, self.p.beside)
+
+    def e_copy(self, i, kind, y, c):
+        half = self.depths[kind] // 2
+        at = self.sums[kind].at[pl.ds(pl.multiple_of(y * half, 8), half), self.lanes(c)]
+        return remote(at, at, self.e_send.at[i, kind], self.e_recv.at[i, kind], self.p.across if i == 0 else self.p.sibling)
+
+    def pieces(self, t, f, y):
+        s, first, row = t * self.p.spread + f, 0, 0
+        for grad, depth in zip(self.grads, self.depths):
+            at = s * depth + y * (depth // 2)
+            mine = grad[pl.ds(pl.multiple_of(at, 16), depth // 2), self.lanes(self.p.c)]
+            other = self.core[pl.ds(pl.multiple_of(first + at, 16), depth // 2), :]
+            yield slice(row, row + depth // 2), mine.astype(F32) + other.astype(F32)
+            first, row = first + grad.shape[0], row + depth // 2
+
+    def order(self, i):
+        return jnp.where(self.p.t >= LINE // 2, i, LINE - 1 - i)
+
+    def begin(self):
+        for kind in (0, 1):
+            self.a_copy(kind).start()
+
+    def after_core(self):
+        for kind in (0, 1):
+            self.a_copy(kind).wait_recv()
+
+        def body(i, carry):
+            t = self.order(i)
+            for f in range(self.p.spread):
+                for where, value in self.pieces(t, f, 1 - self.p.y):
+                    self.stage_y[t, f, where] = value.astype(BF16)
+            self.y_copy(t).start()
+            for f in range(self.p.spread):
+                for where, value in self.pieces(t, f, self.p.y):
+                    self.quarter[t, f, where] = value
+            return carry
+
+        lax.fori_loop(0, LINE, body, 0)
+
+    def after_y(self):
+        p = self.p
+
+        def body(i, carry):
+            t = self.order(i)
+            self.y_copy(t).wait_recv()
+            self.quarter[t] = self.quarter[t] + self.came_y[t].astype(F32)
+            for up, mine, first in ((1, p.t < t, p.t == 0), (0, p.t > t, p.t == LINE - 1)):
+
+                @pl.when(jnp.logical_and(mine, jnp.logical_not(first)))
+                def _(up=up):
+                    self.z_copy(up, t).wait_recv()
+                    self.quarter[t] = self.quarter[t] + self.came_z[up, t].astype(F32)
+
+                @pl.when(mine)
+                def _(up=up):
+                    self.stage_z[t] = self.quarter[t].astype(BF16)
+                    self.z_copy(up, t).start()
+
+            return carry
+
+        lax.fori_loop(0, LINE, body, 0)
+
+    def after_z(self):
+        p = self.p
+        for up, there in ((1, p.below), (0, p.above)):
+
+            @pl.when(there)
+            def _(up=up):
+                self.z_copy(up, p.t).wait_recv()
+                self.quarter[p.t] = self.quarter[p.t] + self.came_z[up, p.t].astype(F32)
+
+        self.stage_x[...] = self.quarter[p.t, 1 - p.f].astype(BF16)
+        self.x_copy().start()
+
+    def after_x(self):
+        p = self.p
+        self.x_copy().wait_recv()
+        row = 0
+        for kind, depth in enumerate(self.depths):
+            half = depth // 2
+            value = self.quarter[p.t, p.f, row : row + half] + self.came_x[row : row + half].astype(F32)
+            self.sums[kind][pl.ds(pl.multiple_of(p.y * half, 8), half), self.lanes(p.c)] = value
+            row += half
+        for kind in (0, 1):
+            self.e_copy(0, kind, p.y, p.c).start()
+        for kind in (0, 1):
+            self.e_copy(1, kind, p.y, p.c).start()
+
+    def finish(self):
+        p = self.p
+        for kind in (0, 1):
+            self.e_copy(0, kind, 1 - p.y, p.c).wait_recv()
+            self.e_copy(2, kind, 1 - p.y, p.c).start()
+        for kind in (0, 1):
+            self.a_copy(kind).wait_send()
+            self.e_copy(0, kind, p.y, p.c).wait_send()
+            self.e_copy(1, kind, p.y, p.c).wait_send()
+            self.e_copy(1, kind, p.y, 1 - p.c).wait_recv()
+            self.e_copy(2, kind, 1 - p.y, p.c).wait_send()
+            self.e_copy(2, kind, 1 - p.y, 1 - p.c).wait_recv()
+        self.x_copy().wait_send()
+
+        def body(t, carry):
+            self.y_copy(t).wait_send()
+
+            @pl.when(t != p.t)
+            def _():
+                self.z_copy(0, t).wait_send()
+
+            return carry
+
+        lax.fori_loop(0, LINE, body, 0)
+
+
+class SmallSum:
+    def __init__(self, place, grads, total, scratch):
+        self.p, self.grads, self.total = place, grads, total
+        self.stage, self.came, self.send, self.recv = scratch
+        p = place
+        near = (p.d + p.spread - 2 * p.spread * lax.rem(p.t, 2), p.e)
+        far = (lax.rem(p.d + 2 * p.spread, LINE * p.spread), p.e)
+        self.partners = [p.sibling, p.across, p.beside, near, far]
+
+    @staticmethod
+    def scratch(rows, width):
+        dma = pltpu.SemaphoreType.DMA
+        return [pltpu.VMEM((5, rows, width // 2), F32), pltpu.VMEM((5, rows, width // 2), F32), dma((6,)), dma((6,))]
+
+    def lanes(self, c):
+        wide = self.grads.shape[1] // 2
+        return pl.ds(pl.multiple_of(c * wide, 128), wide)
+
+    def copy(self, i):
+        src = self.grads.at[:, self.lanes(1 - self.p.c)] if i == 0 else self.stage.at[i]
+        return remote(src, self.came.at[i], self.send.at[i], self.recv.at[i], self.partners[i])
+
+    def last(self, c):
+        at = self.total.at[:, self.lanes(c)]
+        return remote(at, at, self.send.at[5], self.recv.at[5], self.p.sibling)
+
+    def step(self, i):
+        if i == 0:
+            self.copy(0).start()
+            return
+        self.copy(i - 1).wait_recv()
+        mine = self.grads[:, self.lanes(self.p.c)] if i == 1 else self.stage[i - 1]
+        value = mine + self.came[i - 1]
+        if i < 5:
+            self.stage[i] = value
+            self.copy(i).start()
+        else:
+            self.total[:, self.lanes(self.p.c)] = value
+            self.last(self.p.c).start()
+
+    def finish(self):
+        for i in range(5):
+            self.copy(i).wait_send()
+        self.last(self.p.c).wait_send()
+        self.last(1 - self.p.c).wait_recv()
+
+
+REDUCE_REFS = 18
+
+
+def dense_reduce_kernel(spread, layers, small, *refs):
+    p = Place(spread)
+    n = 2 * layers
+    grads, small_sum, sums, scratch = refs[:n], refs[n], refs[n + 1 : 2 * n + 1], refs[2 * n + 1 :]
+    both = [
+        DenseReduce(p, grads[2 * l : 2 * l + 2], sums[2 * l : 2 * l + 2], scratch[REDUCE_REFS * l : REDUCE_REFS * (l + 1)])
+        for l in range(layers)
+    ]
+    little = SmallSum(p, small, small_sum, scratch[REDUCE_REFS * layers :])
+    greet(little.partners[:3] + little.partners[4:], p)
+    for one in both:
+        one.begin()
+    little.step(0)
+    for one in both:
+        one.after_core()
+    little.step(1)
+    both[0].after_y()
+    little.step(2)
+    for one in both[1:]:
+        one.after_y()
+    little.step(3)
+    for one in both:
+        one.after_z()
+    little.step(4)
+    for one in both:
+        one.after_x()
+    little.step(5)
+    for one in both:
+        one.finish()
+    little.finish()
+
+
+def dense_reduce(spread, call_id, grads, small):
+    layers = len(grads)
+    count = LINE * spread
+    flat = [g for layer in grads for g in layer]
+    depths = [g.shape[0] // count for g in grads[0]]
+    width = flat[0].shape[1]
+    scratch = []
+    for _ in range(layers):
+        scratch += DenseReduce.scratch(spread, depths, width)
+    return pl.pallas_call(
+        functools.partial(dense_reduce_kernel, spread, layers),
+        out_shape=[jax.ShapeDtypeStruct(small.shape, F32)]
+        + [jax.ShapeDtypeStruct((g.shape[0] // count, width), F32) for g in flat],
+        in_specs=[VMEM] * (1 + len(flat)),
+        out_specs=[VMEM] * (1 + len(flat)),
+        scratch_shapes=scratch + SmallSum.scratch(*small.shape),
+        compiler_params=pltpu.CompilerParams(
+            collective_id=call_id, has_side_effects=True, vmem_limit_bytes=60 * 2**20),
+    )(small, *flat)
+
+
 def per_device(
     tokens, seq_lengths, block_perm, routes, norm_gains, w_qkv, w_out, w_router, w_residual, w_const, v_const,
     w_gate, w_up, w_down, cotangent,
@@ -716,8 +1192,6 @@
     place = lax.axis_index("expert")
 
     my_place = jnp.sum(jnp.where(jnp.arange(owners) == place, block_perm[0], 0))
-    all_routes = lax.all_gather(routes, "expert", axis=0)
-    my_routes = lax.dynamic_index_in_dim(all_routes, my_place, 0, keepdims=False)
     lengths = lax.dynamic_index_in_dim(seq_lengths[0], place, 0, keepdims=False)
     order = jnp.arange(lengths.shape[0])
     ends = jnp.sum(jnp.where(order[:, None] <= order[None, :], lengths[:, None], 0), axis=0)
@@ -739,10 +1213,25 @@
         axis=2,
     ).astype(BF16)
     qkv_t = jnp.swapaxes(w_qkv, 1, 2).astype(BF16)
-    qkv_all = lax.all_gather(qkv_t, "dp", axis=1, tiled=True)
-    out_all = lax.all_gather(w_out.astype(BF16), "dp", axis=1, tiled=True)
-    small_all = lax.all_gather(small, "dp", axis=1, tiled=True)
-    dense = [(small_all[l], qkv_all[l], out_all[l]) for l in range(layers)]
+    out_rows = w_out.astype(BF16)
+    in_kernels = spread == 2 and owners == 4 and qkv_t.shape[1] % 32 == 0 and depth % 32 == 0
+    if in_kernels:
+        packed_routes = jnp.zeros((8, 256), jnp.int32).at[: 2 * layers, :rows].set(
+            jnp.swapaxes(routes, 1, 2).reshape(2 * layers, rows))
+        dense = []
+        for l in range(layers):
+            qkv_all, out_all, small_all, routes_all = dense_gather(
+                spread, 4 + l, (qkv_t[l], out_rows[l], small[l]), packed_routes)
+            dense.append((small_all, qkv_all, out_all))
+        picked = lax.dynamic_index_in_dim(routes_all, my_place, 0, keepdims=False)
+        my_routes = jnp.swapaxes(picked[: 2 * layers, :rows].reshape(layers, 2, rows), 1, 2)
+    else:
+        all_routes = lax.all_gather(routes, "expert", axis=0)
+        my_routes = lax.dynamic_index_in_dim(all_routes, my_place, 0, keepdims=False)
+        qkv_all = lax.all_gather(qkv_t, "dp", axis=1, tiled=True)
+        out_all = lax.all_gather(out_rows, "dp", axis=1, tiled=True)
+        small_all = lax.all_gather(small, "dp", axis=1, tiled=True)
+        dense = [(small_all[l], qkv_all[l], out_all[l]) for l in range(layers)]
     w_res = jnp.zeros((128, 128), F32).at[: w_residual.shape[0], : w_residual.shape[1]].set(w_residual)
 
     cols = ((rows, width), F32)
@@ -769,7 +1258,8 @@
         turn_kernel, experts, (mid1, dense[1][0], stat1, ret1, cotangent, logits0, w_res),
         [((rows, width), BF16), per_token, per_token, sent, small_grads, ((128, 128), F32)])
     back, *expert_grads1 = expert_backward(spread, 2, group(out), kept1, weights[1])
-    dense_grads = [((3 * width, width), F32), ((width, width), F32), small_grads]
+    grad_type = BF16 if in_kernels else F32
+    dense_grads = [((3 * width, width), grad_type), ((width, width), grad_type), small_grads]
     attention_scratch = [((rows, 3 * width), BF16), ((rows, width), BF16)]
     qkv_grad1, out_grad1, small_grad1, grad, g_small0, out, small_grad0 = local_call(
         between_kernel, experts,
@@ -791,12 +1281,17 @@
             per_layer.append(pair_sum(grads[at * n : (at + 1) * n], axis, spread))
         expert_out.append(jnp.stack(per_layer))
     gate_grad, up_grad, down_grad = expert_out
-    qkv_grad = lax.psum(
-        lax.psum_scatter(jnp.stack([qkv_grad0, qkv_grad1]), "dp", scatter_dimension=1, tiled=True), "expert")
-    out_grad = lax.psum(
-        lax.psum_scatter(jnp.stack([out_grad0, out_grad1]), "dp", scatter_dimension=1, tiled=True), "expert")
     packed = jnp.concatenate([small_grad0, small_grad1, jnp.pad(res_grad[:16], ((0, 0), (0, width - 128)))])
-    packed = lax.psum(packed, ("dp", "expert"))
+    if in_kernels:
+        packed, qkv_sum0, out_sum0, qkv_sum1, out_sum1 = dense_reduce(
+            spread, 6, [(qkv_grad0, out_grad0), (qkv_grad1, out_grad1)], packed)
+        qkv_grad = jnp.stack([qkv_sum0, qkv_sum1])
+        out_grad = jnp.stack([out_sum0, out_sum1])
+    else:
+        packed = lax.psum(packed, ("dp", "expert"))
+        qkv_grad, out_grad = (
+            lax.psum(lax.psum_scatter(jnp.stack(pair), "dp", scatter_dimension=1, tiled=True), "expert")
+            for pair in ((qkv_grad0, qkv_grad1), (out_grad0, out_grad1)))
     mine = lax.dynamic_slice_in_dim(packed, lax.axis_index("dp") * depth, depth, axis=1)
     mine = jnp.stack([mine[:24], mine[24:48]])
     router_grad = jnp.swapaxes(mine[:, :CONST0], 1, 2)

time: 1200 us -> 770 us (0.64)
  waiting for transfers between devices: 528 us -> 16.9 us
  Pallas kernels: 443 us -> 690 us
  blocking collectives: 121 us -> 0 us
  other arithmetic: 41.9 us -> 20 us
  between operations: 17 us -> 3.53 us
    reduce_scatter x2 -> x0, waiting for transfers between devices: 322 us -> none  [the longest x1 232 us: per_device(): lax.psum_scatter(jnp.stack([qkv_grad0, qkv_grad1]), 'dp', scatter_dimensi...]
    pallas_call x0 -> x3, Pallas kernels: none -> 249 us  [the longest x2 143 us: dense_gather(): pl.pallas_call(functools.partial(dense_gather_kernel, spread), out_shape=...]
    psum x2 -> x0, waiting for transfers between devices: 148 us -> none  [the longest x1 101 us: per_device(): packed = lax.psum(packed, ('dp', 'expert'))]
    all_gather x2 -> x0, blocking collectives: 121 us -> none  [the longest x1 116 us: per_device(): small_all = lax.all_gather(small, 'dp', axis=1, tiled=True)]
    all_gather x2 -> x0, waiting for transfers between devices: 57.6 us -> none  [the longest x1 57.6 us: per_device(): qkv_all = lax.all_gather(qkv_t, 'dp', axis=1, tiled=True)]
    another operation x8 -> x7, other arithmetic: 17.8 us -> 4.28 us  [the longest x1 11 us: per_device(): jnp.stack([qkv_grad0, qkv_grad1])]
    ppermute x6, waiting for transfers between devices: 0.02 us -> 12.4 us  [to_partner(): return lax.ppermute(array, 'dp', pairs)]
  transfers between devices with their start and end apart: 18 -> 12, of which waited for: 5 -> 2; matrix products, arithmetic and copies ran while one was open for 5% -> 4% of each run, Pallas kernels for 10% -> 50%
where the time goes in v2:
time: 770 us; the launch traced here: 763 us
  Pallas kernels  690 us (90%)
  other arithmetic  20 us (3%)
  waiting for transfers between devices  16.9 us (2%)
  starting transfers between devices  16.5 us (2%)
  local copies, waits for them, and re-layouts  15.7 us (2%)
    pallas_call x2, Pallas kernels, expert_backward(): pl.pallas_call(functools.partial(expert_backward_kernel, spread, parts),...  196 us
    pallas_call x2, Pallas kernels, expert_forward(): pl.pallas_call(functools.partial(expert_forward_kernel, spread, parts), o...  184 us
    pallas_call x2, Pallas kernels, dense_gather(): pl.pallas_call(functools.partial(dense_gather_kernel, spread), out_shape=...  143 us
    pallas_call x1, Pallas kernels, dense_reduce(): pl.pallas_call(functools.partial(dense_reduce_kernel, spread, layers), ou...  106 us
    pallas_call x5, Pallas kernels, local_call(): pl.pallas_call(functools.partial(kernel, experts), out_shape=[jax.ShapeDt...  60.7 us
  transfers between devices with their start and end apart: 12, of which 2 were waited for; matrix products, arithmetic and copies ran while one was open for 4% of the time, Pallas kernels for 50%

profile of v2, /device:TPU:0, one launch (start us, length us, event | category | flops | bytes accessed | tf_op | source)
XLA Modules:
  0.0 762.7 jit_solution(11651532459754343291)
XLA Ops:
  0.7 2.0 convert.37
  2.9 3.0 collective-permute-start
  5.9 0.2 convert.38
  6.0 1.0 slice_bitcast_fusion.1
  7.0 2.2 collective-permute-start.1
  9.3 0.2 convert.39
  9.5 1.0 slice_bitcast_fusion
  10.5 1.5 collective-permute-start.2
  12.0 0.6 collective-permute-start.3
  12.6 1.5 collective-permute-start.4
  14.0 0.1 copy.40
  14.7 0.2 concatenate.11
  14.8 0.6 slice_bitcast_fusion.14
  15.5 1.1 convert_element_type.53
  16.5 0.7 slice_bitcast_fusion.8
  17.3 1.6 convert_bitcast_fusion
  18.9 1.0 slice_bitcast_fusion.6
  19.9 4.5 collective-permute-done.refs_1_
  24.3 2.1 collective-permute-start.5
  26.4 0.6 fusion.4
  28.4 0.6 scatter.6.routes
  29.6 102.9 %shard_map.239 = (bf16[2304,768]{1,0:T(8,128)(2,1)}, bf16[768,768]{1,0:T(8,128)(2,1)}, bf16[768,128]{1,0:T(8,128)(2,1)}, s32[4,8,256]{2,1,0:T(8,128)}) custom-call(bf16[288,768]{1,0:T(8,128)(2,1)} %get-tuple-element.212.qkv, bf16[96,768]{1,0:T(8,128)(2,1)} %get-tuple-element.214.out, bf16[96,128]{1,0:T(8,128)(2,1)} %get-tuple-element.222.small, ...), custom_call_target="tpu_custom_call" | custom-call | tf_op jit(solution)/shard_map/pallas_call | solution.py:908
  132.5 0.7 dynamic-slice_bitcast_fusion.2
  133.6 0.8 copy.45.doc_col
  134.3 0.6 scatter.9.w_res
  135.0 40.0 %shard_map.238 = (bf16[2304,768]{1,0:T(8,128)(2,1)}, bf16[768,768]{1,0:T(8,128)(2,1)}, bf16[768,128]{1,0:T(8,128)(2,1)}, s32[4,8,256]{2,1,0:T(8,128)}) custom-call(bf16[288,768]{1,0:T(8,128)(2,1)} %get-tuple-element.213.qkv, bf16[96,768]{1,0:T(8,128)(2,1)} %get-tuple-element.215.out, bf16[96,128]{1,0:T(8,128)(2,1)} %get-tuple-element.223.small, ...), custom_call_target="tpu_custom_call" | custom-call | tf_op jit(solution)/shard_map/pallas_call | solution.py:908
  175.0 0.7 slice_bitcast_fusion.10
  175.7 10.8 %shard_map.240 = (bf16[192,768]{1,0:T(8,128)(2,1)}, bf16[192,2304]{1,0:T(8,128)(2,1)}, f32[12,192,192]{2,1,0:T(8,128)}, bf16[192,768]{1,0:T(8,128)(2,1)}, f32[19...) custom-call(bf16[192,768]{1,0:T(8,128)(2,1)} %tokens.3, ...), custom_call_target="tpu_custom_call" | custom-call | tf_op jit(solution)/shard_map/pallas_call | solution.py:335
  186.5 92.3 %shard_map.241 = (bf16[4,2,48,768]{3,2,1,0:T(8,128)(2,1)}, bf16[2,4,4,48,768]{4,3,2,1,0:T(8,128)(2,1)}, f32[4,2,192,512]{3,2,1,0:T(8,128)}, f32[4,2,192,512]{3,2,1,0:T(8,128)}) custom-call(bf16[4,2,48,768]{3,2,1,0:T(8,128)(2,1)} %bitcast.88, bf16[2,768,256]{2,1,0:T(8,128)(2,1)} %copy-done.2, bf16[2,768,256]{2,1,0:T(8,128)(2,1)} %collective-permute-done.refs_1_, ...), custom_call_target="tpu_custom_call" | custom-call | tf_op jit(solution)/shard_map/pallas_call | solution.py:640
  278.8 11.6 %shard_map.242 = (f32[192,768]{1,0:T(8,128)}, bf16[192,768]{1,0:T(8,128)(2,1)}, bf16[192,2304]{1,0:T(8,128)(2,1)}, f32[12,192,192]{2,1,0:T(8,128)}, bf16[192,768...) custom-call(f32[192,768]{1,0:T(8,128)} %get-tuple-element.107.mid_in.mid0.mid, ...), custom_call_target="tpu_custom_call" | custom-call | tf_op jit(solution)/shard_map/pallas_call | solution.py:335
  290.4 0.9 copy-done.8
  291.2 92.0 %shard_map.243 = (bf16[4,2,48,768]{3,2,1,0:T(8,128)(2,1)}, bf16[2,4,4,48,768]{4,3,2,1,0:T(8,128)(2,1)}, f32[4,2,192,512]{3,2,1,0:T(8,128)}, f32[4,2,192,512]{3,2,1,0:T(8,128)}) custom-call(bf16[4,2,48,768]{3,2,1,0:T(8,128)(2,1)} %bitcast.87, bf16[2,768,256]{2,1,0:T(8,128)(2,1)} %copy-done.5, bf16[2,768,256]{2,1,0:T(8,128)(2,1)} %collective-permute-done.3.refs_1_, ...), custom_call_target="tpu_custom_call" | custom-call | tf_op jit(solution)/shard_map/pallas_call | solution.py:640
  383.3 5.6 shard_map.244
  388.9 97.8 %shard_map.245 = (bf16[4,2,48,768]{3,2,1,0:T(8,128)(2,1)}, f32[2,768,256]{2,1,0:T(8,128)}, bf16[2,768,256]{2,1,0:T(8,128)(2,1)}, f32[2,768,256]{2,1,0:T(8,128)},...) custom-call(bf16[4,2,48,768]{3,2,1,0:T(8,128)(2,1)} %bitcast.92, ...), custom_call_target="tpu_custom_call" | custom-call | tf_op jit(solution)/shard_map/pallas_call | solution.py:666
  486.6 17.6 %shard_map.246 = (bf16[2304,768]{1,0:T(8,128)(2,1)}, bf16[768,768]{1,0:T(8,128)(2,1)}, f32[24,768]{1,0:T(8,128)}, f32[192,768]{1,0:T(8,128)}, f32[192,128]{1,0:T...) custom-call(bf16[192,768]{1,0:T(8,128)(2,1)} %cotangent.3, bf16[384,768]{1,0:T(8,128)(2,1)} %bitcast.90, ...), custom_call_target="tpu_custom_call" | custom-call | tf_op jit(solution)/shard_map/pallas_call | solution.py:335
  504.2 97.9 %shard_map.247 = (bf16[4,2,48,768]{3,2,1,0:T(8,128)(2,1)}, f32[2,768,256]{2,1,0:T(8,128)}, bf16[2,768,256]{2,1,0:T(8,128)(2,1)}, f32[2,768,256]{2,1,0:T(8,128)},...) custom-call(bf16[4,2,48,768]{3,2,1,0:T(8,128)(2,1)} %bitcast.91, ...), custom_call_target="tpu_custom_call" | custom-call | tf_op jit(solution)/shard_map/pallas_call | solution.py:666
  602.0 1.6 collective-permute-start.10
  603.7 0.5 collective-permute-start.11
  604.2 1.6 collective-permute-start.8
  605.7 0.5 collective-permute-start.9
  606.2 1.6 collective-permute-start.6
  607.8 0.7 slice.140
  608.5 15.2 %shard_map.248 = (bf16[2304,768]{1,0:T(8,128)(2,1)}, bf16[768,768]{1,0:T(8,128)(2,1)}, f32[24,768]{1,0:T(8,128)}, f32[192,768]{1,0:T(8,128)}) custom-call(f32[192,768]{1,0:T(8,128)} %get-tuple-element.133.grad_in, bf16[384,768]{1,0:T(8,128)(2,1)} %bitcast.86, f32[192,128]{1,0:T(8,128)} %get-tuple-element.139.g_small, ...), custom_call_target="tpu_custom_call" | custom-call | tf_op jit(solution)/shard_map/pallas_call | solution.py:335
  623.7 1.6 select_maximum_fusion.small
  625.3 106.5 %shard_map.249 = (f32[64,768]{1,0:T(8,128)}, f32[288,768]{1,0:T(8,128)}, f32[96,768]{1,0:T(8,128)}, f32[288,768]{1,0:T(8,128)}, f32[96,768]{1,0:T(8,128)}) custom-call(f32[64,768]{1,0:T(8,128)} %select_maximum_fusion.small, bf16[2304,768]{1,0:T(8,128)(2,1)} %get-tuple-element.149.refs_0_, bf16[768,768]{1,0:T(8,128)(2,1)} %get-tuple-element.150.refs_1_, ...), custom_call_target="tpu_custom_call" | custom-call | tf_op jit(solution)/shard_map/pallas_call | solution.py:1168
  731.8 1.4 slice.145
  733.2 0.8 dynamic-slice_bitcast_fusion.1
  734.0 0.6 copy.47
  734.6 0.6 fusion.2
  735.2 0.6 pad_maximum_fusion.4
  735.8 1.9 pad_maximum_fusion.3
  737.7 2.6 maximum_bitcast_fusion
  740.4 0.2 add_bitcast_fusion.1
  740.6 1.2 copy-done.11
  741.8 0.2 add_bitcast_fusion
  742.0 1.9 pad_maximum_fusion.2
  743.9 0.2 add_bitcast_fusion.3
  744.1 1.2 copy-done.10
  745.3 0.2 add_bitcast_fusion.2
  745.5 1.9 pad_maximum_fusion.1
  747.5 0.2 add_bitcast_fusion.5
  747.7 12.4 %collective-permute-done.7 = bf16[2,768,256]{2,1,0:T(8,128)(2,1)S(1)} collective-permute-done((bf16[2,768,256]{2,1,0:T(8,128)(2,1)S(1)}, bf16[2,768,256]{2,1,0:T(8,128)(2,1)S(1)}, u32[]{:S(2)}, u32[]{:S(2)}) %collective-permute-start.7) | collective-permute-done | bytes 786464 | tf_op jit(solution)/shard_map/ppermute | solution.py:689
  760.1 0.2 add_bitcast_fusion.4
  760.3 1.9 pad_maximum_fusion
  (77 shorter events, 1.2 us)
Async XLA Ops:
  0.6 132.7 %copy-start = (s32[1,4,4]{2,1,0:T(4,128)S(1)}, s32[1,4,4]{2,1,0:T(4,128)}, u32[]{:S(2)}) copy-start(s32[1,4,4]{2,1,0:T(4,128)} %param.20) | copy-start | bytes 196
  2.7 3.1 copy-start.6
  2.8 3.2 copy-start.2
  2.8 9.1 %copy-start.5 = (bf16[2,768,256]{2,1,0:T(8,128)(2,1)}, bf16[2,768,256]{2,1,0:T(8,128)(2,1)S(1)}, u32[]{:S(2)}) copy-start(bf16[2,768,256]{2,1,0:T(8,128)(2,1)S(1)} %get-tuple-element.210.refs_0_) | copy-start | bytes 2359300
  2.9 21.5 %collective-permute-start = (bf16[2,768,256]{2,1,0:T(8,128)(2,1)S(1)}, bf16[2,768,256]{2,1,0:T(8,128)(2,1)}, u32[]{:S(2)}, u32[]{:S(2)}) collective-permute-start(bf16[2,768,256]{2,1,0:T(8,128)(2,1)S(1)} %get-tuple-element.211.refs_0_), channel_id=1, source_target_pairs={{4,0},{0,4},{12,8},{8,12},{20,16},{16,20},{28,24},{24,28},{5,1},{1... | collective-permute-start | bytes 2359304 | tf_op jit(solution)/shard_map/ppermute | solution.py:682
  6.0 3.2 copy-start.7
  7.0 2.4 copy-start.3
  7.0 179.4 %collective-permute-start.1 = (bf16[2,768,256]{2,1,0:T(8,128)(2,1)S(1)}, bf16[2,768,256]{2,1,0:T(8,128)(2,1)}, u32[]{:S(2)}, u32[]{:S(2)}) collective-permute-start(bf16[2,768,256]{2,1,0:T(8,128)(2,1)S(1)} %get-tuple-element.209.refs_2_), channel_id=1, source_target_pairs={{4,0},{0,4},{12,8},{8,12},{20,16},{16,20},{28,24},{24,28},{5,1},{1... | collective-permute-start | bytes 2359304 | tf_op jit(solution)/shard_map/ppermute | solution.py:682
  9.4 4.6 copy-start.20
  9.5 4.7 copy-start.17
  9.5 4.9 copy-start.22
  9.5 5.0 copy-start.23
  10.5 8.4 %copy-start.4 = (bf16[2,256,768]{2,1,0:T(8,128)(2,1)}, bf16[2,256,768]{2,1,0:T(8,128)(2,1)S(1)}, u32[]{:S(2)}) copy-start(bf16[2,256,768]{2,1,0:T(8,128)(2,1)S(1)} %get-tuple-element.207.refs_4_) | copy-start | bytes 2359300
  10.5 176.0 %collective-permute-start.2 = (bf16[2,256,768]{2,1,0:T(8,128)(2,1)S(1)}, bf16[2,256,768]{2,1,0:T(8,128)(2,1)}, u32[]{:S(2)}, u32[]{:S(2)}) collective-permute-start(bf16[2,256,768]{2,1,0:T(8,128)(2,1)S(1)} %get-tuple-element.207.refs_4_), channel_id=1, source_target_pairs={{4,0},{0,4},{12,8},{8,12},{20,16},{16,20},{28,24},{24,28},{5,1},{1... | collective-permute-start | bytes 2359304 | tf_op jit(solution)/shard_map/ppermute | solution.py:682
  12.0 278.3 %collective-permute-start.3 = (bf16[2,768,256]{2,1,0:T(8,128)(2,1)S(1)}, bf16[2,768,256]{2,1,0:T(8,128)(2,1)}, u32[]{:S(2)}, u32[]{:S(2)}) collective-permute-start(bf16[2,768,256]{2,1,0:T(8,128)(2,1)S(1)} %get-tuple-element.210.refs_0_), channel_id=1, source_target_pairs={{4,0},{0,4},{12,8},{8,12},{20,16},{16,20},{28,24},{24,28},{5,1},{1... | collective-permute-start | bytes 2359304 | tf_op jit(solution)/shard_map/ppermute | solution.py:682
  12.6 277.8 %collective-permute-start.4 = (bf16[2,768,256]{2,1,0:T(8,128)(2,1)}, bf16[2,768,256]{2,1,0:T(8,128)(2,1)}, u32[]{:S(2)}, u32[]{:S(2)}) collective-permute-start(bf16[2,768,256]{2,1,0:T(8,128)(2,1)} %get-tuple-element.208.refs_2_), channel_id=1, source_target_pairs={{4,0},{0,4},{12,8},{8,12},{20,16},{16,20},{28,24},{24,28},{5,1},{1... | collective-permute-start | bytes 2359304 | tf_op jit(solution)/shard_map/ppermute | solution.py:682
  17.3 9.1 %copy-start.25 = (s32[1,4]{1,0:T(1,128)S(1)}, s32[1,4]{1,0:T(1,128)}, u32[]{:S(2)}) copy-start(s32[1,4]{1,0:T(1,128)} %param.21) | copy-start | bytes 52
  17.3 11.0 %copy-start.21 = (s32[2,192,2]{1,2,0:T(2,128)S(1)}, s32[2,192,2]{1,2,0:T(2,128)}, u32[]{:S(2)}) copy-start(s32[2,192,2]{1,2,0:T(2,128)} %param.22) | copy-start | bytes 9220
  18.9 115.5 %copy-start.19 = (f32[12,12]{1,0:T(8,128)S(1)}, f32[12,12]{1,0:T(8,128)}, u32[]{:S(2)}) copy-start(f32[12,12]{1,0:T(8,128)} %param.27) | copy-start | bytes 1732
  24.3 266.0 %collective-permute-start.5 = (bf16[2,256,768]{2,1,0:T(8,128)(2,1)}, bf16[2,256,768]{2,1,0:T(8,128)(2,1)S(1)}, u32[]{:S(2)}, u32[]{:S(2)}) collective-permute-start(bf16[2,256,768]{2,1,0:T(8,128)(2,1)} %get-tuple-element.206.refs_4_), channel_id=1, source_target_pairs={{4,0},{0,4},{12,8},{8,12},{20,16},{16,20},{28,24},{24,28},{5,1},{1... | collective-permute-start | bytes 2359304 | tf_op jit(solution)/shard_map/ppermute | solution.py:682
  133.6 42.1 %copy-start.18 = (s32[192]{0:T(256)}, s32[192]{0:T(256)S(1)}, u32[]{:S(2)}) copy-start(s32[192]{0:T(256)S(1)} %convert_reduce_fusion) | copy-start | bytes 2308
  290.3 0.9 copy-start.8
  602.0 138.3 %collective-permute-start.10 = (bf16[2,256,768]{2,1,0:T(8,128)(2,1)}, bf16[2,256,768]{2,1,0:T(8,128)(2,1)S(1)}, u32[]{:S(2)}, u32[]{:S(2)}) collective-permute-start(bf16[2,256,768]{2,1,0:T(8,128)(2,1)} %get-tuple-element.167), channel_id=1, source_target_pairs={{0,4},{4,0},{8,12},{12,8},{16,20},{20,16},{24,28},{28,24},{1,5},{5... | collective-permute-start | bytes 2359304 | tf_op jit(solution)/shard_map/ppermute | solution.py:689
  603.7 136.9 %collective-permute-start.11 = (bf16[2,256,768]{2,1,0:T(8,128)(2,1)}, bf16[2,256,768]{2,1,0:T(8,128)(2,1)S(1)}, u32[]{:S(2)}, u32[]{:S(2)}) collective-permute-start(bf16[2,256,768]{2,1,0:T(8,128)(2,1)} %get-tuple-element.169), channel_id=1, source_target_pairs={{0,4},{4,0},{8,12},{12,8},{16,20},{20,16},{24,28},{28,24},{1,5},{5... | collective-permute-start | bytes 2359304 | tf_op jit(solution)/shard_map/ppermute | solution.py:689
  604.2 139.7 %collective-permute-start.8 = (bf16[2,768,256]{2,1,0:T(8,128)(2,1)}, bf16[2,768,256]{2,1,0:T(8,128)(2,1)S(1)}, u32[]{:S(2)}, u32[]{:S(2)}) collective-permute-start(bf16[2,768,256]{2,1,0:T(8,128)(2,1)} %get-tuple-element.163), channel_id=1, source_target_pairs={{0,4},{4,0},{8,12},{12,8},{16,20},{20,16},{24,28},{28,24},{1,5},{5... | collective-permute-start | bytes 2359304 | tf_op jit(solution)/shard_map/ppermute | solution.py:689
  605.7 138.4 %collective-permute-start.9 = (bf16[2,768,256]{2,1,0:T(8,128)(2,1)}, bf16[2,768,256]{2,1,0:T(8,128)(2,1)S(1)}, u32[]{:S(2)}, u32[]{:S(2)}) collective-permute-start(bf16[2,768,256]{2,1,0:T(8,128)(2,1)} %get-tuple-element.165), channel_id=1, source_target_pairs={{0,4},{4,0},{8,12},{12,8},{16,20},{20,16},{24,28},{28,24},{1,5},{5... | collective-permute-start | bytes 2359304 | tf_op jit(solution)/shard_map/ppermute | solution.py:689
  606.2 141.2 %collective-permute-start.6 = (bf16[2,768,256]{2,1,0:T(8,128)(2,1)}, bf16[2,768,256]{2,1,0:T(8,128)(2,1)S(1)}, u32[]{:S(2)}, u32[]{:S(2)}) collective-permute-start(bf16[2,768,256]{2,1,0:T(8,128)(2,1)} %get-tuple-element.159), channel_id=1, source_target_pairs={{0,4},{4,0},{8,12},{12,8},{16,20},{20,16},{24,28},{28,24},{1,5},{5... | collective-permute-start | bytes 2359304 | tf_op jit(solution)/shard_map/ppermute | solution.py:689
  608.4 15.2 %copy-start.16 = (f32[24,768]{1,0:T(8,128)S(1)}, f32[24,768]{1,0:T(8,128)}, u32[]{:S(2)}) copy-start(f32[24,768]{1,0:T(8,128)} %get-tuple-element.147) | copy-start | bytes 221188
  731.8 5.9 copy-start.15
  737.7 2.6 copy-start.24
  737.7 2.7 copy-start.14
  740.3 19.8 %collective-permute-start.7 = (bf16[2,768,256]{2,1,0:T(8,128)(2,1)S(1)}, bf16[2,768,256]{2,1,0:T(8,128)(2,1)S(1)}, u32[]{:S(2)}, u32[]{:S(2)}) collective-permute-start(bf16[2,768,256]{2,1,0:T(8,128)(2,1)S(1)} %copy-done.24), channel_id=1, source_target_pairs={{0,4},{4,0},{8,12},{12,8},{16,20},{20,16},{24,28},{28,24},{1,5},{5... | collective-permute-start | bytes 2359304 | tf_op jit(solution)/shard_map/ppermute | solution.py:689
  740.4 1.4 copy-start.11
  742.0 1.9 copy-start.13
  743.9 1.4 copy-start.10
  745.5 2.0 copy-start.12
  747.5 12.6 %copy-start.9 = (f32[2,768,256]{2,1,0:T(8,128)S(1)}, f32[2,768,256]{2,1,0:T(8,128)}, u32[]{:S(2)}) copy-start(f32[2,768,256]{2,1,0:T(8,128)} %get-tuple-element.160) | copy-start | bytes 4718596
  760.3 1.9 copy-start.1

commit v3 on v1

--- a/solution.py
+++ b/solution.py
@@ -342,149 +342,210 @@
     )(*args)
 
 
-def mate(place, step, owners):
-    if owners != 4 or step == 0:
-        return lax.rem(place + step, owners)
-    if step == 1:
-        return place + 1 - 2 * lax.rem(place, 2)
-    return lax.rem(place + 2, 4) if step == 2 else 3 - place
+class Place:
+    def __init__(self, spread):
+        self.spread = spread
+        self.d, self.e = lax.axis_index("dp"), lax.axis_index("expert")
+        self.t, self.f = self.d // spread, lax.rem(self.d, spread)
+        self.y, self.c = self.e // 2, lax.rem(self.e, 2)
+        self.above, self.below = self.t < LINE - 1, self.t > 0
+        self.sibling = (self.d, self.e + 1 - 2 * self.c)
+        self.across = (self.d, lax.rem(self.e + 2, 4))
+        self.corner = (self.d, 3 - self.e)
+        self.beside = (self.t * spread + 1 - self.f, self.e)
+        self.mates = [(self.d, self.e), self.sibling, self.across, self.corner]
+
+    def on_line(self, up):
+        return (self.d + self.spread if up else self.d - self.spread, self.e)
+
+
+def greet(always, place):
+    barrier = pltpu.get_barrier_semaphore()
+    for device in always:
+        pl.semaphore_signal(barrier, inc=1, device_id=device, device_id_type=MESH)
+    for up, there in ((1, place.above), (0, place.below)):
+
+        @pl.when(there)
+        def _(up=up):
+            pl.semaphore_signal(barrier, inc=1, device_id=place.on_line(up), device_id_type=MESH)
+
+    ends = place.above.astype(jnp.int32) + place.below.astype(jnp.int32)
+    pl.semaphore_wait(barrier, len(always) + ends)
+
+
+def remote(src, dst, send, recv, device):
+    return pltpu.make_async_remote_copy(
+        src_ref=src, dst_ref=dst, send_sem=send, recv_sem=recv, device_id=device, device_id_type=MESH)
+
+
+def dma(*shape):
+    return pltpu.SemaphoreType.DMA(shape)
+
+
+def along(place, body, start=0):
+    if start == 0:
+        body(place.t)
+
+    def step(k, carry):
+        for t in (place.t + k, place.t - k):
+
+            @pl.when(jnp.logical_and(t >= 0, t < LINE))
+            def _(t=t):
+                body(t)
+
+        return carry
+
+    lax.fori_loop(1, LINE, step, 0)
+
+
+class Rider:
+    partners = ()
+
+    def begin(self):
+        pass
+
+    def after_first(self):
+        pass
+
+    def after_line(self):
+        pass
+
+    def after_relay(self):
+        pass
+
+    def finish(self):
+        pass
 
 
 class Line:
-    def __init__(self, spread, owners, x, part, stage, arrived, final, returned, sems):
-        self.owners, self.spread = owners, spread
-        self.d, self.e = lax.axis_index("dp"), lax.axis_index("expert")
-        self.t = self.d // spread
+    def __init__(self, place, x, part, stage, arrived, final, returned, sems):
+        self.p = place
         self.x, self.part, self.stage, self.arrived = x, part, stage, arrived
         self.final, self.returned = final, returned
         (self.out_send, self.x_recv, self.x_send, self.sum_send, self.sum_recv, self.ret_send, self.ret_recv) = sems
-        self.above, self.below = self.t < LINE - 1, self.t > 0
-
-    def greet(self):
-        barrier = pltpu.get_barrier_semaphore()
-        for i in range(1, self.owners):
-            pl.semaphore_signal(barrier, inc=1, device_id=(self.d, mate(self.e, i, self.owners)), device_id_type=MESH)
-
-        @pl.when(self.above)
-        def _():
-            pl.semaphore_signal(barrier, inc=1, device_id=(self.d + self.spread, self.e), device_id_type=MESH)
-
-        @pl.when(self.below)
-        def _():
-            pl.semaphore_signal(barrier, inc=1, device_id=(self.d - self.spread, self.e), device_id_type=MESH)
-
-        ends = self.above.astype(jnp.int32) + self.below.astype(jnp.int32)
-        pl.semaphore_wait(barrier, self.owners - 1 + ends)
+
+    @staticmethod
+    def scratch(local, width):
+        shape = (local, 4, CAP, width)
+        return [
+            pltpu.VMEM((local, LINE, 4, CAP, width), BF16),
+            pltpu.VMEM((LINE,) + shape, F32),
+            pltpu.VMEM((LINE,) + shape, BF16),
+            pltpu.VMEM((2, LINE) + shape, BF16),
+            pltpu.VMEM((4, local, CAP, width), BF16),
+            dma(4), dma(LINE, 4), dma(2, LINE, 4), dma(LINE, 4), dma(2, LINE, 4), dma(4), dma(4),
+        ]
 
     def slot_copy(self, out, i):
-        to = mate(self.e, i, self.owners)
-        return pltpu.make_async_remote_copy(
-            src_ref=out.at[to], dst_ref=self.x.at[:, self.t, self.e], send_sem=self.out_send.at[i],
-            recv_sem=self.x_recv.at[self.t, self.e], device_id=(self.d, to), device_id_type=MESH)
+        to, p = self.p.mates[i], self.p
+        return remote(out.at[to[1]], self.x.at[:, p.t, p.e], self.out_send.at[i], self.x_recv.at[p.t, p.e], to)
 
     def x_copy(self, up, s, b):
-        to = self.d + self.spread if up else self.d - self.spread
-        return pltpu.make_async_remote_copy(
-            src_ref=self.x.at[:, s, b], dst_ref=self.x.at[:, s, b], send_sem=self.x_send.at[up, s, b],
-            recv_sem=self.x_recv.at[s, b], device_id=(to, self.e), device_id_type=MESH)
+        at = self.x.at[:, s, b]
+        return remote(at, at, self.x_send.at[up, s, b], self.x_recv.at[s, b], self.p.on_line(up))
 
     def sum_copy(self, up, s, b):
-        to = self.d + self.spread if up else self.d - self.spread
-        return pltpu.make_async_remote_copy(
-            src_ref=self.stage.at[s, :, b], dst_ref=self.arrived.at[up, s, :, b], send_sem=self.sum_send.at[s, b],
-            recv_sem=self.sum_recv.at[up, s, b], device_id=(to, self.e), device_id_type=MESH)
-
-    def ret_copy(self, i):
-        to = mate(self.e, i, self.owners)
-        return pltpu.make_async_remote_copy(
-            src_ref=self.final.at[to], dst_ref=self.returned.at[self.e], send_sem=self.ret_send.at[i],
-            recv_sem=self.ret_recv.at[self.e], device_id=(self.d, to), device_id_type=MESH)
-
-    def run(self, out, compute, meanwhile, keep):
-        t, e, owners = self.t, self.e, self.owners
-        self.greet()
-        for i in list(range(2, owners)) + [1]:
+        return remote(self.stage.at[s, :, b], self.arrived.at[up, s, :, b], self.sum_send.at[s, b],
+                      self.sum_recv.at[up, s, b], self.p.on_line(up))
+
+    def ret_copy(self, i, to_mate=True):
+        to = self.p.mates[i]
+        row = self.p.e if to_mate else to[1]
+        return remote(self.final.at[to[1]], self.returned.at[row], self.ret_send.at[i], self.ret_recv.at[row], to)
+
+    def send_sum(self, up, s, b, total):
+        self.stage[s, :, b] = total.astype(BF16)
+        self.sum_copy(up, s, b).start()
+
+    def relay(self, stage):
+        p = self.p
+        for up, mine in ((1, p.t == stage), (0, p.t == LINE - 1 - stage)):
+
+            @pl.when(mine)
+            def _(up=up):
+                def one(n, carry):
+                    s = p.t + 1 + n if up else p.t - 1 - n
+                    for _, b in p.mates:
+                        self.sum_copy(up, s, b).wait_recv()
+                        self.send_sum(up, s, b, self.part[s, :, b] + self.arrived[up, s, :, b].astype(F32))
+                    return carry
+
+                lax.fori_loop(0, LINE - 1 - stage, one, 0)
+
+    def run(self, out, compute, kept, meanwhile, rider):
+        p = self.p
+        t, e = p.t, p.e
+        blocks = [b for _, b in p.mates]
+        greet(p.mates[1:] + list(rider.partners), p)
+        for i in (2, 3, 1):
             self.slot_copy(out, i).start()
         self.x[:, t, e] = out[e]
-        for i in range(owners):
-            b = mate(e, i, owners)
-            if i:
-                self.x_copy(0, t, b).wait_recv()
-            for up, there in ((0, self.below), (1, self.above)):
-
-                @pl.when(there)
-                def _(up=up, b=b):
-                    self.x_copy(up, t, b).start()
-
-        keep(t)
-        compute(t)
+        rider.begin()
+        for half in (0, 1):
+            for i in (2 * half, 2 * half + 1):
+                if i:
+                    self.x_copy(0, t, blocks[i]).wait_recv()
+                for up, there in ((0, p.below), (1, p.above)):
+
+                    @pl.when(there)
+                    def _(up=up, i=i):
+                        self.x_copy(up, t, blocks[i]).start()
+
+            compute(t, p.y + half - 2 * p.y * half)
+        kept(t)
+        rider.after_first()
 
         def step(k, carry):
-            for i in range(owners):
-                b = mate(e, i, owners)
-
-                @pl.when(t + k < LINE)
-                def _(b=b):
-                    self.x_copy(0, t + k, b).wait_recv()
-
-                    @pl.when(self.below)
+            def part(half, carry):
+                pair = p.y + half - 2 * p.y * half
+                first = jnp.where(half == 0, blocks[0], blocks[2])
+                second = jnp.where(half == 0, blocks[1], blocks[3])
+                for b in (first, second):
+                    for up, there, onward in ((0, t + k < LINE, p.below), (1, t - k >= 0, p.above)):
+                        s = t - k if up else t + k
+
+                        @pl.when(there)
+                        def _(up=up, onward=onward, s=s, b=b):
+                            self.x_copy(up, s, b).wait_recv()
+
+                            @pl.when(onward)
+                            def _():
+                                self.x_copy(up, s, b).start()
+
+                def side(up, carry):
+                    s = t + k - 2 * k * up
+
+                    @pl.when(jnp.logical_and(s >= 0, s < LINE))
                     def _():
-                        self.x_copy(0, t + k, b).start()
-
-                @pl.when(t - k >= 0)
-                def _(b=b):
-                    self.x_copy(1, t - k, b).wait_recv()
-
-                    @pl.when(self.above)
-                    def _():
-                        self.x_copy(1, t - k, b).start()
-
-            def side(up, carry):
-                s = t + k - 2 * k * up
-
-                @pl.when(jnp.logical_and(s >= 0, s < LINE))
-                def _():
-                    keep(s)
-                    compute(s)
+                        compute(s, pair)
+
+                        @pl.when(half == 1)
+                        def _():
+                            kept(s)
+
+                    return carry
+
+                lax.fori_loop(0, 2, side, 0)
+                for up, starts, s in ((1, t == 0, k), (0, t == LINE - 1, LINE - 1 - k)):
+
+                    @pl.when(starts)
+                    def _(up=up, s=s):
+                        for b in (first, second):
+                            self.send_sum(up, s, b, self.part[s, :, b])
 
                 return carry
 
-            lax.fori_loop(0, 2, side, 0)
-            for up, first, s in ((1, t == 0, k), (0, t == LINE - 1, LINE - 1 - k)):
-
-                @pl.when(first)
-                def _(up=up, s=s):
-                    for i in (list(range(2, owners)) + [0, 1])[:owners]:
-                        b = mate(e, i, owners)
-                        self.stage[s, :, b] = self.part[s, :, b].astype(BF16)
-                        self.sum_copy(up, s, b).start()
-
+            lax.fori_loop(0, 2, part, 0)
             return carry
 
         lax.fori_loop(1, LINE, step, 0)
+        rider.after_line()
         meanwhile()
-
-        def relay(k, carry):
-            for i in (list(range(2, owners)) + [0, 1])[:owners]:
-                b = mate(e, i, owners)
-                for up, s, inside in (
-                    (1, k, jnp.logical_and(t > 0, t < k)),
-                    (0, LINE - 1 - k, jnp.logical_and(t > LINE - 1 - k, t < LINE - 1)),
-                ):
-
-                    @pl.when(inside)
-                    def _(up=up, s=s, b=b):
-                        self.sum_copy(up, s, b).wait_recv()
-                        total = self.part[s, :, b] + self.arrived[up, s, :, b].astype(F32)
-                        self.stage[s, :, b] = total.astype(BF16)
-                        self.sum_copy(up, s, b).start()
-
-            return carry
-
-        lax.fori_loop(2, LINE, relay, 0)
-        for i in (list(range(2, owners)) + [0, 1])[:owners]:
-            b = mate(e, i, owners)
-            for up, there in ((1, self.below), (0, self.above)):
+        for stage in range(1, LINE - 1):
+            self.relay(stage)
+        rider.after_relay()
+        for i, b in enumerate(blocks):
+            for up, there in ((1, p.below), (0, p.above)):
 
                 @pl.when(there)
                 def _(up=up, b=b):
@@ -498,8 +559,8 @@
                 self.returned[e] = self.part[t, :, e].astype(BF16)
 
         def sent(s, carry):
-            for i in range(owners):
-                for up, mine in ((0, jnp.logical_and(self.below, s >= t)), (1, jnp.logical_and(self.above, s <= t))):
+            for i in range(4):
+                for up, mine in ((0, jnp.logical_and(p.below, s >= t)), (1, jnp.logical_and(p.above, s <= t))):
 
                     @pl.when(mine)
                     def _(up=up, i=i):
@@ -511,163 +572,232 @@
 
             return carry
 
-        for i in range(1, owners):
+        for i in (1, 2, 3):
             self.slot_copy(out, i).wait_send()
         lax.fori_loop(0, LINE, sent, 0)
-        for i in range(1, owners):
+        rider.finish()
+        for i in (1, 2, 3):
             self.ret_copy(i).wait_send()
-            pltpu.make_async_remote_copy(
-                src_ref=self.final.at[e], dst_ref=self.returned.at[mate(e, i, owners)], send_sem=self.ret_send.at[i],
-                recv_sem=self.ret_recv.at[mate(e, i, owners)], device_id=(self.d, mate(e, i, owners)), device_id_type=MESH).wait_recv()
-
-
-def line_scratch(local, owners, width):
-    shape = (local, owners, CAP, width)
-    dma = pltpu.SemaphoreType.DMA
-    return [
-        pltpu.VMEM((local, LINE, owners, CAP, width), BF16),
-        pltpu.VMEM((LINE,) + shape, F32),
-        pltpu.VMEM((LINE,) + shape, BF16),
-        pltpu.VMEM((2, LINE) + shape, BF16),
-        pltpu.VMEM((owners, local, CAP, width), BF16),
-        dma((owners,)), dma((LINE, owners)), dma((2, LINE, owners)), dma((LINE, owners)), dma((2, LINE, owners)),
-        dma((owners,)), dma((owners,)),
-    ]
-
-
-def expert_forward_kernel(spread, parts, out, *refs):
-    gate, up, down = refs[:parts], refs[parts : 2 * parts], refs[2 * parts : 3 * parts]
-    returned, x_keep, g_keep, u_keep, x, part, stage, arrived, final = refs[3 * parts : 3 * parts + 9]
-    sems, (g_all, u_all, keep_sem) = refs[3 * parts + 9 : 3 * parts + 16], refs[3 * parts + 16 :]
-    local, _, owners, _, width = x.shape
-    rows = owners * CAP
-    line = Line(spread, owners, x, part, stage, arrived, final, returned, sems)
+            self.ret_copy(i, False).wait_recv()
+
+
+def split(refs, *counts):
+    out, at = [], 0
+    for count in counts:
+        out.append(refs[at : at + count])
+        at += count
+    return out + [refs[at:]]
+
+
+def expert_forward_kernel(spread, parts, ride, out, *refs):
+    weights_in, shards, outs, whole, scratch, line_refs, sems, ride_refs = split(
+        refs, 3 * parts, 9 if ride else 0, 4, 6 if ride else 0, 3 * parts, 5, 7)
+    (g_all, u_all, keep_sem, load_sem), ride_refs = ride_refs[:4], ride_refs[4:]
+    returned, x_keep, g_keep, u_keep = outs
+    gate, up, down = scratch[:parts], scratch[parts : 2 * parts], scratch[2 * parts :]
+    x, part, stage, arrived, final = line_refs
+    local, _, _, _, width = x.shape
+    rows = 2 * CAP
+    p = Place(spread)
+    line = Line(p, x, part, stage, arrived, final, returned, sems)
+    rider = Spread(p, shards, whole, ride_refs) if ride else Rider()
+
+    def load(i):
+        return pltpu.make_async_copy(weights_in[i], scratch[i], load_sem.at[i])
+
+    for i in range(3 * parts):
+        load(i).start()
+
+    def keep_x(s):
+        return pltpu.make_async_copy(x.at[:, s], x_keep.at[:, s], keep_sem.at[0, s])
+
+    def keep_g(s):
+        return pltpu.make_async_copy(g_all.at[s], g_keep.at[s], keep_sem.at[1, s])
+
+    def keep_u(s):
+        return pltpu.make_async_copy(u_all.at[s], u_keep.at[s], keep_sem.at[2, s])
 
     def kept(s):
-        yield pltpu.make_async_copy(x.at[:, s], x_keep.at[:, s], keep_sem.at[0, s])
-        yield pltpu.make_async_copy(g_all.at[s], g_keep.at[s], keep_sem.at[1, s])
-        yield pltpu.make_async_copy(u_all.at[s], u_keep.at[s], keep_sem.at[2, s])
-
-    def compute(s):
+        keep_x(s).start()
+        keep_g(s).start()
+        keep_u(s).start()
+
+    def compute(s, pair):
+        at = pl.multiple_of(pair * rows, rows)
+
         def one(l, carry):
-            rows_in = x[l, s].reshape(rows, width)
+            rows_in = x[l, s, pl.ds(2 * pair, 2)].reshape(rows, width)
             total = jnp.zeros((rows, width), F32)
-            for p in range(parts):
-                cols = gate[p].shape[2]
-                g = dot_nn(rows_in, gate[p][l])
-                u = dot_nn(rows_in, up[p][l])
-                g_all[s, l, :, p * cols : (p + 1) * cols] = g
-                u_all[s, l, :, p * cols : (p + 1) * cols] = u
+            for q in range(parts):
+                cols = gate[q].shape[2]
+                here = slice(q * cols, (q + 1) * cols)
+                g = dot_nn(rows_in, gate[q][l])
+                u = dot_nn(rows_in, up[q][l])
+                g_all[s, l, pl.ds(at, rows), here] = g
+                u_all[s, l, pl.ds(at, rows), here] = u
                 act = (g * jax.nn.sigmoid(g) * u).astype(BF16)
-                total = total + dot_nn(act, down[p][l])
-            part[s, l] = total.reshape(owners, CAP, width)
+                total = total + dot_nn(act, down[q][l])
+            part[s, l, pl.ds(2 * pair, 2)] = total.reshape(2, CAP, width)
             return carry
 
         lax.fori_loop(0, local, one, 0)
-        for copy in list(kept(s))[1:]:
-            copy.start()
-
-    line.run(out, compute, lambda: None, lambda s: next(kept(s)).start())
+
+    class Loaded(Rider):
+        partners = rider.partners
+        after_first, after_line, after_relay, finish = (
+            rider.after_first, rider.after_line, rider.after_relay, rider.finish)
+
+        def begin(self):
+            rider.begin()
+            for i in range(3 * parts):
+                load(i).wait()
+
+    line.run(out, compute, kept, lambda: None, Loaded())
     for s in range(LINE):
-        for copy in kept(s):
-            copy.wait()
-
-
-def expert_backward_kernel(spread, parts, out, x_in, g_all, u_all, *refs):
-    gate, up, down = refs[:parts], refs[parts : 2 * parts], refs[2 * parts : 3 * parts]
-    returned = refs[3 * parts]
-    grads = refs[3 * parts + 1 : 6 * parts + 1]
-    x, part, stage, arrived, final = refs[6 * parts + 1 : 6 * parts + 6]
-    sems, (act_all, gg_all, gu_all) = refs[6 * parts + 6 : 6 * parts + 13], refs[6 * parts + 13 :]
-    local, _, owners, _, width = x.shape
-    rows = owners * CAP
-    line = Line(spread, owners, x, part, stage, arrived, final, returned, sems)
-
-    def compute(s):
-        at = pl.multiple_of(s * rows, rows)
+        keep_x(s).wait()
+        keep_g(s).wait()
+        keep_u(s).wait()
+
+
+def expert_backward_kernel(spread, parts, ride, out, *refs):
+    loads_in, dense, outs, quarter, loads, line_refs, sems, rest = split(
+        refs, 3 + 3 * parts, 2 if ride else 0, 1 + 3 * parts, 1 if ride else 0, 3 + 3 * parts, 5, 7)
+    (act_all, gg_all, gu_all), grads, (load_sem, grad_sem), ride_refs = split(rest, 3, 3 * parts, 2)
+    returned, grads_out = outs[0], outs[1:]
+    x_in, g_all, u_all = loads[:3]
+    gate, up, down = loads[3 : 3 + parts], loads[3 + parts : 3 + 2 * parts], loads[3 + 2 * parts :]
+    x, part, stage, arrived, final = line_refs
+    local, _, _, _, width = x.shape
+    rows = 2 * CAP
+    p = Place(spread)
+    line = Line(p, x, part, stage, arrived, final, returned, sems)
+    rider = Halve(p, dense, quarter[0], ride_refs) if ride else Rider()
+
+    def load(i):
+        return pltpu.make_async_copy(loads_in[i], loads[i], load_sem.at[i])
+
+    def store(i, l):
+        return pltpu.make_async_copy(grads[i].at[l], grads_out[i].at[l], grad_sem.at[i, l])
+
+    for i in range(3 + 3 * parts):
+        load(i).start()
+
+    def compute(s, pair):
+        at = pl.multiple_of(pair * rows, rows)
+        into = pl.ds(pl.multiple_of((2 * s + pair) * rows, rows), rows)
 
         def one(l, carry):
-            rows_in = x[l, s].reshape(rows, width)
+            rows_in = x[l, s, pl.ds(2 * pair, 2)].reshape(rows, width)
             total = jnp.zeros((rows, width), F32)
-            for p in range(parts):
-                cols = gate[p].shape[2]
-                here = slice(p * cols, (p + 1) * cols)
-                g, u = g_all[s, l, :, here], u_all[s, l, :, here]
-                g_act = dot_nt(rows_in, down[p][l])
+            for q in range(parts):
+                cols = gate[q].shape[2]
+                here = slice(q * cols, (q + 1) * cols)
+                g, u = g_all[s, l, pl.ds(at, rows), here], u_all[s, l, pl.ds(at, rows), here]
+                g_act = dot_nt(rows_in, down[q][l])
                 sigma = jax.nn.sigmoid(g)
                 swish = g * sigma
                 gg = (g_act * u * sigma * (1.0 + g * (1.0 - sigma))).astype(BF16)
                 gu = (g_act * swish).astype(BF16)
-                act_all[l, pl.ds(at, rows), here] = (swish * u).astype(BF16)
-                gg_all[l, pl.ds(at, rows), here] = gg
-                gu_all[l, pl.ds(at, rows), here] = gu
-                total = total + dot_nt(gg, gate[p][l]) + dot_nt(gu, up[p][l])
-            part[s, l] = total.reshape(owners, CAP, width)
+                act_all[l, into, here] = (swish * u).astype(BF16)
+                gg_all[l, into, here] = gg
+                gu_all[l, into, here] = gu
+                total = total + dot_nt(gg, gate[q][l]) + dot_nt(gu, up[q][l])
+            part[s, l, pl.ds(2 * pair, 2)] = total.reshape(2, CAP, width)
             return carry
 
         lax.fori_loop(0, local, one, 0)
 
     def weights():
         def one(l, carry):
-            x_rows = x_in[l].reshape(LINE * rows, width)
-            g_rows = x[l].reshape(LINE * rows, width)
-            for p in range(parts):
-                cols = gate[p].shape[2]
-                here = slice(p * cols, (p + 1) * cols)
-                for grad, value in (
-                    (grads[p], dot_tn(x_rows, gg_all[l, :, here])),
-                    (grads[parts + p], dot_tn(x_rows, gu_all[l, :, here])),
-                    (grads[2 * parts + p], dot_tn(act_all[l, :, here], g_rows)),
+            x_rows = x_in[l].reshape(2 * LINE * rows, width)
+            g_rows = x[l].reshape(2 * LINE * rows, width)
+            for q in range(parts):
+                cols = gate[q].shape[2]
+                here = slice(q * cols, (q + 1) * cols)
+                for i, value in (
+                    (q, dot_tn(x_rows, gg_all[l, :, here])),
+                    (parts + q, dot_tn(x_rows, gu_all[l, :, here])),
+                    (2 * parts + q, dot_tn(act_all[l, :, here], g_rows)),
                 ):
-                    grad[l] = value.astype(grad.dtype)
+                    grads[i][l] = value.astype(grads[i].dtype)
+                    store(i, l).start()
             return carry
 
         lax.fori_loop(0, local, one, 0)
 
-    line.run(out, compute, weights, lambda s: None)
-
-
-def expert_forward(spread, call_id, out, weights):
+    class Loaded(Rider):
+        partners = rider.partners
+        after_first, after_line, after_relay, finish = (
+            rider.after_first, rider.after_line, rider.after_relay, rider.finish)
+
+        def begin(self):
+            rider.begin()
+            for i in range(3 + 3 * parts):
+                load(i).wait()
+
+    line.run(out, compute, lambda s: None, weights, Loaded())
+    for i in range(3 * parts):
+        for l in range(local):
+            store(i, l).wait()
+
+
+def remote_params(call_id):
+    return pltpu.CompilerParams(collective_id=call_id, has_side_effects=True, vmem_limit_bytes=61 * 2**20)
+
+
+def struct(shape, dtype):
+    return jax.ShapeDtypeStruct(tuple(shape), dtype)
+
+
+def expert_forward(spread, call_id, out, weights, ride=None):
     parts = len(weights) // 3
-    owners, local, cap, width = out.shape
+    _, local, cap, width = out.shape
     columns = sum(w.shape[2] for w in weights[:parts])
-    kept = (LINE, local, owners * cap, columns)
+    kept = (LINE, local, 4 * cap, columns)
+    outs = [struct(out.shape, BF16), struct((local, LINE, 4, cap, width), BF16), struct(kept, F32), struct(kept, F32)]
+    scratch = [pltpu.VMEM(w.shape, BF16) for w in weights] + Line.scratch(local, width)
+    scratch += [pltpu.VMEM(kept, F32), pltpu.VMEM(kept, F32), dma(3, LINE), dma(len(weights))]
+    more = ()
+    if ride:
+        more = ride
+        count = LINE * spread
+        outs += [struct((count * s.shape[0], s.shape[1]), BF16) for s in ride[3:6]]
+        outs += [struct(w.shape, BF16) for w in ride[6:]]
+        scratch += Spread.scratch(count)
     return pl.pallas_call(
-        functools.partial(expert_forward_kernel, spread, parts),
-        out_shape=[
-            jax.ShapeDtypeStruct(out.shape, BF16),
-            jax.ShapeDtypeStruct((local, LINE, owners, cap, width), BF16),
-            jax.ShapeDtypeStruct(kept, F32),
-            jax.ShapeDtypeStruct(kept, F32),
-        ],
-        in_specs=[VMEM] * (1 + len(weights)),
-        out_specs=[VMEM, ANY, ANY, ANY],
-        scratch_shapes=line_scratch(local, owners, width)
-        + [pltpu.VMEM(kept, F32), pltpu.VMEM(kept, F32), pltpu.SemaphoreType.DMA((3, LINE))],
-        compiler_params=pltpu.CompilerParams(
-            collective_id=call_id, has_side_effects=True, vmem_limit_bytes=60 * 2**20
-        ),
-    )(out, *weights)
-
-
-def expert_backward(spread, call_id, out, kept, weights):
+        functools.partial(expert_forward_kernel, spread, parts, ride is not None),
+        out_shape=outs,
+        in_specs=[VMEM] + [ANY] * (len(weights) + len(more)),
+        out_specs=[VMEM] + [ANY] * (len(outs) - 1),
+        scratch_shapes=scratch,
+        compiler_params=remote_params(call_id),
+    )(out, *weights, *more)
+
+
+def expert_backward(spread, call_id, out, kept, weights, ride=None):
     parts = len(weights) // 3
-    owners, local, cap, width = out.shape
+    _, local, cap, width = out.shape
     columns = sum(w.shape[2] for w in weights[:parts])
-    shapes = [
-        jax.ShapeDtypeStruct(w.shape, F32 if i % parts == 0 else BF16) for i, w in enumerate(weights)
-    ]
-    wide = pltpu.VMEM((local, LINE * owners * cap, columns), BF16)
+    loads = list(kept) + list(weights)
+    grads = [(w.shape, F32 if i % parts == 0 else BF16) for i, w in enumerate(weights)]
+    wide = pltpu.VMEM((local, LINE * 4 * cap, columns), BF16)
+    outs = [struct(out.shape, BF16)] + [struct(*g) for g in grads]
+    scratch = [pltpu.VMEM(a.shape, a.dtype) for a in loads] + Line.scratch(local, width)
+    scratch += [wide] * 3 + [pltpu.VMEM(*g) for g in grads] + [dma(len(loads)), dma(len(grads), local)]
+    more = ()
+    if ride:
+        more = ride
+        depths = [g.shape[0] // (LINE * spread) for g in ride]
+        outs.append(struct((LINE, spread, sum(depths) // 2, width // 2), F32))
+        scratch += Halve.scratch(spread, depths, width)
     return pl.pallas_call(
-        functools.partial(expert_backward_kernel, spread, parts),
-        out_shape=[jax.ShapeDtypeStruct(out.shape, BF16)] + shapes,
-        in_specs=[VMEM] * (4 + len(weights)),
-        out_specs=[VMEM] * (1 + len(weights)),
-        scratch_shapes=line_scratch(local, owners, width) + [wide] * 3,
-        compiler_params=pltpu.CompilerParams(
-            collective_id=call_id, has_side_effects=True, vmem_limit_bytes=60 * 2**20
-        ),
-    )(out, *kept, *weights)
+        functools.partial(expert_backward_kernel, spread, parts, ride is not None),
+        out_shape=outs,
+        in_specs=[VMEM] + [ANY] * (len(loads) + len(more)),
+        out_specs=[VMEM] + [ANY] * len(grads) + [VMEM] * len(more[:1]),
+        scratch_shapes=scratch,
+        compiler_params=remote_params(call_id),
+    )(out, *loads, *more)
 
 
 def from_partner(array, shift, spread, groups):
@@ -685,7 +815,6 @@
 
 
 def pair_weights(shard, axis, spread):
-    shard = shard.astype(BF16)
     parts = [shard] + [from_partner(shard, i, spread, LINE) for i in range(1, spread)]
     if shard.shape[axis] % 128:
         return [jnp.concatenate(parts, axis=axis)]
@@ -699,6 +828,567 @@
     for i in range(1, spread):
         total = total + to_partner(parts[i].astype(BF16), i, spread, LINE).astype(F32)
     return total
+
+
+class LineGather:
+    def __init__(self, place, shards, quarters, sems):
+        self.p, self.shards, self.quarters = place, shards, quarters
+        self.send, self.recv = sems
+
+    @staticmethod
+    def shapes(shards):
+        (a, wide), (b, _), (c, narrow) = (s.shape for s in shards)
+        return [(LINE, a // 2, wide // 2), (LINE, b // 2, wide // 2), (LINE, c, narrow)]
+
+    @staticmethod
+    def scratch():
+        return [dma(2, LINE, 3), dma(LINE, 3)]
+
+    def copy(self, kind, up, t):
+        at = self.quarters[kind].at[t]
+        return remote(at, at, self.send.at[up, t, kind], self.recv.at[t, kind], self.p.on_line(up))
+
+    def begin(self):
+        p = self.p
+        for kind in (0, 1):
+            half, wide = self.quarters[kind].shape[1:]
+            self.quarters[kind][p.t] = self.shards[kind][
+                pl.ds(pl.multiple_of(p.y * half, 16), half), pl.ds(pl.multiple_of(p.c * wide, 128), wide)]
+        self.quarters[2][p.t] = self.shards[2][...]
+        for up, there in ((0, p.below), (1, p.above)):
+
+            @pl.when(there)
+            def _(up=up):
+                for kind in range(3):
+                    self.copy(kind, up, p.t).start()
+
+    def step(self, k, then):
+        p = self.p
+        for up, there, onward in ((0, p.t + k < LINE, p.below), (1, p.t - k >= 0, p.above)):
+            t = p.t - k if up else p.t + k
+
+            @pl.when(there)
+            def _(up=up, onward=onward, t=t):
+                for kind in range(3):
+                    self.copy(kind, up, t).wait_recv()
+
+                @pl.when(onward)
+                def _():
+                    for kind in range(3):
+                        self.copy(kind, up, t).start()
+
+                then(t)
+
+    def finish(self):
+        p = self.p
+
+        def line(t, carry):
+            for up, mine in ((0, jnp.logical_and(p.below, t >= p.t)), (1, jnp.logical_and(p.above, t <= p.t))):
+
+                @pl.when(mine)
+                def _(up=up):
+                    for kind in range(3):
+                        self.copy(kind, up, t).wait_send()
+
+            return carry
+
+        lax.fori_loop(0, LINE, line, 0)
+
+
+class Spread:
+    def __init__(self, place, given, whole, sems):
+        self.p = place
+        self.quarters, self.shards, self.own = given[:3], given[3:6], given[6:]
+        self.whole, self.other = whole[:3], whole[3:]
+        (self.x_send, self.x_recv, self.y_send, self.y_recv, self.c_send, self.c_recv, self.l_sem, self.s_sem,
+         self.w_send, self.w_recv) = sems
+        self.partners = [place.beside]
+
+    @staticmethod
+    def scratch(count):
+        return [dma(LINE, 3), dma(LINE, 3), dma(count, 2), dma(count, 2), dma(count, 2, 2), dma(count, 2, 2),
+                dma(LINE, 3), dma(3), dma(3), dma(3)]
+
+    def region(self, kind, s, y, c):
+        depth = self.shards[kind].shape[0]
+        if kind == 2:
+            return self.whole[2].at[pl.ds(pl.multiple_of(s * depth, 16), depth)]
+        half, wide = depth // 2, self.shards[kind].shape[1] // 2
+        return self.whole[kind].at[
+            pl.ds(pl.multiple_of(s * depth + y * half, 16), half), pl.ds(pl.multiple_of(c * wide, 128), wide)]
+
+    def mine(self, kind, s):
+        return self.region(kind, s, self.p.y, self.p.c)
+
+    def place_of(self, t):
+        return t * self.p.spread + self.p.f
+
+    def beside_of(self, t):
+        return t * self.p.spread + 1 - self.p.f
+
+    def x_copy(self, kind, t):
+        return remote(self.quarters[kind].at[t], self.mine(kind, self.place_of(t)), self.x_send.at[t, kind],
+                      self.x_recv.at[t, kind], self.p.beside)
+
+    def x_came(self, kind, t):
+        return remote(self.quarters[kind].at[t], self.mine(kind, self.beside_of(t)), self.x_send.at[t, kind],
+                      self.x_recv.at[t, kind], self.p.beside)
+
+    def y_copy(self, kind, src, s):
+        return remote(src, self.mine(kind, s), self.y_send.at[s, kind], self.y_recv.at[s, kind], self.p.across)
+
+    def y_came(self, kind, s):
+        at = self.region(kind, s, 1 - self.p.y, self.p.c)
+        return remote(at, at, self.y_send.at[s, kind], self.y_recv.at[s, kind], self.p.across)
+
+    def c_copy(self, kind, src, s, y):
+        return remote(src, self.region(kind, s, y, self.p.c), self.c_send.at[s, y, kind], self.c_recv.at[s, y, kind],
+                      self.p.sibling)
+
+    def c_came(self, kind, s, y):
+        at = self.region(kind, s, y, 1 - self.p.c)
+        return remote(at, at, self.c_send.at[s, y, kind], self.c_recv.at[s, y, kind], self.p.sibling)
+
+    def local(self, kind, t):
+        return pltpu.make_async_copy(self.quarters[kind].at[t], self.mine(kind, self.place_of(t)), self.l_sem.at[t, kind])
+
+    def shard(self, kind):
+        depth = self.shards[kind].shape[0]
+        at = self.whole[kind].at[pl.ds(pl.multiple_of(self.p.d * depth, 16), depth)]
+        return pltpu.make_async_copy(self.shards[kind], at, self.s_sem.at[kind])
+
+    def weight(self, i):
+        return remote(self.own[i], self.other[i], self.w_send.at[i], self.w_recv.at[i], self.p.beside)
+
+    def own_shard(self):
+        for kind in range(3):
+            self.shard(kind).start()
+
+    def from_line(self, t):
+        for kind in range(3):
+            self.x_copy(kind, t).start()
+
+        @pl.when(t != self.p.t)
+        def _():
+            for kind in range(3):
+                self.local(kind, t).start()
+            for kind in (0, 1):
+                self.y_copy(kind, self.quarters[kind].at[t], self.place_of(t)).start()
+                self.c_copy(kind, self.quarters[kind].at[t], self.place_of(t), self.p.y).start()
+
+    def begin(self):
+        self.own_shard()
+        along(self.p, self.from_line)
+        for i in range(len(self.own)):
+            self.weight(i).start()
+
+    def after_first(self):
+        pass
+
+    def after_line(self):
+        def body(t):
+            for kind in range(3):
+                self.x_came(kind, t).wait_recv()
+            for kind in (0, 1):
+                s = self.beside_of(t)
+                self.y_copy(kind, self.mine(kind, s), s).start()
+                self.c_copy(kind, self.mine(kind, s), s, self.p.y).start()
+
+        along(self.p, body)
+
+    def after_relay(self):
+        p = self.p
+
+        def across(s):
+            for kind in (0, 1):
+                at = self.region(kind, s, 1 - p.y, p.c)
+                self.y_came(kind, s).wait_recv()
+                self.c_copy(kind, at, s, 1 - p.y).start()
+
+        along(p, lambda t: across(self.place_of(t)), start=1)
+        along(p, lambda t: across(self.beside_of(t)))
+
+    def finish(self):
+        p = self.p
+        for kind in range(3):
+            self.shard(kind).wait()
+        for i in range(len(self.own)):
+            self.weight(i).wait()
+
+        def line(t, carry):
+            for kind in range(3):
+                self.x_copy(kind, t).wait_send()
+
+            @pl.when(t != p.t)
+            def _():
+                for kind in range(3):
+                    self.local(kind, t).wait()
+
+            for f in range(p.spread):
+                s = t * p.spread + f
+
+                @pl.when(s != p.d)
+                def _(s=s):
+                    for kind in (0, 1):
+                        self.y_came(kind, s).wait_send()
+                        for y in (0, 1):
+                            self.c_came(kind, s, y).wait_send()
+                            self.c_came(kind, s, y).wait_recv()
+
+            return carry
+
+        lax.fori_loop(0, LINE, line, 0)
+
+
+def dense_gather_kernel(spread, *refs):
+    p = Place(spread)
+    shards0, shards1, (routes,), whole, quarters1, (routes_all,), quarters0, rest = split(refs, 3, 3, 1, 3, 3, 1, 3)
+    sems0, sems1, (r_send, r_recv), spread_sems = split(rest, 2, 2, 2)
+    line0 = LineGather(p, shards0, quarters0, sems0)
+    line1 = LineGather(p, shards1, quarters1, sems1)
+    spreading = Spread(p, tuple(quarters0) + tuple(shards0), whole, spread_sems)
+    greet(p.mates[1:] + [p.beside], p)
+
+    def route_copy(i, row):
+        return remote(routes, routes_all.at[row], r_send.at[i], r_recv.at[row], p.mates[i])
+
+    routes_all[p.e] = routes[...]
+    line0.begin()
+    for i in (1, 2, 3):
+        route_copy(i, p.e).start()
+    spreading.own_shard()
+    spreading.from_line(p.t)
+    line1.begin()
+
+    def step(k, carry):
+        line0.step(k, spreading.from_line)
+        line1.step(k, lambda t: None)
+        return carry
+
+    lax.fori_loop(1, LINE, step, 0)
+    spreading.after_line()
+    spreading.after_relay()
+    spreading.finish()
+    line0.finish()
+    line1.finish()
+    for i in (1, 2, 3):
+        route_copy(i, p.e).wait_send()
+        route_copy(i, p.mates[i][1]).wait_recv()
+
+
+def dense_gather(spread, call_id, shards0, shards1, routes):
+    count = spread * LINE
+    quarters = LineGather.shapes(shards0)
+    outs = [struct((count * s.shape[0], s.shape[1]), s.dtype) for s in shards0]
+    outs += [struct(q, BF16) for q in quarters] + [struct((4,) + routes.shape, routes.dtype)]
+    scratch = [pltpu.VMEM(q, BF16) for q in quarters] + LineGather.scratch() * 2 + [dma(4), dma(4)]
+    return pl.pallas_call(
+        functools.partial(dense_gather_kernel, spread),
+        out_shape=outs,
+        in_specs=[VMEM] * 7,
+        out_specs=[ANY] * 3 + [VMEM] * 4,
+        scratch_shapes=scratch + Spread.scratch(count),
+        compiler_params=remote_params(call_id),
+    )(*shards0, *shards1, routes)
+
+
+class Halve:
+    def __init__(self, place, grads, quarter, scratch):
+        self.p, self.grads, self.quarter = place, grads, quarter
+        (self.mine, self.core, self.stage, self.came, self.l_sem, self.a_send, self.a_recv, self.y_send,
+         self.y_recv) = scratch
+        self.depths = [g.shape[0] // (LINE * place.spread) for g in grads]
+        self.wide = grads[0].shape[1] // 2
+        self.partners = []
+
+    @staticmethod
+    def scratch(spread, depths, width):
+        count, rows, wide = LINE * spread, sum(depths) // 2, width // 2
+        half = pltpu.VMEM((LINE, spread, rows, wide), BF16)
+        everything = pltpu.VMEM((count * sum(depths), wide), BF16)
+        return [everything, everything, half, half, dma(2), dma(2), dma(2), dma(LINE), dma(LINE)]
+
+    def rows_of(self, kind):
+        first = 0 if kind == 0 else self.grads[0].shape[0]
+        return slice(first, first + self.grads[kind].shape[0])
+
+    def lanes(self, c):
+        return pl.ds(pl.multiple_of(c * self.wide, 128), self.wide)
+
+    def local(self, kind):
+        return pltpu.make_async_copy(
+            self.grads[kind].at[:, self.lanes(self.p.c)], self.mine.at[self.rows_of(kind)], self.l_sem.at[kind])
+
+    def a_copy(self, kind):
+        return remote(self.grads[kind].at[:, self.lanes(1 - self.p.c)], self.core.at[self.rows_of(kind)],
+                      self.a_send.at[kind], self.a_recv.at[kind], self.p.sibling)
+
+    def y_copy(self, t):
+        return remote(self.stage.at[t], self.came.at[t], self.y_send.at[t], self.y_recv.at[t], self.p.across)
+
+    def pieces(self, t, f, y):
+        s, row = t * self.p.spread + f, 0
+        for kind, depth in enumerate(self.depths):
+            at = self.rows_of(kind).start + s * depth + y * (depth // 2)
+            here = pl.ds(pl.multiple_of(at, 16), depth // 2)
+            yield slice(row, row + depth // 2), self.mine[here, :].astype(F32) + self.core[here, :].astype(F32)
+            row += depth // 2
+
+    def order(self, i):
+        return jnp.where(self.p.t >= LINE // 2, i, LINE - 1 - i)
+
+    def begin(self):
+        for kind in (0, 1):
+            self.a_copy(kind).start()
+            self.local(kind).start()
+
+    def after_first(self):
+        for kind in (0, 1):
+            self.a_copy(kind).wait_recv()
+            self.local(kind).wait()
+
+        def body(i, carry):
+            t = self.order(i)
+            for f in range(self.p.spread):
+                for where, value in self.pieces(t, f, 1 - self.p.y):
+                    self.stage[t, f, where] = value.astype(BF16)
+            self.y_copy(t).start()
+            return carry
+
+        lax.fori_loop(0, LINE, body, 0)
+
+        def own(t, carry):
+            for f in range(self.p.spread):
+                for where, value in self.pieces(t, f, self.p.y):
+                    self.quarter[t, f, where] = value
+            return carry
+
+        lax.fori_loop(0, LINE, own, 0)
+
+    def add(self, t):
+        self.y_copy(t).wait_recv()
+        self.quarter[t] = self.quarter[t] + self.came[t].astype(F32)
+
+    def after_line(self):
+        pass
+
+    def after_relay(self):
+        lax.fori_loop(0, LINE, lambda i, carry: (self.add(self.order(i)), carry)[1], 0)
+
+    def finish(self):
+        for kind in (0, 1):
+            self.a_copy(kind).wait_send()
+        lax.fori_loop(0, LINE, lambda t, carry: (self.y_copy(t).wait_send(), carry)[1], 0)
+
+
+class LineSum:
+    def __init__(self, place, depths, quarter, sums, scratch):
+        self.p, self.depths, self.quarter, self.sums = place, depths, quarter, sums
+        (self.stage, self.came, self.stage_x, self.came_x, self.z_send, self.z_recv, self.x_send, self.x_recv,
+         self.e_send, self.e_recv) = scratch
+        self.wide = sums[0].shape[1] // 2
+
+    @staticmethod
+    def scratch(spread, depths, width):
+        rows, wide = sum(depths) // 2, width // 2
+        return [
+            pltpu.VMEM((LINE, spread, rows, wide), BF16),
+            pltpu.VMEM((2, LINE, spread, rows, wide), BF16),
+            pltpu.VMEM((rows, wide), BF16),
+            pltpu.VMEM((rows, wide), BF16),
+            dma(LINE), dma(2, LINE), dma(1), dma(1), dma(3, 2), dma(3, 2),
+        ]
+
+    def lanes(self, c):
+        return pl.ds(pl.multiple_of(c * self.wide, 128), self.wide)
+
+    def z_copy(self, up, t):
+        return remote(self.stage.at[t], self.came.at[up, t], self.z_send.at[t], self.z_recv.at[up, t], self.p.on_line(up))
+
+    def x_copy(self):
+        return remote(self.stage_x, self.came_x, self.x_send.at[0], self.x_recv.at[0], self.p.beside)
+
+    def e_copy(self, i, kind, y, c):
+        half = self.depths[kind] // 2
+        at = self.sums[kind].at[pl.ds(pl.multiple_of(y * half, 8), half), self.lanes(c)]
+        return remote(at, at, self.e_send.at[i, kind], self.e_recv.at[i, kind], self.p.across if i == 0 else self.p.sibling)
+
+    def start(self, t):
+        p = self.p
+        for up, mine in ((1, jnp.logical_and(p.t == 0, t > 0)), (0, jnp.logical_and(p.t == LINE - 1, t < LINE - 1))):
+
+            @pl.when(mine)
+            def _(up=up):
+                self.stage[t] = self.quarter[t].astype(BF16)
+                self.z_copy(up, t).start()
+
+    def relay(self, stage):
+        p = self.p
+        for up, mine in ((1, p.t == stage), (0, p.t == LINE - 1 - stage)):
+
+            @pl.when(mine)
+            def _(up=up):
+                def one(n, carry):
+                    t = LINE - 1 - n if up else n
+                    self.z_copy(up, t).wait_recv()
+                    self.stage[t] = (self.quarter[t] + self.came[up, t].astype(F32)).astype(BF16)
+                    self.z_copy(up, t).start()
+                    return carry
+
+                lax.fori_loop(0, LINE - 1 - stage, one, 0)
+
+    def after_z(self):
+        p = self.p
+
+        for up, there in ((1, p.below), (0, p.above)):
+
+            @pl.when(there)
+            def _(up=up):
+                self.z_copy(up, p.t).wait_recv()
+                self.quarter[p.t] = self.quarter[p.t] + self.came[up, p.t].astype(F32)
+
+        self.stage_x[...] = self.quarter[p.t, 1 - p.f].astype(BF16)
+        self.x_copy().start()
+
+    def after_x(self):
+        p = self.p
+        self.x_copy().wait_recv()
+        row = 0
+        for kind, depth in enumerate(self.depths):
+            half = depth // 2
+            value = self.quarter[p.t, p.f, row : row + half] + self.came_x[row : row + half].astype(F32)
+            self.sums[kind][pl.ds(pl.multiple_of(p.y * half, 8), half), self.lanes(p.c)] = value
+            row += half
+        for i in (0, 1):
+            for kind in (0, 1):
+                self.e_copy(i, kind, p.y, p.c).start()
+
+    def finish(self):
+        p = self.p
+        for kind in (0, 1):
+            self.e_copy(0, kind, 1 - p.y, p.c).wait_recv()
+            self.e_copy(2, kind, 1 - p.y, p.c).start()
+        for kind in (0, 1):
+            self.e_copy(0, kind, p.y, p.c).wait_send()
+            self.e_copy(1, kind, p.y, p.c).wait_send()
+            self.e_copy(1, kind, p.y, 1 - p.c).wait_recv()
+            self.e_copy(2, kind, 1 - p.y, p.c).wait_send()
+            self.e_copy(2, kind, 1 - p.y, 1 - p.c).wait_recv()
+        self.x_copy().wait_send()
+
+        def body(t, carry):
+            @pl.when(t != p.t)
+            def _():
+                self.z_copy(0, t).wait_send()
+
+            return carry
+
+        lax.fori_loop(0, LINE, body, 0)
+
+
+class SmallSum:
+    def __init__(self, place, grads, total, scratch):
+        self.p, self.grads, self.total = place, grads, total
+        self.stage, self.came, self.send, self.recv = scratch
+        p = place
+        near = (p.d + p.spread - 2 * p.spread * lax.rem(p.t, 2), p.e)
+        self.far = (lax.rem(p.d + 2 * p.spread, LINE * p.spread), p.e)
+        self.partners = [p.sibling, p.across, p.beside, near, self.far]
+
+    @staticmethod
+    def scratch(rows, width):
+        half = pltpu.VMEM((5, rows, width // 2), F32)
+        return [half, half, dma(6), dma(6)]
+
+    def lanes(self, c):
+        wide = self.grads.shape[1] // 2
+        return pl.ds(pl.multiple_of(c * wide, 128), wide)
+
+    def copy(self, i):
+        src = self.grads.at[:, self.lanes(1 - self.p.c)] if i == 0 else self.stage.at[i]
+        return remote(src, self.came.at[i], self.send.at[i], self.recv.at[i], self.partners[i])
+
+    def last(self, c):
+        at = self.total.at[:, self.lanes(c)]
+        return remote(at, at, self.send.at[5], self.recv.at[5], self.p.sibling)
+
+    def step(self, i):
+        if i == 0:
+            self.copy(0).start()
+            return
+        self.copy(i - 1).wait_recv()
+        mine = self.grads[:, self.lanes(self.p.c)] if i == 1 else self.stage[i - 1]
+        value = mine + self.came[i - 1]
+        if i < 5:
+            self.stage[i] = value
+            self.copy(i).start()
+        else:
+            self.total[:, self.lanes(self.p.c)] = value
+            self.last(self.p.c).start()
+
+    def finish(self):
+        for i in range(5):
+            self.copy(i).wait_send()
+        self.last(self.p.c).wait_send()
+        self.last(1 - self.p.c).wait_recv()
+
+
+def dense_reduce_kernel(spread, depths, small, qkv0, out0, quarter1, small_sum, *refs):
+    p = Place(spread)
+    sums0, sums1, (mine0, mine1), halve_refs, line0, line1, small_refs = split(refs, 2, 2, 2, 9, 10, 10)
+    halve = Halve(p, (qkv0, out0), mine0, halve_refs)
+    sum0 = LineSum(p, depths, mine0, sums0, line0)
+    sum1 = LineSum(p, depths, mine1, sums1, line1)
+    little = SmallSum(p, small, small_sum, small_refs)
+    greet([p.sibling, p.across, p.beside, little.far], p)
+    halve.begin()
+    little.step(0)
+    mine1[...] = quarter1[...]
+    for t in range(LINE):
+        sum1.start(t)
+    little.step(1)
+    halve.after_first()
+    little.step(2)
+    for stage in range(1, LINE - 1):
+        sum1.relay(stage)
+    little.step(3)
+    sum1.after_z()
+
+    def arrive(i, carry):
+        t = halve.order(i)
+        halve.add(t)
+        sum0.start(t)
+        return carry
+
+    lax.fori_loop(0, LINE, arrive, 0)
+    little.step(4)
+    sum1.after_x()
+    for stage in range(1, LINE - 1):
+        sum0.relay(stage)
+    little.step(5)
+    sum0.after_z()
+    sum1.finish()
+    sum0.after_x()
+    halve.finish()
+    little.finish()
+    sum0.finish()
+
+
+def dense_reduce(spread, call_id, small, grads0, quarter1):
+    count = LINE * spread
+    depths = [g.shape[0] // count for g in grads0]
+    width = grads0[0].shape[1]
+    shards = [struct((depth, width), F32) for depth in depths]
+    line = LineSum.scratch(spread, depths, width)
+    mine = pltpu.VMEM(quarter1.shape, F32)
+    return pl.pallas_call(
+        functools.partial(dense_reduce_kernel, spread, depths),
+        out_shape=[struct(small.shape, F32)] + shards + shards,
+        in_specs=[VMEM, ANY, ANY, VMEM],
+        out_specs=[VMEM] * 5,
+        scratch_shapes=[mine, mine] + Halve.scratch(spread, depths, width) + line + line + SmallSum.scratch(*small.shape),
+        compiler_params=remote_params(call_id),
+    )(small, *grads0, quarter1)
 
 
 def per_device(
@@ -716,19 +1406,11 @@
     place = lax.axis_index("expert")
 
     my_place = jnp.sum(jnp.where(jnp.arange(owners) == place, block_perm[0], 0))
-    all_routes = lax.all_gather(routes, "expert", axis=0)
-    my_routes = lax.dynamic_index_in_dim(all_routes, my_place, 0, keepdims=False)
     lengths = lax.dynamic_index_in_dim(seq_lengths[0], place, 0, keepdims=False)
     order = jnp.arange(lengths.shape[0])
     ends = jnp.sum(jnp.where(order[:, None] <= order[None, :], lengths[:, None], 0), axis=0)
     doc = jnp.sum((jnp.arange(rows)[:, None] >= ends[None, :]).astype(jnp.int32), axis=1)
     doc_col, doc_row = doc[:, None], doc[None, :]
-
-    weights = []
-    for l in range(layers):
-        weights.append(
-            pair_weights(w_gate[l], 2, spread) + pair_weights(w_up[l], 2, spread) + pair_weights(w_down[l], 1, spread)
-        )
 
     depth = w_out.shape[1]
     small = jnp.concatenate(
@@ -739,10 +1421,28 @@
         axis=2,
     ).astype(BF16)
     qkv_t = jnp.swapaxes(w_qkv, 1, 2).astype(BF16)
-    qkv_all = lax.all_gather(qkv_t, "dp", axis=1, tiled=True)
-    out_all = lax.all_gather(w_out.astype(BF16), "dp", axis=1, tiled=True)
-    small_all = lax.all_gather(small, "dp", axis=1, tiled=True)
-    dense = [(small_all[l], qkv_all[l], out_all[l]) for l in range(layers)]
+    out_rows = w_out.astype(BF16)
+    in_kernels = spread == 2 and owners == 4 and qkv_t.shape[1] % 32 == 0 and depth % 32 == 0
+    if in_kernels:
+        packed_routes = jnp.zeros((8, 256), jnp.int32).at[: 2 * layers, :rows].set(
+            jnp.swapaxes(routes, 1, 2).reshape(2 * layers, rows))
+        shards = [(qkv_t[l], out_rows[l], small[l]) for l in range(layers)]
+        *gathered, routes_all = dense_gather(spread, 4, *shards, packed_routes)
+        dense = [(gathered[2], gathered[0], gathered[1])]
+        picked = lax.dynamic_index_in_dim(routes_all, my_place, 0, keepdims=False)
+        my_routes = jnp.swapaxes(picked[: 2 * layers, :rows].reshape(layers, 2, rows), 1, 2)
+    else:
+        all_routes = lax.all_gather(routes, "expert", axis=0)
+        my_routes = lax.dynamic_index_in_dim(all_routes, my_place, 0, keepdims=False)
+        qkv_all = lax.all_gather(qkv_t, "dp", axis=1, tiled=True)
+        out_all = lax.all_gather(out_rows, "dp", axis=1, tiled=True)
+        small_all = lax.all_gather(small, "dp", axis=1, tiled=True)
+        dense = [(small_all[l], qkv_all[l], out_all[l]) for l in range(layers)]
+
+    own = [[w[l].astype(BF16) for w in (w_gate, w_up, w_down)] for l in range(layers)]
+    weights = []
+    for l in range(1 if in_kernels else layers):
+        weights.append([part for w, axis in zip(own[l], (2, 2, 1)) for part in pair_weights(w, axis, spread)])
     w_res = jnp.zeros((128, 128), F32).at[: w_residual.shape[0], : w_residual.shape[1]].set(w_residual)
 
     cols = ((rows, width), F32)
@@ -755,7 +1455,12 @@
     attn_in0, qkv0, probs0, attn0, mid0, logits0, stat0, out = local_call(
         first_kernel, experts, (tokens, *dense[0], doc_col, doc_row, my_routes[0]),
         attention + [cols, per_token, per_token, sent])
-    ret0, *kept0 = expert_forward(spread, 0, group(out), weights[0])
+    ride = (*gathered[3:], *shards[1], *own[1]) if in_kernels else None
+    ret0, *kept0 = expert_forward(spread, 0, group(out), weights[0], ride)
+    if in_kernels:
+        kept0, (qkv_all, out_all, small_all), partner = kept0[:3], kept0[3:6], kept0[6:]
+        dense.append((small_all, qkv_all, out_all))
+        weights.append([w for pair in zip(own[1], partner) for w in pair])
     ret0 = ret0.reshape(slots, width)
     stream1, attn_in1, qkv1, probs1, attn1, mid1, stat1, out = local_call(
         middle_kernel, experts,
@@ -769,14 +1474,18 @@
         turn_kernel, experts, (mid1, dense[1][0], stat1, ret1, cotangent, logits0, w_res),
         [((rows, width), BF16), per_token, per_token, sent, small_grads, ((128, 128), F32)])
     back, *expert_grads1 = expert_backward(spread, 2, group(out), kept1, weights[1])
-    dense_grads = [((3 * width, width), F32), ((width, width), F32), small_grads]
+    grad_type = BF16 if in_kernels else F32
+    dense_grads = [((3 * width, width), grad_type), ((width, width), grad_type), small_grads]
     attention_scratch = [((rows, 3 * width), BF16), ((rows, width), BF16)]
     qkv_grad1, out_grad1, small_grad1, grad, g_small0, out, small_grad0 = local_call(
         between_kernel, experts,
         (cotangent, back.reshape(slots, width), g_small1, stat1, mid1, dense[1][0], stream1, dense[1][1], dense[1][2],
          attn_in1, qkv1, probs1, attn1, small_grad1, mid0, dense[0][0], stat0, ret0, extra),
         dense_grads + [cols, per_token, sent, small_grads], attention_scratch)
-    back, *expert_grads0 = expert_backward(spread, 3, group(out), kept0, weights[0])
+    ride = (qkv_grad1, out_grad1) if in_kernels else None
+    back, *expert_grads0 = expert_backward(spread, 3, group(out), kept0, weights[0], ride)
+    if in_kernels:
+        *expert_grads0, quarter1 = expert_grads0
     qkv_grad0, out_grad0, small_grad0, tokens_grad = local_call(
         last_kernel, experts,
         (grad, back.reshape(slots, width), g_small0, stat0, mid0, dense[0][0], tokens, dense[0][1], dense[0][2],
@@ -791,12 +1500,17 @@
             per_layer.append(pair_sum(grads[at * n : (at + 1) * n], axis, spread))
         expert_out.append(jnp.stack(per_layer))
     gate_grad, up_grad, down_grad = expert_out
-    qkv_grad = lax.psum(
-        lax.psum_scatter(jnp.stack([qkv_grad0, qkv_grad1]), "dp", scatter_dimension=1, tiled=True), "expert")
-    out_grad = lax.psum(
-        lax.psum_scatter(jnp.stack([out_grad0, out_grad1]), "dp", scatter_dimension=1, tiled=True), "expert")
     packed = jnp.concatenate([small_grad0, small_grad1, jnp.pad(res_grad[:16], ((0, 0), (0, width - 128)))])
-    packed = lax.psum(packed, ("dp", "expert"))
+    if in_kernels:
+        packed, qkv_sum0, out_sum0, qkv_sum1, out_sum1 = dense_reduce(
+            spread, 5, packed, (qkv_grad0, out_grad0), quarter1)
+        qkv_grad = jnp.stack([qkv_sum0, qkv_sum1])
+        out_grad = jnp.stack([out_sum0, out_sum1])
+    else:
+        packed = lax.psum(packed, ("dp", "expert"))
+        qkv_grad, out_grad = (
+            lax.psum(lax.psum_scatter(jnp.stack(pair), "dp", scatter_dimension=1, tiled=True), "expert")
+            for pair in ((qkv_grad0, qkv_grad1), (out_grad0, out_grad1)))
     mine = lax.dynamic_slice_in_dim(packed, lax.axis_index("dp") * depth, depth, axis=1)
     mine = jnp.stack([mine[:24], mine[24:48]])
     router_grad = jnp.swapaxes(mine[:, :CONST0], 1, 2)

time: 1200 us -> 614 us (0.51)
  waiting for transfers between devices: 528 us -> 10.2 us
  blocking collectives: 121 us -> 0 us
  Pallas kernels: 443 us -> 544 us
  other arithmetic: 41.9 us -> 21.3 us
  between operations: 17 us -> 3.47 us
  local copies, waits for them, and re-layouts: 27.5 us -> 14.8 us
    reduce_scatter x2 -> x0, waiting for transfers between devices: 322 us -> none  [the longest x1 232 us: per_device(): lax.psum_scatter(jnp.stack([qkv_grad0, qkv_grad1]), 'dp', scatter_dimensi...]
    psum x2 -> x0, waiting for transfers between devices: 148 us -> none  [the longest x1 101 us: per_device(): packed = lax.psum(packed, ('dp', 'expert'))]
    all_gather x2 -> x0, blocking collectives: 121 us -> none  [the longest x1 116 us: per_device(): small_all = lax.all_gather(small, 'dp', axis=1, tiled=True)]
    pallas_call x4 -> x6, Pallas kernels: 380 us -> 483 us  [the longest x2 160 us: expert_backward(): pl.pallas_call(functools.partial(expert_backward_kernel, spread, parts, r...]
    all_gather x2 -> x0, waiting for transfers between devices: 57.6 us -> none  [the longest x1 57.6 us: per_device(): qkv_all = lax.all_gather(qkv_t, 'dp', axis=1, tiled=True)]
    another operation x8 -> x7, other arithmetic: 17.8 us -> 4.28 us  [the longest x1 11 us: per_device(): jnp.stack([qkv_grad0, qkv_grad1])]
  transfers between devices with their start and end apart: 18 -> 9, of which waited for: 5 -> 1; matrix products, arithmetic and copies ran while one was open for 5% -> 5% of each run, Pallas kernels for 10% -> 32%
where the time goes in v3:
time: 614 us; the launch traced here: 606 us
  Pallas kernels  544 us (89%)
  other arithmetic  21.3 us (3%)
  local copies, waits for them, and re-layouts  14.8 us (2%)
  starting transfers between devices  12.5 us (2%)
  waiting for transfers between devices  10.2 us (2%)
    pallas_call x2, Pallas kernels, expert_backward(): pl.pallas_call(functools.partial(expert_backward_kernel, spread, parts, r...  160 us
    pallas_call x2, Pallas kernels, expert_forward(): pl.pallas_call(functools.partial(expert_forward_kernel, spread, parts, ri...  155 us
    pallas_call x1, Pallas kernels, dense_reduce(): pl.pallas_call(functools.partial(dense_reduce_kernel, spread, depths), ou...  106 us
    pallas_call x1, Pallas kernels, dense_gather(): pl.pallas_call(functools.partial(dense_gather_kernel, spread), out_shape=...  62.6 us
    pallas_call x5, Pallas kernels, local_call(): pl.pallas_call(functools.partial(kernel, experts), out_shape=[jax.ShapeDt...  60.7 us
  transfers between devices with their start and end apart: 9, of which 1 were waited for; matrix products, arithmetic and copies ran while one was open for 5% of the time, Pallas kernels for 32%

profile of v3, /device:TPU:0, one launch (start us, length us, event | category | flops | bytes accessed | tf_op | source)
XLA Modules:
  0.0 606.3 jit_solution(7921062623156641668)
XLA Ops:
  0.7 2.0 convert.37
  2.7 1.0 slice_bitcast_fusion.2
  3.7 2.9 collective-permute-start
  6.7 0.2 convert.38
  6.8 1.0 slice_bitcast_fusion.1
  7.8 1.5 collective-permute-start.1
  9.3 0.2 convert.39
  9.5 1.0 slice_bitcast_fusion
  10.5 1.5 collective-permute-start.2
  12.0 0.1 copy.40
  12.2 0.1 copy.43
  12.3 0.1 copy.41
  12.5 0.1 copy.42
  12.6 0.2 concatenate.11
  12.8 0.6 slice_bitcast_fusion.14
  13.4 1.6 convert_bitcast_fusion
  15.1 1.0 slice_bitcast_fusion.6
  16.1 0.7 slice_bitcast_fusion.8
  16.8 0.6 fusion.4
  18.8 0.6 scatter.6.refs_6_
  20.1 62.6 %shard_map.238 = (bf16[2304,768]{1,0:T(8,128)(2,1)}, bf16[768,768]{1,0:T(8,128)(2,1)}, bf16[768,128]{1,0:T(8,128)(2,1)}, bf16[4,144,384]{2,1,0:T(8,128)(2,1)}, b...) custom-call(bf16[288,768]{1,0:T(8,128)(2,1)} %get-tuple-element.227.refs_0_, ...), custom_call_target="tpu_custom_call" | custom-call | tf_op jit(solution)/shard_map/pallas_call | solution.py:1085
  82.7 0.7 dynamic-slice_bitcast_fusion.2
  83.4 0.1 copy.44
  83.8 0.8 copy.45.doc_col
  84.5 0.6 scatter.9.w_res
  85.1 0.7 slice_bitcast_fusion.10
  85.9 10.8 %shard_map.239 = (bf16[192,768]{1,0:T(8,128)(2,1)}, bf16[192,2304]{1,0:T(8,128)(2,1)}, f32[12,192,192]{2,1,0:T(8,128)}, bf16[192,768]{1,0:T(8,128)(2,1)}, f32[19...) custom-call(bf16[192,768]{1,0:T(8,128)(2,1)} %tokens.3, ...), custom_call_target="tpu_custom_call" | custom-call | tf_op jit(solution)/shard_map/pallas_call | solution.py:335
  96.7 77.3 %shard_map.240 = (bf16[4,2,48,768]{3,2,1,0:T(8,128)(2,1)}, bf16[2,4,4,48,768]{4,3,2,1,0:T(8,128)(2,1)}, f32[4,2,192,512]{3,2,1,0:T(8,128)}, f32[4,2,192,512]{3,2...) custom-call(bf16[4,2,48,768]{3,2,1,0:T(8,128)(2,1)} %bitcast.88, ...), custom_call_target="tpu_custom_call" | custom-call | tf_op jit(solution)/shard_map/pallas_call | solution.py:767
  174.0 11.5 %shard_map.241 = (f32[192,768]{1,0:T(8,128)}, bf16[192,768]{1,0:T(8,128)(2,1)}, bf16[192,2304]{1,0:T(8,128)(2,1)}, f32[12,192,192]{2,1,0:T(8,128)}, bf16[192,768...) custom-call(f32[192,768]{1,0:T(8,128)} %get-tuple-element.114.mid_in.mid0.mid, ...), custom_call_target="tpu_custom_call" | custom-call | tf_op jit(solution)/shard_map/pallas_call | solution.py:335
  185.6 77.5 %shard_map.242 = (bf16[4,2,48,768]{3,2,1,0:T(8,128)(2,1)}, bf16[2,4,4,48,768]{4,3,2,1,0:T(8,128)(2,1)}, f32[4,2,192,512]{3,2,1,0:T(8,128)}, f32[4,2,192,512]{3,2,1,0:T(8,128)}) custom-call(bf16[4,2,48,768]{3,2,1,0:T(8,128)(2,1)} %bitcast.89, bf16[2,768,256]{2,1,0:T(8,128)(2,1)} %get-tuple-element.224.refs_12_.refs_0_.refs_3_, ...), custom_call_target="tpu_custom_call" | custom-call | tf_op jit(solution)/shard_map/pallas_call | solution.py:767
  263.1 5.6 shard_map.243
  268.6 78.9 %shard_map.244 = (bf16[4,2,48,768]{3,2,1,0:T(8,128)(2,1)}, f32[2,768,256]{2,1,0:T(8,128)}, bf16[2,768,256]{2,1,0:T(8,128)(2,1)}, f32[2,768,256]{2,1,0:T(8,128)},...) custom-call(bf16[4,2,48,768]{3,2,1,0:T(8,128)(2,1)} %bitcast.92, ...), custom_call_target="tpu_custom_call" | custom-call | tf_op jit(solution)/shard_map/pallas_call | solution.py:793
  347.5 17.6 %shard_map.245 = (bf16[2304,768]{1,0:T(8,128)(2,1)}, bf16[768,768]{1,0:T(8,128)(2,1)}, f32[24,768]{1,0:T(8,128)}, f32[192,768]{1,0:T(8,128)}, f32[192,128]{1,0:T...) custom-call(bf16[192,768]{1,0:T(8,128)(2,1)} %cotangent.3, bf16[384,768]{1,0:T(8,128)(2,1)} %bitcast.91, ...), custom_call_target="tpu_custom_call" | custom-call | tf_op jit(solution)/shard_map/pallas_call | solution.py:335
  365.1 80.9 %shard_map.246 = (bf16[4,2,48,768]{3,2,1,0:T(8,128)(2,1)}, f32[2,768,256]{2,1,0:T(8,128)}, bf16[2,768,256]{2,1,0:T(8,128)(2,1)}, f32[2,768,256]{2,1,0:T(8,128)},...) custom-call(bf16[4,2,48,768]{3,2,1,0:T(8,128)(2,1)} %bitcast.87, ...), custom_call_target="tpu_custom_call" | custom-call | tf_op jit(solution)/shard_map/pallas_call | solution.py:793
  446.0 1.7 collective-permute-start.7
  447.7 0.4 collective-permute-start.8
  448.1 1.6 collective-permute-start.5
  449.8 0.4 collective-permute-start.6
  450.2 1.6 collective-permute-start.3
  451.8 0.7 slice.140
  452.5 15.2 %shard_map.247 = (bf16[2304,768]{1,0:T(8,128)(2,1)}, bf16[768,768]{1,0:T(8,128)(2,1)}, f32[24,768]{1,0:T(8,128)}, f32[192,768]{1,0:T(8,128)}) custom-call(f32[192,768]{1,0:T(8,128)} %get-tuple-element.146.grad_in, bf16[384,768]{1,0:T(8,128)(2,1)} %bitcast.86, f32[192,128]{1,0:T(8,128)} %get-tuple-element.154.g_small, ...), custom_call_target="tpu_custom_call" | custom-call | tf_op jit(solution)/shard_map/pallas_call | solution.py:335
  467.7 1.6 select_maximum_fusion.small
  469.3 106.1 %shard_map.248 = (f32[64,768]{1,0:T(8,128)}, f32[288,768]{1,0:T(8,128)}, f32[96,768]{1,0:T(8,128)}, f32[288,768]{1,0:T(8,128)}, f32[96,768]{1,0:T(8,128)}) custom-call(f32[64,768]{1,0:T(8,128)} %select_maximum_fusion.small, bf16[2304,768]{1,0:T(8,128)(2,1)} %get-tuple-element.164.qkv0, bf16[768,768]{1,0:T(8,128)(2,1)} %get-tuple-element.165.out0, ...), custom_call_target="tpu_custom_call" | custom-call | tf_op jit(solution)/shard_map/pallas_call | solution.py:1384
  575.4 1.4 slice.145
  576.7 0.8 dynamic-slice_bitcast_fusion.1
  577.6 0.6 copy.47
  578.2 0.6 fusion.2
  578.8 0.6 pad_maximum_fusion.4
  579.4 1.9 pad_maximum_fusion.3
  581.3 2.6 maximum_bitcast_fusion
  583.9 1.0 collective-permute-start.4
  584.9 1.4 add_bitcast_fusion.1
  586.3 0.2 copy-done.9
  586.5 1.3 add_bitcast_fusion
  587.8 1.9 pad_maximum_fusion.2
  589.8 0.2 add_bitcast_fusion.3
  590.0 1.2 copy-done.8
  591.2 0.2 add_bitcast_fusion.2
  591.4 1.9 pad_maximum_fusion.1
  593.2 0.1 copy-done.10
  593.3 0.2 add_bitcast_fusion.5
  593.6 10.2 %collective-permute-done.4 = bf16[2,768,256]{2,1,0:T(8,128)(2,1)S(1)} collective-permute-done((bf16[2,768,256]{2,1,0:T(8,128)(2,1)S(1)}, bf16[2,768,256]{2,1,0:T(8,128)(2,1)S(1)}, u32[]{:S(2)}, u32[]{:S(2)}) %collective-permute-start.4) | collective-permute-done | bytes 786464 | tf_op jit(solution)/shard_map/ppermute | solution.py:814
  603.7 0.2 add_bitcast_fusion.4
  603.9 1.9 pad_maximum_fusion
  (68 shorter events, 0.4 us)
Async XLA Ops:
  0.6 82.9 %copy-start = (s32[1,4,4]{2,1,0:T(4,128)S(1)}, s32[1,4,4]{2,1,0:T(4,128)}, u32[]{:S(2)}) copy-start(s32[1,4,4]{2,1,0:T(4,128)} %param.20) | copy-start | bytes 196
  2.7 3.9 copy-start.5
  3.7 3.1 copy-start.2
  3.7 92.9 %collective-permute-start = (bf16[2,768,256]{2,1,0:T(8,128)(2,1)S(1)}, bf16[2,768,256]{2,1,0:T(8,128)(2,1)}, u32[]{:S(2)}, u32[]{:S(2)}) collective-permute-start(bf16[2,768,256]{2,1,0:T(8,128)(2,1)S(1)} %get-tuple-element.225.refs_0_.refs_3_), channel_id=1, source_target_pairs={{4,0},{0,4},{12,8},{8,12},{20,16},{16,20},{28,24},{24,28},{5,1},{1... | collective-permute-start | bytes 2359304 | tf_op jit(solution)/shard_map/ppermute | solution.py:807
  6.8 2.5 copy-start.6
  7.8 1.6 copy-start.3
  7.8 88.8 %collective-permute-start.1 = (bf16[2,768,256]{2,1,0:T(8,128)(2,1)S(1)}, bf16[2,768,256]{2,1,0:T(8,128)(2,1)}, u32[]{:S(2)}, u32[]{:S(2)}) collective-permute-start(bf16[2,768,256]{2,1,0:T(8,128)(2,1)S(1)} %get-tuple-element.223.refs_2_.refs_5_), channel_id=1, source_target_pairs={{4,0},{0,4},{12,8},{8,12},{20,16},{16,20},{28,24},{24,28},{5,1},{1... | collective-permute-start | bytes 2359304 | tf_op jit(solution)/shard_map/ppermute | solution.py:807
  9.5 2.5 copy-start.19
  9.5 2.7 copy-start.16
  9.5 2.9 copy-start.21
  9.5 3.0 copy-start.22
  10.5 4.5 copy-start.4
  10.5 86.1 %collective-permute-start.2 = (bf16[2,256,768]{2,1,0:T(8,128)(2,1)S(1)}, bf16[2,256,768]{2,1,0:T(8,128)(2,1)}, u32[]{:S(2)}, u32[]{:S(2)}) collective-permute-start(bf16[2,256,768]{2,1,0:T(8,128)(2,1)S(1)} %get-tuple-element.221.refs_4_.refs_7_), channel_id=1, source_target_pairs={{4,0},{0,4},{12,8},{8,12},{20,16},{16,20},{28,24},{24,28},{5,1},{1... | collective-permute-start | bytes 2359304 | tf_op jit(solution)/shard_map/ppermute | solution.py:807
  13.4 2.6 copy-start.14
  15.1 1.8 copy-start.24
  15.1 3.7 copy-start.20
  16.1 68.5 %copy-start.18 = (f32[12,12]{1,0:T(8,128)S(1)}, f32[12,12]{1,0:T(8,128)}, u32[]{:S(2)}) copy-start(f32[12,12]{1,0:T(8,128)} %param.27) | copy-start | bytes 1732
  83.7 2.1 copy-start.17
  446.0 137.9 %collective-permute-start.7 = (bf16[2,256,768]{2,1,0:T(8,128)(2,1)}, bf16[2,256,768]{2,1,0:T(8,128)(2,1)}, u32[]{:S(2)}, u32[]{:S(2)}) collective-permute-start(bf16[2,256,768]{2,1,0:T(8,128)(2,1)} %get-tuple-element.181), channel_id=1, source_target_pairs={{0,4},{4,0},{8,12},{12,8},{16,20},{20,16},{24,28},{28,24},{1,5},{5... | collective-permute-start | bytes 2359304 | tf_op jit(solution)/shard_map/ppermute | solution.py:814
  447.7 138.5 %collective-permute-start.8 = (bf16[2,256,768]{2,1,0:T(8,128)(2,1)}, bf16[2,256,768]{2,1,0:T(8,128)(2,1)}, u32[]{:S(2)}, u32[]{:S(2)}) collective-permute-start(bf16[2,256,768]{2,1,0:T(8,128)(2,1)} %get-tuple-element.183), channel_id=1, source_target_pairs={{0,4},{4,0},{8,12},{12,8},{16,20},{20,16},{24,28},{28,24},{1,5},{5... | collective-permute-start | bytes 2359304 | tf_op jit(solution)/shard_map/ppermute | solution.py:814
  448.1 141.6 %collective-permute-start.5 = (bf16[2,768,256]{2,1,0:T(8,128)(2,1)}, bf16[2,768,256]{2,1,0:T(8,128)(2,1)S(1)}, u32[]{:S(2)}, u32[]{:S(2)}) collective-permute-start(bf16[2,768,256]{2,1,0:T(8,128)(2,1)} %get-tuple-element.177), channel_id=1, source_target_pairs={{0,4},{4,0},{8,12},{12,8},{16,20},{20,16},{24,28},{28,24},{1,5},{5... | collective-permute-start | bytes 2359304 | tf_op jit(solution)/shard_map/ppermute | solution.py:814
  449.8 140.2 %collective-permute-start.6 = (bf16[2,768,256]{2,1,0:T(8,128)(2,1)}, bf16[2,768,256]{2,1,0:T(8,128)(2,1)S(1)}, u32[]{:S(2)}, u32[]{:S(2)}) collective-permute-start(bf16[2,768,256]{2,1,0:T(8,128)(2,1)} %get-tuple-element.179), channel_id=1, source_target_pairs={{0,4},{4,0},{8,12},{12,8},{16,20},{20,16},{24,28},{28,24},{1,5},{5... | collective-permute-start | bytes 2359304 | tf_op jit(solution)/shard_map/ppermute | solution.py:814
  450.2 143.1 %collective-permute-start.3 = (bf16[2,768,256]{2,1,0:T(8,128)(2,1)}, bf16[2,768,256]{2,1,0:T(8,128)(2,1)S(1)}, u32[]{:S(2)}, u32[]{:S(2)}) collective-permute-start(bf16[2,768,256]{2,1,0:T(8,128)(2,1)} %get-tuple-element.173), channel_id=1, source_target_pairs={{0,4},{4,0},{8,12},{12,8},{16,20},{20,16},{24,28},{28,24},{1,5},{5... | collective-permute-start | bytes 2359304 | tf_op jit(solution)/shard_map/ppermute | solution.py:814
  452.5 15.2 %copy-start.15 = (f32[24,768]{1,0:T(8,128)S(1)}, f32[24,768]{1,0:T(8,128)}, u32[]{:S(2)}) copy-start(f32[24,768]{1,0:T(8,128)} %get-tuple-element.162) | copy-start | bytes 221188
  575.3 5.9 copy-start.13
  581.3 2.6 copy-start.23
  581.3 3.6 copy-start.12
  583.9 19.8 %collective-permute-start.4 = (bf16[2,768,256]{2,1,0:T(8,128)(2,1)S(1)}, bf16[2,768,256]{2,1,0:T(8,128)(2,1)S(1)}, u32[]{:S(2)}, u32[]{:S(2)}) collective-permute-start(bf16[2,768,256]{2,1,0:T(8,128)(2,1)S(1)} %copy-done.23), channel_id=1, source_target_pairs={{0,4},{4,0},{8,12},{12,8},{16,20},{20,16},{24,28},{28,24},{1,5},{5... | collective-permute-start | bytes 2359304 | tf_op jit(solution)/shard_map/ppermute | solution.py:814
  584.9 1.6 copy-start.9
  587.8 1.9 copy-start.11
  589.7 1.4 copy-start.8
  591.3 2.0 copy-start.10
  593.3 10.4 %copy-start.7 = (f32[2,768,256]{2,1,0:T(8,128)S(1)}, f32[2,768,256]{2,1,0:T(8,128)}, u32[]{:S(2)}) copy-start(f32[2,768,256]{2,1,0:T(8,128)} %get-tuple-element.174) | copy-start | bytes 4718596
  603.9 1.9 copy-start.1

commit v4 on v3

--- a/solution.py
+++ b/solution.py
@@ -339,6 +339,7 @@
         out_specs=[VMEM] * len(outs),
         scratch_shapes=[pltpu.VMEM(shape, dtype) for shape, dtype in scratch],
         compiler_params=pltpu.CompilerParams(vmem_limit_bytes=60 * 2**20),
+        cost_estimate=pl.CostEstimate(flops=10**10, bytes_accessed=6 * 10**7, transcendentals=0),
     )(*args)
 
 
@@ -356,7 +357,7 @@
         self.mates = [(self.d, self.e), self.sibling, self.across, self.corner]
 
     def on_line(self, up):
-        return (self.d + self.spread if up else self.d - self.spread, self.e)
+        return (self.d + self.spread * (2 * up - 1), self.e)
 
 
 def greet(always, place):
@@ -402,6 +403,9 @@
     partners = ()
 
     def begin(self):
+        pass
+
+    def ready(self):
         pass
 
     def after_first(self):
@@ -457,20 +461,26 @@
         self.stage[s, :, b] = total.astype(BF16)
         self.sum_copy(up, s, b).start()
 
-    def relay(self, stage):
+    def relays(self):
         p = self.p
-        for up, mine in ((1, p.t == stage), (0, p.t == LINE - 1 - stage)):
-
-            @pl.when(mine)
-            def _(up=up):
-                def one(n, carry):
-                    s = p.t + 1 + n if up else p.t - 1 - n
-                    for _, b in p.mates:
-                        self.sum_copy(up, s, b).wait_recv()
-                        self.send_sum(up, s, b, self.part[s, :, b] + self.arrived[up, s, :, b].astype(F32))
-                    return carry
-
-                lax.fori_loop(0, LINE - 1 - stage, one, 0)
+
+        @pl.when(jnp.logical_and(p.above, p.below))
+        def _():
+            up = jnp.where(p.t == 1, 1, 0)
+            ahead = 2 * up - 1
+
+            def on(kind, i):
+                b = p.mates[i][1]
+                s = {"near": p.t + ahead, "far": p.t + 2 * ahead, "back": p.t - ahead}[kind]
+                way = 1 - up if kind == "back" else up
+                self.sum_copy(way, s, b).wait_recv()
+                self.send_sum(way, s, b, self.part[s, :, b] + self.arrived[way, s, :, b].astype(F32))
+
+            for kind, i in (
+                ("near", 0), ("near", 1), ("far", 0), ("far", 1), ("back", 0), ("far", 2), ("back", 1), ("far", 3),
+                ("back", 2), ("near", 2), ("back", 3), ("near", 3),
+            ):
+                on(kind, i)
 
     def run(self, out, compute, kept, meanwhile, rider):
         p = self.p
@@ -481,68 +491,73 @@
             self.slot_copy(out, i).start()
         self.x[:, t, e] = out[e]
         rider.begin()
-        for half in (0, 1):
-            for i in (2 * half, 2 * half + 1):
-                if i:
-                    self.x_copy(0, t, blocks[i]).wait_recv()
-                for up, there in ((0, p.below), (1, p.above)):
-
-                    @pl.when(there)
-                    def _(up=up, i=i):
-                        self.x_copy(up, t, blocks[i]).start()
-
-            compute(t, p.y + half - 2 * p.y * half)
+        for i in range(4):
+            if i:
+                self.x_copy(0, t, blocks[i]).wait_recv()
+            for up, there in ((0, p.below), (1, p.above)):
+
+                @pl.when(there)
+                def _(up=up, i=i):
+                    self.x_copy(up, t, blocks[i]).start()
+
+        rider.ready()
+        lax.fori_loop(0, 2, lambda pair, carry: (compute(t, pair), carry)[1], 0)
         kept(t)
         rider.after_first()
 
-        def step(k, carry):
-            def part(half, carry):
-                pair = p.y + half - 2 * p.y * half
-                first = jnp.where(half == 0, blocks[0], blocks[2])
-                second = jnp.where(half == 0, blocks[1], blocks[3])
-                for b in (first, second):
-                    for up, there, onward in ((0, t + k < LINE, p.below), (1, t - k >= 0, p.above)):
-                        s = t - k if up else t + k
-
-                        @pl.when(there)
-                        def _(up=up, onward=onward, s=s, b=b):
-                            self.x_copy(up, s, b).wait_recv()
-
-                            @pl.when(onward)
-                            def _():
-                                self.x_copy(up, s, b).start()
-
-                def side(up, carry):
-                    s = t + k - 2 * k * up
-
-                    @pl.when(jnp.logical_and(s >= 0, s < LINE))
+        def step(n, carry):
+            k = jnp.where(n < 2, 1, jnp.where(jnp.logical_or(n == 2, n == 5), 2, 3))
+            half = jnp.where(jnp.logical_or(n == 1, n >= 4), 1, 0)
+            pair = p.y + half - 2 * p.y * half
+            first = jnp.where(half == 0, blocks[0], blocks[2])
+            second = jnp.where(half == 0, blocks[1], blocks[3])
+            for b in (first, second):
+                for up, there, onward, before_end in ((0, t + k < LINE, p.below, t == 1), (1, t - k >= 0, p.above, t == LINE - 2)):
+                    s = t - k if up else t + k
+                    put_off = jnp.logical_and(before_end, n == 1)
+
+                    @pl.when(there)
+                    def _(up=up, onward=onward, s=s, b=b, put_off=put_off):
+                        self.x_copy(up, s, b).wait_recv()
+
+                        @pl.when(jnp.logical_and(onward, jnp.logical_not(put_off)))
+                        def _():
+                            self.x_copy(up, s, b).start()
+
+            for up, before_end in ((0, t == 1), (1, t == LINE - 2)):
+
+                @pl.when(jnp.logical_and(before_end, n == 5))
+                def _(up=up):
+                    for b in (first, second):
+                        self.x_copy(up, t - 1 if up else t + 1, b).start()
+
+            def side(up, carry):
+                s = t + k - 2 * k * up
+
+                @pl.when(jnp.logical_and(s >= 0, s < LINE))
+                def _():
+                    compute(s, pair)
+
+                    @pl.when(half == 1)
                     def _():
-                        compute(s, pair)
-
-                        @pl.when(half == 1)
-                        def _():
-                            kept(s)
-
-                    return carry
-
-                lax.fori_loop(0, 2, side, 0)
-                for up, starts, s in ((1, t == 0, k), (0, t == LINE - 1, LINE - 1 - k)):
-
-                    @pl.when(starts)
-                    def _(up=up, s=s):
-                        for b in (first, second):
-                            self.send_sum(up, s, b, self.part[s, :, b])
+                        kept(s)
 
                 return carry
 
-            lax.fori_loop(0, 2, part, 0)
+            lax.fori_loop(0, 2, side, 0)
+            for up, starts, s in ((1, t == 0, k), (0, t == LINE - 1, LINE - 1 - k)):
+
+                @pl.when(starts)
+                def _(up=up, s=s):
+                    for b in (first, second):
+                        self.send_sum(up, s, b, self.part[s, :, b])
+
             return carry
 
-        lax.fori_loop(1, LINE, step, 0)
+        lax.fori_loop(0, 6, step, 0)
         rider.after_line()
         meanwhile()
-        for stage in range(1, LINE - 1):
-            self.relay(stage)
+        self.relays()
         rider.after_relay()
         for i, b in enumerate(blocks):
             for up, there in ((1, p.below), (0, p.above)):
@@ -589,9 +604,11 @@
     return out + [refs[at:]]
 
 
-def expert_forward_kernel(spread, parts, ride, out, *refs):
-    weights_in, shards, outs, whole, scratch, line_refs, sems, ride_refs = split(
-        refs, 3 * parts, 9 if ride else 0, 4, 6 if ride else 0, 3 * parts, 5, 7)
+def expert_forward_kernel(spread, parts, late, ride, out, *refs):
+    own = 3 * parts - late
+    weights_in, given, outs, late_out, whole, scratch, line_refs, sems, ride_refs = split(
+        refs, own, 8 if ride else 0, 4, late, 5 if ride else 0, 3 * parts, 5, 7)
+    weights_in = list(weights_in) + list(late_out)
     (g_all, u_all, keep_sem, load_sem), ride_refs = ride_refs[:4], ride_refs[4:]
     returned, x_keep, g_keep, u_keep = outs
     gate, up, down = scratch[:parts], scratch[parts : 2 * parts], scratch[2 * parts :]
@@ -600,12 +617,12 @@
     rows = 2 * CAP
     p = Place(spread)
     line = Line(p, x, part, stage, arrived, final, returned, sems)
-    rider = Spread(p, shards, whole, ride_refs) if ride else Rider()
+    rider = WeightRider(p, weights_in[-2:], given, whole, ride_refs) if late else Rider()
 
     def load(i):
         return pltpu.make_async_copy(weights_in[i], scratch[i], load_sem.at[i])
 
-    for i in range(3 * parts):
+    for i in range(own):
         load(i).start()
 
     def keep_x(s):
@@ -649,6 +666,11 @@
 
         def begin(self):
             rider.begin()
+
+        def ready(self):
+            rider.ready()
+            for i in range(own, 3 * parts):
+                load(i).start()
             for i in range(3 * parts):
                 load(i).wait()
 
@@ -660,8 +682,8 @@
 
 
 def expert_backward_kernel(spread, parts, ride, out, *refs):
-    loads_in, dense, outs, quarter, loads, line_refs, sems, rest = split(
-        refs, 3 + 3 * parts, 2 if ride else 0, 1 + 3 * parts, 1 if ride else 0, 3 + 3 * parts, 5, 7)
+    loads_in, given, outs, ride_outs, loads, line_refs, sems, rest = split(
+        refs, 3 + 3 * parts, 5 if ride else 0, 1 + 3 * parts, 4 if ride else 0, 3 + 3 * parts, 5, 7)
     (act_all, gg_all, gu_all), grads, (load_sem, grad_sem), ride_refs = split(rest, 3, 3 * parts, 2)
     returned, grads_out = outs[0], outs[1:]
     x_in, g_all, u_all = loads[:3]
@@ -671,7 +693,7 @@
     rows = 2 * CAP
     p = Place(spread)
     line = Line(p, x, part, stage, arrived, final, returned, sems)
-    rider = Halve(p, dense, quarter[0], ride_refs) if ride else Rider()
+    rider = GradientRider(p, given, ride_outs, ride_refs) if ride else Rider()
 
     def load(i):
         return pltpu.make_async_copy(loads_in[i], loads[i], load_sem.at[i])
@@ -732,6 +754,8 @@
 
         def begin(self):
             rider.begin()
+
+        def ready(self):
             for i in range(3 + 3 * parts):
                 load(i).wait()
 
@@ -749,28 +773,31 @@
     return jax.ShapeDtypeStruct(tuple(shape), dtype)
 
 
-def expert_forward(spread, call_id, out, weights, ride=None):
-    parts = len(weights) // 3
+def expert_forward(spread, call_id, out, weights, late=False, ride=None):
+    parts = -(-len(weights) // 3)
     _, local, cap, width = out.shape
     columns = sum(w.shape[2] for w in weights[:parts])
     kept = (LINE, local, 4 * cap, columns)
     outs = [struct(out.shape, BF16), struct((local, LINE, 4, cap, width), BF16), struct(kept, F32), struct(kept, F32)]
-    scratch = [pltpu.VMEM(w.shape, BF16) for w in weights] + Line.scratch(local, width)
-    scratch += [pltpu.VMEM(kept, F32), pltpu.VMEM(kept, F32), dma(3, LINE), dma(len(weights))]
-    more = ()
+    shapes = [w.shape for w in weights] + [weights[-1].shape] * late
+    outs += [struct(weights[-1].shape, BF16)] * late
+    scratch = [pltpu.VMEM(shape, BF16) for shape in shapes] + Line.scratch(local, width)
+    scratch += [pltpu.VMEM(kept, F32), pltpu.VMEM(kept, F32), dma(3, LINE), dma(3 * parts)]
+    more = ride or ()
+    count = LINE * spread
     if ride:
-        more = ride
-        count = LINE * spread
-        outs += [struct((count * s.shape[0], s.shape[1]), BF16) for s in ride[3:6]]
+        outs += [struct((count * s.shape[1], s.shape[2]), BF16) for s in ride[3:6]]
         outs += [struct(w.shape, BF16) for w in ride[6:]]
-        scratch += Spread.scratch(count)
+    if late:
+        scratch += WeightRider.scratch(count if ride else 0)
     return pl.pallas_call(
-        functools.partial(expert_forward_kernel, spread, parts, ride is not None),
+        functools.partial(expert_forward_kernel, spread, parts, int(late), ride is not None),
         out_shape=outs,
         in_specs=[VMEM] + [ANY] * (len(weights) + len(more)),
         out_specs=[VMEM] + [ANY] * (len(outs) - 1),
         scratch_shapes=scratch,
         compiler_params=remote_params(call_id),
+        cost_estimate=pl.CostEstimate(flops=2 * 10**10, bytes_accessed=2 * 10**8, transcendentals=0),
     )(out, *weights, *more)
 
 
@@ -787,16 +814,18 @@
     more = ()
     if ride:
         more = ride
-        depths = [g.shape[0] // (LINE * spread) for g in ride]
+        depths = [g.shape[0] // (LINE * spread) for g in ride[:2]]
         outs.append(struct((LINE, spread, sum(depths) // 2, width // 2), F32))
-        scratch += Halve.scratch(spread, depths, width)
+        outs += [struct(g.shape, BF16) for g in ride[2:]]
+        scratch += GradientRider.scratch(spread, depths, width)
     return pl.pallas_call(
         functools.partial(expert_backward_kernel, spread, parts, ride is not None),
         out_shape=outs,
         in_specs=[VMEM] + [ANY] * (len(loads) + len(more)),
-        out_specs=[VMEM] + [ANY] * len(grads) + [VMEM] * len(more[:1]),
+        out_specs=[VMEM] + [ANY] * len(grads) + ([VMEM] + [ANY] * 3 if ride else []),
         scratch_shapes=scratch,
         compiler_params=remote_params(call_id),
+        cost_estimate=pl.CostEstimate(flops=2 * 10**10, bytes_accessed=2 * 10**8, transcendentals=0),
     )(out, *loads, *more)
 
 
@@ -821,7 +850,9 @@
     return parts
 
 
-def pair_sum(parts, axis, spread):
+def pair_sum(parts, axis, spread, came=None):
+    if came is not None:
+        return parts[0] + came.astype(F32)
     if len(parts) == 1 and spread > 1:
         parts = jnp.split(parts[0], spread, axis=axis)
     total = parts[0]
@@ -831,53 +862,72 @@
 
 
 class LineGather:
-    def __init__(self, place, shards, quarters, sems):
+    def __init__(self, place, pairs, shards, quarters, sems):
         self.p, self.shards, self.quarters = place, shards, quarters
-        self.send, self.recv = sems
+        self.send, self.recv, self.x_send, self.x_recv = sems
+        self.columns = [place.f, 1 - place.f] if pairs else [0]
 
     @staticmethod
-    def shapes(shards):
-        (a, wide), (b, _), (c, narrow) = (s.shape for s in shards)
-        return [(LINE, a // 2, wide // 2), (LINE, b // 2, wide // 2), (LINE, c, narrow)]
+    def shapes(shards, columns):
+        (a, wide), (b, _), (c, narrow) = shards
+        return [(LINE, columns, a // 2, wide // 2), (LINE, columns, b // 2, wide // 2), (LINE, columns, c, narrow)]
 
     @staticmethod
-    def scratch():
-        return [dma(2, LINE, 3), dma(LINE, 3)]
-
-    def copy(self, kind, up, t):
-        at = self.quarters[kind].at[t]
-        return remote(at, at, self.send.at[up, t, kind], self.recv.at[t, kind], self.p.on_line(up))
-
-    def begin(self):
+    def scratch(columns):
+        return [dma(2, LINE, columns, 3), dma(LINE, columns, 3), dma(3), dma(3)]
+
+    def copy(self, kind, up, t, f):
+        at = self.quarters[kind].at[t, f]
+        return remote(at, at, self.send.at[up, t, f, kind], self.recv.at[t, f, kind], self.p.on_line(up))
+
+    def x_copy(self, kind, f):
+        at = self.quarters[kind].at[self.p.t, f]
+        return remote(at, at, self.x_send.at[kind], self.x_recv.at[kind], self.p.beside)
+
+    def both_ways(self, f):
         p = self.p
-        for kind in (0, 1):
-            half, wide = self.quarters[kind].shape[1:]
-            self.quarters[kind][p.t] = self.shards[kind][
-                pl.ds(pl.multiple_of(p.y * half, 16), half), pl.ds(pl.multiple_of(p.c * wide, 128), wide)]
-        self.quarters[2][p.t] = self.shards[2][...]
         for up, there in ((0, p.below), (1, p.above)):
 
             @pl.when(there)
             def _(up=up):
                 for kind in range(3):
-                    self.copy(kind, up, p.t).start()
+                    self.copy(kind, up, p.t, f).start()
+
+    def begin(self):
+        p, f = self.p, self.columns[0]
+        for kind in (0, 1):
+            half, wide = self.quarters[kind].shape[2:]
+            self.quarters[kind][p.t, f] = self.shards[kind][
+                pl.ds(pl.multiple_of(p.y * half, 16), half), pl.ds(pl.multiple_of(p.c * wide, 128), wide)]
+        self.quarters[2][p.t, f] = self.shards[2][...]
+        for kind in range(3 if len(self.columns) == 2 else 0):
+            self.x_copy(kind, f).start()
+        self.both_ways(f)
+
+    def beside(self, then):
+        for f in self.columns[1:]:
+            for kind in range(3):
+                self.x_copy(kind, f).wait_recv()
+            self.both_ways(f)
+            then(self.p.t, f)
 
     def step(self, k, then):
         p = self.p
-        for up, there, onward in ((0, p.t + k < LINE, p.below), (1, p.t - k >= 0, p.above)):
-            t = p.t - k if up else p.t + k
-
-            @pl.when(there)
-            def _(up=up, onward=onward, t=t):
-                for kind in range(3):
-                    self.copy(kind, up, t).wait_recv()
-
-                @pl.when(onward)
-                def _():
+        for f in self.columns:
+            for up, there, onward in ((0, p.t + k < LINE, p.below), (1, p.t - k >= 0, p.above)):
+                t = p.t - k if up else p.t + k
+
+                @pl.when(there)
+                def _(up=up, onward=onward, t=t, f=f):
                     for kind in range(3):
-                        self.copy(kind, up, t).start()
-
-                then(t)
+                        self.copy(kind, up, t, f).wait_recv()
+
+                    @pl.when(onward)
+                    def _():
+                        for kind in range(3):
+                            self.copy(kind, up, t, f).start()
+
+                    then(t, f)
 
     def finish(self):
         p = self.p
@@ -887,27 +937,26 @@
 
                 @pl.when(mine)
                 def _(up=up):
-                    for kind in range(3):
-                        self.copy(kind, up, t).wait_send()
+                    for f in self.columns:
+                        for kind in range(3):
+                            self.copy(kind, up, t, f).wait_send()
 
             return carry
 
         lax.fori_loop(0, LINE, line, 0)
+        for f in self.columns[1:]:
+            for kind in range(3):
+                self.x_copy(kind, 1 - f).wait_send()
 
 
 class Spread:
-    def __init__(self, place, given, whole, sems):
-        self.p = place
-        self.quarters, self.shards, self.own = given[:3], given[3:6], given[6:]
-        self.whole, self.other = whole[:3], whole[3:]
-        (self.x_send, self.x_recv, self.y_send, self.y_recv, self.c_send, self.c_recv, self.l_sem, self.s_sem,
-         self.w_send, self.w_recv) = sems
-        self.partners = [place.beside]
+    def __init__(self, place, quarters, shards, whole, sems):
+        self.p, self.quarters, self.shards, self.whole = place, quarters, shards, whole
+        self.y_send, self.y_recv, self.c_send, self.c_recv, self.l_sem, self.s_sem = sems
 
     @staticmethod
     def scratch(count):
-        return [dma(LINE, 3), dma(LINE, 3), dma(count, 2), dma(count, 2), dma(count, 2, 2), dma(count, 2, 2),
-                dma(LINE, 3), dma(3), dma(3), dma(3)]
+        return [dma(count, 2), dma(count, 2), dma(count, 2, 2), dma(count, 2, 2), dma(count, 3), dma(3)]
 
     def region(self, kind, s, y, c):
         depth = self.shards[kind].shape[0]
@@ -920,20 +969,6 @@
     def mine(self, kind, s):
         return self.region(kind, s, self.p.y, self.p.c)
 
-    def place_of(self, t):
-        return t * self.p.spread + self.p.f
-
-    def beside_of(self, t):
-        return t * self.p.spread + 1 - self.p.f
-
-    def x_copy(self, kind, t):
-        return remote(self.quarters[kind].at[t], self.mine(kind, self.place_of(t)), self.x_send.at[t, kind],
-                      self.x_recv.at[t, kind], self.p.beside)
-
-    def x_came(self, kind, t):
-        return remote(self.quarters[kind].at[t], self.mine(kind, self.beside_of(t)), self.x_send.at[t, kind],
-                      self.x_recv.at[t, kind], self.p.beside)
-
     def y_copy(self, kind, src, s):
         return remote(src, self.mine(kind, s), self.y_send.at[s, kind], self.y_recv.at[s, kind], self.p.across)
 
@@ -949,37 +984,95 @@
         at = self.region(kind, s, y, 1 - self.p.c)
         return remote(at, at, self.c_send.at[s, y, kind], self.c_recv.at[s, y, kind], self.p.sibling)
 
-    def local(self, kind, t):
-        return pltpu.make_async_copy(self.quarters[kind].at[t], self.mine(kind, self.place_of(t)), self.l_sem.at[t, kind])
+    def local(self, kind, src, s):
+        return pltpu.make_async_copy(src, self.mine(kind, s), self.l_sem.at[s, kind])
 
     def shard(self, kind):
         depth = self.shards[kind].shape[0]
         at = self.whole[kind].at[pl.ds(pl.multiple_of(self.p.d * depth, 16), depth)]
         return pltpu.make_async_copy(self.shards[kind], at, self.s_sem.at[kind])
 
-    def weight(self, i):
-        return remote(self.own[i], self.other[i], self.w_send.at[i], self.w_recv.at[i], self.p.beside)
-
     def own_shard(self):
         for kind in range(3):
             self.shard(kind).start()
 
-    def from_line(self, t):
+    def push(self, s, sources, here=True):
+        if here:
+            for kind in range(3):
+                self.local(kind, sources[kind], s).start()
+        for kind in (0, 1):
+            self.y_copy(kind, sources[kind], s).start()
+            self.c_copy(kind, sources[kind], s, self.p.y).start()
+
+    def across(self, s):
+        for kind in (0, 1):
+            self.y_came(kind, s).wait_recv()
+            self.c_copy(kind, self.region(kind, s, 1 - self.p.y, self.p.c), s, 1 - self.p.y).start()
+
+    def finish_shard(self, s, here=True):
+        @pl.when(s != self.p.d)
+        def _():
+            for kind in range(3 if here else 0):
+                self.local(kind, self.mine(kind, s), s).wait()
+            for kind in (0, 1):
+                self.y_came(kind, s).wait_send()
+                for y in (0, 1):
+                    self.c_came(kind, s, y).wait_send()
+                    self.c_came(kind, s, y).wait_recv()
+
+    def finish_own(self):
         for kind in range(3):
-            self.x_copy(kind, t).start()
-
-        @pl.when(t != self.p.t)
-        def _():
+            self.shard(kind).wait()
+
+
+class WeightRider:
+    def __init__(self, place, down, given, whole, sems):
+        self.p, self.quarters = place, given[:3]
+        self.own, self.other = [down[0]] + list(given[6:]), [down[1]] + list(whole[3:])
+        self.w_send, self.w_recv, *more = sems
+        self.spread = None
+        if given:
+            shards = [ref.at[1] for ref in given[3:6]]
+            self.x_send, self.x_recv, *more = more
+            self.spread = Spread(place, self.quarters, shards, whole[:3], more)
+        self.partners = [place.beside]
+
+    @staticmethod
+    def scratch(count):
+        return [dma(3), dma(3)] + ([dma(LINE, 3), dma(LINE, 3)] + Spread.scratch(count) if count else [])
+
+    def place_of(self, t):
+        return t * self.p.spread + self.p.f
+
+    def beside_of(self, t):
+        return t * self.p.spread + 1 - self.p.f
+
+    def x_copy(self, kind, t, s):
+        return remote(self.quarters[kind].at[t, 0], self.spread.mine(kind, s), self.x_send.at[t, kind],
+                      self.x_recv.at[t, kind], self.p.beside)
+
+    def weight(self, i):
+        return remote(self.own[i], self.other[i], self.w_send.at[i], self.w_recv.at[i], self.p.beside)
+
+    def ready(self):
+        self.weight(0).wait_recv()
+
+    def begin(self):
+        self.weight(0).start()
+        if not self.spread:
+            return
+        self.spread.own_shard()
+
+        def body(t):
             for kind in range(3):
-                self.local(kind, t).start()
-            for kind in (0, 1):
-                self.y_copy(kind, self.quarters[kind].at[t], self.place_of(t)).start()
-                self.c_copy(kind, self.quarters[kind].at[t], self.place_of(t), self.p.y).start()
-
-    def begin(self):
-        self.own_shard()
-        along(self.p, self.from_line)
-        for i in range(len(self.own)):
+                self.x_copy(kind, t, self.place_of(t)).start()
+
+            @pl.when(t != self.p.t)
+            def _():
+                self.spread.push(self.place_of(t), [q.at[t, 0] for q in self.quarters])
+
+        along(self.p, body)
+        for i in (1, 2):
             self.weight(i).start()
 
     def after_first(self):
@@ -987,109 +1080,98 @@
 
     def after_line(self):
         def body(t):
+            s = self.beside_of(t)
             for kind in range(3):
-                self.x_came(kind, t).wait_recv()
-            for kind in (0, 1):
-                s = self.beside_of(t)
-                self.y_copy(kind, self.mine(kind, s), s).start()
-                self.c_copy(kind, self.mine(kind, s), s, self.p.y).start()
-
-        along(self.p, body)
+                self.x_copy(kind, t, s).wait_recv()
+            self.spread.push(s, [self.spread.mine(kind, s) for kind in range(3)], here=False)
+
+        if self.spread:
+            along(self.p, body)
 
     def after_relay(self):
-        p = self.p
-
-        def across(s):
-            for kind in (0, 1):
-                at = self.region(kind, s, 1 - p.y, p.c)
-                self.y_came(kind, s).wait_recv()
-                self.c_copy(kind, at, s, 1 - p.y).start()
-
-        along(p, lambda t: across(self.place_of(t)), start=1)
-        along(p, lambda t: across(self.beside_of(t)))
+        if self.spread:
+            along(self.p, lambda t: self.spread.across(self.place_of(t)), start=1)
+            along(self.p, lambda t: self.spread.across(self.beside_of(t)))
 
     def finish(self):
-        p = self.p
-        for kind in range(3):
-            self.shard(kind).wait()
-        for i in range(len(self.own)):
+        self.weight(0).wait_send()
+        if not self.spread:
+            return
+        self.spread.finish_own()
+        for i in (1, 2):
             self.weight(i).wait()
 
         def line(t, carry):
             for kind in range(3):
-                self.x_copy(kind, t).wait_send()
-
-            @pl.when(t != p.t)
-            def _():
-                for kind in range(3):
-                    self.local(kind, t).wait()
-
-            for f in range(p.spread):
-                s = t * p.spread + f
-
-                @pl.when(s != p.d)
-                def _(s=s):
-                    for kind in (0, 1):
-                        self.y_came(kind, s).wait_send()
-                        for y in (0, 1):
-                            self.c_came(kind, s, y).wait_send()
-                            self.c_came(kind, s, y).wait_recv()
-
+                self.x_copy(kind, t, self.place_of(t)).wait_send()
+            self.spread.finish_shard(self.place_of(t))
+            self.spread.finish_shard(self.beside_of(t), here=False)
             return carry
 
         lax.fori_loop(0, LINE, line, 0)
 
 
-def dense_gather_kernel(spread, *refs):
+def dense_gather_kernel(spread, qkv, out, small, routes, gate, *refs):
     p = Place(spread)
-    shards0, shards1, (routes,), whole, quarters1, (routes_all,), quarters0, rest = split(refs, 3, 3, 1, 3, 3, 1, 3)
-    sems0, sems1, (r_send, r_recv), spread_sems = split(rest, 2, 2, 2)
-    line0 = LineGather(p, shards0, quarters0, sems0)
-    line1 = LineGather(p, shards1, quarters1, sems1)
-    spreading = Spread(p, tuple(quarters0) + tuple(shards0), whole, spread_sems)
+    whole, quarters1, (routes_all, partner), quarters0, sems0, sems1, (r_send, r_recv, w_send, w_recv), spread_sems = split(
+        refs, 3, 3, 2, 3, 4, 4, 4)
+    shards0, shards1 = ([ref.at[l] for ref in (qkv, out, small)] for l in (0, 1))
+    line0 = LineGather(p, True, shards0, quarters0, sems0)
+    line1 = LineGather(p, False, shards1, quarters1, sems1)
+    spreading = Spread(p, quarters0, shards0, whole, spread_sems)
     greet(p.mates[1:] + [p.beside], p)
 
     def route_copy(i, row):
         return remote(routes, routes_all.at[row], r_send.at[i], r_recv.at[row], p.mates[i])
 
+    def push(t, f):
+        spreading.push(t * spread + f, [q.at[t, f] for q in quarters0])
+
+    weight = remote(gate, partner, w_send.at[0], w_recv.at[0], p.beside)
+    line0.begin()
+    weight.start()
     routes_all[p.e] = routes[...]
-    line0.begin()
     for i in (1, 2, 3):
         route_copy(i, p.e).start()
     spreading.own_shard()
-    spreading.from_line(p.t)
+    line0.beside(push)
     line1.begin()
 
     def step(k, carry):
-        line0.step(k, spreading.from_line)
-        line1.step(k, lambda t: None)
+        line0.step(k, push)
+        line1.step(k, lambda t, f: None)
         return carry
 
     lax.fori_loop(1, LINE, step, 0)
-    spreading.after_line()
-    spreading.after_relay()
-    spreading.finish()
+    along(p, lambda t: spreading.across(t * spread + p.f), start=1)
+    along(p, lambda t: spreading.across(t * spread + 1 - p.f))
+    spreading.finish_own()
+    lax.fori_loop(0, LINE * spread, lambda s, carry: (spreading.finish_shard(s), carry)[1], 0)
     line0.finish()
     line1.finish()
+    weight.wait()
     for i in (1, 2, 3):
         route_copy(i, p.e).wait_send()
         route_copy(i, p.mates[i][1]).wait_recv()
 
 
-def dense_gather(spread, call_id, shards0, shards1, routes):
+def dense_gather(spread, call_id, arrays, routes, gate):
     count = spread * LINE
-    quarters = LineGather.shapes(shards0)
-    outs = [struct((count * s.shape[0], s.shape[1]), s.dtype) for s in shards0]
-    outs += [struct(q, BF16) for q in quarters] + [struct((4,) + routes.shape, routes.dtype)]
-    scratch = [pltpu.VMEM(q, BF16) for q in quarters] + LineGather.scratch() * 2 + [dma(4), dma(4)]
+    shards = [a.shape[1:] for a in arrays]
+    pairs, single = LineGather.shapes(shards, 2), LineGather.shapes(shards, 1)
+    outs = [struct((count * rows, width), BF16) for rows, width in shards]
+    outs += [struct(q, BF16) for q in single] + [struct((4,) + routes.shape, routes.dtype)]
+    outs.append(struct(gate.shape, BF16))
+    scratch = [pltpu.VMEM(q, BF16) for q in pairs] + LineGather.scratch(2) + LineGather.scratch(1)
+    scratch += [dma(4), dma(4), dma(1), dma(1)]
     return pl.pallas_call(
         functools.partial(dense_gather_kernel, spread),
         out_shape=outs,
-        in_specs=[VMEM] * 7,
-        out_specs=[ANY] * 3 + [VMEM] * 4,
+        in_specs=[VMEM] * 4 + [ANY],
+        out_specs=[ANY] * 3 + [VMEM] * 4 + [ANY],
         scratch_shapes=scratch + Spread.scratch(count),
         compiler_params=remote_params(call_id),
-    )(*shards0, *shards1, routes)
+    )(*arrays, routes, gate)
 
 
 class Halve:
@@ -1099,7 +1181,6 @@
          self.y_recv) = scratch
         self.depths = [g.shape[0] // (LINE * place.spread) for g in grads]
         self.wide = grads[0].shape[1] // 2
-        self.partners = []
 
     @staticmethod
     def scratch(spread, depths, width):
@@ -1135,7 +1216,10 @@
             row += depth // 2
 
     def order(self, i):
-        return jnp.where(self.p.t >= LINE // 2, i, LINE - 1 - i)
+        t = self.p.t
+        down = LINE - 1 - i - jnp.where(LINE - 1 - i <= t, 1, 0)
+        up = i + jnp.where(i >= t, 1, 0)
+        return jnp.where(i == LINE - 1, t, jnp.where(t >= LINE // 2, up, down))
 
     def begin(self):
         for kind in (0, 1):
@@ -1169,9 +1253,6 @@
         self.y_copy(t).wait_recv()
         self.quarter[t] = self.quarter[t] + self.came[t].astype(F32)
 
-    def after_line(self):
-        pass
-
     def after_relay(self):
         lax.fori_loop(0, LINE, lambda i, carry: (self.add(self.order(i)), carry)[1], 0)
 
@@ -1179,6 +1260,41 @@
         for kind in (0, 1):
             self.a_copy(kind).wait_send()
         lax.fori_loop(0, LINE, lambda t, carry: (self.y_copy(t).wait_send(), carry)[1], 0)
+
+
+class GradientRider:
+    def __init__(self, place, given, outs, scratch):
+        self.halve = Halve(place, given[:2], outs[0], scratch[:9])
+        self.own, self.other = given[2:], outs[1:]
+        self.p = place
+        self.w_send, self.w_recv = scratch[9:]
+        self.partners = [place.beside]
+
+    @staticmethod
+    def scratch(spread, depths, width):
+        return Halve.scratch(spread, depths, width) + [dma(3), dma(3)]
+
+    def weight(self, i):
+        return remote(self.own[i], self.other[i], self.w_send.at[i], self.w_recv.at[i], self.p.beside)
+
+    def begin(self):
+        self.halve.begin()
+        for i in range(3):
+            self.weight(i).start()
+
+    def after_first(self):
+        self.halve.after_first()
+
+    def after_line(self):
+        pass
+
+    def after_relay(self):
+        self.halve.after_relay()
+
+    def finish(self):
+        self.halve.finish()
+        for i in range(3):
+            self.weight(i).wait()
 
 
 class LineSum:
@@ -1222,20 +1338,18 @@
                 self.stage[t] = self.quarter[t].astype(BF16)
                 self.z_copy(up, t).start()
 
-    def relay(self, stage):
+    def relay(self, kind):
         p = self.p
-        for up, mine in ((1, p.t == stage), (0, p.t == LINE - 1 - stage)):
-
-            @pl.when(mine)
-            def _(up=up):
-                def one(n, carry):
-                    t = LINE - 1 - n if up else n
-                    self.z_copy(up, t).wait_recv()
-                    self.stage[t] = (self.quarter[t] + self.came[up, t].astype(F32)).astype(BF16)
-                    self.z_copy(up, t).start()
-                    return carry
-
-                lax.fori_loop(0, LINE - 1 - stage, one, 0)
+
+        @pl.when(jnp.logical_and(p.above, p.below))
+        def _():
+            up = jnp.where(p.t == 1, 1, 0)
+            ahead = 2 * up - 1
+            t = {"near": p.t + ahead, "far": p.t + 2 * ahead, "back": p.t - ahead}[kind]
+            way = 1 - up if kind == "back" else up
+            self.z_copy(way, t).wait_recv()
+            self.stage[t] = (self.quarter[t] + self.came[way, t].astype(F32)).astype(BF16)
+            self.z_copy(way, t).start()
 
     def after_z(self):
         p = self.p
@@ -1293,7 +1407,7 @@
         p = place
         near = (p.d + p.spread - 2 * p.spread * lax.rem(p.t, 2), p.e)
         self.far = (lax.rem(p.d + 2 * p.spread, LINE * p.spread), p.e)
-        self.partners = [p.sibling, p.across, p.beside, near, self.far]
+        self.partners = [p.sibling, p.across, near, self.far, p.beside]
 
     @staticmethod
     def scratch(rows, width):
@@ -1333,62 +1447,72 @@
         self.last(1 - self.p.c).wait_recv()
 
 
-def dense_reduce_kernel(spread, depths, small, qkv0, out0, quarter1, small_sum, *refs):
+def dense_reduce_kernel(spread, depths, small0, small1, res, qkv0, out0, quarter1, small_sum, *refs):
     p = Place(spread)
-    sums0, sums1, (mine0, mine1), halve_refs, line0, line1, small_refs = split(refs, 2, 2, 2, 9, 10, 10)
+    sums, (small, mine0, mine1), halve_refs, line0, line1, small_refs = split(refs, 2, 3, 9, 10, 10)
+    sums0, sums1 = ([ref.at[l] for ref in sums] for l in (0, 1))
     halve = Halve(p, (qkv0, out0), mine0, halve_refs)
     sum0 = LineSum(p, depths, mine0, sums0, line0)
     sum1 = LineSum(p, depths, mine1, sums1, line1)
     little = SmallSum(p, small, small_sum, small_refs)
     greet([p.sibling, p.across, p.beside, little.far], p)
     halve.begin()
+    rows = small0.shape[0]
+    small[0:rows, :] = small0[...]
+    small[rows : 2 * rows, :] = small1[...]
+    small[2 * rows :, :] = jnp.zeros((16, small.shape[1]), F32)
+    small[2 * rows :, 0:128] = res[0:16, :]
     little.step(0)
     mine1[...] = quarter1[...]
-    for t in range(LINE):
-        sum1.start(t)
+    for i in range(LINE):
+        sum1.start(halve.order(i))
     little.step(1)
     halve.after_first()
     little.step(2)
-    for stage in range(1, LINE - 1):
-        sum1.relay(stage)
+
+    def arrive(i):
+        halve.add(halve.order(i))
+        sum0.start(halve.order(i))
+
+    sum1.relay("far")
+    sum1.relay("near")
+    arrive(0)
     little.step(3)
+    sum1.relay("back")
+    arrive(1)
+    sum0.relay("far")
     sum1.after_z()
-
-    def arrive(i, carry):
-        t = halve.order(i)
-        halve.add(t)
-        sum0.start(t)
-        return carry
-
-    lax.fori_loop(0, LINE, arrive, 0)
+    arrive(2)
+    sum0.relay("near")
+    sum0.relay("back")
+    arrive(3)
     little.step(4)
+    sum0.after_z()
     sum1.after_x()
-    for stage in range(1, LINE - 1):
-        sum0.relay(stage)
     little.step(5)
-    sum0.after_z()
+    sum0.after_x()
     sum1.finish()
-    sum0.after_x()
     halve.finish()
     little.finish()
     sum0.finish()
 
 
-def dense_reduce(spread, call_id, small, grads0, quarter1):
+def dense_reduce(spread, call_id, smalls, grads0, quarter1):
     count = LINE * spread
     depths = [g.shape[0] // count for g in grads0]
     width = grads0[0].shape[1]
-    shards = [struct((depth, width), F32) for depth in depths]
+    small = (2 * smalls[0].shape[0] + 16, width)
     line = LineSum.scratch(spread, depths, width)
     mine = pltpu.VMEM(quarter1.shape, F32)
+    scratch = [pltpu.VMEM(small, F32), mine, mine] + Halve.scratch(spread, depths, width) + line + line
     return pl.pallas_call(
         functools.partial(dense_reduce_kernel, spread, depths),
-        out_shape=[struct(small.shape, F32)] + shards + shards,
-        in_specs=[VMEM, ANY, ANY, VMEM],
-        out_specs=[VMEM] * 5,
-        scratch_shapes=[mine, mine] + Halve.scratch(spread, depths, width) + line + line + SmallSum.scratch(*small.shape),
+        out_shape=[struct(small, F32)] + [struct((2, depth, width), F32) for depth in depths],
+        in_specs=[VMEM] * 3 + [ANY, ANY, VMEM],
+        out_specs=[VMEM] * 3,
+        scratch_shapes=scratch + SmallSum.scratch(*small),
         compiler_params=remote_params(call_id),
-    )(small, *grads0, quarter1)
+    )(*smalls, *grads0, quarter1)
 
 
 def per_device(
@@ -1411,6 +1535,8 @@
     ends = jnp.sum(jnp.where(order[:, None] <= order[None, :], lengths[:, None], 0), axis=0)
     doc = jnp.sum((jnp.arange(rows)[:, None] >= ends[None, :]).astype(jnp.int32), axis=1)
     doc_col, doc_row = doc[:, None], doc[None, :]
+
+    own = [[w[l].astype(BF16) for w in (w_gate, w_up, w_down)] for l in range(layers)]
 
     depth = w_out.shape[1]
     small = jnp.concatenate(
@@ -1426,12 +1552,15 @@
     if in_kernels:
         packed_routes = jnp.zeros((8, 256), jnp.int32).at[: 2 * layers, :rows].set(
             jnp.swapaxes(routes, 1, 2).reshape(2 * layers, rows))
-        shards = [(qkv_t[l], out_rows[l], small[l]) for l in range(layers)]
-        *gathered, routes_all = dense_gather(spread, 4, *shards, packed_routes)
+        *gathered, routes_all, gate = dense_gather(spread, 4, (qkv_t, out_rows, small), packed_routes, own[0][0])
+        up_own, gate = lax.optimization_barrier((own[0][1], gate))
+        weights = [[own[0][0], gate, up_own, from_partner(up_own, 1, spread, LINE), own[0][2]]]
         dense = [(gathered[2], gathered[0], gathered[1])]
         picked = lax.dynamic_index_in_dim(routes_all, my_place, 0, keepdims=False)
         my_routes = jnp.swapaxes(picked[: 2 * layers, :rows].reshape(layers, 2, rows), 1, 2)
     else:
+        weights = [
+            [part for w, axis in zip(own[l], (2, 2, 1)) for part in pair_weights(w, axis, spread)] for l in range(layers)]
         all_routes = lax.all_gather(routes, "expert", axis=0)
         my_routes = lax.dynamic_index_in_dim(all_routes, my_place, 0, keepdims=False)
         qkv_all = lax.all_gather(qkv_t, "dp", axis=1, tiled=True)
@@ -1439,10 +1568,6 @@
         small_all = lax.all_gather(small, "dp", axis=1, tiled=True)
         dense = [(small_all[l], qkv_all[l], out_all[l]) for l in range(layers)]
 
-    own = [[w[l].astype(BF16) for w in (w_gate, w_up, w_down)] for l in range(layers)]
-    weights = []
-    for l in range(1 if in_kernels else layers):
-        weights.append([part for w, axis in zip(own[l], (2, 2, 1)) for part in pair_weights(w, axis, spread)])
     w_res = jnp.zeros((128, 128), F32).at[: w_residual.shape[0], : w_residual.shape[1]].set(w_residual)
 
     cols = ((rows, width), F32)
@@ -1455,18 +1580,21 @@
     attn_in0, qkv0, probs0, attn0, mid0, logits0, stat0, out = local_call(
         first_kernel, experts, (tokens, *dense[0], doc_col, doc_row, my_routes[0]),
         attention + [cols, per_token, per_token, sent])
-    ride = (*gathered[3:], *shards[1], *own[1]) if in_kernels else None
-    ret0, *kept0 = expert_forward(spread, 0, group(out), weights[0], ride)
+    ride = (*gathered[3:], qkv_t, out_rows, small, *own[1][:2]) if in_kernels else None
+    ret0, *kept0 = expert_forward(spread, 0, group(out), weights[0], in_kernels, ride)
     if in_kernels:
-        kept0, (qkv_all, out_all, small_all), partner = kept0[:3], kept0[3:6], kept0[6:]
+        kept0, down, (qkv_all, out_all, small_all), partner = kept0[:3], kept0[3], kept0[4:7], kept0[7:]
+        weights[0].append(down)
         dense.append((small_all, qkv_all, out_all))
-        weights.append([w for pair in zip(own[1], partner) for w in pair])
+        weights.append([own[1][0], partner[0], own[1][1], partner[1], own[1][2]])
     ret0 = ret0.reshape(slots, width)
     stream1, attn_in1, qkv1, probs1, attn1, mid1, stat1, out = local_call(
         middle_kernel, experts,
         (mid0, dense[0][0], stat0, ret0, *dense[1], doc_col, doc_row, my_routes[1], logits0, w_res),
         [cols] + attention + [cols, per_token, sent])
-    ret1, *kept1 = expert_forward(spread, 1, group(out), weights[1])
+    ret1, *kept1 = expert_forward(spread, 1, group(out), weights[1], in_kernels)
+    if in_kernels:
+        weights[1].append(kept1.pop())
     ret1 = ret1.reshape(slots, width)
 
     small_grads = ((24, width), F32)
@@ -1482,10 +1610,11 @@
         (cotangent, back.reshape(slots, width), g_small1, stat1, mid1, dense[1][0], stream1, dense[1][1], dense[1][2],
          attn_in1, qkv1, probs1, attn1, small_grad1, mid0, dense[0][0], stat0, ret0, extra),
         dense_grads + [cols, per_token, sent, small_grads], attention_scratch)
-    ride = (qkv_grad1, out_grad1) if in_kernels else None
+    ride = (qkv_grad1, out_grad1, *expert_grads1[1::2]) if in_kernels else None
+    came = (None,) * 3
     back, *expert_grads0 = expert_backward(spread, 3, group(out), kept0, weights[0], ride)
     if in_kernels:
-        *expert_grads0, quarter1 = expert_grads0
+        expert_grads0, quarter1, came = expert_grads0[:6], expert_grads0[6], expert_grads0[7:]
     qkv_grad0, out_grad0, small_grad0, tokens_grad = local_call(
         last_kernel, experts,
         (grad, back.reshape(slots, width), g_small0, stat0, mid0, dense[0][0], tokens, dense[0][1], dense[0][2],
@@ -1495,18 +1624,16 @@
     expert_out = []
     for axis, at in ((2, 0), (2, 1), (1, 2)):
         per_layer = []
-        for grads in (expert_grads0, expert_grads1):
+        for grads, sent_here in ((expert_grads0, None), (expert_grads1, came[at])):
             n = len(grads) // 3
-            per_layer.append(pair_sum(grads[at * n : (at + 1) * n], axis, spread))
+            per_layer.append(pair_sum(grads[at * n : (at + 1) * n], axis, spread, sent_here))
         expert_out.append(jnp.stack(per_layer))
     gate_grad, up_grad, down_grad = expert_out
-    packed = jnp.concatenate([small_grad0, small_grad1, jnp.pad(res_grad[:16], ((0, 0), (0, width - 128)))])
     if in_kernels:
-        packed, qkv_sum0, out_sum0, qkv_sum1, out_sum1 = dense_reduce(
-            spread, 5, packed, (qkv_grad0, out_grad0), quarter1)
-        qkv_grad = jnp.stack([qkv_sum0, qkv_sum1])
-        out_grad = jnp.stack([out_sum0, out_sum1])
+        packed, qkv_grad, out_grad = dense_reduce(
+            spread, 5, (small_grad0, small_grad1, res_grad), (qkv_grad0, out_grad0), quarter1)
     else:
+        packed = jnp.concatenate([small_grad0, small_grad1, jnp.pad(res_grad[:16], ((0, 0), (0, width - 128)))])
         packed = lax.psum(packed, ("dp", "expert"))
         qkv_grad, out_grad = (
             lax.psum(lax.psum_scatter(jnp.stack(pair), "dp", scatter_dimension=1, tiled=True), "expert")

time: 614 us -> 525 us (0.86)
  Pallas kernels: 544 us -> 473 us
  waiting for transfers between devices: 10.2 us -> 0.01 us
  starting transfers between devices: 12.5 us -> 3.39 us
    pallas_call x1, Pallas kernels: 106 us -> 66.1 us  [dense_reduce(): pl.pallas_call(functools.partial(dense_reduce_kernel, spread, depths), ou...]
    pallas_call x2, Pallas kernels: 160 us -> 144 us  [expert_backward(): pl.pallas_call(functools.partial(expert_backward_kernel, spread, parts, r...]
    pallas_call x1, Pallas kernels: 62.6 us -> 48.1 us  [dense_gather(): pl.pallas_call(functools.partial(dense_gather_kernel, spread), out_shape=...]
    ppermute x6 -> x3, waiting for transfers between devices: 10.2 us -> 0.01 us  [to_partner(): return lax.ppermute(array, 'dp', pairs)]
  transfers between devices with their start and end apart: 9 -> 4, of which waited for: 1 -> 0; matrix products, arithmetic and copies ran while one was open for 5% -> 4% of each run, Pallas kernels for 32% -> 18%
where the time goes in v4:
time: 525 us; the launch traced here: 517 us
  Pallas kernels  473 us (90%)
  other arithmetic  19.9 us (4%)
  local copies, waits for them, and re-layouts  18.3 us (3%)
    pallas_call x2, Pallas kernels, expert_forward(): pl.pallas_call(functools.partial(expert_forward_kernel, spread, parts, in...  154 us
    pallas_call x2, Pallas kernels, expert_backward(): pl.pallas_call(functools.partial(expert_backward_kernel, spread, parts, r...  144 us
    pallas_call x1, Pallas kernels, dense_reduce(): pl.pallas_call(functools.partial(dense_reduce_kernel, spread, depths), ou...  66.1 us
    pallas_call x5, Pallas kernels, local_call(): pl.pallas_call(functools.partial(kernel, experts), out_shape=[jax.ShapeDt...  60.8 us
    pallas_call x1, Pallas kernels, dense_gather(): pl.pallas_call(functools.partial(dense_gather_kernel, spread), out_shape=...  48.1 us
  transfers between devices with their start and end apart: 4, of which 0 were waited for; matrix products, arithmetic and copies ran while one was open for 4% of the time, Pallas kernels for 18%

profile of v4, /device:TPU:0, one launch (start us, length us, event | category | flops | bytes accessed | tf_op | source)
XLA Modules:
  0.0 517.4 jit_solution(9371188125114704662)
XLA Ops:
  0.6 0.0 copy-start
  0.7 2.2 convert.37
  2.9 0.6 copy-done.2
  3.5 0.2 convert.38
  3.7 0.5 copy-done.17
  4.2 0.1 copy.40
  4.4 0.1 copy.43
  4.5 0.1 copy.41
  4.7 0.1 copy.42
  4.8 0.0 copy-start.18
  4.8 2.5 convert_bitcast_fusion.qkv.refs_8_
  7.4 0.7 convert_element_type.51.out.refs_9_
  8.1 1.7 slice_bitcast_fusion.1
  9.9 0.6 scatter.6.routes
  10.5 0.8 concatenate.8.small.refs_10_
  11.2 48.1 %shard_map.238 = (bf16[2304,768]{1,0:T(8,128)(2,1)}, bf16[768,768]{1,0:T(8,128)(2,1)}, bf16[768,128]{1,0:T(8,128)(2,1)}, bf16[4,1,144,384]{3,2,1,0:T(8,128)(2,1)...) custom-call(bf16[2,288,768]{2,1,0:T(8,128)(2,1)} %convert_bitcast_fu, ...), custom_call_target="tpu_custom_call" | custom-call | tf_op jit(solution)/shard_map/pallas_call | solution.py:1167
  59.4 0.7 collective-permute-start
  60.1 0.6 fusion.4
  62.7 0.7 dynamic-slice_bitcast_fusion.2
  63.4 0.1 copy.44
  63.5 0.7 slice_bitcast_fusion.6
  64.3 0.1 select_reduce_fusion
  64.3 0.1 convert_reduce_fusion
  64.4 0.8 copy.45.doc_col
  65.2 2.0 convert.39
  67.3 0.0 copy-start.16
  67.3 1.3 slice_bitcast_fusion
  68.6 0.6 scatter.9.w_res
  69.2 10.8 %shard_map.239 = (bf16[192,768]{1,0:T(8,128)(2,1)}, bf16[192,2304]{1,0:T(8,128)(2,1)}, f32[12,192,192]{2,1,0:T(8,128)}, bf16[192,768]{1,0:T(8,128)(2,1)}, f32[19...) custom-call(bf16[192,768]{1,0:T(8,128)(2,1)} %tokens.3, ...), custom_call_target="tpu_custom_call" | custom-call | flops 10000000000 | bytes 60000000 | tf_op jit(solution)/shard_map/pallas_call | solution.py:335
  80.0 0.9 copy-done.22
  80.9 78.5 %shard_map.240 = (bf16[4,2,48,768]{3,2,1,0:T(8,128)(2,1)}, bf16[2,4,4,48,768]{4,3,2,1,0:T(8,128)(2,1)}, f32[4,2,192,512]{3,2,1,0:T(8,128)}, f32[4,2,192,512]{3,2...) custom-call(bf16[4,2,48,768]{3,2,1,0:T(8,128)(2,1)} %bitcast.78, ...), custom_call_target="tpu_custom_call" | custom-call | flops 20000000000 | bytes 200000000 | tf_op jit(solution)/shard_map/pallas_call | solution.py:793
  159.4 11.5 %shard_map.241 = (f32[192,768]{1,0:T(8,128)}, bf16[192,768]{1,0:T(8,128)(2,1)}, bf16[192,2304]{1,0:T(8,128)(2,1)}, f32[12,192,192]{2,1,0:T(8,128)}, bf16[192,768...) custom-call(f32[192,768]{1,0:T(8,128)} %get-tuple-element.119.mid_in.mid0.mid, ...), custom_call_target="tpu_custom_call" | custom-call | flops 10000000000 | bytes 60000000 | tf_op jit(solution)/shard_map/pallas_call | solution.py:335
  171.0 75.3 %shard_map.242 = (bf16[4,2,48,768]{3,2,1,0:T(8,128)(2,1)}, bf16[2,4,4,48,768]{4,3,2,1,0:T(8,128)(2,1)}, f32[4,2,192,512]{3,2,1,0:T(8,128)}, f32[4,2,192,512]{3,2,1,0:T(8,128)}, bf16[2,256,768]{2,1,0:T(8,128)(2,1)}) custom-call(bf16[4,2,48,768]{3,2,1,0:T(8,128)(2,1)} %bitcast.80, bf16[2,768,256]{2,1,0:T(8,128)(2,1)} %get-tuple-element.245.refs_11_.refs_0_.refs_3_, ...), custom_call_target="tpu_custom_call" | custom-call | flops 20000000000 | bytes 200000000 | tf_op jit(solution)/shard_map/pallas_call | solution.py:793
  246.3 5.6 %shard_map.243 = (bf16[192,768]{1,0:T(8,128)(2,1)}, f32[192,128]{1,0:T(8,128)}, f32[192,128]{1,0:T(8,128)}, bf16[384,768]{1,0:T(8,128)(2,1)}, f32[24,768]{1,0:T(8,128)}, /*index=5*/f32[128,128]{1,0:T(8,128)}) custom-call(f32[192,768]{1,0:T(8,128)} %get-tuple-element.133.mid, bf16[768,128]{1,0:T(8,128)(2,1)} %get-tuple-element.129.small, ...), custom_call_target="tpu_custom_call" | custom-call | flops 10000000000 | bytes 60000000 | tf_op jit(solution)/shard_map/pallas_call | solution.py:335
  251.9 70.9 %shard_map.244 = (bf16[4,2,48,768]{3,2,1,0:T(8,128)(2,1)}, f32[2,768,256]{2,1,0:T(8,128)}, bf16[2,768,256]{2,1,0:T(8,128)(2,1)}, f32[2,768,256]{2,1,0:T(8,128)},...) custom-call(bf16[4,2,48,768]{3,2,1,0:T(8,128)(2,1)} %bitcast.79, ...), custom_call_target="tpu_custom_call" | custom-call | flops 20000000000 | bytes 200000000 | tf_op jit(solution)/shard_map/pallas_call | solution.py:821
  322.8 17.6 %shard_map.245 = (bf16[2304,768]{1,0:T(8,128)(2,1)}, bf16[768,768]{1,0:T(8,128)(2,1)}, f32[24,768]{1,0:T(8,128)}, f32[192,768]{1,0:T(8,128)}, f32[192,128]{1,0:T...) custom-call(bf16[192,768]{1,0:T(8,128)(2,1)} %cotangent.3, bf16[384,768]{1,0:T(8,128)(2,1)} %bitcast.77, ...), custom_call_target="tpu_custom_call" | custom-call | flops 10000000000 | bytes 60000000 | tf_op jit(solution)/shard_map/pallas_call | solution.py:335
  340.4 72.9 %shard_map.246 = (bf16[4,2,48,768]{3,2,1,0:T(8,128)(2,1)}, f32[2,768,256]{2,1,0:T(8,128)}, bf16[2,768,256]{2,1,0:T(8,128)(2,1)}, f32[2,768,256]{2,1,0:T(8,128)},...) custom-call(bf16[4,2,48,768]{3,2,1,0:T(8,128)(2,1)} %bitcast.76, ...), custom_call_target="tpu_custom_call" | custom-call | flops 20000000000 | bytes 200000000 | tf_op jit(solution)/shard_map/pallas_call | solution.py:821
  413.3 0.7 collective-permute-start.3
  414.0 1.4 collective-permute-start.2
  415.4 0.6 collective-permute-start.1
  416.0 15.2 %shard_map.247 = (bf16[2304,768]{1,0:T(8,128)(2,1)}, bf16[768,768]{1,0:T(8,128)(2,1)}, f32[24,768]{1,0:T(8,128)}, f32[192,768]{1,0:T(8,128)}) custom-call(f32[192,768]{1,0:T(8,128)} %get-tuple-element.154.grad_in, bf16[384,768]{1,0:T(8,128)(2,1)} %bitcast.75, f32[192,128]{1,0:T(8,128)} %get-tuple-element.166.g_small, ...), custom_call_target="tpu_custom_call" | custom-call | flops 10000000000 | bytes 60000000 | tf_op jit(solution)/shard_map/pallas_call | solution.py:335
  431.2 66.1 %shard_map.248 = (f32[64,768]{1,0:T(8,128)}, f32[2,288,768]{2,1,0:T(8,128)}, f32[2,96,768]{2,1,0:T(8,128)}) custom-call(f32[24,768]{1,0:T(8,128)} %get-tuple-element.173.small0, f32[24,768]{1,0:T(8,128)} %get-tuple-element.174.small1, f32[128,128]{1,0:T(8,128)} %get-tuple-element.175.res, bf16[2304,768]{1,0:T(8,128)(2,1)} %get-tuple-element.176.qkv0, ...), custom_call_target="tpu_custom_call" | custom-call | tf_op jit(solution)/shard_map/pallas_call | solution.py:1508
  497.2 1.3 slice.117
  498.5 1.5 add_bitcast_fusion
  500.0 0.8 dynamic-slice_bitcast_fusion.1
  500.9 0.6 fusion.2
  501.5 0.6 copy.47
  502.1 0.6 pad_maximum_fusion.3
  502.7 0.2 add_bitcast_fusion.2
  502.8 1.2 copy-done.4
  504.1 0.2 copy-done.11
  504.3 0.2 add_bitcast_fusion.4
  504.4 1.2 copy-done.9
  505.7 1.3 add_bitcast_fusion.1
  507.0 1.9 pad_maximum_fusion.2
  508.9 1.3 add_bitcast_fusion.3
  510.3 1.9 pad_maximum_fusion.1
  512.1 0.1 copy-done.6
  512.3 0.2 add_bitcast_fusion.5
  512.5 1.9 pad_maximum_fusion
  514.4 0.4 copy-done.3
  514.7 1.2 copy.50
  515.9 0.3 copy-done.14
  516.2 0.8 copy.51
  (50 shorter events, 0.2 us)
Async XLA Ops:
  0.6 63.6 %copy-start = (s32[1,4,4]{2,1,0:T(4,128)S(1)}, s32[1,4,4]{2,1,0:T(4,128)}, u32[]{:S(2)}) copy-start(s32[1,4,4]{2,1,0:T(4,128)} %param.20) | copy-start | bytes 196
  0.7 2.8 copy-start.2
  3.5 0.7 copy-start.17
  3.5 0.9 copy-start.15
  3.5 1.0 copy-start.19
  3.5 1.2 copy-start.20
  4.8 2.6 copy-start.13
  4.8 3.3 copy-start.18
  9.9 49.5 %copy-start.10 = (bf16[2,768,256]{2,1,0:T(8,128)(2,1)S(1)}, bf16[2,768,256]{2,1,0:T(8,128)(2,1)}, u32[]{:S(2)}) copy-start(bf16[2,768,256]{2,1,0:T(8,128)(2,1)} %get-tuple-element.124.refs_2_.refs_5_) | copy-start | bytes 2359300
  9.9 50.2 %copy-start.23 = (s32[1,4]{1,0:T(1,128)S(1)}, s32[1,4]{1,0:T(1,128)}, u32[]{:S(2)}) copy-start(s32[1,4]{1,0:T(1,128)} %param.21) | copy-start | bytes 52
  59.4 20.6 %collective-permute-start = (bf16[2,768,256]{2,1,0:T(8,128)(2,1)S(1)}, bf16[2,768,256]{2,1,0:T(8,128)(2,1)S(1)}, u32[]{:S(2)}, u32[]{:S(2)}) collective-permute-start(bf16[2,768,256]{2,1,0:T(8,128)(2,1)S(1)} %copy-done.10), channel_id=1, source_target_pairs={{4,0},{0,4},{12,8},{8,12},{20,16},{16,20},{28,24},{24,28},{5,1},{1... | collective-permute-start | bytes 2359304 | tf_op jit(solution)/shard_map/ppermute | solution.py:836
  64.4 2.8 copy-start.21
  67.3 1.3 copy-start.16
  80.0 0.9 copy-start.22
  413.3 91.1 %collective-permute-start.3 = (bf16[2,256,768]{2,1,0:T(8,128)(2,1)}, bf16[2,256,768]{2,1,0:T(8,128)(2,1)}, u32[]{:S(2)}, u32[]{:S(2)}) collective-permute-start(bf16[2,256,768]{2,1,0:T(8,128)(2,1)} %get-tuple-element.191), channel_id=1, source_target_pairs={{0,4},{4,0},{8,12},{12,8},{16,20},{20,16},{24,28},{28,24},{1,5},{5... | collective-permute-start | bytes 2359304 | tf_op jit(solution)/shard_map/ppermute | solution.py:843
  414.0 94.9 %collective-permute-start.2 = (bf16[2,768,256]{2,1,0:T(8,128)(2,1)}, bf16[2,768,256]{2,1,0:T(8,128)(2,1)}, u32[]{:S(2)}, u32[]{:S(2)}) collective-permute-start(bf16[2,768,256]{2,1,0:T(8,128)(2,1)} %get-tuple-element.187), channel_id=1, source_target_pairs={{0,4},{4,0},{8,12},{12,8},{16,20},{20,16},{24,28},{28,24},{1,5},{5... | collective-permute-start | bytes 2359304 | tf_op jit(solution)/shard_map/ppermute | solution.py:843
  415.4 96.7 %collective-permute-start.1 = (bf16[2,768,256]{2,1,0:T(8,128)(2,1)}, bf16[2,768,256]{2,1,0:T(8,128)(2,1)S(1)}, u32[]{:S(2)}, u32[]{:S(2)}) collective-permute-start(bf16[2,768,256]{2,1,0:T(8,128)(2,1)} %get-tuple-element.183), channel_id=1, source_target_pairs={{0,4},{4,0},{8,12},{12,8},{16,20},{20,16},{24,28},{28,24},{1,5},{5... | collective-permute-start | bytes 2359304 | tf_op jit(solution)/shard_map/ppermute | solution.py:843
  431.2 67.4 %copy-start.7 = (f32[2,256,768]{2,1,0:T(8,128)S(1)}, f32[2,256,768]{2,1,0:T(8,128)}, u32[]{:S(2)}) copy-start(f32[2,256,768]{2,1,0:T(8,128)} %get-tuple-element.192) | copy-start | bytes 4718596
  498.5 4.1 copy-start.5
  498.5 4.1 copy-start.12
  502.7 1.4 copy-start.4
  502.7 1.6 copy-start.11
  504.3 1.4 copy-start.9
  507.0 1.9 copy-start.8
  510.3 2.0 copy-start.6
  512.5 2.2 copy-start.3
  514.4 2.6 copy-start.1
  514.7 1.5 copy-start.14

commit v5 on v4

--- a/solution.py
+++ b/solution.py
@@ -28,6 +28,9 @@
 }
 
 
+SMEM = pl.BlockSpec(memory_space=pltpu.SMEM)
+
+
 def dot_nn(a, b, **kw):
     return lax.dot_general(a, b, (((1,), (0,)), ((), ())), preferred_element_type=F32, **kw)
 
@@ -75,7 +78,29 @@
     return out
 
 
-def attend_part(stream, small, w_qkv_t, w_out, doc_col, doc_row, attn_in_ref, qkv_ref, probs_ref, attn_ref):
+def doc_index(lengths, places):
+    place, end = lax.axis_index("expert"), 0
+    doc = jnp.zeros_like(places)
+    for j in range(lengths.shape[2]):
+        end = end + lengths[0, place, j]
+        doc = doc + (places >= end).astype(jnp.int32)
+    return doc
+
+
+def block_routes(perm, routes_all, layer, rows):
+    mine = routes_all[perm[0, lax.axis_index("expert")]].astype(F32)
+    routes = jnp.transpose(mine)[:rows].astype(jnp.int32)
+    return routes[:, 2 * layer : 2 * layer + 1], routes[:, 2 * layer + 1 : 2 * layer + 2]
+
+
+def padded(w_res, ref):
+    count = w_res.shape[0]
+    ref[...] = jnp.zeros(ref.shape, F32)
+    ref[0:count, 0:count] = w_res[...]
+    return ref[...]
+
+
+def attend_part(stream, small, w_qkv_t, w_out, lengths, attn_in_ref, qkv_ref, probs_ref, attn_ref):
     rows, width = stream.shape
     gain, _, _, _ = row_vectors(small)
     attn_in_ref[...] = (stream * rms_scale(stream) * gain).astype(BF16)
@@ -91,7 +116,8 @@
     head_dim = width // HEADS
     factor = 1.0 / head_dim**0.5
     allowed = jnp.logical_and(
-        doc_col[...] == doc_row[...],
+        doc_index(lengths, lax.broadcasted_iota(jnp.int32, (rows, 1), 0))
+        == doc_index(lengths, lax.broadcasted_iota(jnp.int32, (1, rows), 1)),
         lax.broadcasted_iota(jnp.int32, (rows, rows), 0)
         >= lax.broadcasted_iota(jnp.int32, (rows, rows), 1),
     )
@@ -127,7 +153,7 @@
     logits = jnp.where(lane < CONST0, raw, 0.0)
     if prev_logits is not None:
         logits = logits + dot_nn(prev_logits, w_res, precision=HIGH)
-    r0, r1 = routes[:, 0:1], routes[:, 1:2]
+    r0, r1 = routes
     hot0, hot1 = (lane == r0).astype(F32), (lane == r1).astype(F32)
     c0 = jnp.sum(hot0 * logits, axis=-1, keepdims=True)
     c1 = jnp.sum(hot1 * logits, axis=-1, keepdims=True)
@@ -220,26 +246,28 @@
     ref[VECTOR0 + 1 : VECTOR0 + 2, :] = vector1
 
 
-def first_kernel(experts, tokens, small, w_qkv_t, w_out, doc_col, doc_row, routes,
+def first_kernel(experts, tokens, small, w_qkv_t, w_out, lengths, perm, routes_all,
                  attn_in, qkv, probs, attn, mid_ref, logits_ref, stat_ref, out_ref):
-    mid = attend_part(tokens[...].astype(F32), small[...], w_qkv_t, w_out, doc_col, doc_row, attn_in, qkv, probs, attn)
+    mid = attend_part(tokens[...].astype(F32), small[...], w_qkv_t, w_out, lengths, attn_in, qkv, probs, attn)
     mid_ref[...] = mid
-    logits, stat, out = route_part(mid, small[...], routes[...], None, None, experts)
+    routes = block_routes(perm, routes_all, 0, mid.shape[0])
+    logits, stat, out = route_part(mid, small[...], routes, None, None, experts)
     logits_ref[...], stat_ref[...], out_ref[...] = logits, stat, out
 
 
-def middle_kernel(experts, mid_in, small_in, stat_in, returned, small, w_qkv_t, w_out, doc_col, doc_row, routes, logits_in, w_res,
-                  stream_ref, attn_in, qkv, probs, attn, mid_ref, stat_ref, out_ref):
+def middle_kernel(experts, mid_in, small_in, stat_in, returned, small, w_qkv_t, w_out, lengths, perm, routes_all, logits_in, w_res,
+                  stream_ref, attn_in, qkv, probs, attn, mid_ref, stat_ref, out_ref, res_ref):
     stream, _, _, _ = combine_part(mid_in[...], small_in[...], stat_columns(stat_in[...]), returned[...], experts)
     stream_ref[...] = stream
-    mid = attend_part(stream, small[...], w_qkv_t, w_out, doc_col, doc_row, attn_in, qkv, probs, attn)
+    mid = attend_part(stream, small[...], w_qkv_t, w_out, lengths, attn_in, qkv, probs, attn)
     mid_ref[...] = mid
-    _, stat, out = route_part(mid, small[...], routes[...], logits_in[...], w_res[...], experts)
+    routes = block_routes(perm, routes_all, 1, mid.shape[0])
+    _, stat, out = route_part(mid, small[...], routes, logits_in[...], padded(w_res, res_ref), experts)
     stat_ref[...], out_ref[...] = stat, out
 
 
 def turn_kernel(experts, mid, small, stat_in, returned, cotangent, logits_in, w_res,
-                output, g_small_ref, extra_ref, out_ref, small_grad, res_grad):
+                output, g_small_ref, extra_ref, out_ref, small_grad, res_grad, res_ref):
     stat = stat_columns(stat_in[...])
     stream, hidden_full, pair0, pair1 = combine_part(mid[...], small[...], stat, returned[...], experts)
     output[...] = stream.astype(BF16)
@@ -249,7 +277,7 @@
     out_ref[...] = out
     store_small(small_grad, projections, v0, v1)
     res_grad[...] = dot_tn(logits_in[...], g_logits, precision=HIGH)
-    extra_ref[...] = dot_nt(g_logits, w_res[...], precision=HIGH)
+    extra_ref[...] = dot_nt(g_logits, padded(w_res, res_ref), precision=HIGH)
 
 
 def layer_backward(experts, grad, back, g_small, stat, mid, small, stream, w_qkv_t, w_out, attn_in, qkv, probs, attn,
@@ -331,11 +359,11 @@
                                    g_qkv, g_attn)
 
 
-def local_call(kernel, experts, args, outs, scratch=()):
+def local_call(kernel, experts, args, outs, scratch=(), scalars=()):
     return pl.pallas_call(
         functools.partial(kernel, experts),
         out_shape=[jax.ShapeDtypeStruct(shape, dtype) for shape, dtype in outs],
-        in_specs=[VMEM] * len(args),
+        in_specs=[SMEM if i in scalars else VMEM for i in range(len(args))],
         out_specs=[VMEM] * len(outs),
         scratch_shapes=[pltpu.VMEM(shape, dtype) for shape, dtype in scratch],
         compiler_params=pltpu.CompilerParams(vmem_limit_bytes=60 * 2**20),
@@ -350,6 +378,9 @@
         self.t, self.f = self.d // spread, lax.rem(self.d, spread)
         self.y, self.c = self.e // 2, lax.rem(self.e, 2)
         self.above, self.below = self.t < LINE - 1, self.t > 0
+        self.inside = jnp.logical_and(self.above, self.below)
+        self.up = jnp.where(self.t == 1, 1, 0)
+        self.ahead = 2 * self.up - 1
         self.sibling = (self.d, self.e + 1 - 2 * self.c)
         self.across = (self.d, lax.rem(self.e + 2, 4))
         self.corner = (self.d, 3 - self.e)
@@ -461,28 +492,18 @@
         self.stage[s, :, b] = total.astype(BF16)
         self.sum_copy(up, s, b).start()
 
-    def relays(self):
+    def relay(self, kind, i):
         p = self.p
 
-        @pl.when(jnp.logical_and(p.above, p.below))
+        @pl.when(p.inside)
         def _():
-            up = jnp.where(p.t == 1, 1, 0)
-            ahead = 2 * up - 1
-
-            def on(kind, i):
-                b = p.mates[i][1]
-                s = {"near": p.t + ahead, "far": p.t + 2 * ahead, "back": p.t - ahead}[kind]
-                way = 1 - up if kind == "back" else up
-                self.sum_copy(way, s, b).wait_recv()
-                self.send_sum(way, s, b, self.part[s, :, b] + self.arrived[way, s, :, b].astype(F32))
-
-            for kind, i in (
-                ("near", 0), ("near", 1), ("far", 0), ("far", 1), ("back", 0), ("far", 2), ("back", 1), ("far", 3),
-                ("back", 2), ("near", 2), ("back", 3), ("near", 3),
-            ):
-                on(kind, i)
-
-    def run(self, out, compute, kept, meanwhile, rider):
+            b = p.mates[i][1]
+            s = {"near": p.t + p.ahead, "far": p.t + 2 * p.ahead, "back": p.t - p.ahead}[kind]
+            way = 1 - p.up if kind == "back" else p.up
+            self.sum_copy(way, s, b).wait_recv()
+            self.send_sum(way, s, b, self.part[s, :, b] + self.arrived[way, s, :, b].astype(F32))
+
+    def run(self, out, compute, kept, pieces, rider):
         p = self.p
         t, e = p.t, p.e
         blocks = [b for _, b in p.mates]
@@ -501,9 +522,6 @@
                     self.x_copy(up, t, blocks[i]).start()
 
         rider.ready()
-        lax.fori_loop(0, 2, lambda pair, carry: (compute(t, pair), carry)[1], 0)
-        kept(t)
-        rider.after_first()
 
         def step(n, carry):
             k = jnp.where(n < 2, 1, jnp.where(jnp.logical_or(n == 2, n == 5), 2, 3))
@@ -531,20 +549,15 @@
                     for b in (first, second):
                         self.x_copy(up, t - 1 if up else t + 1, b).start()
 
-            def side(up, carry):
-                s = t + k - 2 * k * up
-
-                @pl.when(jnp.logical_and(s >= 0, s < LINE))
+            @pl.when(jnp.logical_not(p.inside))
+            def _():
+                s = jnp.where(t == 0, k, LINE - 1 - k)
+                compute(s, 2 * pair, 2)
+
+                @pl.when(half == 1)
                 def _():
-                    compute(s, pair)
-
-                    @pl.when(half == 1)
-                    def _():
-                        kept(s)
-
-                return carry
-
-            lax.fori_loop(0, 2, side, 0)
+                    kept(s)
+
             for up, starts, s in ((1, t == 0, k), (0, t == LINE - 1, LINE - 1 - k)):
 
                 @pl.when(starts)
@@ -552,12 +565,32 @@
                     for b in (first, second):
                         self.send_sum(up, s, b, self.part[s, :, b])
 
+            rest = jnp.logical_and(p.inside, jnp.logical_or(n == 5, jnp.logical_and(n >= 1, n <= 2)))
+
+            @pl.when(jnp.logical_or(n == 0, rest))
+            def _():
+                s = t + p.ahead * jnp.where(n == 0, 0, jnp.where(n == 1, 1, jnp.where(n == 2, -1, 2)))
+                compute(s, 0, 4)
+                kept(s)
+
+            @pl.when(n == 0)
+            def _():
+                rider.after_first()
+
             return carry
 
         lax.fori_loop(0, 6, step, 0)
         rider.after_line()
-        meanwhile()
-        self.relays()
+        todo = list(pieces)
+        for n, (kind, i) in enumerate((
+            ("near", 0), ("near", 1), ("far", 0), ("far", 1), ("back", 0), ("far", 2), ("back", 1), ("far", 3),
+            ("back", 2), ("near", 2), ("back", 3), ("near", 3),
+        )):
+            self.relay(kind, i)
+            if n % 2 == 1 and todo:
+                todo.pop(0)()
+        for piece in todo:
+            piece()
         rider.after_relay()
         for i, b in enumerate(blocks):
             for up, there in ((1, p.below), (0, p.above)):
@@ -604,25 +637,22 @@
     return out + [refs[at:]]
 
 
-def expert_forward_kernel(spread, parts, late, ride, out, *refs):
-    own = 3 * parts - late
-    weights_in, given, outs, late_out, whole, scratch, line_refs, sems, ride_refs = split(
-        refs, own, 8 if ride else 0, 4, late, 5 if ride else 0, 3 * parts, 5, 7)
-    weights_in = list(weights_in) + list(late_out)
+def expert_forward_kernel(spread, parts, ride, out, *refs):
+    weights_in, given, outs, whole, scratch, line_refs, sems, ride_refs = split(
+        refs, 3 * parts, 9 if ride else 0, 4, 6 if ride else 0, 3 * parts, 5, 7)
     (g_all, u_all, keep_sem, load_sem), ride_refs = ride_refs[:4], ride_refs[4:]
     returned, x_keep, g_keep, u_keep = outs
     gate, up, down = scratch[:parts], scratch[parts : 2 * parts], scratch[2 * parts :]
     x, part, stage, arrived, final = line_refs
     local, _, _, _, width = x.shape
-    rows = 2 * CAP
     p = Place(spread)
     line = Line(p, x, part, stage, arrived, final, returned, sems)
-    rider = WeightRider(p, weights_in[-2:], given, whole, ride_refs) if late else Rider()
+    rider = WeightRider(p, given, whole, ride_refs) if ride else Rider()
 
     def load(i):
         return pltpu.make_async_copy(weights_in[i], scratch[i], load_sem.at[i])
 
-    for i in range(own):
+    for i in range(3 * parts):
         load(i).start()
 
     def keep_x(s):
@@ -639,11 +669,12 @@
         keep_g(s).start()
         keep_u(s).start()
 
-    def compute(s, pair):
-        at = pl.multiple_of(pair * rows, rows)
+    def compute(s, first, count):
+        rows = count * CAP
+        at = pl.multiple_of(first * CAP, CAP)
 
         def one(l, carry):
-            rows_in = x[l, s, pl.ds(2 * pair, 2)].reshape(rows, width)
+            rows_in = x[l, s, pl.ds(first, count)].reshape(rows, width)
             total = jnp.zeros((rows, width), F32)
             for q in range(parts):
                 cols = gate[q].shape[2]
@@ -654,7 +685,7 @@
                 u_all[s, l, pl.ds(at, rows), here] = u
                 act = (g * jax.nn.sigmoid(g) * u).astype(BF16)
                 total = total + dot_nn(act, down[q][l])
-            part[s, l, pl.ds(2 * pair, 2)] = total.reshape(2, CAP, width)
+            part[s, l, pl.ds(first, count)] = total.reshape(count, CAP, width)
             return carry
 
         lax.fori_loop(0, local, one, 0)
@@ -668,29 +699,27 @@
             rider.begin()
 
         def ready(self):
-            rider.ready()
-            for i in range(own, 3 * parts):
-                load(i).start()
             for i in range(3 * parts):
                 load(i).wait()
 
-    line.run(out, compute, kept, lambda: None, Loaded())
+    line.run(out, compute, kept, (), Loaded())
     for s in range(LINE):
         keep_x(s).wait()
         keep_g(s).wait()
         keep_u(s).wait()
 
 
-def expert_backward_kernel(spread, parts, ride, out, *refs):
-    loads_in, given, outs, ride_outs, loads, line_refs, sems, rest = split(
-        refs, 3 + 3 * parts, 5 if ride else 0, 1 + 3 * parts, 4 if ride else 0, 3 + 3 * parts, 5, 7)
-    (act_all, gg_all, gu_all), grads, (load_sem, grad_sem), ride_refs = split(rest, 3, 3 * parts, 2)
-    returned, grads_out = outs[0], outs[1:]
+def expert_backward_kernel(spread, parts, exchange, ride, out, *refs):
+    loads_in, given, outs, came, ride_outs, loads, line_refs, sems, rest = split(
+        refs, 3 + 3 * parts, 4 if ride else 0, 1 + 3 * parts - exchange, exchange, 3 if ride else 0, 3 + 3 * parts, 5, 7)
+    (act_all, gg_all, gu_all), grads, (load_sem, grad_sem, w_send, w_recv), ride_refs = split(rest, 3, 3 * parts, 4)
+    returned, grads_out = outs[0], list(outs[1:])
+    if exchange:
+        grads_out.insert(1, None)
     x_in, g_all, u_all = loads[:3]
     gate, up, down = loads[3 : 3 + parts], loads[3 + parts : 3 + 2 * parts], loads[3 + 2 * parts :]
     x, part, stage, arrived, final = line_refs
     local, _, _, _, width = x.shape
-    rows = 2 * CAP
     p = Place(spread)
     line = Line(p, x, part, stage, arrived, final, returned, sems)
     rider = GradientRider(p, given, ride_outs, ride_refs) if ride else Rider()
@@ -704,12 +733,13 @@
     for i in range(3 + 3 * parts):
         load(i).start()
 
-    def compute(s, pair):
-        at = pl.multiple_of(pair * rows, rows)
-        into = pl.ds(pl.multiple_of((2 * s + pair) * rows, rows), rows)
+    def compute(s, first, count):
+        rows = count * CAP
+        at = pl.multiple_of(first * CAP, CAP)
+        into = pl.ds(pl.multiple_of((4 * s + first) * CAP, CAP), rows)
 
         def one(l, carry):
-            rows_in = x[l, s, pl.ds(2 * pair, 2)].reshape(rows, width)
+            rows_in = x[l, s, pl.ds(first, count)].reshape(rows, width)
             total = jnp.zeros((rows, width), F32)
             for q in range(parts):
                 cols = gate[q].shape[2]
@@ -724,31 +754,30 @@
                 gg_all[l, into, here] = gg
                 gu_all[l, into, here] = gu
                 total = total + dot_nt(gg, gate[q][l]) + dot_nt(gu, up[q][l])
-            part[s, l, pl.ds(2 * pair, 2)] = total.reshape(2, CAP, width)
+            part[s, l, pl.ds(first, count)] = total.reshape(count, CAP, width)
             return carry
 
         lax.fori_loop(0, local, one, 0)
 
-    def weights():
-        def one(l, carry):
-            x_rows = x_in[l].reshape(2 * LINE * rows, width)
-            g_rows = x[l].reshape(2 * LINE * rows, width)
-            for q in range(parts):
-                cols = gate[q].shape[2]
-                here = slice(q * cols, (q + 1) * cols)
-                for i, value in (
-                    (q, dot_tn(x_rows, gg_all[l, :, here])),
-                    (parts + q, dot_tn(x_rows, gu_all[l, :, here])),
-                    (2 * parts + q, dot_tn(act_all[l, :, here], g_rows)),
-                ):
-                    grads[i][l] = value.astype(grads[i].dtype)
-                    store(i, l).start()
-            return carry
-
-        lax.fori_loop(0, local, one, 0)
+    def weights(kind, l):
+        x_rows, g_rows = (a[l].reshape(LINE * 4 * CAP, width) for a in (x_in, x))
+        value = dot_tn(act_all[l], g_rows) if kind == 2 else dot_tn(x_rows, (gg_all, gu_all)[kind][l])
+        for q in range(parts):
+            i = kind * parts + q
+            cols = gate[q].shape[2]
+            here = slice(q * cols, (q + 1) * cols)
+            grads[i][l] = (value[here] if kind == 2 else value[:, here]).astype(grads[i].dtype)
+            if grads_out[i] is not None:
+                store(i, l).start()
+        if kind == 0 and l == local - 1:
+            for copy in sent_gate():
+                copy.start()
+
+    def sent_gate():
+        return [remote(grads[1], came[0], w_send.at[0], w_recv.at[0], p.beside)] if exchange else []
 
     class Loaded(Rider):
-        partners = rider.partners
+        partners = [p.beside] if exchange else []
         after_first, after_line, after_relay, finish = (
             rider.after_first, rider.after_line, rider.after_relay, rider.finish)
 
@@ -759,9 +788,12 @@
             for i in range(3 + 3 * parts):
                 load(i).wait()
 
-    line.run(out, compute, lambda s: None, weights, Loaded())
+    pieces = [functools.partial(weights, kind, l) for kind in range(3) for l in range(local)]
+    line.run(out, compute, lambda s: None, pieces, Loaded())
+    for copy in sent_gate():
+        copy.wait()
     for i in range(3 * parts):
-        for l in range(local):
+        for l in range(local if grads_out[i] is not None else 0):
             store(i, l).wait()
 
 
@@ -773,25 +805,22 @@
     return jax.ShapeDtypeStruct(tuple(shape), dtype)
 
 
-def expert_forward(spread, call_id, out, weights, late=False, ride=None):
-    parts = -(-len(weights) // 3)
+def expert_forward(spread, call_id, out, weights, ride=None):
+    parts = len(weights) // 3
     _, local, cap, width = out.shape
     columns = sum(w.shape[2] for w in weights[:parts])
     kept = (LINE, local, 4 * cap, columns)
     outs = [struct(out.shape, BF16), struct((local, LINE, 4, cap, width), BF16), struct(kept, F32), struct(kept, F32)]
-    shapes = [w.shape for w in weights] + [weights[-1].shape] * late
-    outs += [struct(weights[-1].shape, BF16)] * late
-    scratch = [pltpu.VMEM(shape, BF16) for shape in shapes] + Line.scratch(local, width)
+    scratch = [pltpu.VMEM(w.shape, BF16) for w in weights] + Line.scratch(local, width)
     scratch += [pltpu.VMEM(kept, F32), pltpu.VMEM(kept, F32), dma(3, LINE), dma(3 * parts)]
     more = ride or ()
     count = LINE * spread
     if ride:
         outs += [struct((count * s.shape[1], s.shape[2]), BF16) for s in ride[3:6]]
         outs += [struct(w.shape, BF16) for w in ride[6:]]
-    if late:
-        scratch += WeightRider.scratch(count if ride else 0)
+        scratch += WeightRider.scratch(count)
     return pl.pallas_call(
-        functools.partial(expert_forward_kernel, spread, parts, int(late), ride is not None),
+        functools.partial(expert_forward_kernel, spread, parts, ride is not None),
         out_shape=outs,
         in_specs=[VMEM] + [ANY] * (len(weights) + len(more)),
         out_specs=[VMEM] + [ANY] * (len(outs) - 1),
@@ -801,31 +830,34 @@
     )(out, *weights, *more)
 
 
-def expert_backward(spread, call_id, out, kept, weights, ride=None):
+def expert_backward(spread, call_id, out, kept, weights, exchange=False, ride=None):
     parts = len(weights) // 3
     _, local, cap, width = out.shape
     columns = sum(w.shape[2] for w in weights[:parts])
     loads = list(kept) + list(weights)
     grads = [(w.shape, F32 if i % parts == 0 else BF16) for i, w in enumerate(weights)]
     wide = pltpu.VMEM((local, LINE * 4 * cap, columns), BF16)
-    outs = [struct(out.shape, BF16)] + [struct(*g) for g in grads]
+    outs = [struct(out.shape, BF16)] + [struct(*g) for i, g in enumerate(grads) if not exchange or i != 1]
+    if exchange:
+        outs.append(struct(*grads[1]))
+    specs = [VMEM] + [ANY] * len(grads)
     scratch = [pltpu.VMEM(a.shape, a.dtype) for a in loads] + Line.scratch(local, width)
-    scratch += [wide] * 3 + [pltpu.VMEM(*g) for g in grads] + [dma(len(loads)), dma(len(grads), local)]
-    more = ()
+    scratch += [wide] * 3 + [pltpu.VMEM(*g) for g in grads] + [dma(len(loads)), dma(len(grads), local), dma(1), dma(1)]
+    more = ride or ()
     if ride:
-        more = ride
         depths = [g.shape[0] // (LINE * spread) for g in ride[:2]]
         outs.append(struct((LINE, spread, sum(depths) // 2, width // 2), F32))
         outs += [struct(g.shape, BF16) for g in ride[2:]]
+        specs += [VMEM, ANY, ANY]
         scratch += GradientRider.scratch(spread, depths, width)
     return pl.pallas_call(
-        functools.partial(expert_backward_kernel, spread, parts, ride is not None),
+        functools.partial(expert_backward_kernel, spread, parts, int(exchange), ride is not None),
         out_shape=outs,
         in_specs=[VMEM] + [ANY] * (len(loads) + len(more)),
-        out_specs=[VMEM] + [ANY] * len(grads) + ([VMEM] + [ANY] * 3 if ride else []),
+        out_specs=specs,
         scratch_shapes=scratch,
         compiler_params=remote_params(call_id),
-        cost_estimate=pl.CostEstimate(flops=2 * 10**10, bytes_accessed=2 * 10**8, transcendentals=0),
+        cost_estimate=pl.CostEstimate(flops=4 * 10**10, bytes_accessed=2 * 10**8, transcendentals=0),
     )(out, *loads, *more)
 
 
@@ -850,9 +882,7 @@
     return parts
 
 
-def pair_sum(parts, axis, spread, came=None):
-    if came is not None:
-        return parts[0] + came.astype(F32)
+def pair_sum(parts, axis, spread):
     if len(parts) == 1 and spread > 1:
         parts = jnp.split(parts[0], spread, axis=axis)
     total = parts[0]
@@ -1026,20 +1056,15 @@
 
 
 class WeightRider:
-    def __init__(self, place, down, given, whole, sems):
-        self.p, self.quarters = place, given[:3]
-        self.own, self.other = [down[0]] + list(given[6:]), [down[1]] + list(whole[3:])
-        self.w_send, self.w_recv, *more = sems
-        self.spread = None
-        if given:
-            shards = [ref.at[1] for ref in given[3:6]]
-            self.x_send, self.x_recv, *more = more
-            self.spread = Spread(place, self.quarters, shards, whole[:3], more)
+    def __init__(self, place, given, whole, sems):
+        self.p, self.quarters, self.own, self.other = place, given[:3], given[6:], whole[3:]
+        self.w_send, self.w_recv, self.x_send, self.x_recv, *more = sems
+        self.spread = Spread(place, self.quarters, [ref.at[1] for ref in given[3:6]], whole[:3], more)
         self.partners = [place.beside]
 
     @staticmethod
     def scratch(count):
-        return [dma(3), dma(3)] + ([dma(LINE, 3), dma(LINE, 3)] + Spread.scratch(count) if count else [])
+        return [dma(3), dma(3), dma(LINE, 3), dma(LINE, 3)] + Spread.scratch(count)
 
     def place_of(self, t):
         return t * self.p.spread + self.p.f
@@ -1054,13 +1079,7 @@
     def weight(self, i):
         return remote(self.own[i], self.other[i], self.w_send.at[i], self.w_recv.at[i], self.p.beside)
 
-    def ready(self):
-        self.weight(0).wait_recv()
-
     def begin(self):
-        self.weight(0).start()
-        if not self.spread:
-            return
         self.spread.own_shard()
 
         def body(t):
@@ -1072,7 +1091,7 @@
                 self.spread.push(self.place_of(t), [q.at[t, 0] for q in self.quarters])
 
         along(self.p, body)
-        for i in (1, 2):
+        for i in range(3):
             self.weight(i).start()
 
     def after_first(self):
@@ -1085,20 +1104,15 @@
                 self.x_copy(kind, t, s).wait_recv()
             self.spread.push(s, [self.spread.mine(kind, s) for kind in range(3)], here=False)
 
-        if self.spread:
-            along(self.p, body)
+        along(self.p, body)
 
     def after_relay(self):
-        if self.spread:
-            along(self.p, lambda t: self.spread.across(self.place_of(t)), start=1)
-            along(self.p, lambda t: self.spread.across(self.beside_of(t)))
+        along(self.p, lambda t: self.spread.across(self.place_of(t)), start=1)
+        along(self.p, lambda t: self.spread.across(self.beside_of(t)))
 
     def finish(self):
-        self.weight(0).wait_send()
-        if not self.spread:
-            return
         self.spread.finish_own()
-        for i in (1, 2):
+        for i in range(3):
             self.weight(i).wait()
 
         def line(t, carry):
@@ -1111,14 +1125,37 @@
         lax.fori_loop(0, LINE, line, 0)
 
 
-def dense_gather_kernel(spread, qkv, out, small, routes, gate, *refs):
+def dense_gather_kernel(spread, qkv, out, small, routes, *refs):
     p = Place(spread)
-    whole, quarters1, (routes_all, partner), quarters0, sems0, sems1, (r_send, r_recv, w_send, w_recv), spread_sems = split(
-        refs, 3, 3, 2, 3, 4, 4, 4)
+    wide, whole, quarters1, (routes_all,), own, partner, quarters0, loaded, rounded, rest = split(refs, 3, 3, 3, 1, 6, 2, 3, 3, 3)
+    sems0, sems1, (r_send, r_recv, w_send, w_recv, load_sem, own_sem), spread_sems = split(rest, 4, 4, 6)
     shards0, shards1 = ([ref.at[l] for ref in (qkv, out, small)] for l in (0, 1))
     line0 = LineGather(p, True, shards0, quarters0, sems0)
     line1 = LineGather(p, False, shards1, quarters1, sems1)
     spreading = Spread(p, quarters0, shards0, whole, spread_sems)
+
+    def load(l, kind):
+        return pltpu.make_async_copy(wide[kind].at[l], loaded[kind].at[l], load_sem.at[l, kind])
+
+    def store(l, kind):
+        return pltpu.make_async_copy(rounded[kind].at[l], own[3 * l + kind], own_sem.at[l, kind])
+
+    def weight(kind):
+        return remote(rounded[kind].at[0], partner[kind], w_send.at[kind], w_recv.at[kind], p.beside)
+
+    def round_weights(l, kind):
+        load(l, kind).wait()
+
+        def one(i, carry):
+            rounded[kind][l, i] = loaded[kind][l, i].astype(BF16)
+            return carry
+
+        lax.fori_loop(0, rounded[kind].shape[1], one, 0)
+        store(l, kind).start()
+
+    for l in (0, 1):
+        for kind in range(3):
+            load(l, kind).start()
     greet(p.mates[1:] + [p.beside], p)
 
     def route_copy(i, row):
@@ -1127,51 +1164,56 @@
     def push(t, f):
         spreading.push(t * spread + f, [q.at[t, f] for q in quarters0])
 
-    weight = remote(gate, partner, w_send.at[0], w_recv.at[0], p.beside)
     line0.begin()
-    weight.start()
+    for kind in (0, 1):
+        round_weights(0, kind)
+        weight(kind).start()
     routes_all[p.e] = routes[...]
     for i in (1, 2, 3):
         route_copy(i, p.e).start()
     spreading.own_shard()
     line0.beside(push)
     line1.begin()
-
-    def step(k, carry):
-        line0.step(k, push)
-        line1.step(k, lambda t, f: None)
-        return carry
-
-    lax.fori_loop(1, LINE, step, 0)
+    lax.fori_loop(1, LINE, lambda k, carry: (line0.step(k, push), carry)[1], 0)
+    round_weights(0, 2)
+    lax.fori_loop(1, LINE, lambda k, carry: (line1.step(k, lambda t, f: None), carry)[1], 0)
+    for kind in range(3):
+        round_weights(1, kind)
     along(p, lambda t: spreading.across(t * spread + p.f), start=1)
     along(p, lambda t: spreading.across(t * spread + 1 - p.f))
     spreading.finish_own()
     lax.fori_loop(0, LINE * spread, lambda s, carry: (spreading.finish_shard(s), carry)[1], 0)
     line0.finish()
     line1.finish()
-    weight.wait()
+    for l in (0, 1):
+        for kind in range(3):
+            store(l, kind).wait()
+    for kind in (0, 1):
+        weight(kind).wait()
     for i in (1, 2, 3):
         route_copy(i, p.e).wait_send()
         route_copy(i, p.mates[i][1]).wait_recv()
 
 
-def dense_gather(spread, call_id, arrays, routes, gate):
+def dense_gather(spread, call_id, arrays, routes, wide):
     count = spread * LINE
     shards = [a.shape[1:] for a in arrays]
     pairs, single = LineGather.shapes(shards, 2), LineGather.shapes(shards, 1)
     outs = [struct((count * rows, width), BF16) for rows, width in shards]
     outs += [struct(q, BF16) for q in single] + [struct((4,) + routes.shape, routes.dtype)]
-    outs.append(struct(gate.shape, BF16))
-    scratch = [pltpu.VMEM(q, BF16) for q in pairs] + LineGather.scratch(2) + LineGather.scratch(1)
-    scratch += [dma(4), dma(4), dma(1), dma(1)]
+    outs += [struct(w.shape[1:], BF16) for w in wide] * 2 + [struct(w.shape[1:], BF16) for w in wide[:2]]
+    scratch = [pltpu.VMEM(q, BF16) for q in pairs] + [pltpu.VMEM(w.shape, F32) for w in wide]
+    scratch += [pltpu.VMEM(w.shape, BF16) for w in wide] + LineGather.scratch(2) + LineGather.scratch(1)
+    scratch += [dma(4), dma(4), dma(2), dma(2), dma(2, 3), dma(2, 3)]
     return pl.pallas_call(
         functools.partial(dense_gather_kernel, spread),
         out_shape=outs,
-        in_specs=[VMEM] * 4 + [ANY],
-        out_specs=[ANY] * 3 + [VMEM] * 4 + [ANY],
+        in_specs=[VMEM] * 4 + [ANY] * 3,
+        out_specs=[ANY] * 3 + [VMEM] * 4 + [ANY] * 8,
         scratch_shapes=scratch + Spread.scratch(count),
         compiler_params=remote_params(call_id),
-    )(*arrays, routes, gate)
+        cost_estimate=pl.CostEstimate(flops=10**10, bytes_accessed=10**8, transcendentals=0),
+    )(*arrays, routes, *wide)
 
 
 class Halve:
@@ -1268,18 +1310,17 @@
         self.own, self.other = given[2:], outs[1:]
         self.p = place
         self.w_send, self.w_recv = scratch[9:]
-        self.partners = [place.beside]
 
     @staticmethod
     def scratch(spread, depths, width):
-        return Halve.scratch(spread, depths, width) + [dma(3), dma(3)]
+        return Halve.scratch(spread, depths, width) + [dma(2), dma(2)]
 
     def weight(self, i):
         return remote(self.own[i], self.other[i], self.w_send.at[i], self.w_recv.at[i], self.p.beside)
 
     def begin(self):
         self.halve.begin()
-        for i in range(3):
+        for i in range(2):
             self.weight(i).start()
 
     def after_first(self):
@@ -1293,7 +1334,7 @@
 
     def finish(self):
         self.halve.finish()
-        for i in range(3):
+        for i in range(2):
             self.weight(i).wait()
 
 
@@ -1341,12 +1382,10 @@
     def relay(self, kind):
         p = self.p
 
-        @pl.when(jnp.logical_and(p.above, p.below))
+        @pl.when(p.inside)
         def _():
-            up = jnp.where(p.t == 1, 1, 0)
-            ahead = 2 * up - 1
-            t = {"near": p.t + ahead, "far": p.t + 2 * ahead, "back": p.t - ahead}[kind]
-            way = 1 - up if kind == "back" else up
+            t = {"near": p.t + p.ahead, "far": p.t + 2 * p.ahead, "back": p.t - p.ahead}[kind]
+            way = 1 - p.up if kind == "back" else p.up
             self.z_copy(way, t).wait_recv()
             self.stage[t] = (self.quarter[t] + self.came[way, t].astype(F32)).astype(BF16)
             self.z_copy(way, t).start()
@@ -1447,16 +1486,19 @@
         self.last(1 - self.p.c).wait_recv()
 
 
-def dense_reduce_kernel(spread, depths, small0, small1, res, qkv0, out0, quarter1, small_sum, *refs):
+def dense_reduce_kernel(spread, depths, small0, small1, res, qkv0, out0, quarter1, up0, down0, small_sum, *refs):
     p = Place(spread)
-    sums, (small, mine0, mine1), halve_refs, line0, line1, small_refs = split(refs, 2, 3, 9, 10, 10)
+    sums, came, (small, mine0, mine1), (w_send, w_recv), halve_refs, line0, line1, small_refs = split(refs, 2, 2, 3, 2, 9, 10, 10)
     sums0, sums1 = ([ref.at[l] for ref in sums] for l in (0, 1))
     halve = Halve(p, (qkv0, out0), mine0, halve_refs)
     sum0 = LineSum(p, depths, mine0, sums0, line0)
     sum1 = LineSum(p, depths, mine1, sums1, line1)
     little = SmallSum(p, small, small_sum, small_refs)
+    weights = [remote(w, came[i], w_send.at[i], w_recv.at[i], p.beside) for i, w in enumerate((up0, down0))]
     greet([p.sibling, p.across, p.beside, little.far], p)
     halve.begin()
+    for copy in weights:
+        copy.start()
     rows = small0.shape[0]
     small[0:rows, :] = small0[...]
     small[rows : 2 * rows, :] = small1[...]
@@ -1495,24 +1537,28 @@
     halve.finish()
     little.finish()
     sum0.finish()
-
-
-def dense_reduce(spread, call_id, smalls, grads0, quarter1):
+    for copy in weights:
+        copy.wait()
+
+
+def dense_reduce(spread, call_id, smalls, grads0, quarter1, weights0):
     count = LINE * spread
     depths = [g.shape[0] // count for g in grads0]
     width = grads0[0].shape[1]
     small = (2 * smalls[0].shape[0] + 16, width)
     line = LineSum.scratch(spread, depths, width)
     mine = pltpu.VMEM(quarter1.shape, F32)
-    scratch = [pltpu.VMEM(small, F32), mine, mine] + Halve.scratch(spread, depths, width) + line + line
+    scratch = [pltpu.VMEM(small, F32), mine, mine, dma(2), dma(2)] + Halve.scratch(spread, depths, width) + line + line
     return pl.pallas_call(
         functools.partial(dense_reduce_kernel, spread, depths),
-        out_shape=[struct(small, F32)] + [struct((2, depth, width), F32) for depth in depths],
-        in_specs=[VMEM] * 3 + [ANY, ANY, VMEM],
-        out_specs=[VMEM] * 3,
+        out_shape=[struct(small, F32)] + [struct((2, depth, width), F32) for depth in depths]
+        + [struct(w.shape, BF16) for w in weights0],
+        in_specs=[VMEM] * 3 + [ANY, ANY, VMEM, ANY, ANY],
+        out_specs=[VMEM] * 3 + [ANY] * 2,
         scratch_shapes=scratch + SmallSum.scratch(*small),
         compiler_params=remote_params(call_id),
-    )(*smalls, *grads0, quarter1)
+        cost_estimate=pl.CostEstimate(flops=2 * 10**10, bytes_accessed=2 * 10**8, transcendentals=0),
+    )(*smalls, *grads0, quarter1, *weights0)
 
 
 def per_device(
@@ -1527,16 +1573,9 @@
     experts = local * owners
     layers = routes.shape[0]
     slots = experts * CAP
-    place = lax.axis_index("expert")
-
-    my_place = jnp.sum(jnp.where(jnp.arange(owners) == place, block_perm[0], 0))
-    lengths = lax.dynamic_index_in_dim(seq_lengths[0], place, 0, keepdims=False)
-    order = jnp.arange(lengths.shape[0])
-    ends = jnp.sum(jnp.where(order[:, None] <= order[None, :], lengths[:, None], 0), axis=0)
-    doc = jnp.sum((jnp.arange(rows)[:, None] >= ends[None, :]).astype(jnp.int32), axis=1)
-    doc_col, doc_row = doc[:, None], doc[None, :]
-
-    own = [[w[l].astype(BF16) for w in (w_gate, w_up, w_down)] for l in range(layers)]
+
+    packed_routes = jnp.zeros((8, -(-rows // 128) * 128), jnp.int32).at[: 2 * layers, :rows].set(
+        jnp.swapaxes(routes, 1, 2).reshape(2 * layers, rows))
 
     depth = w_out.shape[1]
     small = jnp.concatenate(
@@ -1550,58 +1589,52 @@
     out_rows = w_out.astype(BF16)
     in_kernels = spread == 2 and owners == 4 and qkv_t.shape[1] % 32 == 0 and depth % 32 == 0
     if in_kernels:
-        packed_routes = jnp.zeros((8, 256), jnp.int32).at[: 2 * layers, :rows].set(
-            jnp.swapaxes(routes, 1, 2).reshape(2 * layers, rows))
-        *gathered, routes_all, gate = dense_gather(spread, 4, (qkv_t, out_rows, small), packed_routes, own[0][0])
-        up_own, gate = lax.optimization_barrier((own[0][1], gate))
-        weights = [[own[0][0], gate, up_own, from_partner(up_own, 1, spread, LINE), own[0][2]]]
+        *gathered, routes_all, g0, u0, d0, g1, u1, d1, gate, up = dense_gather(
+            spread, 4, (qkv_t, out_rows, small), packed_routes, (w_gate, w_up, w_down))
+        weights = [[g0, gate, u0, up, d0, from_partner(d0, 1, spread, LINE)]]
         dense = [(gathered[2], gathered[0], gathered[1])]
-        picked = lax.dynamic_index_in_dim(routes_all, my_place, 0, keepdims=False)
-        my_routes = jnp.swapaxes(picked[: 2 * layers, :rows].reshape(layers, 2, rows), 1, 2)
     else:
-        weights = [
-            [part for w, axis in zip(own[l], (2, 2, 1)) for part in pair_weights(w, axis, spread)] for l in range(layers)]
-        all_routes = lax.all_gather(routes, "expert", axis=0)
-        my_routes = lax.dynamic_index_in_dim(all_routes, my_place, 0, keepdims=False)
+        weights = []
+        for l in range(layers):
+            own = [(w_gate[l].astype(BF16), 2), (w_up[l].astype(BF16), 2), (w_down[l].astype(BF16), 1)]
+            weights.append([part for w, axis in own for part in pair_weights(w, axis, spread)])
+        routes_all = lax.all_gather(packed_routes, "expert", axis=0)
         qkv_all = lax.all_gather(qkv_t, "dp", axis=1, tiled=True)
         out_all = lax.all_gather(out_rows, "dp", axis=1, tiled=True)
         small_all = lax.all_gather(small, "dp", axis=1, tiled=True)
         dense = [(small_all[l], qkv_all[l], out_all[l]) for l in range(layers)]
 
-    w_res = jnp.zeros((128, 128), F32).at[: w_residual.shape[0], : w_residual.shape[1]].set(w_residual)
-
     cols = ((rows, width), F32)
     attention = [((rows, width), BF16), ((rows, 3 * width), BF16), ((HEADS, rows, rows), F32), ((rows, width), BF16)]
+    residual = ((128, 128), F32)
     per_token, sent = ((rows, 128), F32), ((slots, width), BF16)
 
     def group(array):
         return array.reshape(owners, local, CAP, width)
 
     attn_in0, qkv0, probs0, attn0, mid0, logits0, stat0, out = local_call(
-        first_kernel, experts, (tokens, *dense[0], doc_col, doc_row, my_routes[0]),
-        attention + [cols, per_token, per_token, sent])
-    ride = (*gathered[3:], qkv_t, out_rows, small, *own[1][:2]) if in_kernels else None
-    ret0, *kept0 = expert_forward(spread, 0, group(out), weights[0], in_kernels, ride)
+        first_kernel, experts, (tokens, *dense[0], seq_lengths, block_perm, routes_all),
+        attention + [cols, per_token, per_token, sent], scalars=(4, 5))
+    ride = (*gathered[3:], qkv_t, out_rows, small, g1, u1, d1) if in_kernels else None
+    ret0, *kept0 = expert_forward(spread, 0, group(out), weights[0], ride)
     if in_kernels:
-        kept0, down, (qkv_all, out_all, small_all), partner = kept0[:3], kept0[3], kept0[4:7], kept0[7:]
-        weights[0].append(down)
+        kept0, (qkv_all, out_all, small_all), (gate, up, down) = kept0[:3], kept0[3:6], kept0[6:]
         dense.append((small_all, qkv_all, out_all))
-        weights.append([own[1][0], partner[0], own[1][1], partner[1], own[1][2]])
+        weights.append([g1, gate, u1, up, d1, down])
     ret0 = ret0.reshape(slots, width)
     stream1, attn_in1, qkv1, probs1, attn1, mid1, stat1, out = local_call(
         middle_kernel, experts,
-        (mid0, dense[0][0], stat0, ret0, *dense[1], doc_col, doc_row, my_routes[1], logits0, w_res),
-        [cols] + attention + [cols, per_token, sent])
-    ret1, *kept1 = expert_forward(spread, 1, group(out), weights[1], in_kernels)
-    if in_kernels:
-        weights[1].append(kept1.pop())
+        (mid0, dense[0][0], stat0, ret0, *dense[1], seq_lengths, block_perm, routes_all, logits0, w_residual),
+        [cols] + attention + [cols, per_token, sent], [residual], scalars=(7, 8))
+    ret1, *kept1 = expert_forward(spread, 1, group(out), weights[1])
     ret1 = ret1.reshape(slots, width)
 
     small_grads = ((24, width), F32)
     output, g_small1, extra, out, small_grad1, res_grad = local_call(
-        turn_kernel, experts, (mid1, dense[1][0], stat1, ret1, cotangent, logits0, w_res),
-        [((rows, width), BF16), per_token, per_token, sent, small_grads, ((128, 128), F32)])
-    back, *expert_grads1 = expert_backward(spread, 2, group(out), kept1, weights[1])
+        turn_kernel, experts, (mid1, dense[1][0], stat1, ret1, cotangent, logits0, w_residual),
+        [((rows, width), BF16), per_token, per_token, sent, small_grads, residual], [residual])
+    back, *expert_grads1 = expert_backward(spread, 2, group(out), kept1, weights[1], in_kernels)
+    ride = None
     grad_type = BF16 if in_kernels else F32
     dense_grads = [((3 * width, width), grad_type), ((width, width), grad_type), small_grads]
     attention_scratch = [((rows, 3 * width), BF16), ((rows, width), BF16)]
@@ -1610,29 +1643,31 @@
         (cotangent, back.reshape(slots, width), g_small1, stat1, mid1, dense[1][0], stream1, dense[1][1], dense[1][2],
          attn_in1, qkv1, probs1, attn1, small_grad1, mid0, dense[0][0], stat0, ret0, extra),
         dense_grads + [cols, per_token, sent, small_grads], attention_scratch)
-    ride = (qkv_grad1, out_grad1, *expert_grads1[1::2]) if in_kernels else None
-    came = (None,) * 3
-    back, *expert_grads0 = expert_backward(spread, 3, group(out), kept0, weights[0], ride)
     if in_kernels:
-        expert_grads0, quarter1, came = expert_grads0[:6], expert_grads0[6], expert_grads0[7:]
+        gate1, up1, up1_sent, down1, down1_sent, gate1_came = expert_grads1
+        ride = (qkv_grad1, out_grad1, up1_sent, down1_sent)
+    back, *expert_grads0 = expert_backward(spread, 3, group(out), kept0, weights[0], in_kernels, ride)
     qkv_grad0, out_grad0, small_grad0, tokens_grad = local_call(
         last_kernel, experts,
         (grad, back.reshape(slots, width), g_small0, stat0, mid0, dense[0][0], tokens, dense[0][1], dense[0][2],
          attn_in0, qkv0, probs0, attn0, small_grad0),
         dense_grads + [cols], attention_scratch)
 
-    expert_out = []
-    for axis, at in ((2, 0), (2, 1), (1, 2)):
-        per_layer = []
-        for grads, sent_here in ((expert_grads0, None), (expert_grads1, came[at])):
-            n = len(grads) // 3
-            per_layer.append(pair_sum(grads[at * n : (at + 1) * n], axis, spread, sent_here))
-        expert_out.append(jnp.stack(per_layer))
-    gate_grad, up_grad, down_grad = expert_out
     if in_kernels:
-        packed, qkv_grad, out_grad = dense_reduce(
-            spread, 5, (small_grad0, small_grad1, res_grad), (qkv_grad0, out_grad0), quarter1)
+        gate0, up0, up0_sent, down0, down0_sent, gate0_came, quarter1, up1_came, down1_came = expert_grads0
+        packed, qkv_grad, out_grad, up0_came, down0_came = dense_reduce(
+            spread, 5, (small_grad0, small_grad1, res_grad), (qkv_grad0, out_grad0), quarter1, (up0_sent, down0_sent))
+        pairs = (
+            ((gate0, gate0_came), (gate1, gate1_came)), ((up0, up0_came), (up1, up1_came)),
+            ((down0, down0_came), (down1, down1_came)))
+        gate_grad, up_grad, down_grad = (
+            jnp.stack([mine + came.astype(F32) for mine, came in layer]) for layer in pairs)
     else:
+        gate_grad, up_grad, down_grad = (
+            jnp.stack([
+                pair_sum(grads[at * len(grads) // 3 : (at + 1) * len(grads) // 3], axis, spread)
+                for grads in (expert_grads0, expert_grads1)])
+            for axis, at in ((2, 0), (2, 1), (1, 2)))
         packed = jnp.concatenate([small_grad0, small_grad1, jnp.pad(res_grad[:16], ((0, 0), (0, width - 128)))])
         packed = lax.psum(packed, ("dp", "expert"))
         qkv_grad, out_grad = (

time: 525 us -> 491 us (0.935)
  Pallas kernels: 473 us -> 447 us
  waiting for transfers between devices: 0.01 us -> 8.6 us
  local copies, waits for them, and re-layouts: 18.3 us -> 12.5 us
    pallas_call x4, Pallas kernels: 298 us -> 273 us  [the longest x2 137 us: expert_backward(): pl.pallas_call(functools.partial(expert_backward_kernel, spread, parts, i...]
    ppermute x1, waiting for transfers between devices: 0.01 us -> 8.6 us  [from_partner(): return lax.ppermute(array, 'dp', pairs)]
    another operation x15 -> x9, other arithmetic: 14.7 us -> 10.3 us  [the longest x6 8.23 us: per_device(): jnp.stack([mine + came.astype(F32) for mine, came in layer])]
  transfers between devices with their start and end apart: 4 -> 1, of which waited for: 0 -> 1; matrix products, arithmetic and copies ran while one was open for 4% -> 0% of each run, Pallas kernels for 18% -> 2%
where the time goes in v5:
time: 491 us; the launch traced here: 485 us
  Pallas kernels  447 us (91%)
  other arithmetic  14.7 us (3%)
  local copies, waits for them, and re-layouts  12.5 us (3%)
  waiting for transfers between devices  8.6 us (2%)
    pallas_call x2, Pallas kernels, expert_backward(): pl.pallas_call(functools.partial(expert_backward_kernel, spread, parts, i...  137 us
    pallas_call x2, Pallas kernels, expert_forward(): pl.pallas_call(functools.partial(expert_forward_kernel, spread, parts, ri...  136 us
    pallas_call x1, Pallas kernels, dense_reduce(): pl.pallas_call(functools.partial(dense_reduce_kernel, spread, depths), ou...  65.3 us
    pallas_call x5, Pallas kernels, local_call(): pl.pallas_call(functools.partial(kernel, experts), out_shape=[jax.ShapeDt...  60.7 us
    pallas_call x1, Pallas kernels, dense_gather(): pl.pallas_call(functools.partial(dense_gather_kernel, spread), out_shape=...  48.2 us
  transfers between devices with their start and end apart: 1, of which 1 were waited for; matrix products, arithmetic and copies ran while one was open for 0% of the time, Pallas kernels for 2%

profile of v5, /device:TPU:0, one launch (start us, length us, event | category | flops | bytes accessed | tf_op | source)
XLA Modules:
  0.0 484.5 jit_solution(12279403586915184243)
XLA Ops:
  0.6 0.0 copy-start.11
  0.7 0.9 copy.27
  1.6 0.7 convert.21
  2.3 0.1 copy.30
  2.4 0.7 convert.23
  3.1 0.1 copy.28
  3.2 0.7 convert.24
  3.9 0.1 copy.29
  4.1 0.0 copy-start.13
  4.1 2.5 convert_bitcast_fusion.qkv.refs_9_
  6.6 0.0 copy-done.11
  6.6 0.7 convert_element_type.29.out.refs_10_
  7.3 0.0 copy-done.13
  7.3 0.6 scatter.4.routes
  7.9 0.8 concatenate.6.small.refs_11_
  8.7 48.2 %shard_map.238 = (bf16[2304,768]{1,0:T(8,128)(2,1)}, bf16[768,768]{1,0:T(8,128)(2,1)}, bf16[768,128]{1,0:T(8,128)(2,1)}, bf16[4,1,144,384]{3,2,1,0:T(8,128)(2,1)...) custom-call(bf16[2,288,768]{2,1,0:T(8,128)(2,1)} %convert_bitcast_fu, ...), custom_call_target="tpu_custom_call" | custom-call | flops 10000000000 | bytes 100000000 | tf_op jit(solution)/shard_map/pallas_call | solution.py:1208
  56.9 0.7 collective-permute-start
  57.6 10.8 %shard_map.239 = (bf16[192,768]{1,0:T(8,128)(2,1)}, bf16[192,2304]{1,0:T(8,128)(2,1)}, f32[12,192,192]{2,1,0:T(8,128)}, bf16[192,768]{1,0:T(8,128)(2,1)}, f32[19...) custom-call(bf16[192,768]{1,0:T(8,128)(2,1)} %tokens.3, ...), custom_call_target="tpu_custom_call" | custom-call | flops 10000000000 | bytes 60000000 | tf_op jit(solution)/shard_map/pallas_call | solution.py:363
  68.4 8.6 %collective-permute-done.refs_5_.refs_8_ = bf16[2,256,768]{2,1,0:T(8,128)(2,1)S(1)} collective-permute-done((bf16[2,256,768]{2,1,0:T(8,128)(2,1)}, bf16[2,256,768]{2,1,0:T(8,128)(2,1)S(1)}, u32[]{:S(2)}, u32[]{:S(2)}) %collective-permute-start) | collective-permute-done | bytes 786464 | tf_op jit(solution)/shard_map/ppermute | solution.py:868
  77.0 0.0 copy-start.14
  77.0 0.9 copy-done.14
  77.9 72.4 %shard_map.240 = (bf16[4,2,48,768]{3,2,1,0:T(8,128)(2,1)}, bf16[2,4,4,48,768]{4,3,2,1,0:T(8,128)(2,1)}, f32[4,2,192,512]{3,2,1,0:T(8,128)}, f32[4,2,192,512]{3,2...) custom-call(bf16[4,2,48,768]{3,2,1,0:T(8,128)(2,1)} %bitcast.49, ...), custom_call_target="tpu_custom_call" | custom-call | flops 20000000000 | bytes 200000000 | tf_op jit(solution)/shard_map/pallas_call | solution.py:822
  150.2 11.6 %shard_map.241 = (f32[192,768]{1,0:T(8,128)}, bf16[192,768]{1,0:T(8,128)(2,1)}, bf16[192,2304]{1,0:T(8,128)(2,1)}, f32[12,192,192]{2,1,0:T(8,128)}, bf16[192,768...) custom-call(f32[192,768]{1,0:T(8,128)} %get-tuple-element.112.mid_in.mid0.mid, ...), custom_call_target="tpu_custom_call" | custom-call | flops 10000000000 | bytes 60000000 | tf_op jit(solution)/shard_map/pallas_call | solution.py:363
  161.9 63.7 %shard_map.242 = (bf16[4,2,48,768]{3,2,1,0:T(8,128)(2,1)}, bf16[2,4,4,48,768]{4,3,2,1,0:T(8,128)(2,1)}, f32[4,2,192,512]{3,2,1,0:T(8,128)}, f32[4,2,192,512]{3,2,1,0:T(8,128)}) custom-call(bf16[4,2,48,768]{3,2,1,0:T(8,128)(2,1)} %bitcast.51, bf16[2,768,256]{2,1,0:T(8,128)(2,1)} %get-tuple-element.123.refs_12_.refs_0_.refs_3_, ...), custom_call_target="tpu_custom_call" | custom-call | flops 20000000000 | bytes 200000000 | tf_op jit(solution)/shard_map/pallas_call | solution.py:822
  225.6 5.6 %shard_map.243 = (bf16[192,768]{1,0:T(8,128)(2,1)}, f32[192,128]{1,0:T(8,128)}, f32[192,128]{1,0:T(8,128)}, bf16[384,768]{1,0:T(8,128)(2,1)}, f32[24,768]{1,0:T(8,128)}, /*index=5*/f32[128,128]{1,0:T(8,128)}) custom-call(f32[192,768]{1,0:T(8,128)} %get-tuple-element.131.mid, bf16[768,128]{1,0:T(8,128)(2,1)} %get-tuple-element.127.small, ...), custom_call_target="tpu_custom_call" | custom-call | flops 10000000000 | bytes 60000000 | tf_op jit(solution)/shard_map/pallas_call | solution.py:363
  231.2 69.8 %shard_map.244 = (bf16[4,2,48,768]{3,2,1,0:T(8,128)(2,1)}, f32[2,768,256]{2,1,0:T(8,128)}, f32[2,768,256]{2,1,0:T(8,128)}, bf16[2,768,256]{2,1,0:T(8,128)(2,1)},...) custom-call(bf16[4,2,48,768]{3,2,1,0:T(8,128)(2,1)} %bitcast.50, ...), custom_call_target="tpu_custom_call" | custom-call | flops 40000000000 | bytes 200000000 | tf_op jit(solution)/shard_map/pallas_call | solution.py:853
  301.0 17.5 %shard_map.245 = (bf16[2304,768]{1,0:T(8,128)(2,1)}, bf16[768,768]{1,0:T(8,128)(2,1)}, f32[24,768]{1,0:T(8,128)}, f32[192,768]{1,0:T(8,128)}, f32[192,128]{1,0:T...) custom-call(bf16[192,768]{1,0:T(8,128)(2,1)} %cotangent.3, bf16[384,768]{1,0:T(8,128)(2,1)} %bitcast.48, ...), custom_call_target="tpu_custom_call" | custom-call | flops 10000000000 | bytes 60000000 | tf_op jit(solution)/shard_map/pallas_call | solution.py:363
  318.5 67.0 %shard_map.246 = (bf16[4,2,48,768]{3,2,1,0:T(8,128)(2,1)}, f32[2,768,256]{2,1,0:T(8,128)}, f32[2,768,256]{2,1,0:T(8,128)}, bf16[2,768,256]{2,1,0:T(8,128)(2,1)},...) custom-call(bf16[4,2,48,768]{3,2,1,0:T(8,128)(2,1)} %bitcast.46, ...), custom_call_target="tpu_custom_call" | custom-call | flops 40000000000 | bytes 200000000 | tf_op jit(solution)/shard_map/pallas_call | solution.py:853
  385.5 15.2 %shard_map.247 = (bf16[2304,768]{1,0:T(8,128)(2,1)}, bf16[768,768]{1,0:T(8,128)(2,1)}, f32[24,768]{1,0:T(8,128)}, f32[192,768]{1,0:T(8,128)}) custom-call(f32[192,768]{1,0:T(8,128)} %get-tuple-element.152.grad_in, bf16[384,768]{1,0:T(8,128)(2,1)} %bitcast.47, f32[192,128]{1,0:T(8,128)} %get-tuple-element.162.g_small, ...), custom_call_target="tpu_custom_call" | custom-call | flops 10000000000 | bytes 60000000 | tf_op jit(solution)/shard_map/pallas_call | solution.py:363
  400.6 0.0 copy-start.3
  400.6 0.0 copy-start.9
  400.7 65.3 %shard_map.248 = (f32[64,768]{1,0:T(8,128)}, f32[2,288,768]{2,1,0:T(8,128)}, f32[2,96,768]{2,1,0:T(8,128)}, bf16[2,768,256]{2,1,0:T(8,128)(2,1)}, bf16[2,256,768]{2,1,0:T(8,128)(2,1)}) custom-call(f32[24,768]{1,0:T(8,128)} %get-tuple-element.169.small0, f32[24,768]{1,0:T(8,128)} %get-tuple-element.170.small1, f32[128,128]{1,0:T(8,128)} %get-tuple-element.171.res, ...), custom_call_target="tpu_custom_call" | custom-call | flops 20000000000 | bytes 200000000 | tf_op jit(solution)/shard_map/pallas_call | solution.py:1552
  465.9 0.8 dynamic-slice_bitcast_fusion.1
  466.8 0.6 fusion.2
  467.4 0.6 pad_maximum_fusion.3
  468.0 1.3 slice.55
  469.3 0.6 copy.31
  469.9 0.0 copy-done.3
  469.9 0.0 copy-done.9
  469.9 1.9 add_bitcast_fusion
  471.8 0.0 copy-start.4
  471.8 0.0 copy-start.5
  471.8 0.0 copy-start.8
  471.8 0.0 copy-start.10
  471.8 1.9 pad_maximum_fusion.2
  473.7 0.0 copy-done.4
  473.7 1.1 copy-done.5
  474.8 0.2 copy-done.8
  475.0 0.2 copy-done.10
  475.2 0.0 copy-start.1
  475.2 0.0 copy-start.2
  475.2 0.0 copy-start.6
  475.2 0.3 add_bitcast_fusion.3
  475.6 1.0 copy-done.1
  476.6 0.5 copy-done.2
  477.1 0.2 copy-done.6
  477.3 0.3 copy-done.7
  477.6 0.3 add_bitcast_fusion.2
  477.9 1.9 pad_maximum_fusion.1
  479.8 1.9 pad_maximum_fusion
  481.7 0.4 copy-done
  482.0 1.2 copy.34
  483.3 0.3 copy-done.12
  483.5 0.8 copy.35
  (7 shorter events, 0.0 us)
Async XLA Ops:
  0.6 5.9 %copy-start.11 = (f32[2,96,768]{2,1,0:T(8,128)S(1)}, f32[2,96,768]{2,1,0:T(8,128)}, u32[]{:S(2)}) copy-start(f32[2,96,768]{2,1,0:T(8,128)} %param.23) | copy-start | bytes 1769476
  4.1 3.2 copy-start.13
  56.9 20.1 %collective-permute-start = (bf16[2,256,768]{2,1,0:T(8,128)(2,1)}, bf16[2,256,768]{2,1,0:T(8,128)(2,1)S(1)}, u32[]{:S(2)}, u32[]{:S(2)}) collective-permute-start(bf16[2,256,768]{2,1,0:T(8,128)(2,1)} %get-tuple-element.119.refs_4_.refs_7_), channel_id=1, source_target_pairs={{4,0},{0,4},{12,8},{8,12},{20,16},{16,20},{28,24},{24,28},{5,1},{1... | collective-permute-start | bytes 2359304 | tf_op jit(solution)/shard_map/ppermute | solution.py:868
  77.0 0.9 copy-start.14
  400.6 69.2 %copy-start.3 = (f32[2,256,768]{2,1,0:T(8,128)S(1)}, f32[2,256,768]{2,1,0:T(8,128)}, u32[]{:S(2)}) copy-start(f32[2,256,768]{2,1,0:T(8,128)} %get-tuple-element.190) | copy-start | bytes 4718596
  400.6 69.2 %copy-start.9 = (bf16[2,256,768]{2,1,0:T(8,128)(2,1)S(1)}, bf16[2,256,768]{2,1,0:T(8,128)(2,1)}, u32[]{:S(2)}) copy-start(bf16[2,256,768]{2,1,0:T(8,128)(2,1)} %get-tuple-element.191) | copy-start | bytes 2359300
  471.8 2.0 copy-start.4
  471.8 3.0 copy-start.5
  471.8 3.2 copy-start.8
  471.8 3.4 copy-start.10
  475.2 1.4 copy-start.1
  475.2 1.9 copy-start.2
  475.2 2.1 copy-start.6
  475.2 2.3 copy-start.7
  479.8 2.3 copy-start
  482.0 1.5 copy-start.12

commit v6 on v5

--- a/solution.py
+++ b/solution.py
@@ -112,7 +112,7 @@
         ).astype(BF16)
         return carry
 
-    lax.fori_loop(0, 3, project, 0)
+    lax.fori_loop(0, 3, project, 0, unroll=True)
     head_dim = width // HEADS
     factor = 1.0 / head_dim**0.5
     allowed = jnp.logical_and(
@@ -140,7 +140,7 @@
         attn_ref[:, pl.ds(at, 2 * head_dim)] = jnp.where(second, mixed[1], mixed[0]).astype(BF16)
         return carry
 
-    lax.fori_loop(0, HEADS // 2, heads, 0, unroll=2)
+    lax.fori_loop(0, HEADS // 2, heads, 0, unroll=True)
     return stream + dot_nn(attn_ref[...], w_out[...])
 
 
@@ -322,7 +322,7 @@
         g_qkv[:, pl.ds(at_v, 2 * head_dim)] = jnp.where(second_half, gv[1], gv[0]).astype(BF16)
         return carry
 
-    lax.fori_loop(0, HEADS // 2, heads, 0, unroll=2)
+    lax.fori_loop(0, HEADS // 2, heads, 0, unroll=True)
 
     def weights(i, carry):
         at = pl.multiple_of(i * width, width)
@@ -387,8 +387,18 @@
         self.beside = (self.t * spread + 1 - self.f, self.e)
         self.mates = [(self.d, self.e), self.sibling, self.across, self.corner]
 
+    def block(self, i):
+        return pick(i, [e for _, e in self.mates])
+
     def on_line(self, up):
         return (self.d + self.spread * (2 * up - 1), self.e)
+
+
+def pick(index, values):
+    out = values[-1]
+    for n in range(len(values) - 2, -1, -1):
+        out = jnp.where(index == n, values[n], out)
+    return out
 
 
 def greet(always, place):
@@ -484,22 +494,23 @@
                       self.sum_recv.at[up, s, b], self.p.on_line(up))
 
     def ret_copy(self, i, to_mate=True):
-        to = self.p.mates[i]
-        row = self.p.e if to_mate else to[1]
-        return remote(self.final.at[to[1]], self.returned.at[row], self.ret_send.at[i], self.ret_recv.at[row], to)
+        to = self.p.block(i)
+        row = self.p.e if to_mate else to
+        return remote(self.final.at[to], self.returned.at[row], self.ret_send.at[i], self.ret_recv.at[row], (self.p.d, to))
 
     def send_sum(self, up, s, b, total):
         self.stage[s, :, b] = total.astype(BF16)
         self.sum_copy(up, s, b).start()
 
-    def relay(self, kind, i):
+    def relay(self, n):
         p = self.p
+        kind = pick(n, (0, 0, 1, 1, 2, 1, 2, 1, 2, 0, 2, 0))
+        b = p.block(pick(n, (0, 1, 0, 1, 0, 2, 1, 3, 2, 2, 3, 3)))
+        s = p.t + p.ahead * pick(kind, (1, 2, -1))
+        way = jnp.where(kind == 2, 1 - p.up, p.up)
 
         @pl.when(p.inside)
         def _():
-            b = p.mates[i][1]
-            s = {"near": p.t + p.ahead, "far": p.t + 2 * p.ahead, "back": p.t - p.ahead}[kind]
-            way = 1 - p.up if kind == "back" else p.up
             self.sum_copy(way, s, b).wait_recv()
             self.send_sum(way, s, b, self.part[s, :, b] + self.arrived[way, s, :, b].astype(F32))
 
@@ -581,48 +592,52 @@
 
         lax.fori_loop(0, 6, step, 0)
         rider.after_line()
-        todo = list(pieces)
-        for n, (kind, i) in enumerate((
-            ("near", 0), ("near", 1), ("far", 0), ("far", 1), ("back", 0), ("far", 2), ("back", 1), ("far", 3),
-            ("back", 2), ("near", 2), ("back", 3), ("near", 3),
-        )):
-            self.relay(kind, i)
-            if n % 2 == 1 and todo:
-                todo.pop(0)()
-        for piece in todo:
-            piece()
+
+        def passing(n, carry):
+            self.relay(n)
+            pieces(n)
+            return carry
+
+        lax.fori_loop(0, 12, passing, 0)
         rider.after_relay()
-        for i, b in enumerate(blocks):
+
+        def end(i, carry):
+            b = p.block(i)
             for up, there in ((1, p.below), (0, p.above)):
 
                 @pl.when(there)
-                def _(up=up, b=b):
+                def _(up=up):
                     self.sum_copy(up, t, b).wait_recv()
                     self.part[t, :, b] = self.part[t, :, b] + self.arrived[up, t, :, b].astype(F32)
 
-            if i:
-                self.final[b] = self.part[t, :, b].astype(BF16)
+            self.final[b] = self.part[t, :, b].astype(BF16)
+
+            @pl.when(i > 0)
+            def _():
                 self.ret_copy(i).start()
-            else:
-                self.returned[e] = self.part[t, :, e].astype(BF16)
-
-        def sent(s, carry):
-            for i in range(4):
-                for up, mine in ((0, jnp.logical_and(p.below, s >= t)), (1, jnp.logical_and(p.above, s <= t))):
-
-                    @pl.when(mine)
-                    def _(up=up, i=i):
-                        self.x_copy(up, s, i).wait_send()
-
-                @pl.when(s != t)
-                def _(i=i):
-                    self.sum_copy(0, s, i).wait_send()
+
+            return carry
+
+        lax.fori_loop(0, 4, end, 0)
+        self.returned[e] = self.final[e]
+
+        def sent(n, carry):
+            s, b = n // 4, lax.rem(n, 4)
+            for up, mine in ((0, jnp.logical_and(p.below, s >= t)), (1, jnp.logical_and(p.above, s <= t))):
+
+                @pl.when(mine)
+                def _(up=up):
+                    self.x_copy(up, s, b).wait_send()
+
+            @pl.when(s != t)
+            def _():
+                self.sum_copy(0, s, b).wait_send()
 
             return carry
 
         for i in (1, 2, 3):
             self.slot_copy(out, i).wait_send()
-        lax.fori_loop(0, LINE, sent, 0)
+        lax.fori_loop(0, 4 * LINE, sent, 0)
         rider.finish()
         for i in (1, 2, 3):
             self.ret_copy(i).wait_send()
@@ -637,10 +652,10 @@
     return out + [refs[at:]]
 
 
-def expert_forward_kernel(spread, parts, ride, out, *refs):
-    weights_in, given, outs, whole, scratch, line_refs, sems, ride_refs = split(
-        refs, 3 * parts, 9 if ride else 0, 4, 6 if ride else 0, 3 * parts, 5, 7)
-    (g_all, u_all, keep_sem, load_sem), ride_refs = ride_refs[:4], ride_refs[4:]
+def expert_forward_kernel(spread, parts, late, ride, out, *refs):
+    weights_in, given, outs, late_out, whole, scratch, line_refs, sems, ride_refs = split(
+        refs, 3 * parts, 8 if ride else 0, 4, late, 5 if ride else 0, 3 * parts, 5, 7)
+    (g_all, u_all, keep_sem, load_sem, late_sem), ride_refs = ride_refs[:5], ride_refs[5:]
     returned, x_keep, g_keep, u_keep = outs
     gate, up, down = scratch[:parts], scratch[parts : 2 * parts], scratch[2 * parts :]
     x, part, stage, arrived, final = line_refs
@@ -650,10 +665,17 @@
     rider = WeightRider(p, given, whole, ride_refs) if ride else Rider()
 
     def load(i):
-        return pltpu.make_async_copy(weights_in[i], scratch[i], load_sem.at[i])
+        given = weights_in[i].shape[0]
+        return pltpu.make_async_copy(weights_in[i], scratch[i].at[0:given], load_sem.at[i])
 
     for i in range(3 * parts):
         load(i).start()
+
+    def late_copy():
+        return remote(weights_in[-2].at[1:local], scratch[-1].at[1:local], late_sem.at[0], late_sem.at[1], p.beside)
+
+    def late_store():
+        return pltpu.make_async_copy(scratch[-1], late_out[0], late_sem.at[2])
 
     def keep_x(s):
         return pltpu.make_async_copy(x.at[:, s], x_keep.at[:, s], keep_sem.at[0, s])
@@ -691,18 +713,28 @@
         lax.fori_loop(0, local, one, 0)
 
     class Loaded(Rider):
-        partners = rider.partners
-        after_first, after_line, after_relay, finish = (
-            rider.after_first, rider.after_line, rider.after_relay, rider.finish)
+        partners = [p.beside] if late else []
+        after_first, after_line, after_relay = rider.after_first, rider.after_line, rider.after_relay
 
         def begin(self):
+            if late:
+                late_copy().start()
             rider.begin()
 
         def ready(self):
             for i in range(3 * parts):
                 load(i).wait()
-
-    line.run(out, compute, kept, (), Loaded())
+            if late:
+                late_copy().wait_recv()
+                late_store().start()
+
+        def finish(self):
+            rider.finish()
+            if late:
+                late_copy().wait_send()
+                late_store().wait()
+
+    line.run(out, compute, kept, lambda n: None, Loaded())
     for s in range(LINE):
         keep_x(s).wait()
         keep_g(s).wait()
@@ -769,7 +801,17 @@
             grads[i][l] = (value[here] if kind == 2 else value[:, here]).astype(grads[i].dtype)
             if grads_out[i] is not None:
                 store(i, l).start()
-        if kind == 0 and l == local - 1:
+
+    def pieces(n):
+        for kind in range(3):
+            at = n - 1 - 2 * local * kind
+
+            @pl.when(jnp.logical_and(lax.rem(n, 2) == 1, jnp.logical_and(at >= 0, at < 2 * local)))
+            def _(kind=kind, at=at):
+                weights(kind, at // 2)
+
+        @pl.when(n == 2 * local - 1)
+        def _():
             for copy in sent_gate():
                 copy.start()
 
@@ -788,7 +830,6 @@
             for i in range(3 + 3 * parts):
                 load(i).wait()
 
-    pieces = [functools.partial(weights, kind, l) for kind in range(3) for l in range(local)]
     line.run(out, compute, lambda s: None, pieces, Loaded())
     for copy in sent_gate():
         copy.wait()
@@ -805,14 +846,15 @@
     return jax.ShapeDtypeStruct(tuple(shape), dtype)
 
 
-def expert_forward(spread, call_id, out, weights, ride=None):
+def expert_forward(spread, call_id, out, weights, late=False, ride=None):
     parts = len(weights) // 3
     _, local, cap, width = out.shape
     columns = sum(w.shape[2] for w in weights[:parts])
     kept = (LINE, local, 4 * cap, columns)
     outs = [struct(out.shape, BF16), struct((local, LINE, 4, cap, width), BF16), struct(kept, F32), struct(kept, F32)]
-    scratch = [pltpu.VMEM(w.shape, BF16) for w in weights] + Line.scratch(local, width)
-    scratch += [pltpu.VMEM(kept, F32), pltpu.VMEM(kept, F32), dma(3, LINE), dma(3 * parts)]
+    outs += [struct(weights[-2].shape, BF16)] * late
+    scratch = [pltpu.VMEM((local,) + w.shape[1:], BF16) for w in weights] + Line.scratch(local, width)
+    scratch += [pltpu.VMEM(kept, F32), pltpu.VMEM(kept, F32), dma(3, LINE), dma(3 * parts), dma(3)]
     more = ride or ()
     count = LINE * spread
     if ride:
@@ -820,7 +862,7 @@
         outs += [struct(w.shape, BF16) for w in ride[6:]]
         scratch += WeightRider.scratch(count)
     return pl.pallas_call(
-        functools.partial(expert_forward_kernel, spread, parts, ride is not None),
+        functools.partial(expert_forward_kernel, spread, parts, int(late), ride is not None),
         out_shape=outs,
         in_specs=[VMEM] + [ANY] * (len(weights) + len(more)),
         out_specs=[VMEM] + [ANY] * (len(outs) - 1),
@@ -1060,11 +1102,10 @@
         self.p, self.quarters, self.own, self.other = place, given[:3], given[6:], whole[3:]
         self.w_send, self.w_recv, self.x_send, self.x_recv, *more = sems
         self.spread = Spread(place, self.quarters, [ref.at[1] for ref in given[3:6]], whole[:3], more)
-        self.partners = [place.beside]
 
     @staticmethod
     def scratch(count):
-        return [dma(3), dma(3), dma(LINE, 3), dma(LINE, 3)] + Spread.scratch(count)
+        return [dma(2), dma(2), dma(LINE, 3), dma(LINE, 3)] + Spread.scratch(count)
 
     def place_of(self, t):
         return t * self.p.spread + self.p.f
@@ -1091,7 +1132,7 @@
                 self.spread.push(self.place_of(t), [q.at[t, 0] for q in self.quarters])
 
         along(self.p, body)
-        for i in range(3):
+        for i in range(2):
             self.weight(i).start()
 
     def after_first(self):
@@ -1112,7 +1153,7 @@
 
     def finish(self):
         self.spread.finish_own()
-        for i in range(3):
+        for i in range(2):
             self.weight(i).wait()
 
         def line(t, carry):
@@ -1127,8 +1168,9 @@
 
 def dense_gather_kernel(spread, qkv, out, small, routes, *refs):
     p = Place(spread)
-    wide, whole, quarters1, (routes_all,), own, partner, quarters0, loaded, rounded, rest = split(refs, 3, 3, 3, 1, 6, 2, 3, 3, 3)
-    sems0, sems1, (r_send, r_recv, w_send, w_recv, load_sem, own_sem), spread_sems = split(rest, 4, 4, 6)
+    wide, whole, quarters1, (routes_all,), own, firsts, partner, quarters0, loaded, rounded, rest = split(
+        refs, 3, 3, 3, 1, 6, 2, 2, 3, 3, 3)
+    sems0, sems1, (r_send, r_recv, w_send, w_recv, load_sem, own_sem, first_sem), spread_sems = split(rest, 4, 4, 7)
     shards0, shards1 = ([ref.at[l] for ref in (qkv, out, small)] for l in (0, 1))
     line0 = LineGather(p, True, shards0, quarters0, sems0)
     line1 = LineGather(p, False, shards1, quarters1, sems1)
@@ -1140,6 +1182,9 @@
     def store(l, kind):
         return pltpu.make_async_copy(rounded[kind].at[l], own[3 * l + kind], own_sem.at[l, kind])
 
+    def first(l):
+        return pltpu.make_async_copy(rounded[2].at[l, 0:1], firsts[l], first_sem.at[l])
+
     def weight(kind):
         return remote(rounded[kind].at[0], partner[kind], w_send.at[kind], w_recv.at[kind], p.beside)
 
@@ -1152,6 +1197,8 @@
 
         lax.fori_loop(0, rounded[kind].shape[1], one, 0)
         store(l, kind).start()
+        if kind == 2:
+            first(l).start()
 
     for l in (0, 1):
         for kind in range(3):
@@ -1188,6 +1235,7 @@
     for l in (0, 1):
         for kind in range(3):
             store(l, kind).wait()
+        first(l).wait()
     for kind in (0, 1):
         weight(kind).wait()
     for i in (1, 2, 3):
@@ -1201,15 +1249,16 @@
     pairs, single = LineGather.shapes(shards, 2), LineGather.shapes(shards, 1)
     outs = [struct((count * rows, width), BF16) for rows, width in shards]
     outs += [struct(q, BF16) for q in single] + [struct((4,) + routes.shape, routes.dtype)]
-    outs += [struct(w.shape[1:], BF16) for w in wide] * 2 + [struct(w.shape[1:], BF16) for w in wide[:2]]
+    outs += [struct(w.shape[1:], BF16) for w in wide] * 2 + [struct((1,) + wide[2].shape[2:], BF16)] * 2
+    outs += [struct(w.shape[1:], BF16) for w in wide[:2]]
     scratch = [pltpu.VMEM(q, BF16) for q in pairs] + [pltpu.VMEM(w.shape, F32) for w in wide]
     scratch += [pltpu.VMEM(w.shape, BF16) for w in wide] + LineGather.scratch(2) + LineGather.scratch(1)
-    scratch += [dma(4), dma(4), dma(2), dma(2), dma(2, 3), dma(2, 3)]
+    scratch += [dma(4), dma(4), dma(2), dma(2), dma(2, 3), dma(2, 3), dma(2)]
     return pl.pallas_call(
         functools.partial(dense_gather_kernel, spread),
         out_shape=outs,
         in_specs=[VMEM] * 4 + [ANY] * 3,
-        out_specs=[ANY] * 3 + [VMEM] * 4 + [ANY] * 8,
+        out_specs=[ANY] * 3 + [VMEM] * 4 + [ANY] * 10,
         scratch_shapes=scratch + Spread.scratch(count),
         compiler_params=remote_params(call_id),
         cost_estimate=pl.CostEstimate(flops=10**10, bytes_accessed=10**8, transcendentals=0),
@@ -1589,9 +1638,9 @@
     out_rows = w_out.astype(BF16)
     in_kernels = spread == 2 and owners == 4 and qkv_t.shape[1] % 32 == 0 and depth % 32 == 0
     if in_kernels:
-        *gathered, routes_all, g0, u0, d0, g1, u1, d1, gate, up = dense_gather(
+        *gathered, routes_all, g0, u0, d0, g1, u1, d1, first0, first1, gate, up = dense_gather(
             spread, 4, (qkv_t, out_rows, small), packed_routes, (w_gate, w_up, w_down))
-        weights = [[g0, gate, u0, up, d0, from_partner(d0, 1, spread, LINE)]]
+        weights = [[g0, gate, u0, up, d0, from_partner(first0, 1, spread, LINE)]]
         dense = [(gathered[2], gathered[0], gathered[1])]
     else:
         weights = []
@@ -1615,18 +1664,21 @@
     attn_in0, qkv0, probs0, attn0, mid0, logits0, stat0, out = local_call(
         first_kernel, experts, (tokens, *dense[0], seq_lengths, block_perm, routes_all),
         attention + [cols, per_token, per_token, sent], scalars=(4, 5))
-    ride = (*gathered[3:], qkv_t, out_rows, small, g1, u1, d1) if in_kernels else None
-    ret0, *kept0 = expert_forward(spread, 0, group(out), weights[0], ride)
+    ride = (*gathered[3:], qkv_t, out_rows, small, g1, u1) if in_kernels else None
+    ret0, *kept0 = expert_forward(spread, 0, group(out), weights[0], in_kernels, ride)
     if in_kernels:
-        kept0, (qkv_all, out_all, small_all), (gate, up, down) = kept0[:3], kept0[3:6], kept0[6:]
+        kept0, weights[0][5], (qkv_all, out_all, small_all), (gate, up) = kept0[:3], kept0[3], kept0[4:7], kept0[7:]
         dense.append((small_all, qkv_all, out_all))
-        weights.append([g1, gate, u1, up, d1, down])
+        first1, ret0 = lax.optimization_barrier((first1, ret0))
+        weights.append([g1, gate, u1, up, d1, from_partner(first1, 1, spread, LINE)])
     ret0 = ret0.reshape(slots, width)
     stream1, attn_in1, qkv1, probs1, attn1, mid1, stat1, out = local_call(
         middle_kernel, experts,
         (mid0, dense[0][0], stat0, ret0, *dense[1], seq_lengths, block_perm, routes_all, logits0, w_residual),
         [cols] + attention + [cols, per_token, sent], [residual], scalars=(7, 8))
-    ret1, *kept1 = expert_forward(spread, 1, group(out), weights[1])
+    ret1, *kept1 = expert_forward(spread, 1, group(out), weights[1], in_kernels)
+    if in_kernels:
+        weights[1][5] = kept1.pop()
     ret1 = ret1.reshape(slots, width)
 
     small_grads = ((24, width), F32)

time: 491 us -> 484 us (0.986); the launches traced: 485 us -> 483 us
  waiting for transfers between devices: 8.6 us -> 3.4 us
    pallas_call x2, Pallas kernels: 137 us -> 144 us  [expert_backward(): pl.pallas_call(functools.partial(expert_backward_kernel, spread, parts, i...]
    pallas_call x5, Pallas kernels: 60.7 us -> 55.4 us  [local_call(): pl.pallas_call(functools.partial(kernel, experts), out_shape=[jax.ShapeDt...]
    ppermute x1 -> x2, waiting for transfers between devices: 8.6 us -> 3.4 us  [from_partner(): return lax.ppermute(array, 'dp', pairs)]
  transfers between devices with their start and end apart: 1 -> 2, of which waited for: 1 -> 2; matrix products, arithmetic and copies ran while one was open for 0% -> 0% of each run, Pallas kernels for 2% -> 4%
where the time goes in v6:
time: 484 us; the launch traced here: 483 us
  Pallas kernels  449 us (93%)
  other arithmetic  14.7 us (3%)
  local copies, waits for them, and re-layouts  13.2 us (3%)
    pallas_call x2, Pallas kernels, expert_backward(): pl.pallas_call(functools.partial(expert_backward_kernel, spread, parts, i...  144 us
    pallas_call x2, Pallas kernels, expert_forward(): pl.pallas_call(functools.partial(expert_forward_kernel, spread, parts, in...  133 us
    pallas_call x1, Pallas kernels, dense_reduce(): pl.pallas_call(functools.partial(dense_reduce_kernel, spread, depths), ou...  69.4 us
    pallas_call x5, Pallas kernels, local_call(): pl.pallas_call(functools.partial(kernel, experts), out_shape=[jax.ShapeDt...  55.4 us
    pallas_call x1, Pallas kernels, dense_gather(): pl.pallas_call(functools.partial(dense_gather_kernel, spread), out_shape=...  48.2 us
  transfers between devices with their start and end apart: 2, of which 2 were waited for; matrix products, arithmetic and copies ran while one was open for 0% of the time, Pallas kernels for 4%

profile of v6, /device:TPU:0, one launch (start us, length us, event | category | flops | bytes accessed | tf_op | source)
XLA Modules:
  0.0 483.2 jit_solution(17335498461452495729)
XLA Ops:
  0.6 0.0 copy-start.11
  0.7 0.9 copy.27
  1.6 0.7 convert.21
  2.3 0.1 copy.30
  2.4 0.7 convert.23
  3.1 0.1 copy.28
  3.2 0.7 convert.24
  3.9 0.1 copy.29
  4.1 0.0 copy-start.13
  4.1 2.5 convert_bitcast_fusion.qkv.refs_9_
  6.6 0.0 copy-done.11
  6.6 0.7 convert_element_type.29.out.refs_10_
  7.3 0.0 copy-done.13
  7.3 0.6 scatter.4.routes
  7.9 0.8 concatenate.6.small.refs_11_
  8.7 48.2 %shard_map.238 = (bf16[2304,768]{1,0:T(8,128)(2,1)}, bf16[768,768]{1,0:T(8,128)(2,1)}, bf16[768,128]{1,0:T(8,128)(2,1)}, bf16[4,1,144,384]{3,2,1,0:T(8,128)(2,1)...) custom-call(bf16[2,288,768]{2,1,0:T(8,128)(2,1)} %convert_bitcast_fu, ...), custom_call_target="tpu_custom_call" | custom-call | flops 10000000000 | bytes 100000000 | tf_op jit(solution)/shard_map/pallas_call | solution.py:1257
  56.9 0.7 collective-permute-start
  57.6 8.6 %shard_map.239 = (bf16[192,768]{1,0:T(8,128)(2,1)}, bf16[192,2304]{1,0:T(8,128)(2,1)}, f32[12,192,192]{2,1,0:T(8,128)}, bf16[192,768]{1,0:T(8,128)(2,1)}, f32[19...) custom-call(bf16[192,768]{1,0:T(8,128)(2,1)} %tokens.3, ...), custom_call_target="tpu_custom_call" | custom-call | flops 10000000000 | bytes 60000000 | tf_op jit(solution)/shard_map/pallas_call | solution.py:363
  66.3 2.3 collective-permute-done.refs_5_
  68.6 0.0 copy-start.15
  68.6 0.7 copy-done.15
  69.3 0.0 copy-start.14
  69.3 67.9 %shard_map.240 = (bf16[4,2,48,768]{3,2,1,0:T(8,128)(2,1)}, bf16[2,4,4,48,768]{4,3,2,1,0:T(8,128)(2,1)}, f32[4,2,192,512]{3,2,1,0:T(8,128)}, f32[4,2,192,512]{3,2...) custom-call(bf16[4,2,48,768]{3,2,1,0:T(8,128)(2,1)} %bitcast.46, ...), custom_call_target="tpu_custom_call" | custom-call | flops 20000000000 | bytes 200000000 | tf_op jit(solution)/shard_map/pallas_call | solution.py:864
  137.3 0.0 copy-done.14
  137.3 0.7 collective-permute-start.1
  138.0 9.1 %shard_map.241 = (f32[192,768]{1,0:T(8,128)}, bf16[192,768]{1,0:T(8,128)(2,1)}, bf16[192,2304]{1,0:T(8,128)(2,1)}, f32[12,192,192]{2,1,0:T(8,128)}, bf16[192,768...) custom-call(f32[192,768]{1,0:T(8,128)} %get-tuple-element.117.mid_in.mid0.mid, ...), custom_call_target="tpu_custom_call" | custom-call | flops 10000000000 | bytes 60000000 | tf_op jit(solution)/shard_map/pallas_call | solution.py:363
  147.1 1.1 collective-permute-done.1.refs_5_
  148.2 0.8 copy-done.16
  148.9 64.8 %shard_map.242 = (bf16[4,2,48,768]{3,2,1,0:T(8,128)(2,1)}, bf16[2,4,4,48,768]{4,3,2,1,0:T(8,128)(2,1)}, f32[4,2,192,512]{3,2,1,0:T(8,128)}, f32[4,2,192,512]{3,2,1,0:T(8,128)}, bf16[2,256,768]{2,1,0:T(8,128)(2,1)}) custom-call(bf16[4,2,48,768]{3,2,1,0:T(8,128)(2,1)} %bitcast.51, bf16[2,768,256]{2,1,0:T(8,128)(2,1)} %get-tuple-element.130.refs_12_.refs_0_.refs_3_, ...), custom_call_target="tpu_custom_call" | custom-call | flops 20000000000 | bytes 200000000 | tf_op jit(solution)/shard_map/pallas_call | solution.py:864
  213.7 5.6 %shard_map.243 = (bf16[192,768]{1,0:T(8,128)(2,1)}, f32[192,128]{1,0:T(8,128)}, f32[192,128]{1,0:T(8,128)}, bf16[384,768]{1,0:T(8,128)(2,1)}, f32[24,768]{1,0:T(8,128)}, /*index=5*/f32[128,128]{1,0:T(8,128)}) custom-call(f32[192,768]{1,0:T(8,128)} %get-tuple-element.138.mid, bf16[768,128]{1,0:T(8,128)(2,1)} %get-tuple-element.134.small, ...), custom_call_target="tpu_custom_call" | custom-call | flops 10000000000 | bytes 60000000 | tf_op jit(solution)/shard_map/pallas_call | solution.py:363
  219.3 70.2 %shard_map.244 = (bf16[4,2,48,768]{3,2,1,0:T(8,128)(2,1)}, f32[2,768,256]{2,1,0:T(8,128)}, f32[2,768,256]{2,1,0:T(8,128)}, bf16[2,768,256]{2,1,0:T(8,128)(2,1)},...) custom-call(bf16[4,2,48,768]{3,2,1,0:T(8,128)(2,1)} %bitcast.50, ...), custom_call_target="tpu_custom_call" | custom-call | flops 40000000000 | bytes 200000000 | tf_op jit(solution)/shard_map/pallas_call | solution.py:895
  289.5 17.6 %shard_map.245 = (bf16[2304,768]{1,0:T(8,128)(2,1)}, bf16[768,768]{1,0:T(8,128)(2,1)}, f32[24,768]{1,0:T(8,128)}, f32[192,768]{1,0:T(8,128)}, f32[192,128]{1,0:T...) custom-call(bf16[192,768]{1,0:T(8,128)(2,1)} %cotangent.3, bf16[384,768]{1,0:T(8,128)(2,1)} %bitcast.49, ...), custom_call_target="tpu_custom_call" | custom-call | flops 10000000000 | bytes 60000000 | tf_op jit(solution)/shard_map/pallas_call | solution.py:363
  307.1 73.6 %shard_map.246 = (bf16[4,2,48,768]{3,2,1,0:T(8,128)(2,1)}, f32[2,768,256]{2,1,0:T(8,128)}, f32[2,768,256]{2,1,0:T(8,128)}, bf16[2,768,256]{2,1,0:T(8,128)(2,1)},...) custom-call(bf16[4,2,48,768]{3,2,1,0:T(8,128)(2,1)} %bitcast.47, ...), custom_call_target="tpu_custom_call" | custom-call | flops 40000000000 | bytes 200000000 | tf_op jit(solution)/shard_map/pallas_call | solution.py:895
  380.7 14.5 %shard_map.247 = (bf16[2304,768]{1,0:T(8,128)(2,1)}, bf16[768,768]{1,0:T(8,128)(2,1)}, f32[24,768]{1,0:T(8,128)}, f32[192,768]{1,0:T(8,128)}) custom-call(f32[192,768]{1,0:T(8,128)} %get-tuple-element.161.grad_in, bf16[384,768]{1,0:T(8,128)(2,1)} %bitcast.48, f32[192,128]{1,0:T(8,128)} %get-tuple-element.172.g_small, ...), custom_call_target="tpu_custom_call" | custom-call | flops 10000000000 | bytes 60000000 | tf_op jit(solution)/shard_map/pallas_call | solution.py:363
  395.2 69.4 %shard_map.248 = (f32[64,768]{1,0:T(8,128)}, f32[2,288,768]{2,1,0:T(8,128)}, f32[2,96,768]{2,1,0:T(8,128)}, bf16[2,768,256]{2,1,0:T(8,128)(2,1)}, bf16[2,256,768]{2,1,0:T(8,128)(2,1)}) custom-call(f32[24,768]{1,0:T(8,128)} %get-tuple-element.179.small0, f32[24,768]{1,0:T(8,128)} %get-tuple-element.180.small1, f32[128,128]{1,0:T(8,128)} %get-tuple-element.181.res, ...), custom_call_target="tpu_custom_call" | custom-call | flops 20000000000 | bytes 200000000 | tf_op jit(solution)/shard_map/pallas_call | solution.py:1601
  464.6 0.8 dynamic-slice_bitcast_fusion.1
  465.4 0.6 fusion.2
  466.0 0.6 pad_maximum_fusion.3
  466.6 1.3 slice.55
  467.9 0.6 copy.31
  468.5 0.0 copy-done.3
  468.5 0.0 copy-done.9
  468.5 1.9 add_bitcast_fusion
  470.4 0.0 copy-start.4
  470.4 0.0 copy-start.5
  470.5 0.0 copy-start.8
  470.5 0.0 copy-start.10
  470.5 1.9 pad_maximum_fusion.2
  472.4 0.0 copy-done.4
  472.4 1.1 copy-done.5
  473.5 0.2 copy-done.8
  473.7 0.2 copy-done.10
  473.9 0.3 add_bitcast_fusion.3
  474.2 1.0 copy-done.1
  475.3 0.5 copy-done.2
  475.8 0.2 copy-done.6
  476.0 0.3 copy-done.7
  476.3 0.3 add_bitcast_fusion.2
  476.6 1.9 pad_maximum_fusion.1
  478.5 1.9 pad_maximum_fusion
  480.4 0.4 copy-done
  480.7 1.2 copy.34
  482.0 0.3 copy-done.12
  482.2 0.8 copy.35
  (13 shorter events, 0.1 us)
Async XLA Ops:
  0.6 5.9 %copy-start.11 = (f32[2,96,768]{2,1,0:T(8,128)S(1)}, f32[2,96,768]{2,1,0:T(8,128)}, u32[]{:S(2)}) copy-start(f32[2,96,768]{2,1,0:T(8,128)} %param.23) | copy-start | bytes 1769476
  4.1 3.2 copy-start.13
  56.9 11.7 %collective-permute-start = (bf16[1,256,768]{2,1,0:T(8,128)(2,1)}, bf16[1,256,768]{2,1,0:T(8,128)(2,1)S(1)}, u32[]{:S(2)}, u32[]{:S(2)}) collective-permute-start(bf16[1,256,768]{2,1,0:T(8,128)(2,1)} %get-tuple-element.126), channel_id=1, source_target_pairs={{4,0},{0,4},{12,8},{8,12},{20,16},{16,20},{28,24},{24,28},{5,1},{1... | collective-permute-start | bytes 1179656 | tf_op jit(solution)/shard_map/ppermute | solution.py:910
  68.6 0.7 copy-start.15
  69.3 68.0 %copy-start.14 = (bf16[1,256,768]{2,1,0:T(8,128)(2,1)S(1)}, bf16[1,256,768]{2,1,0:T(8,128)(2,1)}, u32[]{:S(2)}) copy-start(bf16[1,256,768]{2,1,0:T(8,128)(2,1)} %get-tuple-element.144) | copy-start | bytes 1179652
  137.3 10.8 %collective-permute-start.1 = (bf16[1,256,768]{2,1,0:T(8,128)(2,1)S(1)}, bf16[1,256,768]{2,1,0:T(8,128)(2,1)S(1)}, u32[]{:S(2)}, u32[]{:S(2)}) collective-permute-start(bf16[1,256,768]{2,1,0:T(8,128)(2,1)S(1)} %copy-done.14), channel_id=1, source_target_pairs={{4,0},{0,4},{12,8},{8,12},{20,16},{16,20},{28,24},{24,28},{5,1},{1... | collective-permute-start | bytes 1179656 | tf_op jit(solution)/shard_map/ppermute | solution.py:910
  148.2 0.8 copy-start.16
  395.2 73.3 %copy-start.3 = (f32[2,256,768]{2,1,0:T(8,128)S(1)}, f32[2,256,768]{2,1,0:T(8,128)}, u32[]{:S(2)}) copy-start(f32[2,256,768]{2,1,0:T(8,128)} %get-tuple-element.200) | copy-start | bytes 4718596
  395.2 73.3 %copy-start.9 = (bf16[2,256,768]{2,1,0:T(8,128)(2,1)S(1)}, bf16[2,256,768]{2,1,0:T(8,128)(2,1)}, u32[]{:S(2)}) copy-start(bf16[2,256,768]{2,1,0:T(8,128)(2,1)} %get-tuple-element.201) | copy-start | bytes 2359300
  470.4 2.0 copy-start.4
  470.4 3.0 copy-start.5
  470.5 3.2 copy-start.8
  470.5 3.4 copy-start.10
  473.9 1.4 copy-start.1
  473.9 1.9 copy-start.2
  473.9 2.1 copy-start.6
  473.9 2.4 copy-start.7
  478.5 2.3 copy-start
  480.7 1.5 copy-start.12

commit v7 on v6

--- a/solution.py
+++ b/solution.py
@@ -858,7 +858,7 @@
     more = ride or ()
     count = LINE * spread
     if ride:
-        outs += [struct((count * s.shape[1], s.shape[2]), BF16) for s in ride[3:6]]
+        outs += [struct((count * s.shape[0], s.shape[1]), BF16) for s in ride[3:6]]
         outs += [struct(w.shape, BF16) for w in ride[6:]]
         scratch += WeightRider.scratch(count)
     return pl.pallas_call(
@@ -1101,7 +1101,7 @@
     def __init__(self, place, given, whole, sems):
         self.p, self.quarters, self.own, self.other = place, given[:3], given[6:], whole[3:]
         self.w_send, self.w_recv, self.x_send, self.x_recv, *more = sems
-        self.spread = Spread(place, self.quarters, [ref.at[1] for ref in given[3:6]], whole[:3], more)
+        self.spread = Spread(place, self.quarters, given[3:6], whole[:3], more)
 
     @staticmethod
     def scratch(count):
@@ -1166,11 +1166,24 @@
         lax.fori_loop(0, LINE, line, 0)
 
 
-def dense_gather_kernel(spread, qkv, out, small, routes, *refs):
+def pack_small(l, router, const, gains, vectors, rows, small):
+    rows[...] = jnp.zeros(rows.shape, F32)
+    for r in range(router.shape[0]):
+        rows[r : r + 1, :] = router[r, l : l + 1, :]
+    for j in (0, 1):
+        rows[CONST0 + 2 * j : CONST0 + 2 * j + 2, :] = const[l, j]
+    rows[GAIN0 : GAIN0 + 2, :] = gains[l]
+    rows[VECTOR0 : VECTOR0 + 2, :] = vectors[l]
+    place = lax.broadcasted_iota(jnp.int32, (rows.shape[0], 128), 0) == lanes(rows.shape[0])
+    small[l] = dot_tn(rows[...].astype(BF16), place.astype(BF16)).astype(BF16)
+
+
+def dense_gather_kernel(spread, qkv_wide, out_wide, router, const, gains, vectors, routes, *refs):
     p = Place(spread)
-    wide, whole, quarters1, (routes_all,), own, firsts, partner, quarters0, loaded, rounded, rest = split(
-        refs, 3, 3, 3, 1, 6, 2, 2, 3, 3, 3)
-    sems0, sems1, (r_send, r_recv, w_send, w_recv, load_sem, own_sem, first_sem), spread_sems = split(rest, 4, 4, 7)
+    wide, whole, quarters1, (routes_all,), own, firsts, partner, shards1_out, quarters0, loaded, rounded, shards, (rows,), rest = split(
+        refs, 3, 3, 3, 1, 6, 2, 2, 3, 3, 3, 3, 3, 1)
+    qkv, out, small = shards
+    sems0, sems1, (r_send, r_recv, w_send, w_recv, load_sem, own_sem, first_sem, shard_sem), spread_sems = split(rest, 4, 4, 8)
     shards0, shards1 = ([ref.at[l] for ref in (qkv, out, small)] for l in (0, 1))
     line0 = LineGather(p, True, shards0, quarters0, sems0)
     line1 = LineGather(p, False, shards1, quarters1, sems1)
@@ -1200,9 +1213,17 @@
         if kind == 2:
             first(l).start()
 
+    def shard1(kind):
+        return pltpu.make_async_copy(shards[kind].at[1], shards1_out[kind], shard_sem.at[kind])
+
     for l in (0, 1):
         for kind in range(3):
             load(l, kind).start()
+    for l in (0, 1):
+        qkv[l], out[l] = qkv_wide[l].astype(BF16), out_wide[l].astype(BF16)
+        pack_small(l, router, const, gains, vectors, rows, small)
+    for kind in range(3):
+        shard1(kind).start()
     greet(p.mates[1:] + [p.beside], p)
 
     def route_copy(i, row):
@@ -1238,6 +1259,8 @@
         first(l).wait()
     for kind in (0, 1):
         weight(kind).wait()
+    for kind in range(3):
+        shard1(kind).wait()
     for i in (1, 2, 3):
         route_copy(i, p.e).wait_send()
         route_copy(i, p.mates[i][1]).wait_recv()
@@ -1245,20 +1268,22 @@
 
 def dense_gather(spread, call_id, arrays, routes, wide):
     count = spread * LINE
-    shards = [a.shape[1:] for a in arrays]
+    layers, depth = arrays[1].shape[:2]
+    shards = [arrays[0].shape[1:], arrays[1].shape[1:], (depth, 128)]
     pairs, single = LineGather.shapes(shards, 2), LineGather.shapes(shards, 1)
     outs = [struct((count * rows, width), BF16) for rows, width in shards]
     outs += [struct(q, BF16) for q in single] + [struct((4,) + routes.shape, routes.dtype)]
     outs += [struct(w.shape[1:], BF16) for w in wide] * 2 + [struct((1,) + wide[2].shape[2:], BF16)] * 2
-    outs += [struct(w.shape[1:], BF16) for w in wide[:2]]
+    outs += [struct(w.shape[1:], BF16) for w in wide[:2]] + [struct(s, BF16) for s in shards]
     scratch = [pltpu.VMEM(q, BF16) for q in pairs] + [pltpu.VMEM(w.shape, F32) for w in wide]
-    scratch += [pltpu.VMEM(w.shape, BF16) for w in wide] + LineGather.scratch(2) + LineGather.scratch(1)
-    scratch += [dma(4), dma(4), dma(2), dma(2), dma(2, 3), dma(2, 3), dma(2)]
+    scratch += [pltpu.VMEM(w.shape, BF16) for w in wide] + [pltpu.VMEM((layers,) + s, BF16) for s in shards]
+    scratch += [pltpu.VMEM((32, depth), F32)] + LineGather.scratch(2) + LineGather.scratch(1)
+    scratch += [dma(4), dma(4), dma(2), dma(2), dma(2, 3), dma(2, 3), dma(2), dma(3)]
     return pl.pallas_call(
         functools.partial(dense_gather_kernel, spread),
         out_shape=outs,
-        in_specs=[VMEM] * 4 + [ANY] * 3,
-        out_specs=[ANY] * 3 + [VMEM] * 4 + [ANY] * 10,
+        in_specs=[VMEM] * (len(arrays) + 1) + [ANY] * 3,
+        out_specs=[ANY] * 3 + [VMEM] * 4 + [ANY] * 13,
         scratch_shapes=scratch + Spread.scratch(count),
         compiler_params=remote_params(call_id),
         cost_estimate=pl.CostEstimate(flops=10**10, bytes_accessed=10**8, transcendentals=0),
@@ -1610,6 +1635,37 @@
     )(*smalls, *grads0, quarter1, *weights0)
 
 
+def stack_kernel(qkv, out, *refs):
+    parts, (qkv_out, out_out, *stacked) = refs[:12], refs[12:]
+    qkv_out[...], out_out[...] = qkv[...], out[...]
+    for kind, ref in enumerate(stacked):
+        for l in (0, 1):
+            mine, came = parts[4 * kind + 2 * l], parts[4 * kind + 2 * l + 1]
+            ref[l] = mine[...] + came[...].astype(F32)
+
+
+def stack_results(qkv, out, parts):
+    flat = [part for kind in parts for layer in kind for part in layer]
+    local, steps = flat[0].shape[0], 2
+
+    def rows_of(shape, lead):
+        block = (shape[0] if lead else 1, *((1,) if lead else ()), shape[-2] // steps, shape[-1])
+        if lead:
+            return pl.BlockSpec(block, lambda l, n: (0, l, n, 0))
+        return pl.BlockSpec(block, lambda l, n: (l, n, 0))
+
+    stacked = [(2,) + kind[0][0].shape for kind in parts]
+    return pl.pallas_call(
+        stack_kernel,
+        out_shape=[struct(a.shape, F32) for a in (qkv, out)] + [struct(s, F32) for s in stacked],
+        grid=(local, steps),
+        in_specs=[rows_of(a.shape, False) for a in (qkv, out, *flat)],
+        out_specs=[rows_of(a.shape, False) for a in (qkv, out)] + [rows_of(s, True) for s in stacked],
+        compiler_params=pltpu.CompilerParams(vmem_limit_bytes=60 * 2**20),
+        cost_estimate=pl.CostEstimate(flops=10**7, bytes_accessed=3 * 10**7, transcendentals=0),
+    )(qkv, out, *flat)
+
+
 def per_device(
     tokens, seq_lengths, block_perm, routes, norm_gains, w_qkv, w_out, w_router, w_residual, w_const, v_const,
     w_gate, w_up, w_down, cotangent,
@@ -1627,19 +1683,12 @@
         jnp.swapaxes(routes, 1, 2).reshape(2 * layers, rows))
 
     depth = w_out.shape[1]
-    small = jnp.concatenate(
-        [
-            w_router, w_const[:, 0], w_const[:, 1], jnp.swapaxes(norm_gains, 1, 2), jnp.swapaxes(v_const, 1, 2),
-            jnp.zeros((layers, depth, 108), F32),
-        ],
-        axis=2,
-    ).astype(BF16)
-    qkv_t = jnp.swapaxes(w_qkv, 1, 2).astype(BF16)
-    out_rows = w_out.astype(BF16)
-    in_kernels = spread == 2 and owners == 4 and qkv_t.shape[1] % 32 == 0 and depth % 32 == 0
+    qkv_t = jnp.swapaxes(w_qkv, 1, 2)
+    in_kernels = spread == 2 and owners == 4 and layers == local == 2 and qkv_t.shape[1] % 32 == 0 and depth % 32 == 0
     if in_kernels:
-        *gathered, routes_all, g0, u0, d0, g1, u1, d1, first0, first1, gate, up = dense_gather(
-            spread, 4, (qkv_t, out_rows, small), packed_routes, (w_gate, w_up, w_down))
+        arrays = (qkv_t, w_out, jnp.transpose(w_router, (2, 0, 1)), jnp.swapaxes(w_const, 2, 3), norm_gains, v_const)
+        *gathered, routes_all, g0, u0, d0, g1, u1, d1, first0, first1, gate, up, qkv1_own, out1_own, small1_own = dense_gather(
+            spread, 4, arrays, packed_routes, (w_gate, w_up, w_down))
         weights = [[g0, gate, u0, up, d0, from_partner(first0, 1, spread, LINE)]]
         dense = [(gathered[2], gathered[0], gathered[1])]
     else:
@@ -1647,9 +1696,16 @@
         for l in range(layers):
             own = [(w_gate[l].astype(BF16), 2), (w_up[l].astype(BF16), 2), (w_down[l].astype(BF16), 1)]
             weights.append([part for w, axis in own for part in pair_weights(w, axis, spread)])
+        small = jnp.concatenate(
+            [
+                w_router, w_const[:, 0], w_const[:, 1], jnp.swapaxes(norm_gains, 1, 2), jnp.swapaxes(v_const, 1, 2),
+                jnp.zeros((layers, depth, 108), F32),
+            ],
+            axis=2,
+        ).astype(BF16)
         routes_all = lax.all_gather(packed_routes, "expert", axis=0)
-        qkv_all = lax.all_gather(qkv_t, "dp", axis=1, tiled=True)
-        out_all = lax.all_gather(out_rows, "dp", axis=1, tiled=True)
+        qkv_all = lax.all_gather(qkv_t.astype(BF16), "dp", axis=1, tiled=True)
+        out_all = lax.all_gather(w_out.astype(BF16), "dp", axis=1, tiled=True)
         small_all = lax.all_gather(small, "dp", axis=1, tiled=True)
         dense = [(small_all[l], qkv_all[l], out_all[l]) for l in range(layers)]
 
@@ -1664,7 +1720,7 @@
     attn_in0, qkv0, probs0, attn0, mid0, logits0, stat0, out = local_call(
         first_kernel, experts, (tokens, *dense[0], seq_lengths, block_perm, routes_all),
         attention + [cols, per_token, per_token, sent], scalars=(4, 5))
-    ride = (*gathered[3:], qkv_t, out_rows, small, g1, u1) if in_kernels else None
+    ride = (*gathered[3:], qkv1_own, out1_own, small1_own, g1, u1) if in_kernels else None
     ret0, *kept0 = expert_forward(spread, 0, group(out), weights[0], in_kernels, ride)
     if in_kernels:
         kept0, weights[0][5], (qkv_all, out_all, small_all), (gate, up) = kept0[:3], kept0[3], kept0[4:7], kept0[7:]
@@ -1712,8 +1768,7 @@
         pairs = (
             ((gate0, gate0_came), (gate1, gate1_came)), ((up0, up0_came), (up1, up1_came)),
             ((down0, down0_came), (down1, down1_came)))
-        gate_grad, up_grad, down_grad = (
-            jnp.stack([mine + came.astype(F32) for mine, came in layer]) for layer in pairs)
+        qkv_grad, out_grad, gate_grad, up_grad, down_grad = stack_results(qkv_grad, out_grad, pairs)
     else:
         gate_grad, up_grad, down_grad = (
             jnp.stack([

time: 484 us -> 471 us (0.973)
  other arithmetic: 14.7 us -> 1.19 us
  Pallas kernels: 449 us -> 459 us
  local copies, waits for them, and re-layouts: 13.2 us -> 5.56 us
    another operation x9 -> x0, other arithmetic: 10.3 us -> none  [the longest x6 8.23 us: per_device(): jnp.stack([mine + came.astype(F32) for mine, came in layer])]
    pallas_call x0 -> x1, Pallas kernels: none -> 9.78 us  [stack_results(): pl.pallas_call(stack_kernel, out_shape=[struct(a.shape, F32) for a in (qk...]
    unnamed x38 -> x7, local copies, waits for them, and re-layouts: 9.22 us -> 2.11 us
where the time goes in v7:
time: 471 us
  Pallas kernels  459 us (97%)
  local copies, waits for them, and re-layouts  5.56 us (1%)
    pallas_call x2, Pallas kernels, expert_backward(): pl.pallas_call(functools.partial(expert_backward_kernel, spread, parts, i...  143 us
    pallas_call x2, Pallas kernels, expert_forward(): pl.pallas_call(functools.partial(expert_forward_kernel, spread, parts, in...  133 us
    pallas_call x1, Pallas kernels, dense_reduce(): pl.pallas_call(functools.partial(dense_reduce_kernel, spread, depths), ou...  68.7 us
    pallas_call x5, Pallas kernels, local_call(): pl.pallas_call(functools.partial(kernel, experts), out_shape=[jax.ShapeDt...  55.4 us
    pallas_call x1, Pallas kernels, dense_gather(): pl.pallas_call(functools.partial(dense_gather_kernel, spread), out_shape=...  48.9 us
    pallas_call x1, Pallas kernels, stack_results(): pl.pallas_call(stack_kernel, out_shape=[struct(a.shape, F32) for a in (qk...  9.78 us
  transfers between devices with their start and end apart: 2, of which 2 were waited for; matrix products, arithmetic and copies ran while one was open for 0% of the time, Pallas kernels for 4%

profile of v7, /device:TPU:0, one launch (start us, length us, event | category | flops | bytes accessed | tf_op | source)
XLA Modules:
  0.0 471.3 jit_solution(9353052324564189869)
XLA Ops:
  0.6 0.7 reshape.85
  1.3 0.6 scatter.4.routes
  2.0 48.9 %shard_map.238 = (bf16[2304,768]{1,0:T(8,128)(2,1)}, bf16[768,768]{1,0:T(8,128)(2,1)}, bf16[768,128]{1,0:T(8,128)(2,1)}, bf16[4,1,144,384]{3,2,1,0:T(8,128)(2,1)...) custom-call(f32[2,288,768]{2,1,0:T(8,128)} %bitcast.24, ...), custom_call_target="tpu_custom_call" | custom-call | flops 10000000000 | bytes 100000000 | tf_op jit(solution)/shard_map/pallas_call | solution.py:1282
  50.9 0.7 collective-permute-start
  51.5 8.6 %shard_map.239 = (bf16[192,768]{1,0:T(8,128)(2,1)}, bf16[192,2304]{1,0:T(8,128)(2,1)}, f32[12,192,192]{2,1,0:T(8,128)}, bf16[192,768]{1,0:T(8,128)(2,1)}, f32[19...) custom-call(bf16[192,768]{1,0:T(8,128)(2,1)} %tokens.3, ...), custom_call_target="tpu_custom_call" | custom-call | flops 10000000000 | bytes 60000000 | tf_op jit(solution)/shard_map/pallas_call | solution.py:363
  60.2 2.4 collective-permute-done.refs_5_
  62.5 0.0 copy-start.1
  62.5 0.7 copy-done.1
  63.3 0.0 copy-start
  63.3 68.0 %shard_map.240 = (bf16[4,2,48,768]{3,2,1,0:T(8,128)(2,1)}, bf16[2,4,4,48,768]{4,3,2,1,0:T(8,128)(2,1)}, f32[4,2,192,512]{3,2,1,0:T(8,128)}, f32[4,2,192,512]{3,2...) custom-call(bf16[4,2,48,768]{3,2,1,0:T(8,128)(2,1)} %bitcast.30, ...), custom_call_target="tpu_custom_call" | custom-call | flops 20000000000 | bytes 200000000 | tf_op jit(solution)/shard_map/pallas_call | solution.py:864
  131.2 0.0 copy-done
  131.2 0.7 collective-permute-start.1
  131.9 9.1 %shard_map.241 = (f32[192,768]{1,0:T(8,128)}, bf16[192,768]{1,0:T(8,128)(2,1)}, bf16[192,2304]{1,0:T(8,128)(2,1)}, f32[12,192,192]{2,1,0:T(8,128)}, bf16[192,768...) custom-call(f32[192,768]{1,0:T(8,128)} %get-tuple-element.125.mid_in.mid0.mid, ...), custom_call_target="tpu_custom_call" | custom-call | flops 10000000000 | bytes 60000000 | tf_op jit(solution)/shard_map/pallas_call | solution.py:363
  141.0 1.2 collective-permute-done.1.refs_5_
  142.3 0.0 copy-start.2
  142.3 0.8 copy-done.2
  143.0 64.6 %shard_map.242 = (bf16[4,2,48,768]{3,2,1,0:T(8,128)(2,1)}, bf16[2,4,4,48,768]{4,3,2,1,0:T(8,128)(2,1)}, f32[4,2,192,512]{3,2,1,0:T(8,128)}, f32[4,2,192,512]{3,2,1,0:T(8,128)}, bf16[2,256,768]{2,1,0:T(8,128)(2,1)}) custom-call(bf16[4,2,48,768]{3,2,1,0:T(8,128)(2,1)} %bitcast.35, bf16[2,768,256]{2,1,0:T(8,128)(2,1)} %get-tuple-element.141.refs_12_.refs_0_.refs_3_, ...), custom_call_target="tpu_custom_call" | custom-call | flops 20000000000 | bytes 200000000 | tf_op jit(solution)/shard_map/pallas_call | solution.py:864
  207.6 5.6 %shard_map.243 = (bf16[192,768]{1,0:T(8,128)(2,1)}, f32[192,128]{1,0:T(8,128)}, f32[192,128]{1,0:T(8,128)}, bf16[384,768]{1,0:T(8,128)(2,1)}, f32[24,768]{1,0:T(8,128)}, /*index=5*/f32[128,128]{1,0:T(8,128)}) custom-call(f32[192,768]{1,0:T(8,128)} %get-tuple-element.149.mid, bf16[768,128]{1,0:T(8,128)(2,1)} %get-tuple-element.145.small, ...), custom_call_target="tpu_custom_call" | custom-call | flops 10000000000 | bytes 60000000 | tf_op jit(solution)/shard_map/pallas_call | solution.py:363
  213.2 70.3 %shard_map.244 = (bf16[4,2,48,768]{3,2,1,0:T(8,128)(2,1)}, f32[2,768,256]{2,1,0:T(8,128)}, f32[2,768,256]{2,1,0:T(8,128)}, bf16[2,768,256]{2,1,0:T(8,128)(2,1)},...) custom-call(bf16[4,2,48,768]{3,2,1,0:T(8,128)(2,1)} %bitcast.34, ...), custom_call_target="tpu_custom_call" | custom-call | flops 40000000000 | bytes 200000000 | tf_op jit(solution)/shard_map/pallas_call | solution.py:895
  283.6 17.7 %shard_map.245 = (bf16[2304,768]{1,0:T(8,128)(2,1)}, bf16[768,768]{1,0:T(8,128)(2,1)}, f32[24,768]{1,0:T(8,128)}, f32[192,768]{1,0:T(8,128)}, f32[192,128]{1,0:T...) custom-call(bf16[192,768]{1,0:T(8,128)(2,1)} %cotangent.3, bf16[384,768]{1,0:T(8,128)(2,1)} %bitcast.33, ...), custom_call_target="tpu_custom_call" | custom-call | flops 10000000000 | bytes 60000000 | tf_op jit(solution)/shard_map/pallas_call | solution.py:363
  301.3 73.0 %shard_map.246 = (bf16[4,2,48,768]{3,2,1,0:T(8,128)(2,1)}, f32[2,768,256]{2,1,0:T(8,128)}, f32[2,768,256]{2,1,0:T(8,128)}, bf16[2,768,256]{2,1,0:T(8,128)(2,1)},...) custom-call(bf16[4,2,48,768]{3,2,1,0:T(8,128)(2,1)} %bitcast.31, ...), custom_call_target="tpu_custom_call" | custom-call | flops 40000000000 | bytes 200000000 | tf_op jit(solution)/shard_map/pallas_call | solution.py:895
  374.3 14.4 %shard_map.247 = (bf16[2304,768]{1,0:T(8,128)(2,1)}, bf16[768,768]{1,0:T(8,128)(2,1)}, f32[24,768]{1,0:T(8,128)}, f32[192,768]{1,0:T(8,128)}) custom-call(f32[192,768]{1,0:T(8,128)} %get-tuple-element.172.grad_in, bf16[384,768]{1,0:T(8,128)(2,1)} %bitcast.32, f32[192,128]{1,0:T(8,128)} %get-tuple-element.183.g_small, ...), custom_call_target="tpu_custom_call" | custom-call | flops 10000000000 | bytes 60000000 | tf_op jit(solution)/shard_map/pallas_call | solution.py:363
  388.7 68.7 %shard_map.248 = (f32[64,768]{1,0:T(8,128)}, f32[2,288,768]{2,1,0:T(8,128)}, f32[2,96,768]{2,1,0:T(8,128)}, bf16[2,768,256]{2,1,0:T(8,128)(2,1)}, bf16[2,256,768]{2,1,0:T(8,128)(2,1)}) custom-call(f32[24,768]{1,0:T(8,128)} %get-tuple-element.190.small0, f32[24,768]{1,0:T(8,128)} %get-tuple-element.191.small1, f32[128,128]{1,0:T(8,128)} %get-tuple-element.192.res, ...), custom_call_target="tpu_custom_call" | custom-call | flops 20000000000 | bytes 200000000 | tf_op jit(solution)/shard_map/pallas_call | solution.py:1626
  457.4 0.8 dynamic-slice_bitcast_fusion.1
  458.3 0.6 fusion.2
  458.9 0.6 pad_maximum_fusion
  459.5 1.3 slice.45
  460.7 0.6 copy.27
  461.4 9.8 %shard_map.249 = (f32[2,288,768]{2,1,0:T(8,128)}, f32[2,96,768]{2,1,0:T(8,128)}, f32[2,2,768,256]{3,2,1,0:T(8,128)}, f32[2,2,768,256]{3,2,1,0:T(8,128)}, f32[2,2,256,768]{3,2,1,0:T(8,128)}) custom-call(f32[2,288,768]{2,1,0:T(8,128)} %get-tuple-element.199.qkv, f32[2,96,768]{2,1,0:T(8,128)} %get-tuple-element.200.out, ...), custom_call_target="tpu_custom_call" | custom-call | flops 10000000 | bytes 30000000 | tf_op jit(solution)/shard_map/pallas_call | solution.py:1658
  (1 shorter events, 0.0 us)
Async XLA Ops:
  50.9 11.7 %collective-permute-start = (bf16[1,256,768]{2,1,0:T(8,128)(2,1)}, bf16[1,256,768]{2,1,0:T(8,128)(2,1)S(1)}, u32[]{:S(2)}, u32[]{:S(2)}) collective-permute-start(bf16[1,256,768]{2,1,0:T(8,128)(2,1)} %get-tuple-element.134), channel_id=1, source_target_pairs={{4,0},{0,4},{12,8},{8,12},{20,16},{16,20},{28,24},{24,28},{5,1},{1... | collective-permute-start | bytes 1179656 | tf_op jit(solution)/shard_map/ppermute | solution.py:910
  62.5 0.7 copy-start.1
  63.3 68.0 %copy-start = (bf16[1,256,768]{2,1,0:T(8,128)(2,1)S(1)}, bf16[1,256,768]{2,1,0:T(8,128)(2,1)}, u32[]{:S(2)}) copy-start(bf16[1,256,768]{2,1,0:T(8,128)(2,1)} %get-tuple-element.155) | copy-start | bytes 1179652
  131.2 11.0 %collective-permute-start.1 = (bf16[1,256,768]{2,1,0:T(8,128)(2,1)S(1)}, bf16[1,256,768]{2,1,0:T(8,128)(2,1)S(1)}, u32[]{:S(2)}, u32[]{:S(2)}) collective-permute-start(bf16[1,256,768]{2,1,0:T(8,128)(2,1)S(1)} %copy-done), channel_id=1, source_target_pairs={{4,0},{0,4},{12,8},{8,12},{20,16},{16,20},{28,24},{24,28},{5,1},{1... | collective-permute-start | bytes 1179656 | tf_op jit(solution)/shard_map/ppermute | solution.py:910
  142.3 0.8 copy-start.2

commit v8 on v7

--- a/solution.py
+++ b/solution.py
@@ -41,6 +41,14 @@
 
 def dot_tn(a, b, **kw):
     return lax.dot_general(a, b, (((0,), (0,)), ((), ())), preferred_element_type=F32, **kw)
+
+
+def thirds(values):
+    out = []
+    for _ in range(3):
+        out.append(values.astype(BF16))
+        values = values - out[-1].astype(F32)
+    return out
 
 
 def lanes(rows, width=128):
@@ -232,8 +240,8 @@
     sent0 = (jnp.where(stat["r0"] < experts, stat["share0"], 0.0) * grad).astype(BF16)
     sent1 = (jnp.where(stat["r1"] < experts, stat["share1"], 0.0) * grad).astype(BF16)
     outgoing = (dot_tn(first, sent0) + dot_tn(second, sent1)).astype(BF16)
-    hidden = hidden_full.astype(BF16).astype(F32)
-    projections = dot_tn(g_small, hidden, precision=HIGH)
+    hidden = hidden_full.astype(BF16)
+    projections = sum(dot_tn(part, hidden) for part in thirds(g_small)[::-1])
     vector0 = jnp.sum((const0 * stat["p01"]) * grad, axis=0, keepdims=True)
     vector1 = jnp.sum((const1 * stat["p11"]) * grad, axis=0, keepdims=True)
     return g_small, g_logits, outgoing, projections, vector0, vector1
@@ -287,7 +295,7 @@
     first, second = slot_picks(stat, experts * CAP)
     copy, const0, const1 = const_weights(stat, experts)
     local = copy + const0 * stat["p00"] + const1 * stat["p10"]
-    g_full = dot_nt(g_small, small.astype(F32), precision=HIGH) + dot_nn(first + second, back)
+    g_full = sum(dot_nt(part, small) for part in thirds(g_small)[::-1]) + dot_nn(first + second, back)
     g_full = g_full + grad * local
     s2 = rms_scale(mid)
     small_grad[GAIN0 + 1 : GAIN0 + 2, :] = jnp.sum(g_full * mid * s2, axis=0, keepdims=True)
@@ -401,7 +409,7 @@
     return out
 
 
-def greet(always, place):
+def greet(always, place, meanwhile=lambda: None):
     barrier = pltpu.get_barrier_semaphore()
     for device in always:
         pl.semaphore_signal(barrier, inc=1, device_id=device, device_id_type=MESH)
@@ -411,6 +419,7 @@
         def _(up=up):
             pl.semaphore_signal(barrier, inc=1, device_id=place.on_line(up), device_id_type=MESH)
 
+    meanwhile()
     ends = place.above.astype(jnp.int32) + place.below.astype(jnp.int32)
     pl.semaphore_wait(barrier, len(always) + ends)
 
@@ -864,7 +873,7 @@
     return pl.pallas_call(
         functools.partial(expert_forward_kernel, spread, parts, int(late), ride is not None),
         out_shape=outs,
-        in_specs=[VMEM] + [ANY] * (len(weights) + len(more)),
+        in_specs=[VMEM] + [ANY] * (len(weights) - 1) + [VMEM if late else ANY] + [ANY] * len(more),
         out_specs=[VMEM] + [ANY] * (len(outs) - 1),
         scratch_shapes=scratch,
         compiler_params=remote_params(call_id),
@@ -1178,10 +1187,10 @@
     small[l] = dot_tn(rows[...].astype(BF16), place.astype(BF16)).astype(BF16)
 
 
-def dense_gather_kernel(spread, qkv_wide, out_wide, router, const, gains, vectors, routes, *refs):
+def dense_gather_kernel(spread, qkv_wide, out_wide, router, const, gains, vectors, routes_in, *refs):
     p = Place(spread)
-    wide, whole, quarters1, (routes_all,), own, firsts, partner, shards1_out, quarters0, loaded, rounded, shards, (rows,), rest = split(
-        refs, 3, 3, 3, 1, 6, 2, 2, 3, 3, 3, 3, 3, 1)
+    wide, whole, quarters1, (routes_all,), own, firsts, partner, shards1_out, quarters0, loaded, rounded, shards, (rows, routes), rest = split(
+        refs, 3, 3, 3, 1, 6, 2, 2, 3, 3, 3, 3, 3, 2)
     qkv, out, small = shards
     sems0, sems1, (r_send, r_recv, w_send, w_recv, load_sem, own_sem, first_sem, shard_sem), spread_sems = split(rest, 4, 4, 8)
     shards0, shards1 = ([ref.at[l] for ref in (qkv, out, small)] for l in (0, 1))
@@ -1219,12 +1228,17 @@
     for l in (0, 1):
         for kind in range(3):
             load(l, kind).start()
-    for l in (0, 1):
-        qkv[l], out[l] = qkv_wide[l].astype(BF16), out_wide[l].astype(BF16)
-        pack_small(l, router, const, gains, vectors, rows, small)
-    for kind in range(3):
-        shard1(kind).start()
-    greet(p.mates[1:] + [p.beside], p)
+    def round_shards():
+        for l in (0, 1):
+            qkv[l], out[l] = qkv_wide[l].astype(BF16), out_wide[l].astype(BF16)
+            pack_small(l, router, const, gains, vectors, rows, small)
+        for kind in range(3):
+            shard1(kind).start()
+        routes[...] = jnp.zeros(routes.shape, jnp.int32)
+        for l in (0, 1):
+            routes[2 * l : 2 * l + 2, 0 : routes_in.shape[2]] = routes_in[l]
+
+    greet(p.mates[1:] + [p.beside], p, round_shards)
 
     def route_copy(i, row):
         return remote(routes, routes_all.at[row], r_send.at[i], r_recv.at[row], p.mates[i])
@@ -1272,12 +1286,13 @@
     shards = [arrays[0].shape[1:], arrays[1].shape[1:], (depth, 128)]
     pairs, single = LineGather.shapes(shards, 2), LineGather.shapes(shards, 1)
     outs = [struct((count * rows, width), BF16) for rows, width in shards]
-    outs += [struct(q, BF16) for q in single] + [struct((4,) + routes.shape, routes.dtype)]
+    packed = (8, -(-routes.shape[2] // 128) * 128)
+    outs += [struct(q, BF16) for q in single] + [struct((4,) + packed, jnp.int32)]
     outs += [struct(w.shape[1:], BF16) for w in wide] * 2 + [struct((1,) + wide[2].shape[2:], BF16)] * 2
     outs += [struct(w.shape[1:], BF16) for w in wide[:2]] + [struct(s, BF16) for s in shards]
     scratch = [pltpu.VMEM(q, BF16) for q in pairs] + [pltpu.VMEM(w.shape, F32) for w in wide]
     scratch += [pltpu.VMEM(w.shape, BF16) for w in wide] + [pltpu.VMEM((layers,) + s, BF16) for s in shards]
-    scratch += [pltpu.VMEM((32, depth), F32)] + LineGather.scratch(2) + LineGather.scratch(1)
+    scratch += [pltpu.VMEM((32, depth), F32), pltpu.VMEM(packed, jnp.int32)] + LineGather.scratch(2) + LineGather.scratch(1)
     scratch += [dma(4), dma(4), dma(2), dma(2), dma(2, 3), dma(2, 3), dma(2), dma(3)]
     return pl.pallas_call(
         functools.partial(dense_gather_kernel, spread),
@@ -1635,35 +1650,55 @@
     )(*smalls, *grads0, quarter1, *weights0)
 
 
-def stack_kernel(qkv, out, *refs):
-    parts, (qkv_out, out_out, *stacked) = refs[:12], refs[12:]
+def stack_kernel(small, qkv, out, *refs):
+    parts, (qkv_out, out_out, *stacked), (router, const, gains, vectors, residual) = split(refs, 12, 5)
     qkv_out[...], out_out[...] = qkv[...], out[...]
     for kind, ref in enumerate(stacked):
         for l in (0, 1):
             mine, came = parts[4 * kind + 2 * l], parts[4 * kind + 2 * l + 1]
             ref[l] = mine[...] + came[...].astype(F32)
 
-
-def stack_results(qkv, out, parts):
+    @pl.when(jnp.logical_and(pl.program_id(0) == 0, pl.program_id(1) == 0))
+    def _():
+        depth, width = gains.shape[2], small.shape[1]
+        here = lanes(depth, width) == lax.axis_index("dp") * depth + lax.broadcasted_iota(jnp.int32, (depth, width), 0)
+        rows = dot_nt(small[...], here.astype(F32), precision=HIGH)
+        for l in (0, 1):
+            first = 24 * l
+            for r in range(CONST0):
+                router[r, l : l + 1, :] = rows[first + r : first + r + 1]
+            for j in (0, 1):
+                at = first + CONST0 + 2 * j
+                const[l, j] = rows[at : at + 2]
+            gains[l] = rows[first + GAIN0 : first + GAIN0 + 2]
+            vectors[l] = rows[first + VECTOR0 : first + VECTOR0 + 2]
+        residual[...] = small[48 : 48 + CONST0, 0:CONST0]
+
+
+def stack_results(small, qkv, out, parts, depth):
     flat = [part for kind in parts for layer in kind for part in layer]
     local, steps = flat[0].shape[0], 2
 
-    def rows_of(shape, lead):
-        block = (shape[0] if lead else 1, *((1,) if lead else ()), shape[-2] // steps, shape[-1])
+    def rows_of(shape, lead=None):
+        rows, wide = shape[-2] // steps, shape[-1]
         if lead:
-            return pl.BlockSpec(block, lambda l, n: (0, l, n, 0))
-        return pl.BlockSpec(block, lambda l, n: (l, n, 0))
+            return pl.BlockSpec((lead, 1, rows, wide), lambda l, n: (0, l, n, 0))
+        return pl.BlockSpec((1, rows, wide), lambda l, n: (l, n, 0))
+
+    def whole(shape):
+        return pl.BlockSpec(shape, lambda l, n: (0,) * len(shape))
 
     stacked = [(2,) + kind[0][0].shape for kind in parts]
+    little = [(CONST0, 2, depth), (2, 2, 2, depth), (2, 2, depth), (2, 2, depth), (CONST0, CONST0)]
     return pl.pallas_call(
         stack_kernel,
-        out_shape=[struct(a.shape, F32) for a in (qkv, out)] + [struct(s, F32) for s in stacked],
+        out_shape=[struct(a.shape, F32) for a in (qkv, out)] + [struct(s, F32) for s in stacked + little],
         grid=(local, steps),
-        in_specs=[rows_of(a.shape, False) for a in (qkv, out, *flat)],
-        out_specs=[rows_of(a.shape, False) for a in (qkv, out)] + [rows_of(s, True) for s in stacked],
+        in_specs=[whole(small.shape)] + [rows_of(a.shape) for a in (qkv, out, *flat)],
+        out_specs=[rows_of(a.shape) for a in (qkv, out)] + [rows_of(s, 2) for s in stacked] + [whole(s) for s in little],
         compiler_params=pltpu.CompilerParams(vmem_limit_bytes=60 * 2**20),
         cost_estimate=pl.CostEstimate(flops=10**7, bytes_accessed=3 * 10**7, transcendentals=0),
-    )(qkv, out, *flat)
+    )(small, qkv, out, *flat)
 
 
 def per_device(
@@ -1679,16 +1714,13 @@
     layers = routes.shape[0]
     slots = experts * CAP
 
-    packed_routes = jnp.zeros((8, -(-rows // 128) * 128), jnp.int32).at[: 2 * layers, :rows].set(
-        jnp.swapaxes(routes, 1, 2).reshape(2 * layers, rows))
-
     depth = w_out.shape[1]
     qkv_t = jnp.swapaxes(w_qkv, 1, 2)
     in_kernels = spread == 2 and owners == 4 and layers == local == 2 and qkv_t.shape[1] % 32 == 0 and depth % 32 == 0
     if in_kernels:
         arrays = (qkv_t, w_out, jnp.transpose(w_router, (2, 0, 1)), jnp.swapaxes(w_const, 2, 3), norm_gains, v_const)
         *gathered, routes_all, g0, u0, d0, g1, u1, d1, first0, first1, gate, up, qkv1_own, out1_own, small1_own = dense_gather(
-            spread, 4, arrays, packed_routes, (w_gate, w_up, w_down))
+            spread, 4, arrays, jnp.swapaxes(routes, 1, 2), (w_gate, w_up, w_down))
         weights = [[g0, gate, u0, up, d0, from_partner(first0, 1, spread, LINE)]]
         dense = [(gathered[2], gathered[0], gathered[1])]
     else:
@@ -1703,6 +1735,8 @@
             ],
             axis=2,
         ).astype(BF16)
+        packed_routes = jnp.zeros((8, -(-rows // 128) * 128), jnp.int32).at[: 2 * layers, :rows].set(
+            jnp.swapaxes(routes, 1, 2).reshape(2 * layers, rows))
         routes_all = lax.all_gather(packed_routes, "expert", axis=0)
         qkv_all = lax.all_gather(qkv_t.astype(BF16), "dp", axis=1, tiled=True)
         out_all = lax.all_gather(w_out.astype(BF16), "dp", axis=1, tiled=True)
@@ -1768,7 +1802,10 @@
         pairs = (
             ((gate0, gate0_came), (gate1, gate1_came)), ((up0, up0_came), (up1, up1_came)),
             ((down0, down0_came), (down1, down1_came)))
-        qkv_grad, out_grad, gate_grad, up_grad, down_grad = stack_results(qkv_grad, out_grad, pairs)
+        qkv_grad, out_grad, gate_grad, up_grad, down_grad, router_grad, const_grad, gains_grad, vector_grad, residual_grad = (
+            stack_results(packed, qkv_grad, out_grad, pairs, depth))
+        router_grad = jnp.transpose(router_grad, (1, 2, 0))
+        const_grad = jnp.swapaxes(const_grad, 2, 3)
     else:
         gate_grad, up_grad, down_grad = (
             jnp.stack([
@@ -1780,14 +1817,15 @@
         qkv_grad, out_grad = (
             lax.psum(lax.psum_scatter(jnp.stack(pair), "dp", scatter_dimension=1, tiled=True), "expert")
             for pair in ((qkv_grad0, qkv_grad1), (out_grad0, out_grad1)))
-    mine = lax.dynamic_slice_in_dim(packed, lax.axis_index("dp") * depth, depth, axis=1)
-    mine = jnp.stack([mine[:24], mine[24:48]])
-    router_grad = jnp.swapaxes(mine[:, :CONST0], 1, 2)
-    const_grad = jnp.swapaxes(mine[:, CONST0:GAIN0].reshape(layers, 2, 2, depth), 2, 3)
-    residual_grad = packed[48 : 48 + CONST0, :CONST0]
+        mine = lax.dynamic_slice_in_dim(packed, lax.axis_index("dp") * depth, depth, axis=1)
+        mine = jnp.stack([mine[:24], mine[24:48]])
+        router_grad = jnp.swapaxes(mine[:, :CONST0], 1, 2)
+        const_grad = jnp.swapaxes(mine[:, CONST0:GAIN0].reshape(layers, 2, 2, depth), 2, 3)
+        residual_grad = packed[48 : 48 + CONST0, :CONST0]
+        gains_grad, vector_grad = mine[:, GAIN0 : GAIN0 + 2], mine[:, VECTOR0 : VECTOR0 + 2]
     return (
-        output, tokens_grad, mine[:, GAIN0 : GAIN0 + 2], jnp.swapaxes(qkv_grad, 1, 2), out_grad, router_grad,
-        residual_grad, const_grad, mine[:, VECTOR0 : VECTOR0 + 2], gate_grad, up_grad, down_grad,
+        output, tokens_grad, gains_grad, jnp.swapaxes(qkv_grad, 1, 2), out_grad, router_grad,
+        residual_grad, const_grad, vector_grad, gate_grad, up_grad, down_grad,
     )
 
 

time: 471 us -> 462 us (0.981)
  Pallas kernels: 459 us -> 450 us
    pallas_call x2, Pallas kernels: 143 us -> 138 us  [expert_backward(): pl.pallas_call(functools.partial(expert_backward_kernel, spread, parts, i...]
where the time goes in v8:
time: 462 us; the launch traced here: 458 us
  Pallas kernels  450 us (97%)
    pallas_call x2, Pallas kernels, expert_backward(): pl.pallas_call(functools.partial(expert_backward_kernel, spread, parts, i...  138 us
    pallas_call x2, Pallas kernels, expert_forward(): pl.pallas_call(functools.partial(expert_forward_kernel, spread, parts, in...  133 us
    pallas_call x1, Pallas kernels, dense_reduce(): pl.pallas_call(functools.partial(dense_reduce_kernel, spread, depths), ou...  65.2 us
    pallas_call x5, Pallas kernels, local_call(): pl.pallas_call(functools.partial(kernel, experts), out_shape=[jax.ShapeDt...  55.1 us
    pallas_call x1, Pallas kernels, dense_gather(): pl.pallas_call(functools.partial(dense_gather_kernel, spread), out_shape=...  48.8 us
    pallas_call x1, Pallas kernels, stack_results(): pl.pallas_call(stack_kernel, out_shape=[struct(a.shape, F32) for a in (qk...  10.3 us
  transfers between devices with their start and end apart: 2, of which 2 were waited for; matrix products, arithmetic and copies ran while one was open for 0% of the time, Pallas kernels for 4%

profile of v8, /device:TPU:0, one launch (start us, length us, event | category | flops | bytes accessed | tf_op | source)
XLA Modules:
  0.0 457.7 jit_solution(15504980104736319632)
XLA Ops:
  0.6 48.8 %shard_map.238 = (bf16[2304,768]{1,0:T(8,128)(2,1)}, bf16[768,768]{1,0:T(8,128)(2,1)}, bf16[768,128]{1,0:T(8,128)(2,1)}, bf16[4,1,144,384]{3,2,1,0:T(8,128)(2,1)...) custom-call(f32[2,288,768]{2,1,0:T(8,128)} %bitcast.15, ...), custom_call_target="tpu_custom_call" | custom-call | flops 10000000000 | bytes 100000000 | tf_op jit(solution)/shard_map/pallas_call | solution.py:1297
  49.4 0.7 collective-permute-start
  50.1 8.6 %shard_map.239 = (bf16[192,768]{1,0:T(8,128)(2,1)}, bf16[192,2304]{1,0:T(8,128)(2,1)}, f32[12,192,192]{2,1,0:T(8,128)}, bf16[192,768]{1,0:T(8,128)(2,1)}, f32[19...) custom-call(bf16[192,768]{1,0:T(8,128)(2,1)} %tokens.3, ...), custom_call_target="tpu_custom_call" | custom-call | flops 10000000000 | bytes 60000000 | tf_op jit(solution)/shard_map/pallas_call | solution.py:371
  58.7 2.3 collective-permute-done.refs_5_
  61.1 0.0 copy-start.1
  61.1 0.7 copy-done.1
  61.8 0.0 copy-start
  61.8 68.3 %shard_map.240 = (bf16[4,2,48,768]{3,2,1,0:T(8,128)(2,1)}, bf16[2,4,4,48,768]{4,3,2,1,0:T(8,128)(2,1)}, f32[4,2,192,512]{3,2,1,0:T(8,128)}, f32[4,2,192,512]{3,2...) custom-call(bf16[4,2,48,768]{3,2,1,0:T(8,128)(2,1)} %bitcast.27, ...), custom_call_target="tpu_custom_call" | custom-call | flops 20000000000 | bytes 200000000 | tf_op jit(solution)/shard_map/pallas_call | solution.py:873
  130.1 0.0 copy-done
  130.1 0.7 collective-permute-start.1
  130.8 9.1 %shard_map.241 = (f32[192,768]{1,0:T(8,128)}, bf16[192,768]{1,0:T(8,128)(2,1)}, bf16[192,2304]{1,0:T(8,128)(2,1)}, f32[12,192,192]{2,1,0:T(8,128)}, bf16[192,768...) custom-call(f32[192,768]{1,0:T(8,128)} %get-tuple-element.118.mid_in.mid0.mid, ...), custom_call_target="tpu_custom_call" | custom-call | flops 10000000000 | bytes 60000000 | tf_op jit(solution)/shard_map/pallas_call | solution.py:371
  139.9 1.0 collective-permute-done.1.refs_5_
  141.0 0.0 copy-start.2
  141.0 0.7 copy-done.2
  141.7 65.1 %shard_map.242 = (bf16[4,2,48,768]{3,2,1,0:T(8,128)(2,1)}, bf16[2,4,4,48,768]{4,3,2,1,0:T(8,128)(2,1)}, f32[4,2,192,512]{3,2,1,0:T(8,128)}, f32[4,2,192,512]{3,2,1,0:T(8,128)}, bf16[2,256,768]{2,1,0:T(8,128)(2,1)}) custom-call(bf16[4,2,48,768]{3,2,1,0:T(8,128)(2,1)} %bitcast.29, bf16[2,768,256]{2,1,0:T(8,128)(2,1)} %get-tuple-element.134.refs_12_.refs_0_.refs_3_, ...), custom_call_target="tpu_custom_call" | custom-call | flops 20000000000 | bytes 200000000 | tf_op jit(solution)/shard_map/pallas_call | solution.py:873
  206.8 5.3 %shard_map.243 = (bf16[192,768]{1,0:T(8,128)(2,1)}, f32[192,128]{1,0:T(8,128)}, f32[192,128]{1,0:T(8,128)}, bf16[384,768]{1,0:T(8,128)(2,1)}, f32[24,768]{1,0:T(8,128)}, /*index=5*/f32[128,128]{1,0:T(8,128)}) custom-call(f32[192,768]{1,0:T(8,128)} %get-tuple-element.142.mid, bf16[768,128]{1,0:T(8,128)(2,1)} %get-tuple-element.138.small, ...), custom_call_target="tpu_custom_call" | custom-call | flops 10000000000 | bytes 60000000 | tf_op jit(solution)/shard_map/pallas_call | solution.py:371
  212.1 70.5 %shard_map.244 = (bf16[4,2,48,768]{3,2,1,0:T(8,128)(2,1)}, f32[2,768,256]{2,1,0:T(8,128)}, f32[2,768,256]{2,1,0:T(8,128)}, bf16[2,768,256]{2,1,0:T(8,128)(2,1)},...) custom-call(bf16[4,2,48,768]{3,2,1,0:T(8,128)(2,1)} %bitcast.28, ...), custom_call_target="tpu_custom_call" | custom-call | flops 40000000000 | bytes 200000000 | tf_op jit(solution)/shard_map/pallas_call | solution.py:904
  282.6 17.9 %shard_map.245 = (bf16[2304,768]{1,0:T(8,128)(2,1)}, bf16[768,768]{1,0:T(8,128)(2,1)}, f32[24,768]{1,0:T(8,128)}, f32[192,768]{1,0:T(8,128)}, f32[192,128]{1,0:T...) custom-call(bf16[192,768]{1,0:T(8,128)(2,1)} %cotangent.3, bf16[384,768]{1,0:T(8,128)(2,1)} %bitcast.26, ...), custom_call_target="tpu_custom_call" | custom-call | flops 10000000000 | bytes 60000000 | tf_op jit(solution)/shard_map/pallas_call | solution.py:371
  300.6 67.2 %shard_map.246 = (bf16[4,2,48,768]{3,2,1,0:T(8,128)(2,1)}, f32[2,768,256]{2,1,0:T(8,128)}, f32[2,768,256]{2,1,0:T(8,128)}, bf16[2,768,256]{2,1,0:T(8,128)(2,1)},...) custom-call(bf16[4,2,48,768]{3,2,1,0:T(8,128)(2,1)} %bitcast.24, ...), custom_call_target="tpu_custom_call" | custom-call | flops 40000000000 | bytes 200000000 | tf_op jit(solution)/shard_map/pallas_call | solution.py:904
  367.8 14.1 %shard_map.247 = (bf16[2304,768]{1,0:T(8,128)(2,1)}, bf16[768,768]{1,0:T(8,128)(2,1)}, f32[24,768]{1,0:T(8,128)}, f32[192,768]{1,0:T(8,128)}) custom-call(f32[192,768]{1,0:T(8,128)} %get-tuple-element.165.grad_in, bf16[384,768]{1,0:T(8,128)(2,1)} %bitcast.25, f32[192,128]{1,0:T(8,128)} %get-tuple-element.176.g_small, ...), custom_call_target="tpu_custom_call" | custom-call | flops 10000000000 | bytes 60000000 | tf_op jit(solution)/shard_map/pallas_call | solution.py:371
  382.0 65.2 %shard_map.248 = (f32[64,768]{1,0:T(8,128)}, f32[2,288,768]{2,1,0:T(8,128)}, f32[2,96,768]{2,1,0:T(8,128)}, bf16[2,768,256]{2,1,0:T(8,128)(2,1)}, bf16[2,256,768]{2,1,0:T(8,128)(2,1)}) custom-call(f32[24,768]{1,0:T(8,128)} %get-tuple-element.183.small0, f32[24,768]{1,0:T(8,128)} %get-tuple-element.184.small1, f32[128,128]{1,0:T(8,128)} %get-tuple-element.185.res, ...), custom_call_target="tpu_custom_call" | custom-call | flops 20000000000 | bytes 200000000 | tf_op jit(solution)/shard_map/pallas_call | solution.py:1641
  447.2 10.3 %shard_map.249 = (f32[2,288,768]{2,1,0:T(8,128)}, f32[2,96,768]{2,1,0:T(8,128)}, f32[2,2,768,256]{3,2,1,0:T(8,128)}, f32[2,2,768,256]{3,2,1,0:T(8,128)}, f32[2,2...) custom-call(f32[64,768]{1,0:T(8,128)} %get-tuple-element.191.small, ...), custom_call_target="tpu_custom_call" | custom-call | flops 10000000 | bytes 30000000 | tf_op jit(solution)/shard_map/pallas_call | solution.py:1693
Async XLA Ops:
  49.4 11.7 %collective-permute-start = (bf16[1,256,768]{2,1,0:T(8,128)(2,1)}, bf16[1,256,768]{2,1,0:T(8,128)(2,1)S(1)}, u32[]{:S(2)}, u32[]{:S(2)}) collective-permute-start(bf16[1,256,768]{2,1,0:T(8,128)(2,1)} %get-tuple-element.127), channel_id=1, source_target_pairs={{4,0},{0,4},{12,8},{8,12},{20,16},{16,20},{28,24},{24,28},{5,1},{1... | collective-permute-start | bytes 1179656 | tf_op jit(solution)/shard_map/ppermute | solution.py:919
  61.1 0.7 copy-start.1
  61.8 68.3 %copy-start = (bf16[1,256,768]{2,1,0:T(8,128)(2,1)S(1)}, bf16[1,256,768]{2,1,0:T(8,128)(2,1)}, u32[]{:S(2)}) copy-start(bf16[1,256,768]{2,1,0:T(8,128)(2,1)} %get-tuple-element.148) | copy-start | bytes 1179652
  130.1 10.8 %collective-permute-start.1 = (bf16[1,256,768]{2,1,0:T(8,128)(2,1)S(1)}, bf16[1,256,768]{2,1,0:T(8,128)(2,1)S(1)}, u32[]{:S(2)}, u32[]{:S(2)}) collective-permute-start(bf16[1,256,768]{2,1,0:T(8,128)(2,1)S(1)} %copy-done), channel_id=1, source_target_pairs={{4,0},{0,4},{12,8},{8,12},{20,16},{16,20},{28,24},{24,28},{5,1},{1... | collective-permute-start | bytes 1179656 | tf_op jit(solution)/shard_map/ppermute | solution.py:919
  141.0 0.7 copy-start.2

commit v9 on v8

--- a/solution.py
+++ b/solution.py
@@ -461,7 +461,7 @@
     def after_first(self):
         pass
 
-    def after_line(self):
+    def in_line(self):
         pass
 
     def after_relay(self):
@@ -597,10 +597,13 @@
             def _():
                 rider.after_first()
 
+            @pl.when(n == 3)
+            def _():
+                rider.in_line()
+
             return carry
 
         lax.fori_loop(0, 6, step, 0)
-        rider.after_line()
 
         def passing(n, carry):
             self.relay(n)
@@ -723,7 +726,7 @@
 
     class Loaded(Rider):
         partners = [p.beside] if late else []
-        after_first, after_line, after_relay = rider.after_first, rider.after_line, rider.after_relay
+        after_first, in_line, after_relay = rider.after_first, rider.in_line, rider.after_relay
 
         def begin(self):
             if late:
@@ -829,8 +832,8 @@
 
     class Loaded(Rider):
         partners = [p.beside] if exchange else []
-        after_first, after_line, after_relay, finish = (
-            rider.after_first, rider.after_line, rider.after_relay, rider.finish)
+        after_first, in_line, after_relay, finish = (
+            rider.after_first, rider.in_line, rider.after_relay, rider.finish)
 
         def begin(self):
             rider.begin()
@@ -1147,7 +1150,7 @@
     def after_first(self):
         pass
 
-    def after_line(self):
+    def in_line(self):
         def body(t):
             s = self.beside_of(t)
             for kind in range(3):
@@ -1415,7 +1418,7 @@
     def after_first(self):
         self.halve.after_first()
 
-    def after_line(self):
+    def in_line(self):
         pass
 
     def after_relay(self):
@@ -1583,11 +1586,11 @@
     sum0 = LineSum(p, depths, mine0, sums0, line0)
     sum1 = LineSum(p, depths, mine1, sums1, line1)
     little = SmallSum(p, small, small_sum, small_refs)
-    weights = [remote(w, came[i], w_send.at[i], w_recv.at[i], p.beside) for i, w in enumerate((up0, down0))]
+    pieces = ((up0, came[0]), (down0.at[0], came[1].at[0]), (down0.at[1], came[1].at[1]))
+    weights = [remote(mine, other, w_send.at[i], w_recv.at[i], p.beside) for i, (mine, other) in enumerate(pieces)]
     greet([p.sibling, p.across, p.beside, little.far], p)
     halve.begin()
-    for copy in weights:
-        copy.start()
+    weights[0].start()
     rows = small0.shape[0]
     small[0:rows, :] = small0[...]
     small[rows : 2 * rows, :] = small1[...]
@@ -1613,13 +1616,15 @@
     arrive(1)
     sum0.relay("far")
     sum1.after_z()
+    weights[1].start()
     arrive(2)
     sum0.relay("near")
+    sum1.after_x()
     sum0.relay("back")
     arrive(3)
     little.step(4)
     sum0.after_z()
-    sum1.after_x()
+    weights[2].start()
     little.step(5)
     sum0.after_x()
     sum1.finish()
@@ -1637,7 +1642,7 @@
     small = (2 * smalls[0].shape[0] + 16, width)
     line = LineSum.scratch(spread, depths, width)
     mine = pltpu.VMEM(quarter1.shape, F32)
-    scratch = [pltpu.VMEM(small, F32), mine, mine, dma(2), dma(2)] + Halve.scratch(spread, depths, width) + line + line
+    scratch = [pltpu.VMEM(small, F32), mine, mine, dma(3), dma(3)] + Halve.scratch(spread, depths, width) + line + line
     return pl.pallas_call(
         functools.partial(dense_reduce_kernel, spread, depths),
         out_shape=[struct(small, F32)] + [struct((2, depth, width), F32) for depth in depths]

time: 462 us -> 461 us (level)
  no operation moved by 1% of the time
where the time goes in v9:
time: 461 us; the launch traced here: 456 us
  Pallas kernels  448 us (97%)
  waiting for transfers between devices  4.67 us (1%)
    pallas_call x2, Pallas kernels, expert_backward(): pl.pallas_call(functools.partial(expert_backward_kernel, spread, parts, i...  137 us
    pallas_call x2, Pallas kernels, expert_forward(): pl.pallas_call(functools.partial(expert_forward_kernel, spread, parts, in...  131 us
    pallas_call x1, Pallas kernels, dense_reduce(): pl.pallas_call(functools.partial(dense_reduce_kernel, spread, depths), ou...  65.3 us
    pallas_call x5, Pallas kernels, local_call(): pl.pallas_call(functools.partial(kernel, experts), out_shape=[jax.ShapeDt...  55.1 us
    pallas_call x1, Pallas kernels, dense_gather(): pl.pallas_call(functools.partial(dense_gather_kernel, spread), out_shape=...  48.8 us
    pallas_call x1, Pallas kernels, stack_results(): pl.pallas_call(stack_kernel, out_shape=[struct(a.shape, F32) for a in (qk...  10.3 us
  transfers between devices with their start and end apart: 2, of which 2 were waited for; matrix products, arithmetic and copies ran while one was open for 0% of the time, Pallas kernels for 4%

profile of v9, /device:TPU:0, one launch (start us, length us, event | category | flops | bytes accessed | tf_op | source)
XLA Modules:
  0.0 455.9 jit_solution(16781775951965787519)
XLA Ops:
  0.6 48.8 %shard_map.238 = (bf16[2304,768]{1,0:T(8,128)(2,1)}, bf16[768,768]{1,0:T(8,128)(2,1)}, bf16[768,128]{1,0:T(8,128)(2,1)}, bf16[4,1,144,384]{3,2,1,0:T(8,128)(2,1)...) custom-call(f32[2,288,768]{2,1,0:T(8,128)} %bitcast.15, ...), custom_call_target="tpu_custom_call" | custom-call | flops 10000000000 | bytes 100000000 | tf_op jit(solution)/shard_map/pallas_call | solution.py:1300
  49.4 0.7 collective-permute-start
  50.1 8.6 %shard_map.239 = (bf16[192,768]{1,0:T(8,128)(2,1)}, bf16[192,2304]{1,0:T(8,128)(2,1)}, f32[12,192,192]{2,1,0:T(8,128)}, bf16[192,768]{1,0:T(8,128)(2,1)}, f32[19...) custom-call(bf16[192,768]{1,0:T(8,128)(2,1)} %tokens.3, ...), custom_call_target="tpu_custom_call" | custom-call | flops 10000000000 | bytes 60000000 | tf_op jit(solution)/shard_map/pallas_call | solution.py:371
  58.7 2.3 collective-permute-done.refs_5_
  61.1 0.0 copy-start.1
  61.1 0.7 copy-done.1
  61.8 0.0 copy-start
  61.8 66.1 %shard_map.240 = (bf16[4,2,48,768]{3,2,1,0:T(8,128)(2,1)}, bf16[2,4,4,48,768]{4,3,2,1,0:T(8,128)(2,1)}, f32[4,2,192,512]{3,2,1,0:T(8,128)}, f32[4,2,192,512]{3,2...) custom-call(bf16[4,2,48,768]{3,2,1,0:T(8,128)(2,1)} %bitcast.27, ...), custom_call_target="tpu_custom_call" | custom-call | flops 20000000000 | bytes 200000000 | tf_op jit(solution)/shard_map/pallas_call | solution.py:876
  128.0 0.0 copy-done
  128.0 0.1 collective-permute-start.1
  128.1 9.1 %shard_map.241 = (f32[192,768]{1,0:T(8,128)}, bf16[192,768]{1,0:T(8,128)(2,1)}, bf16[192,2304]{1,0:T(8,128)(2,1)}, f32[12,192,192]{2,1,0:T(8,128)}, bf16[192,768...) custom-call(f32[192,768]{1,0:T(8,128)} %get-tuple-element.118.mid_in.mid0.mid, ...), custom_call_target="tpu_custom_call" | custom-call | flops 10000000000 | bytes 60000000 | tf_op jit(solution)/shard_map/pallas_call | solution.py:371
  137.2 2.3 collective-permute-done.1.refs_5_
  139.5 0.0 copy-start.2
  139.5 0.7 copy-done.2
  140.2 65.4 %shard_map.242 = (bf16[4,2,48,768]{3,2,1,0:T(8,128)(2,1)}, bf16[2,4,4,48,768]{4,3,2,1,0:T(8,128)(2,1)}, f32[4,2,192,512]{3,2,1,0:T(8,128)}, f32[4,2,192,512]{3,2,1,0:T(8,128)}, bf16[2,256,768]{2,1,0:T(8,128)(2,1)}) custom-call(bf16[4,2,48,768]{3,2,1,0:T(8,128)(2,1)} %bitcast.29, bf16[2,768,256]{2,1,0:T(8,128)(2,1)} %get-tuple-element.134.refs_12_.refs_0_.refs_3_, ...), custom_call_target="tpu_custom_call" | custom-call | flops 20000000000 | bytes 200000000 | tf_op jit(solution)/shard_map/pallas_call | solution.py:876
  205.6 5.3 %shard_map.243 = (bf16[192,768]{1,0:T(8,128)(2,1)}, f32[192,128]{1,0:T(8,128)}, f32[192,128]{1,0:T(8,128)}, bf16[384,768]{1,0:T(8,128)(2,1)}, f32[24,768]{1,0:T(8,128)}, /*index=5*/f32[128,128]{1,0:T(8,128)}) custom-call(f32[192,768]{1,0:T(8,128)} %get-tuple-element.142.mid, bf16[768,128]{1,0:T(8,128)(2,1)} %get-tuple-element.138.small, ...), custom_call_target="tpu_custom_call" | custom-call | flops 10000000000 | bytes 60000000 | tf_op jit(solution)/shard_map/pallas_call | solution.py:371
  210.9 69.4 %shard_map.244 = (bf16[4,2,48,768]{3,2,1,0:T(8,128)(2,1)}, f32[2,768,256]{2,1,0:T(8,128)}, f32[2,768,256]{2,1,0:T(8,128)}, bf16[2,768,256]{2,1,0:T(8,128)(2,1)},...) custom-call(bf16[4,2,48,768]{3,2,1,0:T(8,128)(2,1)} %bitcast.28, ...), custom_call_target="tpu_custom_call" | custom-call | flops 40000000000 | bytes 200000000 | tf_op jit(solution)/shard_map/pallas_call | solution.py:907
  280.3 17.9 %shard_map.245 = (bf16[2304,768]{1,0:T(8,128)(2,1)}, bf16[768,768]{1,0:T(8,128)(2,1)}, f32[24,768]{1,0:T(8,128)}, f32[192,768]{1,0:T(8,128)}, f32[192,128]{1,0:T...) custom-call(bf16[192,768]{1,0:T(8,128)(2,1)} %cotangent.3, bf16[384,768]{1,0:T(8,128)(2,1)} %bitcast.26, ...), custom_call_target="tpu_custom_call" | custom-call | flops 10000000000 | bytes 60000000 | tf_op jit(solution)/shard_map/pallas_call | solution.py:371
  298.2 67.7 %shard_map.246 = (bf16[4,2,48,768]{3,2,1,0:T(8,128)(2,1)}, f32[2,768,256]{2,1,0:T(8,128)}, f32[2,768,256]{2,1,0:T(8,128)}, bf16[2,768,256]{2,1,0:T(8,128)(2,1)},...) custom-call(bf16[4,2,48,768]{3,2,1,0:T(8,128)(2,1)} %bitcast.24, ...), custom_call_target="tpu_custom_call" | custom-call | flops 40000000000 | bytes 200000000 | tf_op jit(solution)/shard_map/pallas_call | solution.py:907
  365.9 14.1 %shard_map.247 = (bf16[2304,768]{1,0:T(8,128)(2,1)}, bf16[768,768]{1,0:T(8,128)(2,1)}, f32[24,768]{1,0:T(8,128)}, f32[192,768]{1,0:T(8,128)}) custom-call(f32[192,768]{1,0:T(8,128)} %get-tuple-element.165.grad_in, bf16[384,768]{1,0:T(8,128)(2,1)} %bitcast.25, f32[192,128]{1,0:T(8,128)} %get-tuple-element.176.g_small, ...), custom_call_target="tpu_custom_call" | custom-call | flops 10000000000 | bytes 60000000 | tf_op jit(solution)/shard_map/pallas_call | solution.py:371
  380.0 65.3 %shard_map.248 = (f32[64,768]{1,0:T(8,128)}, f32[2,288,768]{2,1,0:T(8,128)}, f32[2,96,768]{2,1,0:T(8,128)}, bf16[2,768,256]{2,1,0:T(8,128)(2,1)}, bf16[2,256,768]{2,1,0:T(8,128)(2,1)}) custom-call(f32[24,768]{1,0:T(8,128)} %get-tuple-element.183.small0, f32[24,768]{1,0:T(8,128)} %get-tuple-element.184.small1, f32[128,128]{1,0:T(8,128)} %get-tuple-element.185.res, ...), custom_call_target="tpu_custom_call" | custom-call | flops 20000000000 | bytes 200000000 | tf_op jit(solution)/shard_map/pallas_call | solution.py:1646
  445.4 10.3 %shard_map.249 = (f32[2,288,768]{2,1,0:T(8,128)}, f32[2,96,768]{2,1,0:T(8,128)}, f32[2,2,768,256]{3,2,1,0:T(8,128)}, f32[2,2,768,256]{3,2,1,0:T(8,128)}, f32[2,2...) custom-call(f32[64,768]{1,0:T(8,128)} %get-tuple-element.191.small, ...), custom_call_target="tpu_custom_call" | custom-call | flops 10000000 | bytes 30000000 | tf_op jit(solution)/shard_map/pallas_call | solution.py:1698
Async XLA Ops:
  49.4 11.7 %collective-permute-start = (bf16[1,256,768]{2,1,0:T(8,128)(2,1)}, bf16[1,256,768]{2,1,0:T(8,128)(2,1)S(1)}, u32[]{:S(2)}, u32[]{:S(2)}) collective-permute-start(bf16[1,256,768]{2,1,0:T(8,128)(2,1)} %get-tuple-element.127), channel_id=1, source_target_pairs={{4,0},{0,4},{12,8},{8,12},{20,16},{16,20},{28,24},{24,28},{5,1},{1... | collective-permute-start | bytes 1179656 | tf_op jit(solution)/shard_map/ppermute | solution.py:922
  61.1 0.7 copy-start.1
  61.8 66.1 %copy-start = (bf16[1,256,768]{2,1,0:T(8,128)(2,1)S(1)}, bf16[1,256,768]{2,1,0:T(8,128)(2,1)}, u32[]{:S(2)}) copy-start(bf16[1,256,768]{2,1,0:T(8,128)(2,1)} %get-tuple-element.148) | copy-start | bytes 1179652
  128.0 11.5 %collective-permute-start.1 = (bf16[1,256,768]{2,1,0:T(8,128)(2,1)S(1)}, bf16[1,256,768]{2,1,0:T(8,128)(2,1)S(1)}, u32[]{:S(2)}, u32[]{:S(2)}) collective-permute-start(bf16[1,256,768]{2,1,0:T(8,128)(2,1)S(1)} %copy-done), channel_id=1, source_target_pairs={{4,0},{0,4},{12,8},{8,12},{20,16},{16,20},{28,24},{24,28},{5,1},{1... | collective-permute-start | bytes 1179656 | tf_op jit(solution)/shard_map/ppermute | solution.py:922
  139.5 0.7 copy-start.2

commit v10 on v9

--- a/solution.py
+++ b/solution.py
@@ -1682,7 +1682,7 @@
 
 def stack_results(small, qkv, out, parts, depth):
     flat = [part for kind in parts for layer in kind for part in layer]
-    local, steps = flat[0].shape[0], 2
+    local, steps = flat[0].shape[0], 1
 
     def rows_of(shape, lead=None):
         rows, wide = shape[-2] // steps, shape[-1]

time: 461 us -> 461 us (level)
  no operation moved by 1% of the time
where the time goes in v10:
time: 461 us; the launch traced here: 456 us
  Pallas kernels  448 us (97%)
  waiting for transfers between devices  4.67 us (1%)
    pallas_call x2, Pallas kernels, expert_backward(): pl.pallas_call(functools.partial(expert_backward_kernel, spread, parts, i...  137 us
    pallas_call x2, Pallas kernels, expert_forward(): pl.pallas_call(functools.partial(expert_forward_kernel, spread, parts, in...  131 us
    pallas_call x1, Pallas kernels, dense_reduce(): pl.pallas_call(functools.partial(dense_reduce_kernel, spread, depths), ou...  65.3 us
    pallas_call x5, Pallas kernels, local_call(): pl.pallas_call(functools.partial(kernel, experts), out_shape=[jax.ShapeDt...  55.1 us
    pallas_call x1, Pallas kernels, dense_gather(): pl.pallas_call(functools.partial(dense_gather_kernel, spread), out_shape=...  48.8 us
    pallas_call x1, Pallas kernels, stack_results(): pl.pallas_call(stack_kernel, out_shape=[struct(a.shape, F32) for a in (qk...  10.2 us
  transfers between devices with their start and end apart: 2, of which 2 were waited for; matrix products, arithmetic and copies ran while one was open for 0% of the time, Pallas kernels for 4%

profile of v10, /device:TPU:0, one launch (start us, length us, event | category | flops | bytes accessed | tf_op | source)
XLA Modules:
  0.0 455.7 jit_solution(12335257563095745752)
XLA Ops:
  0.6 48.8 %shard_map.238 = (bf16[2304,768]{1,0:T(8,128)(2,1)}, bf16[768,768]{1,0:T(8,128)(2,1)}, bf16[768,128]{1,0:T(8,128)(2,1)}, bf16[4,1,144,384]{3,2,1,0:T(8,128)(2,1)...) custom-call(f32[2,288,768]{2,1,0:T(8,128)} %bitcast.15, ...), custom_call_target="tpu_custom_call" | custom-call | flops 10000000000 | bytes 100000000 | tf_op jit(solution)/shard_map/pallas_call | solution.py:1300
  49.4 0.7 collective-permute-start
  50.1 8.6 %shard_map.239 = (bf16[192,768]{1,0:T(8,128)(2,1)}, bf16[192,2304]{1,0:T(8,128)(2,1)}, f32[12,192,192]{2,1,0:T(8,128)}, bf16[192,768]{1,0:T(8,128)(2,1)}, f32[19...) custom-call(bf16[192,768]{1,0:T(8,128)(2,1)} %tokens.3, ...), custom_call_target="tpu_custom_call" | custom-call | flops 10000000000 | bytes 60000000 | tf_op jit(solution)/shard_map/pallas_call | solution.py:371
  58.7 2.3 collective-permute-done.refs_5_
  61.1 0.0 copy-start.1
  61.1 0.7 copy-done.1
  61.8 0.0 copy-start
  61.8 66.1 %shard_map.240 = (bf16[4,2,48,768]{3,2,1,0:T(8,128)(2,1)}, bf16[2,4,4,48,768]{4,3,2,1,0:T(8,128)(2,1)}, f32[4,2,192,512]{3,2,1,0:T(8,128)}, f32[4,2,192,512]{3,2...) custom-call(bf16[4,2,48,768]{3,2,1,0:T(8,128)(2,1)} %bitcast.27, ...), custom_call_target="tpu_custom_call" | custom-call | flops 20000000000 | bytes 200000000 | tf_op jit(solution)/shard_map/pallas_call | solution.py:876
  128.0 0.0 copy-done
  128.0 0.1 collective-permute-start.1
  128.1 9.1 %shard_map.241 = (f32[192,768]{1,0:T(8,128)}, bf16[192,768]{1,0:T(8,128)(2,1)}, bf16[192,2304]{1,0:T(8,128)(2,1)}, f32[12,192,192]{2,1,0:T(8,128)}, bf16[192,768...) custom-call(f32[192,768]{1,0:T(8,128)} %get-tuple-element.118.mid_in.mid0.mid, ...), custom_call_target="tpu_custom_call" | custom-call | flops 10000000000 | bytes 60000000 | tf_op jit(solution)/shard_map/pallas_call | solution.py:371
  137.2 2.3 collective-permute-done.1.refs_5_
  139.5 0.0 copy-start.2
  139.5 0.7 copy-done.2
  140.2 65.4 %shard_map.242 = (bf16[4,2,48,768]{3,2,1,0:T(8,128)(2,1)}, bf16[2,4,4,48,768]{4,3,2,1,0:T(8,128)(2,1)}, f32[4,2,192,512]{3,2,1,0:T(8,128)}, f32[4,2,192,512]{3,2,1,0:T(8,128)}, bf16[2,256,768]{2,1,0:T(8,128)(2,1)}) custom-call(bf16[4,2,48,768]{3,2,1,0:T(8,128)(2,1)} %bitcast.29, bf16[2,768,256]{2,1,0:T(8,128)(2,1)} %get-tuple-element.134.refs_12_.refs_0_.refs_3_, ...), custom_call_target="tpu_custom_call" | custom-call | flops 20000000000 | bytes 200000000 | tf_op jit(solution)/shard_map/pallas_call | solution.py:876
  205.6 5.3 %shard_map.243 = (bf16[192,768]{1,0:T(8,128)(2,1)}, f32[192,128]{1,0:T(8,128)}, f32[192,128]{1,0:T(8,128)}, bf16[384,768]{1,0:T(8,128)(2,1)}, f32[24,768]{1,0:T(8,128)}, /*index=5*/f32[128,128]{1,0:T(8,128)}) custom-call(f32[192,768]{1,0:T(8,128)} %get-tuple-element.142.mid, bf16[768,128]{1,0:T(8,128)(2,1)} %get-tuple-element.138.small, ...), custom_call_target="tpu_custom_call" | custom-call | flops 10000000000 | bytes 60000000 | tf_op jit(solution)/shard_map/pallas_call | solution.py:371
  210.9 69.4 %shard_map.244 = (bf16[4,2,48,768]{3,2,1,0:T(8,128)(2,1)}, f32[2,768,256]{2,1,0:T(8,128)}, f32[2,768,256]{2,1,0:T(8,128)}, bf16[2,768,256]{2,1,0:T(8,128)(2,1)},...) custom-call(bf16[4,2,48,768]{3,2,1,0:T(8,128)(2,1)} %bitcast.28, ...), custom_call_target="tpu_custom_call" | custom-call | flops 40000000000 | bytes 200000000 | tf_op jit(solution)/shard_map/pallas_call | solution.py:907
  280.3 17.9 %shard_map.245 = (bf16[2304,768]{1,0:T(8,128)(2,1)}, bf16[768,768]{1,0:T(8,128)(2,1)}, f32[24,768]{1,0:T(8,128)}, f32[192,768]{1,0:T(8,128)}, f32[192,128]{1,0:T...) custom-call(bf16[192,768]{1,0:T(8,128)(2,1)} %cotangent.3, bf16[384,768]{1,0:T(8,128)(2,1)} %bitcast.26, ...), custom_call_target="tpu_custom_call" | custom-call | flops 10000000000 | bytes 60000000 | tf_op jit(solution)/shard_map/pallas_call | solution.py:371
  298.2 67.7 %shard_map.246 = (bf16[4,2,48,768]{3,2,1,0:T(8,128)(2,1)}, f32[2,768,256]{2,1,0:T(8,128)}, f32[2,768,256]{2,1,0:T(8,128)}, bf16[2,768,256]{2,1,0:T(8,128)(2,1)},...) custom-call(bf16[4,2,48,768]{3,2,1,0:T(8,128)(2,1)} %bitcast.24, ...), custom_call_target="tpu_custom_call" | custom-call | flops 40000000000 | bytes 200000000 | tf_op jit(solution)/shard_map/pallas_call | solution.py:907
  365.9 14.1 %shard_map.247 = (bf16[2304,768]{1,0:T(8,128)(2,1)}, bf16[768,768]{1,0:T(8,128)(2,1)}, f32[24,768]{1,0:T(8,128)}, f32[192,768]{1,0:T(8,128)}) custom-call(f32[192,768]{1,0:T(8,128)} %get-tuple-element.165.grad_in, bf16[384,768]{1,0:T(8,128)(2,1)} %bitcast.25, f32[192,128]{1,0:T(8,128)} %get-tuple-element.176.g_small, ...), custom_call_target="tpu_custom_call" | custom-call | flops 10000000000 | bytes 60000000 | tf_op jit(solution)/shard_map/pallas_call | solution.py:371
  380.0 65.3 %shard_map.248 = (f32[64,768]{1,0:T(8,128)}, f32[2,288,768]{2,1,0:T(8,128)}, f32[2,96,768]{2,1,0:T(8,128)}, bf16[2,768,256]{2,1,0:T(8,128)(2,1)}, bf16[2,256,768]{2,1,0:T(8,128)(2,1)}) custom-call(f32[24,768]{1,0:T(8,128)} %get-tuple-element.183.small0, f32[24,768]{1,0:T(8,128)} %get-tuple-element.184.small1, f32[128,128]{1,0:T(8,128)} %get-tuple-element.185.res, ...), custom_call_target="tpu_custom_call" | custom-call | flops 20000000000 | bytes 200000000 | tf_op jit(solution)/shard_map/pallas_call | solution.py:1646
  445.4 10.2 %shard_map.249 = (f32[2,288,768]{2,1,0:T(8,128)}, f32[2,96,768]{2,1,0:T(8,128)}, f32[2,2,768,256]{3,2,1,0:T(8,128)}, f32[2,2,768,256]{3,2,1,0:T(8,128)}, f32[2,2...) custom-call(f32[64,768]{1,0:T(8,128)} %get-tuple-element.191.small, ...), custom_call_target="tpu_custom_call" | custom-call | flops 10000000 | bytes 30000000 | tf_op jit(solution)/shard_map/pallas_call | solution.py:1698
Async XLA Ops:
  49.4 11.7 %collective-permute-start = (bf16[1,256,768]{2,1,0:T(8,128)(2,1)}, bf16[1,256,768]{2,1,0:T(8,128)(2,1)S(1)}, u32[]{:S(2)}, u32[]{:S(2)}) collective-permute-start(bf16[1,256,768]{2,1,0:T(8,128)(2,1)} %get-tuple-element.127), channel_id=1, source_target_pairs={{4,0},{0,4},{12,8},{8,12},{20,16},{16,20},{28,24},{24,28},{5,1},{1... | collective-permute-start | bytes 1179656 | tf_op jit(solution)/shard_map/ppermute | solution.py:922
  61.1 0.7 copy-start.1
  61.8 66.1 %copy-start = (bf16[1,256,768]{2,1,0:T(8,128)(2,1)S(1)}, bf16[1,256,768]{2,1,0:T(8,128)(2,1)}, u32[]{:S(2)}) copy-start(bf16[1,256,768]{2,1,0:T(8,128)(2,1)} %get-tuple-element.148) | copy-start | bytes 1179652
  128.0 11.5 %collective-permute-start.1 = (bf16[1,256,768]{2,1,0:T(8,128)(2,1)S(1)}, bf16[1,256,768]{2,1,0:T(8,128)(2,1)S(1)}, u32[]{:S(2)}, u32[]{:S(2)}) collective-permute-start(bf16[1,256,768]{2,1,0:T(8,128)(2,1)S(1)} %copy-done), channel_id=1, source_target_pairs={{4,0},{0,4},{12,8},{8,12},{20,16},{16,20},{28,24},{24,28},{5,1},{1... | collective-permute-start | bytes 1179656 | tf_op jit(solution)/shard_map/ppermute | solution.py:922
  139.5 0.7 copy-start.2
